TPU v7x, 32 devices: a whole 2x2x4 slice. The times are simulated.
32 devices in a mesh: dp: 8 (over z, x), mp: 4 (over y, core).
Axes of the slice: x: 2, y: 2, z: 4, core: 2. Of those that a mesh axis runs over, the one named last changes fastest.
Arguments:
- image_in: bfloat16 [32, 1024, 512], P('dp', None, 'mp'), may hold values from -6 to 6
- out_cotangent: bfloat16 [32, 1024, 512], P('dp', None, 'mp'), may hold values from -6 to 6
- timesteps: int32 [32], P('dp'), may hold values from 0 to 999
- clip_embed: bfloat16 [32, 2048], P('dp'), may hold values from -6 to 6
- context_tokens: bfloat16 [32, 4, 2048], P('dp'), may hold values from -6 to 6
- image_count: int32 [8], P('dp'), may hold values from 1 to 4, as said below
- norm1_gain: float32 [512], P('mp'), may hold values from 0.5 to 1.5
- norm1_bias: float32 [512], P('mp'), may hold values from -3 to 3
- conv1_weight: bfloat16 [3, 3, 512, 512], P(None, None, None, 'mp'), may hold values from -0.09375 to 0.09375
- embed_weight: bfloat16 [2048, 2, 512], P(None, None, 'mp'), may hold values from -0.125 to 0.125
- norm2_gain: float32 [512], P('mp'), may hold values from 0.5 to 1.5
- norm2_bias: float32 [512], P('mp'), may hold values from -3 to 3
- conv2_weight: bfloat16 [3, 3, 512, 512], P(None, None, None, 'mp'), may hold values from -0.09375 to 0.09375
- conv2_bias: float32 [512], P('mp'), may hold values from -3 to 3
- norm3_gain: float32 [512], P('mp'), may hold values from 0.5 to 1.5
- norm3_bias: float32 [512], P('mp'), may hold values from -3 to 3
- qkv_weight: bfloat16 [512, 3, 512], P(None, None, 'mp'), may hold values from -0.375 to 0.375
- context_weight: bfloat16 [2048, 2, 512], P(None, None, 'mp'), may hold values from -0.1875 to 0.1875
- proj_weight: bfloat16 [512, 512], P('mp'), may hold values from -1 to 1
Outputs:
- block_out: bfloat16 [32, 1024, 512], P('dp', None, 'mp')
- image_grad: bfloat16 [32, 1024, 512], P('dp', None, 'mp')
- norm1_gain_grad: float32 [512], P('mp')
- norm1_bias_grad: float32 [512], P('mp')
- conv1_grad: float32 [3, 3, 512, 512], P(None, None, None, 'mp')
- embed_grad: float32 [2048, 2, 512], P(None, None, 'mp')
- norm2_gain_grad: float32 [512], P('mp')
- norm2_bias_grad: float32 [512], P('mp')
- conv2_grad: float32 [3, 3, 512, 512], P(None, None, None, 'mp')
- conv2_bias_grad: float32 [512], P('mp')
- norm3_gain_grad: float32 [512], P('mp')
- norm3_bias_grad: float32 [512], P('mp')
- qkv_grad: float32 [512, 3, 512], P(None, None, 'mp')
- context_grad: float32 [2048, 2, 512], P(None, None, 'mp')
- proj_grad: float32 [512, 512], P('mp')
Inputs may be any that keep to these rules, and one draw needn't show every extreme that they name: `image_count`: the live images of a group fill its first slots; counts rise along the groups with a jitter of one, and the last group holds exactly 4.
All inputs are finite; a program needn't handle non-finite values.
Results may differ from a plain program's by a relative error of at most 0.039.
Values may be sent and summed in bfloat16 or wider, within the bound.
No kernel may reach another device: no remote copies, remote signals or barrier semaphores. Data moves between devices by JAX's collectives and lax.ppermute only.
A program may use at most 128 MiB of HBM per device.

v0:
```python
import math

import jax
import jax.numpy as jnp
from jax import lax
from jax.sharding import PartitionSpec as P

C = 512
GROUPS = 32
HEAD = 64
EMB = 2048
CTX = 4
SIDE = 32
QBLOCK = 512


EPSILON = 1e-05
HIGHEST = lax.Precision.HIGHEST


def silu_grad(before, grad_out):
    sigmoid_value = jax.nn.sigmoid(before)
    return grad_out * sigmoid_value * (1.0 + before * (1.0 - sigmoid_value))


def norm_stats(values):
    row_count, channels = values.shape
    per_group = C // GROUPS
    grouped = values.reshape(row_count, channels // per_group, per_group)
    center = jnp.mean(grouped, axis=(0, 2), keepdims=True)
    spread = jnp.mean(jnp.square(grouped - center), axis=(0, 2), keepdims=True)
    inverse = lax.rsqrt(spread + EPSILON)
    normed = ((grouped - center) * inverse).reshape(row_count, channels)
    return (normed, inverse)


def norm_back(normed, inverse, gain, grad_out):
    row_count, channels = normed.shape
    per_group = C // GROUPS
    grad_normed = (grad_out * gain).reshape(row_count, channels // per_group, per_group)
    shaped = normed.reshape(row_count, channels // per_group, per_group)
    first_term = jnp.mean(grad_normed, axis=(0, 2), keepdims=True)
    second_term = jnp.mean(grad_normed * shaped, axis=(0, 2), keepdims=True)
    grad_in = inverse * (grad_normed - first_term - shaped * second_term)
    return (
        grad_in.reshape(row_count, channels),
        jnp.sum(grad_out * normed, axis=0),
        jnp.sum(grad_out, axis=0),
    )


def patches(field):
    channels = field.shape[1]
    grid = field.reshape(SIDE, SIDE, channels)
    padded = jnp.pad(grid, ((1, 1), (1, 1), (0, 0)))
    windows = [
        padded[tap_row : tap_row + SIDE, tap_col : tap_col + SIDE]
        for tap_row in range(3)
        for tap_col in range(3)
    ]
    return jnp.concatenate(windows, axis=2).reshape(SIDE * SIDE, 9 * channels)


def flipped(weight):
    turned = jnp.transpose(weight[::-1, ::-1], (0, 1, 3, 2))
    return turned.reshape(9 * weight.shape[3], weight.shape[2])


def contract_rows(left, right):
    return lax.dot_general(
        left, right, (((0,), (0,)), ((), ())), preferred_element_type=jnp.float32
    )


def contract_cols(left, right):
    return lax.dot_general(
        left, right, (((1,), (1,)), ((), ())), preferred_element_type=jnp.float32
    )


def attention_forward(query, key_pix, value_pix, key_ctx, value_ctx, head_scale):
    pixels, local_width = query.shape
    head_count = local_width // HEAD
    query_heads = query.reshape(pixels, head_count, HEAD)
    key_heads = key_pix.reshape(pixels, head_count, HEAD)
    value_heads = value_pix.reshape(pixels, head_count, HEAD)
    ctx_keys = key_ctx.reshape(CTX, head_count, HEAD)
    ctx_values = value_ctx.reshape(CTX, head_count, HEAD)
    outputs = []
    log_sums = []
    for block_start in range(0, pixels, QBLOCK):
        block_query = query_heads[block_start : block_start + QBLOCK]
        raw_pix = jnp.einsum(
            "qhd,khd->hqk", block_query, key_heads, preferred_element_type=jnp.float32
        )
        raw_ctx = jnp.einsum(
            "qhd,khd->hqk", block_query, ctx_keys, preferred_element_type=jnp.float32
        )
        top_score = jnp.maximum(jnp.max(raw_pix, axis=2), jnp.max(raw_ctx, axis=2)) * head_scale
        exp_pix = jnp.exp(raw_pix * head_scale - top_score[:, :, None])
        exp_ctx = jnp.exp(raw_ctx * head_scale - top_score[:, :, None])
        denominator = jnp.sum(exp_pix, axis=2) + jnp.sum(exp_ctx, axis=2)
        reciprocal = 1.0 / denominator
        probs_pix = (exp_pix * reciprocal[:, :, None]).astype(jnp.bfloat16)
        probs_ctx = (exp_ctx * reciprocal[:, :, None]).astype(jnp.bfloat16)
        mixed = jnp.einsum(
            "hqk,khd->qhd", probs_pix, value_heads, preferred_element_type=jnp.float32
        )
        mixed = mixed + jnp.einsum(
            "hqk,khd->qhd", probs_ctx, ctx_values, preferred_element_type=jnp.float32
        )
        outputs.append(mixed.reshape(QBLOCK, local_width))
        log_sums.append(top_score + jnp.log(denominator))
    return (
        jnp.concatenate(outputs, axis=0).astype(jnp.bfloat16),
        jnp.concatenate(log_sums, axis=1),
    )


def attention_backward(
    query, key_pix, value_pix, key_ctx, value_ctx, grad_mixed, log_sums, head_scale
):
    pixels, local_width = query.shape
    head_count = local_width // HEAD
    query_heads = query.reshape(pixels, head_count, HEAD)
    key_heads = key_pix.reshape(pixels, head_count, HEAD)
    value_heads = value_pix.reshape(pixels, head_count, HEAD)
    ctx_keys = key_ctx.reshape(CTX, head_count, HEAD)
    ctx_values = value_ctx.reshape(CTX, head_count, HEAD)
    grad_heads = grad_mixed.reshape(pixels, head_count, HEAD)
    grad_key = jnp.zeros((pixels, head_count, HEAD), jnp.float32)
    grad_value = jnp.zeros((pixels, head_count, HEAD), jnp.float32)
    grad_ctx_key = jnp.zeros((CTX, head_count, HEAD), jnp.float32)
    grad_ctx_value = jnp.zeros((CTX, head_count, HEAD), jnp.float32)
    grad_queries = []
    for block_start in range(0, pixels, QBLOCK):
        block_query = query_heads[block_start : block_start + QBLOCK]
        block_grad = grad_heads[block_start : block_start + QBLOCK]
        block_sums = log_sums[:, block_start : block_start + QBLOCK, None]
        raw_pix = jnp.einsum(
            "qhd,khd->hqk", block_query, key_heads, preferred_element_type=jnp.float32
        )
        raw_ctx = jnp.einsum(
            "qhd,khd->hqk", block_query, ctx_keys, preferred_element_type=jnp.float32
        )
        probs_pix = jnp.exp(raw_pix * head_scale - block_sums)
        probs_ctx = jnp.exp(raw_ctx * head_scale - block_sums)
        rounded_pix = probs_pix.astype(jnp.bfloat16)
        rounded_ctx = probs_ctx.astype(jnp.bfloat16)
        grad_value = grad_value + jnp.einsum(
            "hqk,qhd->khd", rounded_pix, block_grad, preferred_element_type=jnp.float32
        )
        grad_ctx_value = grad_ctx_value + jnp.einsum(
            "hqk,qhd->khd", rounded_ctx, block_grad, preferred_element_type=jnp.float32
        )
        weight_pix = jnp.einsum(
            "qhd,khd->hqk", block_grad, value_heads, preferred_element_type=jnp.float32
        )
        weight_ctx = jnp.einsum(
            "qhd,khd->hqk", block_grad, ctx_values, preferred_element_type=jnp.float32
        )
        inner_sum = jnp.sum(probs_pix * weight_pix, axis=2) + jnp.sum(
            probs_ctx * weight_ctx, axis=2
        )
        score_pix = (probs_pix * (weight_pix - inner_sum[:, :, None]) * head_scale).astype(
            jnp.bfloat16
        )
        score_ctx = (probs_ctx * (weight_ctx - inner_sum[:, :, None]) * head_scale).astype(
            jnp.bfloat16
        )
        block_dq = jnp.einsum(
            "hqk,khd->qhd", score_pix, key_heads, preferred_element_type=jnp.float32
        )
        block_dq = block_dq + jnp.einsum(
            "hqk,khd->qhd", score_ctx, ctx_keys, preferred_element_type=jnp.float32
        )
        grad_queries.append(block_dq.reshape(QBLOCK, local_width))
        grad_key = grad_key + jnp.einsum(
            "hqk,qhd->khd", score_pix, block_query, preferred_element_type=jnp.float32
        )
        grad_ctx_key = grad_ctx_key + jnp.einsum(
            "hqk,qhd->khd", score_ctx, block_query, preferred_element_type=jnp.float32
        )
    grad_query = jnp.concatenate(grad_queries, axis=0).astype(jnp.bfloat16)
    grad_qkv = jnp.concatenate(
        [
            grad_query,
            grad_key.reshape(pixels, local_width).astype(jnp.bfloat16),
            grad_value.reshape(pixels, local_width).astype(jnp.bfloat16),
        ],
        axis=1,
    )
    grad_ctx = jnp.concatenate(
        [
            grad_ctx_key.reshape(CTX, local_width).astype(jnp.bfloat16),
            grad_ctx_value.reshape(CTX, local_width).astype(jnp.bfloat16),
        ],
        axis=1,
    )
    return (grad_qkv, grad_ctx)


def local(
    image_in,
    out_cotangent,
    timesteps,
    clip_embed,
    context_tokens,
    image_count,
    norm1_gain,
    norm1_bias,
    conv1_weight,
    embed_weight,
    norm2_gain,
    norm2_bias,
    conv2_weight,
    conv2_bias,
    norm3_gain,
    norm3_bias,
    qkv_weight,
    context_weight,
    proj_weight,
):
    slot_count, pixels, local_width = image_in.shape
    full_width = local_width * lax.axis_size("mp")
    head_scale = 1.0 / math.sqrt(HEAD)
    live_count = image_count[0]
    count_value = image_count.astype(jnp.float32)[0]
    image_total = lax.psum(count_value, "dp")
    half_width = EMB // 2
    frequency = jnp.exp(-math.log(10000.0) * jnp.arange(half_width, dtype=jnp.float32) / half_width)
    angles = timesteps.astype(jnp.float32)[:, None] * frequency[None, :]
    condition = jax.nn.silu(
        jnp.concatenate([jnp.cos(angles), jnp.sin(angles)], axis=1) + clip_embed.astype(jnp.float32)
    ).astype(jnp.bfloat16)
    scale_shift_all = jnp.dot(
        condition, embed_weight.reshape(EMB, 2 * local_width), preferred_element_type=jnp.float32
    )
    conv1_flat = conv1_weight.reshape(9 * full_width, local_width)
    conv2_flat = conv2_weight.reshape(9 * full_width, local_width)
    qkv_flat = qkv_weight.reshape(full_width, 3 * local_width)
    context_flat = context_weight.reshape(context_weight.shape[0], 2 * local_width)
    conv1_back = flipped(conv1_weight)
    conv2_back = flipped(conv2_weight)

    def gather_features(field):
        return lax.all_gather(field, "mp", axis=1, tiled=True)

    def partial_grads(terms):
        return lax.psum_scatter(
            terms.astype(jnp.bfloat16), "mp", scatter_dimension=1, tiled=True
        ).astype(jnp.float32)

    def conv_input_grad(grad_low, back_weight):
        return partial_grads(
            jnp.dot(patches(grad_low), back_weight, preferred_element_type=jnp.float32)
        )

    def one_image(slot_index, carry):
        (
            block_buffer,
            grad_buffer,
            gain1_sum,
            bias1_sum,
            conv1_sum,
            gain2_sum,
            bias2_sum,
            conv2_sum,
            cbias_sum,
            gain3_sum,
            bias3_sum,
            qkv_sum,
            proj_sum,
            shift_buffer,
            context_buffer,
        ) = carry
        alive = (slot_index < live_count).astype(jnp.float32)
        image = lax.dynamic_index_in_dim(image_in, slot_index, 0, keepdims=False).astype(
            jnp.float32
        )
        cot_raw = lax.dynamic_index_in_dim(out_cotangent, slot_index, 0, keepdims=False)
        cot_low = cot_raw * alive.astype(jnp.bfloat16)
        scale_shift = lax.dynamic_index_in_dim(scale_shift_all, slot_index, 0, keepdims=False)
        context = lax.dynamic_index_in_dim(context_tokens, slot_index, 0, keepdims=False)
        scale_part = scale_shift[:local_width]
        shift_part = scale_shift[local_width:]
        normed1, inverse1 = norm_stats(image)
        before1 = normed1 * norm1_gain + norm1_bias
        first_all = gather_features(jax.nn.silu(before1).astype(jnp.bfloat16))
        first_cols = patches(first_all)
        inner = jnp.dot(first_cols, conv1_flat, preferred_element_type=jnp.float32)
        normed2, inverse2 = norm_stats(inner)
        shaped2 = normed2 * norm2_gain + norm2_bias
        modulated = shaped2 * (1.0 + scale_part) + shift_part
        second_all = gather_features(jax.nn.silu(modulated).astype(jnp.bfloat16))
        second_cols = patches(second_all)
        branch = jnp.dot(second_cols, conv2_flat, preferred_element_type=jnp.float32) + conv2_bias
        middle = image + branch
        normed3, inverse3 = norm_stats(middle)
        attn_all = gather_features((normed3 * norm3_gain + norm3_bias).astype(jnp.bfloat16))
        qkv_low = jnp.dot(attn_all, qkv_flat, preferred_element_type=jnp.float32).astype(
            jnp.bfloat16
        )
        ctx_low = jnp.dot(context, context_flat, preferred_element_type=jnp.float32).astype(
            jnp.bfloat16
        )
        query = qkv_low[:, :local_width]
        key_pix = qkv_low[:, local_width : 2 * local_width]
        value_pix = qkv_low[:, 2 * local_width :]
        key_ctx = ctx_low[:, :local_width]
        value_ctx = ctx_low[:, local_width:]
        mixed, log_sums = attention_forward(
            query, key_pix, value_pix, key_ctx, value_ctx, head_scale
        )
        proj_out = lax.psum_scatter(
            jnp.dot(mixed, proj_weight, preferred_element_type=jnp.float32).astype(jnp.bfloat16),
            "mp",
            scatter_dimension=1,
            tiled=True,
        ).astype(jnp.float32)
        result = ((middle + proj_out) * alive).astype(jnp.bfloat16)
        cot_all = lax.all_gather(cot_low, "mp", axis=1, tiled=True)
        grad_mixed = contract_cols(cot_all, proj_weight).astype(jnp.bfloat16)
        proj_term = contract_rows(mixed, cot_all)
        grad_qkv, grad_ctx = attention_backward(
            query, key_pix, value_pix, key_ctx, value_ctx, grad_mixed, log_sums, head_scale
        )
        qkv_term = contract_rows(attn_all, grad_qkv)
        attn_grad = partial_grads(contract_cols(grad_qkv, qkv_flat))
        back3, gain3_term, bias3_term = norm_back(normed3, inverse3, norm3_gain, attn_grad)
        grad_middle = cot_low.astype(jnp.float32) + back3
        grad_branch = grad_middle.astype(jnp.bfloat16)
        cbias_term = jnp.sum(grad_branch.astype(jnp.float32), axis=0)
        conv2_term = contract_rows(second_cols, grad_branch)
        grad_second = conv_input_grad(grad_branch, conv2_back)
        grad_modulated = silu_grad(modulated, grad_second)
        scale_term = jnp.sum(grad_modulated * shaped2, axis=0)
        shift_term = jnp.sum(grad_modulated, axis=0)
        back2, gain2_term, bias2_term = norm_back(
            normed2, inverse2, norm2_gain, grad_modulated * (1.0 + scale_part)
        )
        grad_inner = back2.astype(jnp.bfloat16)
        conv1_term = contract_rows(first_cols, grad_inner)
        grad_first = conv_input_grad(grad_inner, conv1_back)
        back1, gain1_term, bias1_term = norm_back(
            normed1, inverse1, norm1_gain, silu_grad(before1, grad_first)
        )
        input_grad = (grad_middle + back1).astype(jnp.bfloat16)
        block_buffer = lax.dynamic_update_index_in_dim(block_buffer, result, slot_index, 0)
        grad_buffer = lax.dynamic_update_index_in_dim(grad_buffer, input_grad, slot_index, 0)
        shift_buffer = lax.dynamic_update_index_in_dim(
            shift_buffer, jnp.concatenate([scale_term, shift_term]), slot_index, 0
        )
        context_buffer = lax.dynamic_update_index_in_dim(context_buffer, grad_ctx, slot_index, 0)
        return (
            block_buffer,
            grad_buffer,
            gain1_sum + gain1_term,
            bias1_sum + bias1_term,
            conv1_sum + conv1_term,
            gain2_sum + gain2_term,
            bias2_sum + bias2_term,
            conv2_sum + conv2_term,
            cbias_sum + cbias_term,
            gain3_sum + gain3_term,
            bias3_sum + bias3_term,
            qkv_sum + qkv_term,
            proj_sum + proj_term,
            shift_buffer,
            context_buffer,
        )

    vector_zero = jnp.zeros((local_width,), jnp.float32)
    initial = (
        jnp.zeros(image_in.shape, jnp.bfloat16),
        jnp.zeros(image_in.shape, jnp.bfloat16),
        vector_zero,
        vector_zero,
        jnp.zeros((9 * full_width, local_width), jnp.float32),
        vector_zero,
        vector_zero,
        jnp.zeros((9 * full_width, local_width), jnp.float32),
        vector_zero,
        vector_zero,
        vector_zero,
        jnp.zeros((full_width, 3 * local_width), jnp.float32),
        jnp.zeros((local_width, full_width), jnp.float32),
        jnp.zeros((slot_count, 2 * local_width), jnp.float32),
        jnp.zeros((slot_count, CTX, 2 * local_width), jnp.bfloat16),
    )
    (
        block_out,
        image_grad,
        gain1_sum,
        bias1_sum,
        conv1_sum,
        gain2_sum,
        bias2_sum,
        conv2_sum,
        cbias_sum,
        gain3_sum,
        bias3_sum,
        qkv_sum,
        proj_sum,
        shift_buffer,
        context_buffer,
    ) = lax.fori_loop(0, slot_count, one_image, initial)
    embed_sum = lax.dot_general(
        condition.astype(jnp.float32),
        shift_buffer,
        (((0,), (0,)), ((), ())),
        precision=HIGHEST,
        preferred_element_type=jnp.float32,
    )
    context_sum = contract_rows(
        context_tokens.reshape(slot_count * CTX, context_tokens.shape[2]),
        context_buffer.reshape(slot_count * CTX, 2 * local_width),
    )
    conv1_sum = conv1_sum.reshape(3, 3, full_width, local_width)
    conv2_sum = conv2_sum.reshape(3, 3, full_width, local_width)
    embed_sum = embed_sum.reshape(EMB, 2, local_width)
    qkv_sum = qkv_sum.reshape(full_width, 3, local_width)
    context_sum = context_sum.reshape(context_tokens.shape[2], 2, local_width)
    finals = lax.psum(
        (
            gain1_sum / image_total,
            bias1_sum / image_total,
            conv1_sum / image_total,
            embed_sum / image_total,
            gain2_sum / image_total,
            bias2_sum / image_total,
            conv2_sum / image_total,
            cbias_sum / image_total,
            gain3_sum / image_total,
            bias3_sum / image_total,
            qkv_sum / image_total,
            context_sum / image_total,
            proj_sum / image_total,
        ),
        "dp",
    )
    return (
        block_out,
        image_grad,
        finals[0],
        finals[1],
        finals[2],
        finals[3],
        finals[4],
        finals[5],
        finals[6],
        finals[7],
        finals[8],
        finals[9],
        finals[10],
        finals[11],
        finals[12],
    )


def solution(mesh):
    return jax.shard_map(
        local,
        mesh=mesh,
        in_specs=(
            P("dp", None, "mp"),
            P("dp", None, "mp"),
            P("dp"),
            P("dp", None),
            P("dp", None, None),
            P("dp"),
            P("mp"),
            P("mp"),
            P(None, None, None, "mp"),
            P(None, None, "mp"),
            P("mp"),
            P("mp"),
            P(None, None, None, "mp"),
            P("mp"),
            P("mp"),
            P("mp"),
            P(None, None, "mp"),
            P(None, None, "mp"),
            P("mp", None),
        ),
        out_specs=(
            P("dp", None, "mp"),
            P("dp", None, "mp"),
            P("mp"),
            P("mp"),
            P(None, None, None, "mp"),
            P(None, None, "mp"),
            P("mp"),
            P("mp"),
            P(None, None, None, "mp"),
            P("mp"),
            P("mp"),
            P("mp"),
            P(None, None, "mp"),
            P(None, None, "mp"),
            P("mp", None),
        ),
        check_vma=False,
    )
```

profile of v0, /device:TPU:0, one launch (start us, length us, event | category | flops | bytes accessed | tf_op | source)
XLA Modules:
  0.0 1537.4 jit_solution(7283062025309797196)
XLA Ops:
  23.1 24.4 %psum.98 = f32[]{:T(128)} all-reduce(f32[]{:T(128)} %bitcast.8), channel_id=1, replica_groups=mesh['dp'=8,'mp'=4] {'dp'}, use_global_device_ids=true, to_apply=%region_48.49 | all-reduce | flops 1 | bytes 8 | tf_op jit(solution)/shard_map/psum | solution.py:229
  49.8 1124.9 %while.44 = (s32[]{:T(128)}, bf16[4,1024,128]{2,1,0:T(8,128)(2,1)}, bf16[4,1024,128]{2,1,0:T(8,128)(2,1)}, f32[128]{0:T(128)}, f32[128]{0:T(128)}, /*index=5*/f3...) while((s32[]{:T(128)}, bf16[4,1024,128]{2,1,0:T(8,128)(2,1)}, ...), condition=%wide.region_47.48_spmd.clone, body=%wide.region_0.47_spmd.clone.sunk | while | flops 10557372416 | bytes 482545312 | solution.py:407
  55.8 13.5 all-gather.9.cloned.1.call-done
  89.2 14.5 all-gather.11.cloned.1.call-done
  103.7 7.0 pad_slice_fusion.37
  127.5 13.0 all-gather.13.cloned.1.call-done
  166.4 23.2 %reduce-scatter.23.cloned.1.call-done = bf16[128,1024]{1,0:T(8,128)(2,1)} async-done(((bf16[512,1024]{1,0:T(8,128)(2,1)}), bf16[128,1024]{1,0:T(8,128)(2,1)}) %reduce-scatter.23.cloned.1.call-update) | async-done | bytes 262160 | tf_op jit(solution)/shard_map/while
  250.2 9.5 pad_slice_fusion.39
  297.6 8.0 convolution_add_fusion.15
  334.3 16.2 %all-gather.9.cloned.1.call-done = bf16[1024,512]{1,0:T(8,128)(2,1)} async-done(((bf16[1024,128]{1,0:T(8,128)(2,1)}), bf16[1024,512]{1,0:T(8,128)(2,1)}) %all-gather.9.cloned.1.call-update) | async-done | bytes 1048592 | tf_op jit(solution)/shard_map/while/body/eval_jaxpr/all_gather | solution.py:247
  370.3 14.6 all-gather.11.cloned.1.call-done
  384.9 7.0 pad_slice_fusion.37
  408.3 13.3 all-gather.13.cloned.1.call-done
  447.8 23.0 %reduce-scatter.23.cloned.1.call-done = bf16[128,1024]{1,0:T(8,128)(2,1)} async-done(((bf16[512,1024]{1,0:T(8,128)(2,1)}), bf16[128,1024]{1,0:T(8,128)(2,1)}) %reduce-scatter.23.cloned.1.call-update) | async-done | bytes 262160 | tf_op jit(solution)/shard_map/while
  531.4 9.5 pad_slice_fusion.39
  578.6 8.9 convolution_add_fusion.15
  615.4 16.2 %all-gather.9.cloned.1.call-done = bf16[1024,512]{1,0:T(8,128)(2,1)} async-done(((bf16[1024,128]{1,0:T(8,128)(2,1)}), bf16[1024,512]{1,0:T(8,128)(2,1)}) %all-gather.9.cloned.1.call-update) | async-done | bytes 1048592 | tf_op jit(solution)/shard_map/while/body/eval_jaxpr/all_gather | solution.py:247
  651.5 14.5 all-gather.11.cloned.1.call-done
  666.1 7.0 pad_slice_fusion.37
  689.4 13.4 all-gather.13.cloned.1.call-done
  728.8 23.2 %reduce-scatter.23.cloned.1.call-done = bf16[128,1024]{1,0:T(8,128)(2,1)} async-done(((bf16[512,1024]{1,0:T(8,128)(2,1)}), bf16[128,1024]{1,0:T(8,128)(2,1)}) %reduce-scatter.23.cloned.1.call-update) | async-done | bytes 262160 | tf_op jit(solution)/shard_map/while
  812.7 9.5 pad_slice_fusion.39
  859.9 8.8 convolution_add_fusion.15
  896.7 16.2 %all-gather.9.cloned.1.call-done = bf16[1024,512]{1,0:T(8,128)(2,1)} async-done(((bf16[1024,128]{1,0:T(8,128)(2,1)}), bf16[1024,512]{1,0:T(8,128)(2,1)}) %all-gather.9.cloned.1.call-update) | async-done | bytes 1048592 | tf_op jit(solution)/shard_map/while/body/eval_jaxpr/all_gather | solution.py:247
  932.7 14.5 all-gather.11.cloned.1.call-done
  947.3 7.0 pad_slice_fusion.37
  970.9 13.1 all-gather.13.cloned.1.call-done
  1010.0 23.2 %reduce-scatter.23.cloned.1.call-done = bf16[128,1024]{1,0:T(8,128)(2,1)} async-done(((bf16[512,1024]{1,0:T(8,128)(2,1)}), bf16[128,1024]{1,0:T(8,128)(2,1)}) %reduce-scatter.23.cloned.1.call-update) | async-done | bytes 262160 | tf_op jit(solution)/shard_map/while
  1093.7 9.5 pad_slice_fusion.39
  1141.1 8.8 convolution_add_fusion.15
  1205.6 22.5 %all-reduce.4 = (f32[128]{0:T(128)}, f32[128]{0:T(128)}, f32[128]{0:T(128)}, f32[128]{0:T(128)}, f32[128]{0:T(128)}, /*index=5*/f32[128]{0:T(128)}, f32[128]{0:T(128)}) all-reduce(f32[128]{0:T(128)S(1)} %broadcast_divide_fusion.12, f32[128]{0:T(128)S(1)} %get-tuple-element.1226, ...), channel_id=1, replica_groups=mesh['dp'=8,'mp'=4] {'dp'}, use_global_device_ids=true, to_apply=%region_49.50 | all-reduce | flops 896 | bytes 7168 | tf_op jit(solution)/shard_map/psum | solution.py:424
  1228.1 289.4 %all-reduce.8.cloned.1.call-done = (f32[3,3,512,128]{3,2,1,0:T(8,128)}, f32[2048,2,128]{2,1,0:T(2,128)}, f32[3,3,512,128]{3,2,1,0:T(8,128)}, f32[512,3,128]{0,2,...) async-done(((f32[3,3,512,128]{3,2,1,0:T(8,128)}, f32[2048,2,128]{2,1,0:T(2,128)}, f32[3,3,512,128]{3,2,1,0:T(8,128)}, f32[512,3,128]{0,2,1:T(8,128)}, ...) | async-done | bytes 9961488 | tf_op jit(solution)/shard_map/psum | solution.py:424
  (1527 shorter events, 806.5 us)
Async XLA Ops:
  55.0 48.7 %all-gather.11.cloned.1.call-start = ((), (), s32[]{:S(2)}) async-start(), calls=%async_computation.6 | async-start | bytes 1310720 | tf_op jit(solution)/shard_map/while/body/eval_jaxpr/all_gather | solution.py:247
  86.7 38.4 %all-gather.15.cloned.1.call-start = ((), (), s32[]{:S(2)}) async-start(), calls=%async_computation.9 | async-start | bytes 1310720 | tf_op jit(solution)/shard_map/while/body/eval_jaxpr/all_gather | solution.py:322
  89.1 51.3 %all-gather.13.cloned.1.call-start = ((), (), s32[]{:S(2)}) async-start(), calls=%async_computation.7 | async-start | bytes 1310720 | tf_op jit(solution)/shard_map/while/body/eval_jaxpr/all_gather | solution.py:247
  120.4 69.2 %reduce-scatter.23.cloned.1.call-start = ((), (), s32[]{:S(2)}) async-start(), calls=%async_computation.10 | async-start | bytes 1310720 | tf_op jit(solution)/shard_map/while
  164.6 72.2 %reduce-scatter.25.cloned.1.call-start = ((), (), s32[]{:S(2)}) async-start(), calls=%async_computation.11 | async-start | bytes 1310720 | tf_op jit(solution)/shard_map/while
  211.7 82.4 %reduce-scatter.21.cloned.1.call-start = ((), (), s32[]{:S(2)}) async-start(), calls=%async_computation.8 | async-start | bytes 1310720 | tf_op jit(solution)/shard_map/while
  227.0 92.0 %reduce-scatter.27.cloned.1.call-start = ((), (), s32[]{:S(2)}) async-start(), calls=%async_computation.12 | async-start | bytes 1310720 | tf_op jit(solution)/shard_map/while
  328.5 21.9 %all-gather.9.cloned.1.call-start = ((), (), s32[]{:S(2)}) async-start(), calls=%async_computation.5 | async-start | bytes 1310720 | tf_op jit(solution)/shard_map/while/body/eval_jaxpr/all_gather | solution.py:247
  333.4 51.5 %all-gather.11.cloned.1.call-start = ((), (), s32[]{:S(2)}) async-start(), calls=%async_computation.6 | async-start | bytes 1310720 | tf_op jit(solution)/shard_map/while/body/eval_jaxpr/all_gather | solution.py:247
  367.9 38.0 %all-gather.15.cloned.1.call-start = ((), (), s32[]{:S(2)}) async-start(), calls=%async_computation.9 | async-start | bytes 1310720 | tf_op jit(solution)/shard_map/while/body/eval_jaxpr/all_gather | solution.py:322
  370.3 51.3 %all-gather.13.cloned.1.call-start = ((), (), s32[]{:S(2)}) async-start(), calls=%async_computation.7 | async-start | bytes 1310720 | tf_op jit(solution)/shard_map/while/body/eval_jaxpr/all_gather | solution.py:247
  401.6 69.2 %reduce-scatter.23.cloned.1.call-start = ((), (), s32[]{:S(2)}) async-start(), calls=%async_computation.10 | async-start | bytes 1310720 | tf_op jit(solution)/shard_map/while
  445.8 72.2 %reduce-scatter.25.cloned.1.call-start = ((), (), s32[]{:S(2)}) async-start(), calls=%async_computation.11 | async-start | bytes 1310720 | tf_op jit(solution)/shard_map/while
  492.8 82.2 %reduce-scatter.21.cloned.1.call-start = ((), (), s32[]{:S(2)}) async-start(), calls=%async_computation.8 | async-start | bytes 1310720 | tf_op jit(solution)/shard_map/while
  508.1 91.8 %reduce-scatter.27.cloned.1.call-start = ((), (), s32[]{:S(2)}) async-start(), calls=%async_computation.12 | async-start | bytes 1310720 | tf_op jit(solution)/shard_map/while
  609.7 21.9 %all-gather.9.cloned.1.call-start = ((), (), s32[]{:S(2)}) async-start(), calls=%async_computation.5 | async-start | bytes 1310720 | tf_op jit(solution)/shard_map/while/body/eval_jaxpr/all_gather | solution.py:247
  614.6 51.5 %all-gather.11.cloned.1.call-start = ((), (), s32[]{:S(2)}) async-start(), calls=%async_computation.6 | async-start | bytes 1310720 | tf_op jit(solution)/shard_map/while/body/eval_jaxpr/all_gather | solution.py:247
  649.1 37.9 %all-gather.15.cloned.1.call-start = ((), (), s32[]{:S(2)}) async-start(), calls=%async_computation.9 | async-start | bytes 1310720 | tf_op jit(solution)/shard_map/while/body/eval_jaxpr/all_gather | solution.py:322
  651.5 51.3 %all-gather.13.cloned.1.call-start = ((), (), s32[]{:S(2)}) async-start(), calls=%async_computation.7 | async-start | bytes 1310720 | tf_op jit(solution)/shard_map/while/body/eval_jaxpr/all_gather | solution.py:247
  682.7 69.3 %reduce-scatter.23.cloned.1.call-start = ((), (), s32[]{:S(2)}) async-start(), calls=%async_computation.10 | async-start | bytes 1310720 | tf_op jit(solution)/shard_map/while
  726.9 72.2 %reduce-scatter.25.cloned.1.call-start = ((), (), s32[]{:S(2)}) async-start(), calls=%async_computation.11 | async-start | bytes 1310720 | tf_op jit(solution)/shard_map/while
  774.0 82.3 %reduce-scatter.21.cloned.1.call-start = ((), (), s32[]{:S(2)}) async-start(), calls=%async_computation.8 | async-start | bytes 1310720 | tf_op jit(solution)/shard_map/while
  789.3 92.1 %reduce-scatter.27.cloned.1.call-start = ((), (), s32[]{:S(2)}) async-start(), calls=%async_computation.12 | async-start | bytes 1310720 | tf_op jit(solution)/shard_map/while
  890.9 21.9 %all-gather.9.cloned.1.call-start = ((), (), s32[]{:S(2)}) async-start(), calls=%async_computation.5 | async-start | bytes 1310720 | tf_op jit(solution)/shard_map/while/body/eval_jaxpr/all_gather | solution.py:247
  895.8 51.4 %all-gather.11.cloned.1.call-start = ((), (), s32[]{:S(2)}) async-start(), calls=%async_computation.6 | async-start | bytes 1310720 | tf_op jit(solution)/shard_map/while/body/eval_jaxpr/all_gather | solution.py:247
  930.3 38.2 %all-gather.15.cloned.1.call-start = ((), (), s32[]{:S(2)}) async-start(), calls=%async_computation.9 | async-start | bytes 1310720 | tf_op jit(solution)/shard_map/while/body/eval_jaxpr/all_gather | solution.py:322
  932.7 51.3 %all-gather.13.cloned.1.call-start = ((), (), s32[]{:S(2)}) async-start(), calls=%async_computation.7 | async-start | bytes 1310720 | tf_op jit(solution)/shard_map/while/body/eval_jaxpr/all_gather | solution.py:247
  964.0 69.2 %reduce-scatter.23.cloned.1.call-start = ((), (), s32[]{:S(2)}) async-start(), calls=%async_computation.10 | async-start | bytes 1310720 | tf_op jit(solution)/shard_map/while
  1008.1 72.2 %reduce-scatter.25.cloned.1.call-start = ((), (), s32[]{:S(2)}) async-start(), calls=%async_computation.11 | async-start | bytes 1310720 | tf_op jit(solution)/shard_map/while
  1055.2 82.3 %reduce-scatter.21.cloned.1.call-start = ((), (), s32[]{:S(2)}) async-start(), calls=%async_computation.8 | async-start | bytes 1310720 | tf_op jit(solution)/shard_map/while
  1070.5 92.1 %reduce-scatter.27.cloned.1.call-start = ((), (), s32[]{:S(2)}) async-start(), calls=%async_computation.12 | async-start | bytes 1310720 | tf_op jit(solution)/shard_map/while
  1174.7 342.7 %all-reduce.8.cloned.1.call-start = ((), (), s32[]{:S(2)}) async-start(), calls=%async_computation.4 | async-start | bytes 19922944 | tf_op jit(solution)/shard_map/psum | solution.py:424
  (321 other events, 2458.3 us)
Sparse Core Ops, SparseCore 0:
  55.1 14.1 all-gather.8
  86.9 16.8 all-gather.10
  105.3 16.8 all-gather.14
  123.6 16.8 all-gather.12
  164.7 24.8 reduce-scatter.22
  211.8 24.9 reduce-scatter.24
  239.4 24.8 reduce-scatter.20
  294.1 24.8 reduce-scatter.26
  333.5 16.8 all-gather.8
  368.0 16.8 all-gather.10
  386.5 16.8 all-gather.14
  404.7 16.8 all-gather.12
  445.9 24.8 reduce-scatter.22
  493.0 24.9 reduce-scatter.24
  520.4 24.9 reduce-scatter.20
  575.1 24.7 reduce-scatter.26
  614.7 16.8 all-gather.8
  649.2 16.8 all-gather.10
  667.6 16.9 all-gather.14
  686.0 16.7 all-gather.12
  727.1 24.8 reduce-scatter.22
  774.1 24.9 reduce-scatter.24
  801.7 24.8 reduce-scatter.20
  856.4 24.9 reduce-scatter.26
  896.0 16.8 all-gather.8
  930.4 16.8 all-gather.10
  948.7 16.8 all-gather.14
  967.1 16.8 all-gather.12
  1008.3 24.8 reduce-scatter.22
  1055.3 24.9 reduce-scatter.24
  1082.8 24.8 reduce-scatter.20
  1137.6 24.9 reduce-scatter.26
Sparse Core Ops, SparseCore 1:
  1200.9 316.5 all-reduce.7
where the time goes:
time: 1550 us; the launch traced here: 1540 us
  waiting for transfers between devices  592 us (38%)
  local copies, waits for them, and re-layouts  437 us (28%)
  matrix products  252 us (16%)
  other arithmetic  177 us (11%)
  blocking collectives  46.9 us (3%)
  between operations  16.3 us (1%)
    psum x1, waiting for transfers between devices, local(): lax.psum((gain1_sum / image_total, bias1_sum / image_total, conv1_sum / i...  289 us
    slice x48, local copies, waits for them, and re-layouts, patches(): padded[tap_row:tap_row + SIDE, tap_col:tap_col + SIDE]  185 us
    all_gather x12, waiting for transfers between devices, gather_features(): return lax.all_gather(field, 'mp', axis=1, tiled=True)  173 us
    while x760, local copies, waits for them, and re-layouts  129 us
    while x48, waiting for transfers between devices  129 us
    dot_general x17, matrix products, contract_rows(): lax.dot_general(left, right, (((0,), (0,)), ((), ())), preferred_element_...  74.4 us
  transfers between devices with their start and end apart: 33, of which 25 were waited for; matrix products, arithmetic and copies ran while one was open for 31% of the time, Pallas kernels for 0%

commit v1 on v0

v1 whole, which is shorter than its diff:
```python
import functools
import math

import jax
import jax.numpy as jnp
from jax import lax
from jax.experimental import pallas as pl
from jax.experimental.pallas import tpu as pltpu
from jax.sharding import PartitionSpec as P

C = 512
GROUPS = 32
HEAD = 64
EMB = 2048
CTX = 4
SIDE = 32
LANES = 128
PAD = SIDE
EPSILON = 1e-05
F32 = jnp.float32
BF16 = jnp.bfloat16
NEG = -1e30

E_SCALE, E_SHIFT, E_G1, E_B1, E_G2, E_B2, E_CB2, E_G3, E_B3 = range(9)
E_KEY, E_VALUE, E_ROWS = 16, 24, 32
S_G3, S_B3, S_CB2, S_G2, S_B2, S_SCALE, S_SHIFT, S_LIVE = range(8)
S_KEY, S_VALUE, S_ROWS = 8, 12, 16
VMEM_LIMIT = 56 << 20


def vmem():
    return pl.BlockSpec(memory_space=pltpu.VMEM)


def anywhere():
    return pl.BlockSpec(memory_space=pl.ANY)


def smem():
    return pl.BlockSpec(memory_space=pltpu.SMEM)


def struct(shape, dtype):
    return jax.ShapeDtypeStruct(shape, dtype)


def call(body, name, out_shape, in_specs, scratch, flops=0, moved=0):
    many = isinstance(out_shape, (list, tuple))
    return pl.pallas_call(
        body,
        name=name,
        out_shape=out_shape,
        in_specs=in_specs,
        out_specs=[vmem() for _ in out_shape] if many else vmem(),
        scratch_shapes=scratch,
        compiler_params=pltpu.CompilerParams(vmem_limit_bytes=VMEM_LIMIT),
        cost_estimate=pl.CostEstimate(flops=flops, transcendentals=0, bytes_accessed=moved),
    )


def fetch(sources, target, me, sems, first):
    copies = []
    for offset, source in enumerate(sources):
        copy = pltpu.make_async_copy(
            source, target.at[jnp.bitwise_xor(me, offset)], sems.at[first + offset]
        )
        copy.start()
        copies.append(copy)
    return copies


def wait_all(copies):
    for copy in copies:
        copy.wait()


def fold(values):
    rows = values.shape[0]
    return jnp.sum(values.reshape(rows // 8, 8, values.shape[1]), axis=0)


def group_sum(rows8):
    lane = lax.broadcasted_iota(jnp.int32, rows8.shape, 1)
    total = jnp.broadcast_to(jnp.sum(rows8, axis=0, keepdims=True), rows8.shape)
    for step in (1, 2, 4, 8):
        up = pltpu.roll(total, step, axis=1)
        down = pltpu.roll(total, LANES - step, axis=1)
        total = total + jnp.where((lane & step) != 0, up, down)
    return total[0:1]


def column_sum(rows8):
    return jnp.sum(rows8, axis=0, keepdims=True)


def accumulate(rows, strip, functions):
    def body(index, carry):
        start = pl.multiple_of(index * strip, strip)
        found = functions(start)
        return tuple(old + fold(new) for old, new in zip(carry, found))

    count = len(jax.eval_shape(lambda: functions(0))) if False else None
    del count
    return body


def sum_strips(pixels, strip, width, function):
    zero = tuple(jnp.zeros((8, LANES), F32) for _ in range(width))

    def body(index, carry):
        start = pl.multiple_of(index * strip, strip)
        return tuple(old + fold(new) for old, new in zip(carry, function(start)))

    return lax.fori_loop(0, pixels // strip, body, zero)


def norm_rows(pixels, strip, read):
    count = pixels * (C // GROUPS)
    sums = sum_strips(pixels, strip, 4, lambda start: [read(b, start) for b in range(4)])
    means = [group_sum(s) * (1.0 / count) for s in sums]
    squares = sum_strips(
        pixels,
        strip,
        4,
        lambda start: [jnp.square(read(b, start) - means[b]) for b in range(4)],
    )
    inverses = [lax.rsqrt(group_sum(s) * (1.0 / count) + EPSILON) for s in squares]
    return means, inverses


def shifted(values):
    rows = values.shape[0]
    column = lax.broadcasted_iota(jnp.int32, values.shape, 0) & (SIDE - 1)
    left = jnp.where(column == 0, 0.0, pltpu.roll(values, 1, axis=0))
    right = jnp.where(column == SIDE - 1, 0.0, pltpu.roll(values, rows - 1, axis=0))
    return left, values, right


def store_shifted(target, block, start, values):
    rows = values.shape[0]
    for position, part in enumerate(shifted(values)):
        target[position, block, pl.ds(pl.multiple_of(PAD + start, 32), rows), :] = part.astype(BF16)


def clear_padding(target, pixels):
    zero = jnp.zeros((PAD, LANES), BF16)
    for position in range(3):
        for block in range(4):
            target[position, block, 0:PAD, :] = zero
            target[position, block, PAD + pixels : PAD + pixels + PAD, :] = zero


def conv_tiles(field, weight, pixels, tile, write):
    def body(index, carry):
        start = pl.multiple_of(index * tile, tile)
        left = jnp.concatenate(
            [
                field[b, block, pl.ds(pl.multiple_of(start + a * SIDE, 32), tile), :]
                for a in range(3)
                for b in range(3)
                for block in range(4)
            ],
            axis=1,
        )
        right = jnp.concatenate([weight[s].reshape(9 * C, LANES) for s in range(4)], axis=1)
        write(start, jnp.dot(left, right, preferred_element_type=F32))
        return carry

    lax.fori_loop(0, pixels // tile, body, 0)


def conv_back_tiles(field, weight, pixels, tile, write):
    def body(index, carry):
        start = pl.multiple_of((index // 2) * tile, tile)
        half = index % 2
        left = jnp.concatenate(
            [
                field[2 - b, block, pl.ds(pl.multiple_of(start + (2 - a) * SIDE, 32), tile), :]
                for a in range(3)
                for b in range(3)
                for block in range(4)
            ],
            axis=1,
        )
        right = jnp.concatenate(
            [
                weight[block, 3 * a + b, pl.ds(pl.multiple_of(half * 256, 256), 256), :]
                for a in range(3)
                for b in range(3)
                for block in range(4)
            ],
            axis=1,
        )
        write(
            start,
            half,
            lax.dot_general(left, right, (((1,), (1,)), ((), ())), preferred_element_type=F32),
        )
        return carry

    lax.fori_loop(0, 2 * (pixels // tile), body, 0)


def silu_slope(before, grad_out):
    gate = jax.nn.sigmoid(before)
    return grad_out * gate * (1.0 + before * (1.0 - gate))


def kernel_first(
    meta, i0, i1, i2, i3, w0, w1, w2, w3, e0, e1, e2, e3,
    image, pack, first_t, inner, second, second_t, field, weight, sems,
):
    pixels = image.shape[1]
    me = meta[0]
    image_copies = fetch((i0, i1, i2, i3), image, me, sems, 0)
    pack_copies = fetch((e0, e1, e2, e3), pack, me, sems, 4)
    weight_copies = fetch((w0, w1, w2, w3), weight, me, sems, 8)
    clear_padding(field, pixels)
    wait_all(image_copies)
    wait_all(pack_copies)
    strip = 128

    def read(block, start):
        return image[block, pl.ds(start, strip), :].astype(F32)

    means, inverses = norm_rows(pixels, strip, read)

    def normalise(index, carry):
        start = pl.multiple_of(index * strip, strip)
        for b in range(4):
            gain = pack[b, E_G1 : E_G1 + 1, :]
            bias = pack[b, E_B1 : E_B1 + 1, :]
            before = (read(b, start) - means[b]) * inverses[b] * gain + bias
            after = before * jax.nn.sigmoid(before)
            store_shifted(field, b, start, after)
            first_t[b, :, pl.ds(start, strip)] = after.T.astype(BF16)
        return carry

    lax.fori_loop(0, pixels // strip, normalise, 0)
    wait_all(weight_copies)

    def write(start, tile):
        for b in range(4):
            inner[b, pl.ds(start, tile.shape[0]), :] = tile[:, b * LANES : (b + 1) * LANES]

    conv_tiles(field, weight, pixels, 512, write)
    means2, inverses2 = norm_rows(pixels, strip, lambda b, start: inner[b, pl.ds(start, strip), :])

    def modulate(index, carry):
        start = pl.multiple_of(index * strip, strip)
        for b in range(4):
            gain = pack[b, E_G2 : E_G2 + 1, :]
            bias = pack[b, E_B2 : E_B2 + 1, :]
            scale = pack[b, E_SCALE : E_SCALE + 1, :]
            shift = pack[b, E_SHIFT : E_SHIFT + 1, :]
            normed = (inner[b, pl.ds(start, strip), :] - means2[b]) * inverses2[b]
            modulated = (normed * gain + bias) * (1.0 + scale) + shift
            after = modulated * jax.nn.sigmoid(modulated)
            second[b, pl.ds(start, strip), :] = after.astype(BF16)
            second_t[b, :, pl.ds(start, strip)] = after.T.astype(BF16)
        return carry

    lax.fori_loop(0, pixels // strip, modulate, 0)


def kernel_second(
    meta, second, image, pack, w0, w1, w2, w3, p0, p1, p2, p3,
    middle, attn_t, qkv, field, weight, qkv_weight, attn, sems,
):
    pixels = image.shape[1]
    me = meta[0]
    weight_copies = fetch((w0, w1, w2, w3), weight, me, sems, 0)
    qkv_copies = fetch((p0, p1, p2, p3), qkv_weight, me, sems, 4)
    clear_padding(field, pixels)
    strip = 128

    def spread(index, carry):
        start = pl.multiple_of(index * strip, strip)
        for b in range(4):
            store_shifted(field, b, start, second[b, pl.ds(start, strip), :].astype(F32))
        return carry

    lax.fori_loop(0, pixels // strip, spread, 0)
    wait_all(weight_copies)

    def write(start, tile):
        rows = tile.shape[0]
        for b in range(4):
            branch = tile[:, b * LANES : (b + 1) * LANES] + pack[b, E_CB2 : E_CB2 + 1, :]
            middle[b, pl.ds(start, rows), :] = image[b, pl.ds(start, rows), :].astype(F32) + branch

    conv_tiles(field, weight, pixels, 512, write)
    means, inverses = norm_rows(pixels, strip, lambda b, start: middle[b, pl.ds(start, strip), :])

    def normalise(index, carry):
        start = pl.multiple_of(index * strip, strip)
        for b in range(4):
            normed = (middle[b, pl.ds(start, strip), :] - means[b]) * inverses[b]
            value = normed * pack[b, E_G3 : E_G3 + 1, :] + pack[b, E_B3 : E_B3 + 1, :]
            attn[b, pl.ds(start, strip), :] = value.astype(BF16)
            attn_t[b, :, pl.ds(start, strip)] = value.T.astype(BF16)
        return carry

    lax.fori_loop(0, pixels // strip, normalise, 0)
    wait_all(qkv_copies)

    def project(index, carry):
        s = index // 2
        start = pl.multiple_of((index % 2) * 512, 512)
        left = jnp.concatenate([attn[b, pl.ds(start, 512), :] for b in range(4)], axis=1)
        right = jnp.concatenate([qkv_weight[s, kind] for kind in range(3)], axis=1)
        qkv[s, pl.ds(start, 512), :] = jnp.dot(left, right, preferred_element_type=F32).astype(BF16)
        return carry

    lax.fori_loop(0, 4 * (pixels // 512), project, 0)


def kernel_attention(
    meta, qkv, pack, middle, c0, c1, c2, c3, w0, w1, w2, w3,
    o0, o1, o2, o3, cot, mixed, dqkv, dctx,
    weight, grad_mixed, score_ctx, grad_ctx_prob, prob_ctx, dscore_ctx, out_pix, dquery, dkey_t, dvalue_t, sems,
):
    pixels = qkv.shape[1]
    me = meta[0]
    alive = meta[1].astype(F32)
    cot_copies = fetch((c0, c1, c2, c3), cot, me, sems, 0)
    weight_copies = fetch((w0, w1, w2, w3), weight, me, sems, 4)
    scale = 1.0 / math.sqrt(HEAD)
    block = 256

    row32 = lax.broadcasted_iota(jnp.int32, (32, LANES), 0)
    lane32 = lax.broadcasted_iota(jnp.int32, (32, LANES), 1)

    def diagonal(kind):
        found = []
        for s in range(4):
            rows8 = pack[s, kind : kind + 8, :]
            tiled = jnp.concatenate([rows8] * 4, axis=0)
            own = (row32 // 4) == (2 * s + lane32 // HEAD)
            kept = jnp.where(own, tiled, 0.0)
            found.append(jnp.concatenate([kept, jnp.zeros((96, LANES), F32)], axis=0).astype(BF16))
        return jnp.concatenate(found, axis=1)

    keys_ctx = diagonal(E_KEY)
    values_ctx = diagonal(E_VALUE)
    wait_all(cot_copies)
    wait_all(weight_copies)

    def prepare(index, carry):
        start = pl.multiple_of(index * block, block)
        rows = pl.ds(start, block)
        for s in range(4):
            cot[s, rows, :] = (cot[s, rows, :].astype(F32) * alive).astype(BF16)
        all_cot = jnp.concatenate([cot[s, rows, :] for s in range(4)], axis=1)
        all_weight = weight[...].reshape(C, C)
        grad = lax.dot_general(
            all_cot, all_weight, (((1,), (1,)), ((), ())), preferred_element_type=F32
        ).astype(BF16)
        for s in range(4):
            grad_mixed[s, rows, :] = grad[:, s * LANES : (s + 1) * LANES]
        query = jnp.concatenate([qkv[s, rows, 0:LANES] for s in range(4)], axis=1)
        score_ctx[rows, :] = lax.dot_general(
            query, keys_ctx, (((1,), (1,)), ((), ())), preferred_element_type=F32
        )
        grad_ctx_prob[rows, :] = lax.dot_general(
            grad, values_ctx, (((1,), (1,)), ((), ())), preferred_element_type=F32
        )
        prob_ctx[rows, :] = jnp.zeros((block, LANES), F32)
        dscore_ctx[rows, :] = jnp.zeros((block, LANES), F32)
        return carry

    lax.fori_loop(0, pixels // block, prepare, 0)
    lane = lax.broadcasted_iota(jnp.int32, (block, LANES), 1)
    low = lane < HEAD
    ones = jnp.ones((pixels, LANES), BF16)
    blocks = pixels // block

    def attend(index, carry):
        s = index // blocks
        part = index % blocks
        rows = pl.ds(pl.multiple_of(part * block, block), block)

        @pl.when(part == 0)
        def _():
            dkey_t[...] = jnp.zeros((LANES, pixels), F32)
            dvalue_t[...] = jnp.zeros((LANES, pixels), F32)

        query = qkv[s, rows, 0:LANES]
        key = qkv[s, :, LANES : 2 * LANES]
        value = qkv[s, :, 2 * LANES : 3 * LANES]
        value_ones = jnp.concatenate([value, ones], axis=1)
        grad = grad_mixed[s, rows, :]
        ctx_scores = score_ctx[rows, :]
        ctx_grads = grad_ctx_prob[rows, :]
        exps, outs, inverses, ctx_exps, owns = [], [], [], [], []
        for h in range(2):
            mine = low if h == 0 else jnp.logical_not(low)
            own = lane // CTX == 2 * s + h
            score = lax.dot_general(
                jnp.where(mine, query, jnp.zeros_like(query)),
                key,
                (((1,), (1,)), ((), ())),
                preferred_element_type=F32,
            )
            top = jnp.maximum(
                jnp.max(score, axis=1, keepdims=True),
                jnp.max(jnp.where(own, ctx_scores, NEG), axis=1, keepdims=True),
            )
            exp = jnp.exp((score - top) * scale).astype(BF16)
            ctx_exp = jnp.where(own, jnp.exp((ctx_scores - top) * scale), 0.0)
            out = jnp.dot(exp, value_ones, preferred_element_type=F32)
            total = out[:, LANES:] + jnp.sum(ctx_exp, axis=1, keepdims=True)
            inverse = 1.0 / total
            exps.append(exp)
            outs.append(out[:, :LANES] * inverse)
            inverses.append(inverse)
            ctx_exps.append(ctx_exp)
            owns.append(own)
        out_pair = jnp.where(low, outs[0], outs[1])
        out_pix[s, rows, :] = out_pair
        inverse_pair = jnp.where(low, inverses[0], inverses[1])
        scaled = (grad.astype(F32) * (inverse_pair * scale)).astype(BF16)
        product = out_pair * scaled.astype(F32)
        query_t = query.astype(F32).T.astype(BF16)
        scaled_t = scaled.astype(F32).T.astype(BF16)
        prob_keep = prob_ctx[rows, :]
        dscore_keep = dscore_ctx[rows, :]
        dqs = []
        for h in range(2):
            mine = low if h == 0 else jnp.logical_not(low)
            own = owns[h]
            ctx_prob = ctx_exps[h] * inverses[h]
            ctx_grad = ctx_grads * (inverses[h] * scale)
            dot = jnp.sum(
                jnp.where(mine, product, 0.0) + ctx_prob * jnp.where(own, ctx_grad, 0.0),
                axis=1,
                keepdims=True,
            )
            weight_grad = lax.dot_general(
                jnp.where(mine, scaled, jnp.zeros_like(scaled)),
                value,
                (((1,), (1,)), ((), ())),
                preferred_element_type=F32,
            )
            dscore = (exps[h].astype(F32) * (weight_grad - dot)).astype(BF16)
            prob_keep = jnp.where(own, ctx_prob, prob_keep)
            dscore_keep = jnp.where(own, ctx_exps[h] * (ctx_grad - dot), dscore_keep)
            dqs.append(jnp.dot(dscore, key, preferred_element_type=F32))
            half = slice(h * HEAD, (h + 1) * HEAD)
            dkey_t[half, :] += jnp.dot(query_t[half], dscore, preferred_element_type=F32)
            dvalue_t[half, :] += jnp.dot(scaled_t[half], exps[h], preferred_element_type=F32)
        prob_ctx[rows, :] = prob_keep
        dscore_ctx[rows, :] = dscore_keep
        dquery[s, rows, :] = jnp.where(low, dqs[0], dqs[1])

        @pl.when(part == blocks - 1)
        def _():
            for piece in range(pixels // LANES):
                cut = slice(piece * LANES, (piece + 1) * LANES)
                dqkv[s, cut, LANES : 2 * LANES] = dkey_t[:, cut].T.astype(BF16)
                dqkv[s, cut, 2 * LANES : 3 * LANES] = (dvalue_t[:, cut] * (1.0 / scale)).T.astype(BF16)

        return carry

    lax.fori_loop(0, 4 * blocks, attend, 0)

    def finish(index, carry):
        dkeys, dvalues = carry
        start = pl.multiple_of(index * block, block)
        rows = pl.ds(start, block)
        prob = prob_ctx[rows, :].astype(BF16)
        dscore = dscore_ctx[rows, :].astype(BF16)
        out_ctx = jnp.dot(prob, values_ctx, preferred_element_type=F32)
        dquery_ctx = jnp.dot(dscore, keys_ctx, preferred_element_type=F32)
        parts = []
        for s in range(4):
            cut = slice(s * LANES, (s + 1) * LANES)
            both = (out_pix[s, rows, :] + out_ctx[:, cut]).astype(BF16)
            mixed[s, rows, :] = both
            parts.append(both)
            dqkv[s, rows, 0:LANES] = (dquery[s, rows, :] + dquery_ctx[:, cut]).astype(BF16)
        result = jnp.dot(
            jnp.concatenate(parts, axis=1), weight[...].reshape(C, C), preferred_element_type=F32
        )
        for offset, target in enumerate((o0, o1, o2, o3)):
            other = jnp.bitwise_xor(me, offset)
            value = jnp.zeros((block, LANES), F32)
            for s in range(4):
                value = jnp.where(other == s, result[:, s * LANES : (s + 1) * LANES], value)
            target[rows, :] = ((middle[other, rows, :] + value) * alive).astype(BF16)
        query = jnp.concatenate([qkv[s, rows, 0:LANES] for s in range(4)], axis=1)
        grad = jnp.concatenate([grad_mixed[s, rows, :] for s in range(4)], axis=1)
        dkeys = dkeys + jnp.dot(dscore_ctx[rows, :].T[0:32].astype(BF16), query, preferred_element_type=F32)
        dvalues = dvalues + jnp.dot(prob_ctx[rows, :].T[0:32].astype(BF16), grad, preferred_element_type=F32)
        return dkeys, dvalues

    zero = jnp.zeros((32, C), F32)
    dkeys, dvalues = lax.fori_loop(0, pixels // block, finish, (zero, zero))
    for s in range(4):
        own = (row32 // 4) == (2 * s + lane32 // HEAD)
        for position, source in enumerate((dkeys, dvalues)):
            kept = jnp.where(own, source[:, s * LANES : (s + 1) * LANES], 0.0)
            eight = jnp.sum(kept.reshape(4, 8, LANES), axis=0)
            folded = eight + pltpu.roll(eight, 4, axis=0)
            dctx[s, position * CTX : (position + 1) * CTX, :] = folded[0:CTX]


def norm_back_strips(pixels, strip, read_normed, read_grad, gains, inverses, write):
    count = pixels * (C // GROUPS)

    def terms(start):
        found = []
        for b in range(4):
            grad = read_grad(b, start)
            found += [grad, grad * read_normed(b, start)]
        return found

    sums = sum_strips(pixels, strip, 8, terms)
    bias_sums = [column_sum(sums[2 * b]) for b in range(4)]
    gain_sums = [column_sum(sums[2 * b + 1]) for b in range(4)]
    firsts = [
        group_sum(jnp.broadcast_to(bias_sums[b] * gains[b], (8, LANES)) * (1.0 / 8)) * (1.0 / count)
        for b in range(4)
    ]
    seconds = [
        group_sum(jnp.broadcast_to(gain_sums[b] * gains[b], (8, LANES)) * (1.0 / 8)) * (1.0 / count)
        for b in range(4)
    ]

    def body(index, carry):
        start = pl.multiple_of(index * strip, strip)
        for b in range(4):
            normed = read_normed(b, start)
            grad = read_grad(b, start) * gains[b]
            write(b, start, inverses[b] * (grad - firsts[b] - normed * seconds[b]))
        return carry

    lax.fori_loop(0, pixels // strip, body, 0)
    return gain_sums, bias_sums


def kernel_back_attention(
    meta, dqkv, mixed, attn_t, cot, middle, pack, dctx, p0, p1, p2, p3,
    keep, send, dmiddle, field, sums, qkv_weight, cot_t, dattn, sems,
):
    pixels = cot.shape[1]
    me = meta[0]
    alive = meta[1].astype(F32)
    qkv_copies = fetch((p0, p1, p2, p3), qkv_weight, me, sems, 0)
    strip = 128
    clear_padding(field, pixels)

    def turn(index, carry):
        start = pl.multiple_of(index * strip, strip)
        for b in range(4):
            cot_t[b, :, pl.ds(start, strip)] = cot[b, pl.ds(start, strip), :].astype(F32).T.astype(BF16)
        return carry

    lax.fori_loop(0, pixels // strip, turn, 0)
    wait_all(qkv_copies)

    def back(index, carry):
        start = pl.multiple_of(index * 256, 256)
        left = jnp.concatenate([dqkv[s, pl.ds(start, 256), :] for s in range(4)], axis=1)
        right = jnp.concatenate([qkv_weight[s, kind] for s in range(4) for kind in range(3)], axis=1)
        tile = lax.dot_general(left, right, (((1,), (1,)), ((), ())), preferred_element_type=F32)
        for b in range(4):
            dattn[b, pl.ds(start, 256), :] = tile[:, b * LANES : (b + 1) * LANES]
        return carry

    lax.fori_loop(0, pixels // 256, back, 0)

    def weights(offset, carry):
        s = jnp.bitwise_xor(me, offset)
        place = offset // 2
        attn_all = attn_t[...].reshape(C, pixels)
        cot_all = cot_t[...].reshape(C, pixels)
        grad = jnp.dot(attn_all, dqkv[s], preferred_element_type=F32).astype(BF16)
        other = jnp.dot(cot_all, mixed[s], preferred_element_type=F32).astype(BF16)

        def put(target):
            for kind in range(3):
                target[place, kind] = grad[:, kind * LANES : (kind + 1) * LANES]
            target[place, 3] = other

        @pl.when(offset % 2 == 0)
        def _():
            put(keep)

        @pl.when(offset % 2 == 1)
        def _():
            put(send)

        return carry

    lax.fori_loop(0, 4, weights, 0)
    means, inverses = norm_rows(pixels, strip, lambda b, start: middle[b, pl.ds(start, strip), :])
    gains = [pack[b, E_G3 : E_G3 + 1, :] for b in range(4)]

    def read_normed(b, start):
        return (middle[b, pl.ds(start, strip), :] - means[b]) * inverses[b]

    def write(b, start, value):
        total = cot[b, pl.ds(start, strip), :].astype(F32) + value
        dmiddle[b, pl.ds(start, strip), :] = total
        store_shifted(field, b, start, total.astype(BF16).astype(F32))

    gain_sums, bias_sums = norm_back_strips(
        pixels, strip, read_normed, lambda b, start: dattn[b, pl.ds(start, strip), :], gains, inverses, write
    )
    branch = sum_strips(
        pixels,
        strip,
        4,
        lambda start: [
            field[1, b, pl.ds(pl.multiple_of(PAD + start, 32), strip), :].astype(F32) for b in range(4)
        ],
    )
    for b in range(4):
        sums[b] = jnp.zeros((S_ROWS, LANES), F32)
        sums[b, S_G3 : S_G3 + 1, :] = gain_sums[b]
        sums[b, S_B3 : S_B3 + 1, :] = bias_sums[b]
        sums[b, S_CB2 : S_CB2 + 1, :] = column_sum(branch[b])
        sums[b, S_LIVE : S_LIVE + 1, :] = jnp.full((1, LANES), 1.0, F32) * alive
        sums[b, S_KEY : S_KEY + 8, :] = dctx[b]


def kernel_weight_grad(meta, source_t, field, keep, send):
    pixels = source_t.shape[2]
    me = meta[0]
    left = source_t[...].reshape(C, pixels)

    def body(index, carry):
        tap = index // 2
        side = index % 2
        a = tap // 3
        b = tap % 3
        start = pl.multiple_of((2 - a) * SIDE, 32)
        first = jnp.bitwise_xor(me, side)
        right = jnp.concatenate(
            [
                field[2 - b, first, pl.ds(start, pixels), :],
                field[2 - b, jnp.bitwise_xor(first, 2), pl.ds(start, pixels), :],
            ],
            axis=1,
        )
        grad = jnp.dot(left, right, preferred_element_type=F32).astype(BF16)

        @pl.when(side == 0)
        def _():
            keep[0, tap] = grad[:, :LANES]
            keep[1, tap] = grad[:, LANES:]

        @pl.when(side == 1)
        def _():
            send[0, tap] = grad[:, :LANES]
            send[1, tap] = grad[:, LANES:]

        return carry

    lax.fori_loop(0, 18, body, 0)


def kernel_back_second(
    meta, grad_field, inner, pack, sums_in, w0, w1, w2, w3,
    field, s0, s1, s2, s3, weight, grad, sems,
):
    pixels = inner.shape[1]
    me = meta[0]
    strip = 128
    weight_copies = fetch((w0, w1, w2, w3), weight, me, sems, 0)
    clear_padding(field, pixels)
    means, inverses = norm_rows(pixels, strip, lambda b, start: inner[b, pl.ds(start, strip), :])
    wait_all(weight_copies)

    def write_grad(start, half, tile):
        for b in range(2):
            grad[2 * half + b, pl.ds(start, tile.shape[0]), :] = tile[:, b * LANES : (b + 1) * LANES]

    conv_back_tiles(grad_field, weight, pixels, 512, write_grad)
    gains = [pack[b, E_G2 : E_G2 + 1, :] for b in range(4)]

    def read_normed(b, start):
        return (inner[b, pl.ds(start, strip), :] - means[b]) * inverses[b]

    def slope(index, carry):
        start = pl.multiple_of(index * strip, strip)
        found = []
        for b in range(4):
            bias = pack[b, E_B2 : E_B2 + 1, :]
            scale = pack[b, E_SCALE : E_SCALE + 1, :]
            shift = pack[b, E_SHIFT : E_SHIFT + 1, :]
            shaped = read_normed(b, start) * gains[b] + bias
            modulated = shaped * (1.0 + scale) + shift
            dmod = silu_slope(modulated, grad[b, pl.ds(start, strip), :])
            grad[b, pl.ds(start, strip), :] = dmod * (1.0 + scale)
            found += [dmod * shaped, dmod]
        return tuple(old + fold(new) for old, new in zip(carry, found))

    zero = tuple(jnp.zeros((8, LANES), F32) for _ in range(8))
    modulation = lax.fori_loop(0, pixels // strip, slope, zero)

    def write(b, start, value):
        store_shifted(field, b, start, value)

    gain_sums, bias_sums = norm_back_strips(
        pixels, strip, read_normed, lambda b, start: grad[b, pl.ds(start, strip), :], gains, inverses, write
    )
    for offset, target in enumerate((s0, s1, s2, s3)):
        other = jnp.bitwise_xor(me, offset)
        target[...] = sums_in[other]
        for b in range(4):

            @pl.when(other == b)
            def _():
                target[S_G2 : S_G2 + 1, :] = gain_sums[b]
                target[S_B2 : S_B2 + 1, :] = bias_sums[b]
                target[S_SCALE : S_SCALE + 1, :] = column_sum(modulation[2 * b])
                target[S_SHIFT : S_SHIFT + 1, :] = column_sum(modulation[2 * b + 1])


def kernel_back_first(
    meta, grad_field, image, pack, dmiddle, w0, w1, w2, w3,
    g0, g1, g2, g3, s0, s1, s2, s3, weight, grad, sems,
):
    pixels = image.shape[1]
    me = meta[0]
    strip = 128
    weight_copies = fetch((w0, w1, w2, w3), weight, me, sems, 0)

    def read(b, start):
        return image[b, pl.ds(start, strip), :].astype(F32)

    means, inverses = norm_rows(pixels, strip, read)
    wait_all(weight_copies)

    def write_grad(start, half, tile):
        for b in range(2):
            grad[2 * half + b, pl.ds(start, tile.shape[0]), :] = tile[:, b * LANES : (b + 1) * LANES]

    conv_back_tiles(grad_field, weight, pixels, 512, write_grad)
    gains = [pack[b, E_G1 : E_G1 + 1, :] for b in range(4)]

    def read_normed(b, start):
        return (read(b, start) - means[b]) * inverses[b]

    def slope(index, carry):
        start = pl.multiple_of(index * strip, strip)
        for b in range(4):
            before = read_normed(b, start) * gains[b] + pack[b, E_B1 : E_B1 + 1, :]
            grad[b, pl.ds(start, strip), :] = silu_slope(before, grad[b, pl.ds(start, strip), :])
        return carry

    lax.fori_loop(0, pixels // strip, slope, 0)

    def write(b, start, value):
        grad[b, pl.ds(start, strip), :] = dmiddle[b, pl.ds(start, strip), :] + value

    gain_sums, bias_sums = norm_back_strips(
        pixels, strip, read_normed, lambda b, start: grad[b, pl.ds(start, strip), :], gains, inverses, write
    )
    for offset, (target, small) in enumerate(zip((g0, g1, g2, g3), (s0, s1, s2, s3))):
        other = jnp.bitwise_xor(me, offset)
        target[...] = grad[other].astype(BF16)
        small[...] = jnp.zeros((8, LANES), F32)
        for b in range(4):

            @pl.when(other == b)
            def _():
                small[0:1, :] = gain_sums[b]
                small[1:2, :] = bias_sums[b]


def swap(value, axis, offset):
    size = lax.axis_size(axis)
    return lax.ppermute(value, axis, [(i, i ^ offset) for i in range(size)])


def share(shard):
    near = swap(shard, "mp", 1)
    far = swap(shard, "mp", 2)
    return shard, near, far, swap(far, "mp", 1)


def exchange(pieces):
    return (pieces[0],) + tuple(swap(pieces[k], "mp", k) for k in range(1, 4))


def pick(stack, me):
    return [lax.dynamic_index_in_dim(stack, me ^ k, 0, keepdims=False) for k in range(4)]


def dp_levels(size):
    levels = []
    low = 1
    while low < size:
        width = 2 if low == 1 or size // low < 4 else 4
        levels.append((low, width))
        low *= width
    return levels


def gather_dp(value):
    stacked = value[None]
    for low, width in dp_levels(lax.axis_size("dp")):
        stacked = jnp.concatenate(
            [stacked] + [swap(stacked, "dp", low * k) for k in range(1, width)], axis=0
        )
    return stacked


def reduce_grads(keep, send):
    got = swap(send, "mp", 1)
    far = keep[1].astype(F32) + got[1].astype(F32)
    own = keep[0].astype(F32) + got[0].astype(F32)
    value = (own + swap(far.astype(BF16), "mp", 2).astype(F32)).astype(BF16)
    blocks = value.shape[0]
    place = lax.axis_index("dp")
    path = []
    for low, width in dp_levels(lax.axis_size("dp")):
        rows = value.shape[1] // width
        digit = (place // low) % width
        cut = value.reshape(blocks, width, rows, LANES)
        parts = [
            lax.dynamic_index_in_dim(cut, digit ^ k, 1, keepdims=False) for k in range(width)
        ]
        total = parts[0].astype(F32)
        for k in range(1, width):
            total = total + swap(parts[k], "dp", low * k).astype(F32)
        value = total.astype(BF16)
        path.append((low, width, digit))
    for low, width, digit in reversed(path):
        rows = value.shape[1]
        whole = jnp.zeros((blocks, width, rows, LANES), BF16)
        for k in range(width):
            part = value if k == 0 else swap(value, "dp", low * k)
            whole = lax.dynamic_update_index_in_dim(whole, part, digit ^ k, 1)
        value = whole.reshape(blocks, width * rows, LANES)
    return value


def local(
    image_in,
    out_cotangent,
    timesteps,
    clip_embed,
    context_tokens,
    image_count,
    norm1_gain,
    norm1_bias,
    conv1_weight,
    embed_weight,
    norm2_gain,
    norm2_bias,
    conv2_weight,
    conv2_bias,
    norm3_gain,
    norm3_bias,
    qkv_weight,
    context_weight,
    proj_weight,
):
    slots, pixels, width = image_in.shape
    me = lax.axis_index("mp")
    meta = jnp.stack([me, (me < image_count[0]).astype(jnp.int32)]).astype(jnp.int32)

    images = exchange(pick(image_in, me))
    conv1 = share(conv1_weight.reshape(9, C, LANES))

    half = EMB // 2
    frequency = jnp.exp(-math.log(10000.0) * jnp.arange(half, dtype=F32) / half)
    angles = timesteps.astype(F32)[:, None] * frequency[None, :]
    condition = jax.nn.silu(
        jnp.concatenate([jnp.cos(angles), jnp.sin(angles)], axis=1) + clip_embed.astype(F32)
    ).astype(BF16)
    scale_shift = jnp.dot(
        condition, embed_weight.reshape(EMB, 2 * LANES), preferred_element_type=F32
    ).reshape(slots, 2, LANES)
    doubled = jnp.concatenate([context_tokens, context_tokens], axis=1)
    context = jnp.dot(
        doubled.reshape(slots * 2 * CTX, EMB),
        context_weight.reshape(EMB, 2 * LANES),
        preferred_element_type=F32,
    ).astype(BF16).astype(F32).reshape(slots, 2 * CTX, 2, LANES)
    vectors = jnp.stack(
        [norm1_gain, norm1_bias, norm2_gain, norm2_bias, conv2_bias, norm3_gain, norm3_bias]
    )
    early = jnp.concatenate(
        [
            scale_shift,
            jnp.broadcast_to(vectors[None], (slots, 7, LANES)),
            jnp.zeros((slots, 7, LANES), F32),
            context[:, :, 0],
            context[:, :, 1],
        ],
        axis=1,
    )
    packs = exchange(pick(early, me))
    conv2 = share(conv2_weight.reshape(9, C, LANES))
    qkv_w = share(jnp.transpose(qkv_weight, (1, 0, 2)))
    proj_w = share(proj_weight)
    cots = exchange(pick(out_cotangent, me))

    factors = gather_dp(jnp.concatenate([condition, context_tokens.reshape(slots * CTX, EMB)], axis=0))

    block = struct((4, pixels, LANES), BF16)
    block32 = struct((4, pixels, LANES), F32)
    turned = struct((4, LANES, pixels), BF16)
    fields = struct((3, 4, pixels + 2 * PAD, LANES), BF16)
    field_scratch = pltpu.VMEM((3, 4, pixels + 2 * PAD, LANES), BF16)
    conv_scratch = pltpu.VMEM((4, 9, C, LANES), BF16)
    qkv_scratch = pltpu.VMEM((4, 3, C, LANES), BF16)
    grad_scratch = pltpu.VMEM((4, pixels, LANES), F32)
    conv_flops = 2 * pixels * 9 * C * C

    image, pack, first_t, inner, second, second_t = call(
        kernel_first,
        "first",
        [block, struct((4, E_ROWS, LANES), F32), turned, block32, block, turned],
        [smem()] + [anywhere()] * 12,
        [field_scratch, conv_scratch, pltpu.SemaphoreType.DMA((12,))],
        conv_flops,
    )(meta, *images, *conv1, *packs)
    middle, attn_t, qkv = call(
        kernel_second,
        "second",
        [block32, turned, struct((4, pixels, 3 * LANES), BF16)],
        [smem()] + [vmem()] * 3 + [anywhere()] * 8,
        [
            field_scratch,
            conv_scratch,
            qkv_scratch,
            pltpu.VMEM((4, pixels, LANES), BF16),
            pltpu.SemaphoreType.DMA((8,)),
        ],
        conv_flops + 6 * pixels * C * C,
    )(meta, second, image, pack, *conv2, *qkv_w)
    ctx_scratch = pltpu.VMEM((pixels, LANES), F32)
    turned_scratch = pltpu.VMEM((LANES, pixels), F32)
    *outs, cot, mixed, dqkv, dctx = call(
        kernel_attention,
        "attention",
        [struct((pixels, LANES), BF16)] * 4
        + [block, block, struct((4, pixels, 3 * LANES), BF16), struct((4, 2 * CTX, LANES), F32)],
        [smem()] + [vmem()] * 3 + [anywhere()] * 8,
        [
            pltpu.VMEM((4, LANES, C), BF16),
            pltpu.VMEM((4, pixels, LANES), BF16),
            ctx_scratch,
            ctx_scratch,
            ctx_scratch,
            ctx_scratch,
            grad_scratch,
            grad_scratch,
            turned_scratch,
            turned_scratch,
            pltpu.SemaphoreType.DMA((8,)),
        ],
        4 * 12 * pixels * pixels * C,
    )(meta, qkv, pack, middle, *cots, *proj_w)
    att_keep, att_send, dmiddle, field2, sums = call(
        kernel_back_attention,
        "back_attention",
        [struct((2, 4, C, LANES), BF16)] * 2 + [block32, fields, struct((4, S_ROWS, LANES), F32)],
        [smem()] + [vmem()] * 7 + [anywhere()] * 4,
        [
            qkv_scratch,
            pltpu.VMEM((4, LANES, pixels), BF16),
            grad_scratch,
            pltpu.SemaphoreType.DMA((4,)),
        ],
        14 * pixels * C * C,
    )(meta, dqkv, mixed, attn_t, cot, middle, pack, dctx, *qkv_w)
    weight_grad = call(
        kernel_weight_grad,
        "weight_grad",
        [struct((2, 9, C, LANES), BF16)] * 2,
        [smem()] + [vmem()] * 2,
        [],
        conv_flops,
    )
    conv2_keep, conv2_send = weight_grad(meta, second_t, field2)
    field1, *terms = call(
        kernel_back_second,
        "back_second",
        [fields] + [struct((S_ROWS, LANES), F32)] * 4,
        [smem()] + [vmem()] * 4 + [anywhere()] * 4,
        [conv_scratch, grad_scratch, pltpu.SemaphoreType.DMA((4,))],
        conv_flops,
    )(meta, field2, inner, pack, sums, *conv2)
    conv1_keep, conv1_send = weight_grad(meta, first_t, field1)
    back = call(
        kernel_back_first,
        "back_first",
        [struct((pixels, LANES), BF16)] * 4 + [struct((8, LANES), F32)] * 4,
        [smem()] + [vmem()] * 4 + [anywhere()] * 4,
        [conv_scratch, grad_scratch, pltpu.SemaphoreType.DMA((4,))],
        conv_flops,
    )(meta, field1, image, pack, dmiddle, *conv1)
    image_grads, last_terms = back[:4], back[4:]

    order = me ^ jnp.arange(4)

    def in_slots(parts):
        whole = jnp.zeros((4,) + parts[0].shape, parts[0].dtype)
        for k in range(4):
            whole = lax.dynamic_update_index_in_dim(whole, parts[k], me ^ k, 0)
        return whole

    del order
    block_out = in_slots(exchange(outs))
    image_grad = in_slots(exchange(image_grads))
    small = gather_dp(in_slots(exchange(terms)))
    last = gather_dp(sum(exchange(last_terms)))
    groups = small.shape[0]
    small = small.reshape(groups * slots, S_ROWS, LANES)
    inverse_total = 1.0 / jnp.sum(small[:, S_LIVE, 0])
    vector_sums = jnp.sum(small[:, :S_SCALE], axis=0) * inverse_total
    last_sums = jnp.sum(last, axis=0) * inverse_total
    all_condition = factors[:, :slots].reshape(groups * slots, EMB)
    all_tokens = factors[:, slots:].reshape(groups * slots * CTX, EMB)
    dscale_shift = small[:, S_SCALE : S_SHIFT + 1].reshape(groups * slots, 2 * LANES)
    dcontext = jnp.concatenate(
        [small[:, S_KEY : S_KEY + CTX], small[:, S_VALUE : S_VALUE + CTX]], axis=2
    ).reshape(groups * slots * CTX, 2 * LANES)
    over_rows = (((0,), (0,)), ((), ()))
    embed_grad = (
        lax.dot_general(
            all_condition.astype(F32),
            dscale_shift,
            over_rows,
            precision=lax.Precision.HIGHEST,
            preferred_element_type=F32,
        )
        * inverse_total
    ).reshape(EMB, 2, LANES)
    context_grad = (
        lax.dot_general(all_tokens, dcontext.astype(BF16), over_rows, preferred_element_type=F32)
        * inverse_total
    ).reshape(EMB, 2, LANES)
    att = reduce_grads(att_keep, att_send).astype(F32) * inverse_total
    conv2_grad = reduce_grads(conv2_keep, conv2_send).astype(F32) * inverse_total
    conv1_grad = reduce_grads(conv1_keep, conv1_send).astype(F32) * inverse_total
    return (
        block_out,
        image_grad,
        last_sums[0],
        last_sums[1],
        conv1_grad.reshape(3, 3, C, LANES),
        embed_grad,
        vector_sums[S_G2],
        vector_sums[S_B2],
        conv2_grad.reshape(3, 3, C, LANES),
        vector_sums[S_CB2],
        vector_sums[S_G3],
        vector_sums[S_B3],
        jnp.transpose(att[:3], (1, 0, 2)),
        context_grad,
        att[3].T,
    )


def solution(mesh):
    return jax.shard_map(
        local,
        mesh=mesh,
        in_specs=(
            P("dp", None, "mp"),
            P("dp", None, "mp"),
            P("dp"),
            P("dp", None),
            P("dp", None, None),
            P("dp"),
            P("mp"),
            P("mp"),
            P(None, None, None, "mp"),
            P(None, None, "mp"),
            P("mp"),
            P("mp"),
            P(None, None, None, "mp"),
            P("mp"),
            P("mp"),
            P("mp"),
            P(None, None, "mp"),
            P(None, None, "mp"),
            P("mp", None),
        ),
        out_specs=(
            P("dp", None, "mp"),
            P("dp", None, "mp"),
            P("mp"),
            P("mp"),
            P(None, None, None, "mp"),
            P(None, None, "mp"),
            P("mp"),
            P("mp"),
            P(None, None, None, "mp"),
            P("mp"),
            P("mp"),
            P("mp"),
            P(None, None, "mp"),
            P(None, None, "mp"),
            P("mp", None),
        ),
        check_vma=False,
    )
```

time: 1550 us -> 473 us (0.31)
  waiting for transfers between devices: 592 us -> 176 us
  local copies, waits for them, and re-layouts: 437 us -> 28.2 us
  matrix products: 252 us -> 2.16 us
  other arithmetic: 177 us -> 31.6 us
  Pallas kernels: 0 us -> 137 us
  starting transfers between devices: 3.76 us -> 89.3 us
  blocking collectives: 46.9 us -> 0 us
    psum x1 -> x0, waiting for transfers between devices: 289 us -> none  [local(): lax.psum((gain1_sum / image_total, bias1_sum / image_total, conv1_sum / i...]
    dot_general x151 -> x4, matrix products: 252 us -> 2.16 us  [the longest x1 1.03 us: local(): lax.dot_general(all_condition.astype(F32), dscale_shift, over_rows, preci...]
    slice x64 -> x6, local copies, waits for them, and re-layouts: 190 us -> 1.18 us  [the longest x1 0.93 us: local(): att[:3]]
    ppermute x0 -> x75, waiting for transfers between devices: none -> 176 us  [swap(): return lax.ppermute(value, axis, [(i, i ^ offset) for i in range(size)])]
    all_gather x16 -> x0, waiting for transfers between devices: 173 us -> none  [the longest x12 173 us: gather_features(): return lax.all_gather(field, 'mp', axis=1, tiled=True)]
    pallas_call x0 -> x7, Pallas kernels: none -> 137 us  [the longest x1 45 us: local(): call(kernel_attention, 'attention', [struct((pixels, LANES), BF16)] * 4 +...]
    while x761 -> x0, local copies, waits for them, and re-layouts: 132 us -> none
    while x48 -> x0, waiting for transfers between devices: 129 us -> none
  transfers between devices with their start and end apart: 33 -> 75, of which waited for: 25 -> 23; matrix products, arithmetic and copies ran while one was open for 31% -> 12% of each run, Pallas kernels for 0% -> 13%
where the time goes in v1:
time: 473 us; the launch traced here: 467 us
  waiting for transfers between devices  176 us (37%)
  Pallas kernels  137 us (29%)
  starting transfers between devices  89.3 us (19%)
  other arithmetic  31.6 us (7%)
  local copies, waits for them, and re-layouts  28.2 us (6%)
    ppermute x75, waiting for transfers between devices, swap(): return lax.ppermute(value, axis, [(i, i ^ offset) for i in range(size)])  176 us
    ppermute x75, starting transfers between devices, swap(): return lax.ppermute(value, axis, [(i, i ^ offset) for i in range(size)])  89.3 us
    pallas_call x1, Pallas kernels, local(): call(kernel_attention, 'attention', [struct((pixels, LANES), BF16)] * 4 +...  45 us
    pallas_call x1, Pallas kernels, local(): call(kernel_back_attention, 'back_attention', [struct((2, 4, C, LANES), B...  17.7 us
    pallas_call x1, Pallas kernels, local(): call(kernel_second, 'second', [block32, turned, struct((4, pixels, 3 * LA...  17 us
    pallas_call x1, Pallas kernels, local(): call(kernel_back_second, 'back_second', [fields] + [struct((S_ROWS, LANES...  15.4 us
    pallas_call x1, Pallas kernels, local(): call(kernel_first, 'first', [block, struct((4, E_ROWS, LANES), F32), turn...  14.9 us
    pallas_call x1, Pallas kernels, local(): conv1_keep, conv1_send = weight_grad(meta, first_t, field1)  13.4 us
  transfers between devices with their start and end apart: 75, of which 23 were waited for; matrix products, arithmetic and copies ran while one was open for 12% of the time, Pallas kernels for 13%

profile of v1, /device:TPU:0, one launch (start us, length us, event | category | flops | bytes accessed | tf_op | source)
XLA Modules:
  0.0 467.4 jit_solution(8997088062497383032)
XLA Ops:
  0.6 3.0 collective-permute-start.4
  16.2 39.4 %collective-permute-done.7.e2 = f32[32,128]{1,0:T(8,128)S(1)} collective-permute-done((f32[32,128]{1,0:T(8,128)S(1)}, f32[32,128]{1,0:T(8,128)S(1)}, u32[]{:S(2)}, u32[]{:S(2)}) %collective-permute-start.7) | collective-permute-done | bytes 16416 | tf_op jit(solution)/shard_map/ppermute | solution.py:776
  55.7 2.8 collective-permute-start.53
  62.9 9.4 %collective-permute-done.53 = bf16[2,20,2048]{2,1,0:T(8,128)(2,1)S(1)} collective-permute-done((bf16[2,20,2048]{2,1,0:T(8,128)(2,1)}, bf16[2,20,2048]{2,1,0:T(8,128)(2,1)S(1)}, u32[]{:S(2)}, u32[]{:S(2)}) %collective-permute-start.53) | collective-permute-done | bytes 163872 | tf_op jit(solution)/shard_map/ppermute | solution.py:776
  75.0 6.1 %collective-permute-done.1.i2 = bf16[1024,128]{1,0:T(8,128)(2,1)} collective-permute-done((bf16[1024,128]{1,0:T(8,128)(2,1)S(1)}, bf16[1024,128]{1,0:T(8,128)(2,1)}, u32[]{:S(2)}, u32[]{:S(2)}) %collective-permute-start.1) | collective-permute-done | bytes 262176 | tf_op jit(solution)/shard_map/ppermute | solution.py:776
  82.8 6.9 %collective-permute-done.2.i3 = bf16[1024,128]{1,0:T(8,128)(2,1)S(1)} collective-permute-done((bf16[1024,128]{1,0:T(8,128)(2,1)S(1)}, bf16[1024,128]{1,0:T(8,128)(2,1)S(1)}, u32[]{:S(2)}, u32[]{:S(2)}) %collective-permute-start.2) | collective-permute-done | bytes 262176 | tf_op jit(solution)/shard_map/ppermute | solution.py:776
  93.1 8.8 %collective-permute-done.13.p2 = bf16[3,512,128]{2,1,0:T(8,128)(2,1)} collective-permute-done((bf16[3,512,128]{2,1,0:T(8,128)(2,1)}, bf16[3,512,128]{2,1,0:T(8,128)(2,1)}, u32[]{:S(2)}, u32[]{:S(2)}) %collective-permute-start.13) | collective-permute-done | bytes 393248 | tf_op jit(solution)/shard_map/ppermute | solution.py:776
  103.5 14.9 %first.1 = (bf16[4,1024,128]{2,1,0:T(8,128)(2,1)}, f32[4,32,128]{2,1,0:T(8,128)}, bf16[4,128,1024]{2,1,0:T(8,128)(2,1)}, f32[4,1024,128]{2,1,0:T(8,128)}, bf16[4...) custom-call(s32[2]{0:T(128)} %pad_add_fusion.meta, bf16[1024,128]{1,0:T(8,128)(2,1)} %get-tuple-element.181.i0, ...), custom_call_target="tpu_custom_call" | custom-call | flops 4831838208 | tf_op jit(solution)/shard_map/first/pallas_call | solution.py:916
  121.2 17.0 %second.1 = (f32[4,1024,128]{2,1,0:T(8,128)}, bf16[4,128,1024]{2,1,0:T(8,128)(2,1)}, bf16[4,1024,384]{2,1,0:T(8,128)(2,1)}) custom-call(s32[2]{0:T(128)} %pad_add_fusion.meta, bf16[4,1024,128]{2,1,0:T(8,128)(2,1)} %get-tuple-element.54.second, bf16[4,1024,128]{2,1,0:T(8,128)(2,1)} %get-tuple-element.55.image, f32[4,32,128]{2,1,0:T(8,128)} %get-tuple-element.56.pack, ...), custom_call_target="tpu_custom_call" | custom-call | flops 6442450944 | tf_op jit(solution)/shard_map/second/pallas_call | solution.py:924
  139.2 45.0 %attention.1 = (bf16[1024,128]{1,0:T(8,128)(2,1)}, bf16[1024,128]{1,0:T(8,128)(2,1)}, bf16[1024,128]{1,0:T(8,128)(2,1)}, bf16[1024,128]{1,0:T(8,128)(2,1)}, bf16...) custom-call(s32[2]{0:T(128)} %pad_add_fusion.meta, ...), custom_call_target="tpu_custom_call" | custom-call | flops 25769803776 | tf_op jit(solution)/shard_map/attention/pallas_call | solution.py:940
  184.2 17.7 %back_attention.1 = (bf16[2,4,512,128]{3,2,1,0:T(8,128)(2,1)}, bf16[2,4,512,128]{3,2,1,0:T(8,128)(2,1)}, f32[4,1024,128]{2,1,0:T(8,128)}, bf16[3,4,1088,128]{3,2,1,0:T(8,128)(2,1)}, f32[4,16,128]{2,1,0:T(8,128)}) custom-call(s32[2]{0:T(128)} %pad_add_fusion.meta, bf16[4,1024,384]{2,1,0:T(8,128)(2,1)} %get-tuple-element.63.dqkv, ...), custom_call_target="tpu_custom_call" | custom-call | flops 3758096384 | tf_op jit(solution)/shard_map/back_attention/pallas_call | solution.py:961
  201.9 15.4 %back_second.1 = (bf16[3,4,1088,128]{3,2,1,0:T(8,128)(2,1)}, f32[16,128]{1,0:T(8,128)}, f32[16,128]{1,0:T(8,128)}, f32[16,128]{1,0:T(8,128)}, f32[16,128]{1,0:T(8,128)}) custom-call(s32[2]{0:T(128)} %pad_add_fusion.meta, bf16[3,4,1088,128]{3,2,1,0:T(8,128)(2,1)} %get-tuple-element.68.grad_field.field, f32[4,1024,128]{2,1,0:T(8,128)} %get-tuple-element.69.inner, ...), custom_call_target="tpu_custom_call" | custom-call | flops 4831838208 | tf_op jit(solution)/shard_map/back_second/pallas_call | solution.py:983
  218.3 13.3 %weight_grad.3 = (bf16[2,9,512,128]{3,2,1,0:T(8,128)(2,1)}, bf16[2,9,512,128]{3,2,1,0:T(8,128)(2,1)}) custom-call(s32[2]{0:T(128)} %pad_add_fusion.meta, bf16[4,128,1024]{2,1,0:T(8,128)(2,1)} %get-tuple-element.88.source_t, bf16[3,4,1088,128]{3,2,1,0:T(8,128)(2,1)} %get-tuple-element.68.grad_field.field), custom_call_target="tpu_custom_call" | custom-call | flops 4831838208 | tf_op jit(solution)/shard_map/weight_grad/pallas_call | solution.py:982
  231.7 13.4 %weight_grad.2 = (bf16[2,9,512,128]{3,2,1,0:T(8,128)(2,1)}, bf16[2,9,512,128]{3,2,1,0:T(8,128)(2,1)}) custom-call(s32[2]{0:T(128)} %pad_add_fusion.meta, bf16[4,128,1024]{2,1,0:T(8,128)(2,1)} %get-tuple-element.85.source_t, bf16[3,4,1088,128]{3,2,1,0:T(8,128)(2,1)} %get-tuple-element.71.field), custom_call_target="tpu_custom_call" | custom-call | flops 4831838208 | tf_op jit(solution)/shard_map/weight_grad/pallas_call | solution.py:991
  246.2 12.4 %back_first.1 = (bf16[4,1024,128]{2,1,0:T(8,128)(2,1)}, bf16[1024,128]{1,0:T(8,128)(2,1)}, bf16[1024,128]{1,0:T(8,128)(2,1)}, bf16[1024,128]{1,0:T(8,128)(2,1)},...) fusion(bf16[4,1024,128]{2,1,0:T(8,128)(2,1)} %broadcast.33.clone.1, ...), kind=kCustom, calls=%fused_computation.48 | custom fusion | flops 4831838208 | bytes 12337164 | tf_op jit(solution)/shard_map/back_first/pallas_call | solution.py:992
  267.4 2.8 collective-permute-start.31
  278.2 4.0 collective-permute-done.38
  283.9 4.0 collective-permute-done.39
  290.2 3.7 collective-permute-done.40
  306.1 9.3 %collective-permute-done.66 = bf16[4,512,128]{2,1,0:T(8,128)(2,1)S(1)} collective-permute-done((bf16[4,512,128]{2,1,0:T(8,128)(2,1)S(1)}, bf16[4,512,128]{2,1,0:T(8,128)(2,1)S(1)}, u32[]{:S(2)}, u32[]{:S(2)}) %collective-permute-start.66) | collective-permute-done | bytes 524320 | tf_op jit(solution)/shard_map/ppermute | solution.py:776
  322.4 3.5 collective-permute-done.67
  340.1 2.7 collective-permute-done.71
  351.8 4.0 collective-permute-done.74
  355.9 18.7 %collective-permute-done.56 = bf16[9,512,128]{2,1,0:T(8,128)(2,1)S(1)} collective-permute-done((bf16[9,512,128]{2,1,0:T(8,128)(2,1)S(1)}, bf16[9,512,128]{2,1,0:T(8,128)(2,1)S(1)}, u32[]{:S(2)}, u32[]{:S(2)}) %collective-permute-start.56) | collective-permute-done | bytes 1179680 | tf_op jit(solution)/shard_map/ppermute | solution.py:776
  378.6 18.0 %collective-permute-done.42 = bf16[9,512,128]{2,1,0:T(8,128)(2,1)S(1)} collective-permute-done((bf16[9,512,128]{2,1,0:T(8,128)(2,1)S(1)}, bf16[9,512,128]{2,1,0:T(8,128)(2,1)S(1)}, u32[]{:S(2)}, u32[]{:S(2)}) %collective-permute-start.42) | collective-permute-done | bytes 1179680 | tf_op jit(solution)/shard_map/ppermute | solution.py:776
  403.2 3.0 collective-permute-start.59
  407.6 3.2 collective-permute-done.43
  416.8 11.3 %collective-permute-start.61 = (bf16[9,64,128]{2,1,0:T(8,128)(2,1)S(1)}, bf16[9,64,128]{2,1,0:T(8,128)(2,1)S(1)}, u32[]{:S(2)}, u32[]{:S(2)}) collective-permute-start(bf16[9,64,128]{2,1,0:T(8,128)(2,1)S(1)} %get-tuple-element.172), channel_id=1, source_target_pairs={{0,8},{4,12},{8,0},{12,4},{16,24},{20,28},{24,16},{28,20},{1,9},{5... | collective-permute-start | bytes 442376 | tf_op jit(solution)/shard_map/ppermute | solution.py:776
  430.8 3.8 collective-permute-start.47
  438.5 4.5 collective-permute-done.62
  443.8 8.7 %collective-permute-done.48 = bf16[9,64,128]{2,1,0:T(8,128)(2,1)S(1)} collective-permute-done((bf16[9,64,128]{2,1,0:T(8,128)(2,1)S(1)}, bf16[9,64,128]{2,1,0:T(8,128)(2,1)S(1)}, u32[]{:S(2)}, u32[]{:S(2)}) %collective-permute-start.48) | collective-permute-done | bytes 147488 | tf_op jit(solution)/shard_map/ppermute | solution.py:776
  455.6 10.1 %collective-permute-done.50 = bf16[9,256,128]{2,1,0:T(8,128)(2,1)S(1)} collective-permute-done((bf16[9,256,128]{2,1,0:T(8,128)(2,1)S(1)}, bf16[9,256,128]{2,1,0:T(8,128)(2,1)S(1)}, u32[]{:S(2)}, u32[]{:S(2)}) %collective-permute-start.50) | collective-permute-done | bytes 589856 | tf_op jit(solution)/shard_map/ppermute | solution.py:776
  (320 shorter events, 123.4 us)
Async XLA Ops:
  0.6 73.2 %collective-permute-start.4 = (bf16[9,512,128]{2,1,0:T(8,128)(2,1)}, bf16[9,512,128]{2,1,0:T(8,128)(2,1)}, u32[]{:S(2)}, u32[]{:S(2)}) collective-permute-start(bf16[9,512,128]{2,1,0:T(8,128)(2,1)} %bitcast.7.w0), channel_id=1, source_target_pairs={{0,2},{1,3},{2,0},{3,1},{4,6},{5,7},{6,4},{7,5},{8,10},{9,11},{10,... | collective-permute-start | bytes 3538952 | tf_op jit(solution)/shard_map/ppermute | solution.py:776
  3.7 78.3 %collective-permute-start.10 = (bf16[9,512,128]{2,1,0:T(8,128)(2,1)}, bf16[9,512,128]{2,1,0:T(8,128)(2,1)}, u32[]{:S(2)}, u32[]{:S(2)}) collective-permute-start(bf16[9,512,128]{2,1,0:T(8,128)(2,1)} %bitcast.328), channel_id=1, source_target_pairs={{0,2},{1,3},{2,0},{3,1},{4,6},{5,7},{6,4},{7,5},{8,10},{9,11},{10,... | collective-permute-start | bytes 3538952 | tf_op jit(solution)/shard_map/ppermute | solution.py:776
  12.1 43.6 %collective-permute-start.7 = (f32[32,128]{1,0:T(8,128)S(1)}, f32[32,128]{1,0:T(8,128)S(1)}, u32[]{:S(2)}, u32[]{:S(2)}) collective-permute-start(f32[32,128]{1,0:T(8,128)S(1)} %get-tuple-element.195), channel_id=1, source_target_pairs={{0,2},{1,3},{2,0},{3,1},{4,6},{5,7},{6,4},{7,5},{8,10},{9,11},{10,... | collective-permute-start | bytes 49160 | tf_op jit(solution)/shard_map/ppermute | solution.py:776
  13.6 44.9 %collective-permute-start.8 = (f32[32,128]{1,0:T(8,128)S(1)}, f32[32,128]{1,0:T(8,128)S(1)}, u32[]{:S(2)}, u32[]{:S(2)}) collective-permute-start(f32[32,128]{1,0:T(8,128)S(1)} %get-tuple-element.194), channel_id=1, source_target_pairs={{0,3},{1,2},{2,1},{3,0},{4,7},{5,6},{6,5},{7,4},{8,11},{9,10},{10,... | collective-permute-start | bytes 49160 | tf_op jit(solution)/shard_map/ppermute | solution.py:776
  14.7 48.2 %collective-permute-start.52 = (bf16[2,20,2048]{2,1,0:T(8,128)(2,1)}, bf16[2,20,2048]{2,1,0:T(8,128)(2,1)S(1)}, u32[]{:S(2)}, u32[]{:S(2)}) collective-permute-start(bf16[2,20,2048]{2,1,0:T(8,128)(2,1)} %pad_maximum_fusion), channel_id=1, source_target_pairs={{0,8},{4,12},{8,0},{12,4},{16,24},{20,28},{24,16},{28,20},{1,9},{5... | collective-permute-start | bytes 491528 | tf_op jit(solution)/shard_map/ppermute | solution.py:776
  55.7 16.6 %collective-permute-start.53 = (bf16[2,20,2048]{2,1,0:T(8,128)(2,1)}, bf16[2,20,2048]{2,1,0:T(8,128)(2,1)S(1)}, u32[]{:S(2)}, u32[]{:S(2)}) collective-permute-start(bf16[2,20,2048]{2,1,0:T(8,128)(2,1)} %pad_maximum_fusion), channel_id=1, source_target_pairs={{0,16},{4,20},{8,24},{12,28},{16,0},{20,4},{24,8},{28,12},{1,17},{... | collective-permute-start | bytes 491528 | tf_op jit(solution)/shard_map/ppermute | solution.py:776
  62.9 38.9 %collective-permute-start.3 = (bf16[9,512,128]{2,1,0:T(8,128)(2,1)}, bf16[9,512,128]{2,1,0:T(8,128)(2,1)S(1)}, u32[]{:S(2)}, u32[]{:S(2)}) collective-permute-start(bf16[9,512,128]{2,1,0:T(8,128)(2,1)} %bitcast.7.w0), channel_id=1, source_target_pairs={{0,1},{1,0},{2,3},{3,2},{4,5},{5,4},{6,7},{7,6},{8,9},{9,8},{10,11... | collective-permute-start | bytes 3538952 | tf_op jit(solution)/shard_map/ppermute | solution.py:776
  73.8 29.5 %collective-permute-start.5 = (bf16[9,512,128]{2,1,0:T(8,128)(2,1)}, bf16[9,512,128]{2,1,0:T(8,128)(2,1)}, u32[]{:S(2)}, u32[]{:S(2)}) collective-permute-start(bf16[9,512,128]{2,1,0:T(8,128)(2,1)} %collective-permute-done.4.w2), channel_id=1, source_target_pairs={{0,1},{1,0},{2,3},{3,2},{4,5},{5,4},{6,7},{7,6},{8,9},{9,8},{10,11... | collective-permute-start | bytes 3538952 | tf_op jit(solution)/shard_map/ppermute | solution.py:776
  74.7 45.2 %collective-permute-start.9 = (bf16[9,512,128]{2,1,0:T(8,128)(2,1)}, bf16[9,512,128]{2,1,0:T(8,128)(2,1)}, u32[]{:S(2)}, u32[]{:S(2)}) collective-permute-start(bf16[9,512,128]{2,1,0:T(8,128)(2,1)} %bitcast.329), channel_id=1, source_target_pairs={{0,1},{1,0},{2,3},{3,2},{4,5},{5,4},{6,7},{7,6},{8,9},{9,8},{10,11... | collective-permute-start | bytes 3538952 | tf_op jit(solution)/shard_map/ppermute | solution.py:776
  82.0 38.7 %collective-permute-start.11 = (bf16[9,512,128]{2,1,0:T(8,128)(2,1)}, bf16[9,512,128]{2,1,0:T(8,128)(2,1)}, u32[]{:S(2)}, u32[]{:S(2)}) collective-permute-start(bf16[9,512,128]{2,1,0:T(8,128)(2,1)} %collective-permute-done.10.w2), channel_id=1, source_target_pairs={{0,1},{1,0},{2,3},{3,2},{4,5},{5,4},{6,7},{7,6},{8,9},{9,8},{10,11... | collective-permute-start | bytes 3538952 | tf_op jit(solution)/shard_map/ppermute | solution.py:776
  101.8 17.0 %collective-permute-start.12 = (bf16[3,512,128]{2,1,0:T(8,128)(2,1)S(1)}, bf16[3,512,128]{2,1,0:T(8,128)(2,1)S(1)}, u32[]{:S(2)}, u32[]{:S(2)}) collective-permute-start(bf16[3,512,128]{2,1,0:T(8,128)(2,1)S(1)} %bitcast.336), channel_id=1, source_target_pairs={{0,1},{1,0},{2,3},{3,2},{4,5},{5,4},{6,7},{7,6},{8,9},{9,8},{10,11... | collective-permute-start | bytes 1179656 | tf_op jit(solution)/shard_map/ppermute | solution.py:776
  101.9 16.6 %collective-permute-start.19 = (bf16[128,512]{1,0:T(8,128)(2,1)S(1)}, bf16[128,512]{1,0:T(8,128)(2,1)S(1)}, u32[]{:S(2)}, u32[]{:S(2)}) collective-permute-start(bf16[128,512]{1,0:T(8,128)(2,1)S(1)} %copy-done.29), channel_id=1, source_target_pairs={{0,2},{1,3},{2,0},{3,1},{4,6},{5,7},{6,4},{7,5},{8,10},{9,11},{10,... | collective-permute-start | bytes 393224 | tf_op jit(solution)/shard_map/ppermute | solution.py:776
  118.4 19.8 %collective-permute-start.18 = (bf16[128,512]{1,0:T(8,128)(2,1)S(1)}, bf16[128,512]{1,0:T(8,128)(2,1)S(1)}, u32[]{:S(2)}, u32[]{:S(2)}) collective-permute-start(bf16[128,512]{1,0:T(8,128)(2,1)S(1)} %copy-done.29), channel_id=1, source_target_pairs={{0,1},{1,0},{2,3},{3,2},{4,5},{5,4},{6,7},{7,6},{8,9},{9,8},{10,11... | collective-permute-start | bytes 393224 | tf_op jit(solution)/shard_map/ppermute | solution.py:776
  118.8 19.4 %collective-permute-start.15 = (bf16[1024,128]{1,0:T(8,128)(2,1)S(1)}, bf16[1024,128]{1,0:T(8,128)(2,1)S(1)}, u32[]{:S(2)}, u32[]{:S(2)}) collective-permute-start(bf16[1024,128]{1,0:T(8,128)(2,1)S(1)} %get-tuple-element.176), channel_id=1, source_target_pairs={{0,1},{1,0},{2,3},{3,2},{4,5},{5,4},{6,7},{7,6},{8,9},{9,8},{10,11... | collective-permute-start | bytes 786440 | tf_op jit(solution)/shard_map/ppermute | solution.py:776
  119.0 19.3 %collective-permute-start.16 = (bf16[1024,128]{1,0:T(8,128)(2,1)S(1)}, bf16[1024,128]{1,0:T(8,128)(2,1)S(1)}, u32[]{:S(2)}, u32[]{:S(2)}) collective-permute-start(bf16[1024,128]{1,0:T(8,128)(2,1)S(1)} %get-tuple-element.178), channel_id=1, source_target_pairs={{0,2},{1,3},{2,0},{3,1},{4,6},{5,7},{6,4},{7,5},{8,10},{9,11},{10,... | collective-permute-start | bytes 786440 | tf_op jit(solution)/shard_map/ppermute | solution.py:776
  119.9 18.4 %collective-permute-start.17 = (bf16[1024,128]{1,0:T(8,128)(2,1)S(1)}, bf16[1024,128]{1,0:T(8,128)(2,1)S(1)}, u32[]{:S(2)}, u32[]{:S(2)}) collective-permute-start(bf16[1024,128]{1,0:T(8,128)(2,1)S(1)} %get-tuple-element.175), channel_id=1, source_target_pairs={{0,3},{1,2},{2,1},{3,0},{4,7},{5,6},{6,5},{7,4},{8,11},{9,10},{10,... | collective-permute-start | bytes 786440 | tf_op jit(solution)/shard_map/ppermute | solution.py:776
  120.7 17.6 %collective-permute-start.20 = (bf16[128,512]{1,0:T(8,128)(2,1)S(1)}, bf16[128,512]{1,0:T(8,128)(2,1)S(1)}, u32[]{:S(2)}, u32[]{:S(2)}) collective-permute-start(bf16[128,512]{1,0:T(8,128)(2,1)S(1)} %collective-permute-done.19.w2), channel_id=1, source_target_pairs={{0,1},{1,0},{2,3},{3,2},{4,5},{5,4},{6,7},{7,6},{8,9},{9,8},{10,11... | collective-permute-start | bytes 393224 | tf_op jit(solution)/shard_map/ppermute | solution.py:776
  217.3 52.9 %collective-permute-start.34 = (f32[16,128]{1,0:T(8,128)}, f32[16,128]{1,0:T(8,128)S(1)}, u32[]{:S(2)}, u32[]{:S(2)}) collective-permute-start(f32[16,128]{1,0:T(8,128)} %get-tuple-element.82), channel_id=1, source_target_pairs={{0,1},{1,0},{2,3},{3,2},{4,5},{5,4},{6,7},{7,6},{8,9},{9,8},{10,11... | collective-permute-start | bytes 24584 | tf_op jit(solution)/shard_map/ppermute | solution.py:776
  217.4 54.9 %collective-permute-start.35 = (f32[16,128]{1,0:T(8,128)}, f32[16,128]{1,0:T(8,128)S(1)}, u32[]{:S(2)}, u32[]{:S(2)}) collective-permute-start(f32[16,128]{1,0:T(8,128)} %get-tuple-element.83), channel_id=1, source_target_pairs={{0,2},{1,3},{2,0},{3,1},{4,6},{5,7},{6,4},{7,5},{8,10},{9,11},{10,... | collective-permute-start | bytes 24584 | tf_op jit(solution)/shard_map/ppermute | solution.py:776
  263.6 39.7 %collective-permute-start.65 = (bf16[2,4,512,128]{3,2,1,0:T(8,128)(2,1)}, bf16[2,4,512,128]{3,2,1,0:T(8,128)(2,1)}, u32[]{:S(2)}, u32[]{:S(2)}) collective-permute-start(bf16[2,4,512,128]{3,2,1,0:T(8,128)(2,1)} %get-tuple-element.92), channel_id=1, source_target_pairs={{0,1},{1,0},{2,3},{3,2},{4,5},{5,4},{6,7},{7,6},{8,9},{9,8},{10,11... | collective-permute-start | bytes 3145736 | tf_op jit(solution)/shard_map/ppermute | solution.py:776
  275.2 68.6 %collective-permute-start.55 = (bf16[2,9,512,128]{3,2,1,0:T(8,128)(2,1)}, bf16[2,9,512,128]{3,2,1,0:T(8,128)(2,1)}, u32[]{:S(2)}, u32[]{:S(2)}) collective-permute-start(bf16[2,9,512,128]{3,2,1,0:T(8,128)(2,1)} %get-tuple-element.90), channel_id=1, source_target_pairs={{0,1},{1,0},{2,3},{3,2},{4,5},{5,4},{6,7},{7,6},{8,9},{9,8},{10,11... | collective-permute-start | bytes 7077896 | tf_op jit(solution)/shard_map/ppermute | solution.py:776
  275.2 71.6 %collective-permute-start.41 = (bf16[2,9,512,128]{3,2,1,0:T(8,128)(2,1)}, bf16[2,9,512,128]{3,2,1,0:T(8,128)(2,1)}, u32[]{:S(2)}, u32[]{:S(2)}) collective-permute-start(bf16[2,9,512,128]{3,2,1,0:T(8,128)(2,1)} %get-tuple-element.87), channel_id=1, source_target_pairs={{0,1},{1,0},{2,3},{3,2},{4,5},{5,4},{6,7},{7,6},{8,9},{9,8},{10,11... | collective-permute-start | bytes 7077896 | tf_op jit(solution)/shard_map/ppermute | solution.py:776
  277.7 39.1 %collective-permute-start.24 = (bf16[1024,128]{1,0:T(8,128)(2,1)}, bf16[1024,128]{1,0:T(8,128)(2,1)}, u32[]{:S(2)}, u32[]{:S(2)}) collective-permute-start(bf16[1024,128]{1,0:T(8,128)(2,1)} %get-tuple-element.156), channel_id=1, source_target_pairs={{0,1},{1,0},{2,3},{3,2},{4,5},{5,4},{6,7},{7,6},{8,9},{9,8},{10,11... | collective-permute-start | bytes 786440 | tf_op jit(solution)/shard_map/ppermute | solution.py:776
  293.9 26.1 %collective-permute-start.25 = (bf16[1024,128]{1,0:T(8,128)(2,1)}, bf16[1024,128]{1,0:T(8,128)(2,1)}, u32[]{:S(2)}, u32[]{:S(2)}) collective-permute-start(bf16[1024,128]{1,0:T(8,128)(2,1)} %get-tuple-element.158), channel_id=1, source_target_pairs={{0,2},{1,3},{2,0},{3,1},{4,6},{5,7},{6,4},{7,5},{8,10},{9,11},{10,... | collective-permute-start | bytes 786440 | tf_op jit(solution)/shard_map/ppermute | solution.py:776
  345.6 29.0 %collective-permute-start.56 = (bf16[9,512,128]{2,1,0:T(8,128)(2,1)S(1)}, bf16[9,512,128]{2,1,0:T(8,128)(2,1)S(1)}, u32[]{:S(2)}, u32[]{:S(2)}) collective-permute-start(bf16[9,512,128]{2,1,0:T(8,128)(2,1)S(1)} %fusion.3), channel_id=1, source_target_pairs={{0,2},{1,3},{2,0},{3,1},{4,6},{5,7},{6,4},{7,5},{8,10},{9,11},{10,... | collective-permute-start | bytes 3538952 | tf_op jit(solution)/shard_map/ppermute | solution.py:776
  348.5 48.2 %collective-permute-start.42 = (bf16[9,512,128]{2,1,0:T(8,128)(2,1)S(1)}, bf16[9,512,128]{2,1,0:T(8,128)(2,1)S(1)}, u32[]{:S(2)}, u32[]{:S(2)}) collective-permute-start(bf16[9,512,128]{2,1,0:T(8,128)(2,1)S(1)} %fusion.2), channel_id=1, source_target_pairs={{0,2},{1,3},{2,0},{3,1},{4,6},{5,7},{6,4},{7,5},{8,10},{9,11},{10,... | collective-permute-start | bytes 3538952 | tf_op jit(solution)/shard_map/ppermute | solution.py:776
  377.1 24.8 %collective-permute-start.57 = (bf16[9,256,128]{2,1,0:T(8,128)(2,1)}, bf16[9,256,128]{2,1,0:T(8,128)(2,1)}, u32[]{:S(2)}, u32[]{:S(2)}) collective-permute-start(bf16[9,256,128]{2,1,0:T(8,128)(2,1)} %dynamic-slice_bitcast_fusion), channel_id=1, source_target_pairs={{0,4},{4,0},{8,12},{12,8},{16,20},{20,16},{24,28},{28,24},{1,5},{5... | collective-permute-start | bytes 1769480 | tf_op jit(solution)/shard_map/ppermute | solution.py:776
  412.1 17.0 %collective-permute-start.44 = (bf16[9,64,128]{2,1,0:T(8,128)(2,1)S(1)}, bf16[9,64,128]{2,1,0:T(8,128)(2,1)S(1)}, u32[]{:S(2)}, u32[]{:S(2)}) collective-permute-start(bf16[9,64,128]{2,1,0:T(8,128)(2,1)S(1)} %get-tuple-element.186), channel_id=1, source_target_pairs={{0,8},{4,12},{8,0},{12,4},{16,24},{20,28},{24,16},{28,20},{1,9},{5... | collective-permute-start | bytes 442376 | tf_op jit(solution)/shard_map/ppermute | solution.py:776
  412.2 18.4 %collective-permute-start.45 = (bf16[9,64,128]{2,1,0:T(8,128)(2,1)S(1)}, bf16[9,64,128]{2,1,0:T(8,128)(2,1)S(1)}, u32[]{:S(2)}, u32[]{:S(2)}) collective-permute-start(bf16[9,64,128]{2,1,0:T(8,128)(2,1)S(1)} %get-tuple-element.188), channel_id=1, source_target_pairs={{0,16},{4,20},{8,24},{12,28},{16,0},{20,4},{24,8},{28,12},{1,17},{... | collective-permute-start | bytes 442376 | tf_op jit(solution)/shard_map/ppermute | solution.py:776
  414.7 15.8 %collective-permute-start.46 = (bf16[9,64,128]{2,1,0:T(8,128)(2,1)S(1)}, bf16[9,64,128]{2,1,0:T(8,128)(2,1)S(1)}, u32[]{:S(2)}, u32[]{:S(2)}) collective-permute-start(bf16[9,64,128]{2,1,0:T(8,128)(2,1)S(1)} %get-tuple-element.187), channel_id=1, source_target_pairs={{0,24},{4,28},{8,16},{12,20},{16,8},{20,12},{24,0},{28,4},{1,25},{... | collective-permute-start | bytes 442376 | tf_op jit(solution)/shard_map/ppermute | solution.py:776
  416.8 20.3 %collective-permute-start.61 = (bf16[9,64,128]{2,1,0:T(8,128)(2,1)S(1)}, bf16[9,64,128]{2,1,0:T(8,128)(2,1)S(1)}, u32[]{:S(2)}, u32[]{:S(2)}) collective-permute-start(bf16[9,64,128]{2,1,0:T(8,128)(2,1)S(1)} %get-tuple-element.172), channel_id=1, source_target_pairs={{0,8},{4,12},{8,0},{12,4},{16,24},{20,28},{24,16},{28,20},{1,9},{5... | collective-permute-start | bytes 442376 | tf_op jit(solution)/shard_map/ppermute | solution.py:776
  434.6 17.9 %collective-permute-start.48 = (bf16[9,64,128]{2,1,0:T(8,128)(2,1)S(1)}, bf16[9,64,128]{2,1,0:T(8,128)(2,1)S(1)}, u32[]{:S(2)}, u32[]{:S(2)}) collective-permute-start(bf16[9,64,128]{2,1,0:T(8,128)(2,1)S(1)} %get-tuple-element.174), channel_id=1, source_target_pairs={{0,16},{4,20},{8,24},{12,28},{16,0},{20,4},{24,8},{28,12},{1,17},{... | collective-permute-start | bytes 442376 | tf_op jit(solution)/shard_map/ppermute | solution.py:776
  (84 other events, 733.9 us)

commit v2 on v1

--- a/solution.py
+++ b/solution.py
@@ -24,8 +24,8 @@
 E_SCALE, E_SHIFT, E_G1, E_B1, E_G2, E_B2, E_CB2, E_G3, E_B3 = range(9)
 E_KEY, E_VALUE, E_ROWS = 16, 24, 32
 S_G3, S_B3, S_CB2, S_G2, S_B2, S_SCALE, S_SHIFT, S_LIVE = range(8)
-S_KEY, S_VALUE, S_ROWS = 8, 12, 16
-VMEM_LIMIT = 56 << 20
+S_KEY, S_VALUE, S_G1, S_B1, S_ROWS = 8, 12, 16, 17, 24
+VMEM_LIMIT = 30 << 20
 
 
 def vmem():
@@ -33,7 +33,7 @@
 
 
 def anywhere():
-    return pl.BlockSpec(memory_space=pl.ANY)
+    return pl.BlockSpec(memory_space=pltpu.HBM)
 
 
 def smem():
@@ -69,6 +69,26 @@
     return copies
 
 
+def fetch_routed(sources, target, me, parity, sems, first):
+    quarter = target.shape[-2] // 4
+    copies = []
+    for index, source in enumerate(sources):
+        slot = jnp.bitwise_xor(me, (0, 1, 2, 2, 2, 3, 3, 3)[index])
+        place = target.at[slot]
+        if index >= 2:
+            kind = (index - 2) % 3
+            rows = 2 * quarter if kind == 0 else quarter
+            half = parity if kind == 0 else 1 - parity
+            start = half * 2 * quarter + (quarter if kind == 2 else 0)
+            start = pl.multiple_of(start, quarter)
+            lead = (slice(None),) * (len(place.shape) - 2)
+            place = place.at[lead + (pl.ds(start, rows), slice(None))]
+        copy = pltpu.make_async_copy(source, place, sems.at[first + index])
+        copy.start()
+        copies.append(copy)
+    return copies
+
+
 def wait_all(copies):
     for copy in copies:
         copy.wait()
@@ -91,17 +111,6 @@
 
 def column_sum(rows8):
     return jnp.sum(rows8, axis=0, keepdims=True)
-
-
-def accumulate(rows, strip, functions):
-    def body(index, carry):
-        start = pl.multiple_of(index * strip, strip)
-        found = functions(start)
-        return tuple(old + fold(new) for old, new in zip(carry, found))
-
-    count = len(jax.eval_shape(lambda: functions(0))) if False else None
-    del count
-    return body
 
 
 def sum_strips(pixels, strip, width, function):
@@ -207,14 +216,14 @@
 
 
 def kernel_first(
-    meta, i0, i1, i2, i3, w0, w1, w2, w3, e0, e1, e2, e3,
-    image, pack, first_t, inner, second, second_t, field, weight, sems,
+    meta, i0, i1, i2, i3, e0, e1, e2, e3, w0, w1, w2, w3, w4, w5, w6, w7,
+    image, pack, first_t, inner, field, weight, sems,
 ):
     pixels = image.shape[1]
     me = meta[0]
     image_copies = fetch((i0, i1, i2, i3), image, me, sems, 0)
     pack_copies = fetch((e0, e1, e2, e3), pack, me, sems, 4)
-    weight_copies = fetch((w0, w1, w2, w3), weight, me, sems, 8)
+    weight_copies = fetch_routed((w0, w1, w2, w3, w4, w5, w6, w7), weight, me, meta[2], sems, 8)
     clear_padding(field, pixels)
     wait_all(image_copies)
     wait_all(pack_copies)
@@ -244,6 +253,18 @@
             inner[b, pl.ds(start, tile.shape[0]), :] = tile[:, b * LANES : (b + 1) * LANES]
 
     conv_tiles(field, weight, pixels, 512, write)
+
+
+def kernel_second(
+    meta, inner, image, pack, p0, p1, p2, p3, w0, w1, w2, w3, w4, w5, w6, w7,
+    middle, second_t, attn_t, qkv, field, weight, qkv_weight, attn, sems,
+):
+    pixels = image.shape[1]
+    me = meta[0]
+    qkv_copies = fetch((p0, p1, p2, p3), qkv_weight, me, sems, 0)
+    weight_copies = fetch_routed((w0, w1, w2, w3, w4, w5, w6, w7), weight, me, meta[2], sems, 4)
+    clear_padding(field, pixels)
+    strip = 128
     means2, inverses2 = norm_rows(pixels, strip, lambda b, start: inner[b, pl.ds(start, strip), :])
 
     def modulate(index, carry):
@@ -256,31 +277,11 @@
             normed = (inner[b, pl.ds(start, strip), :] - means2[b]) * inverses2[b]
             modulated = (normed * gain + bias) * (1.0 + scale) + shift
             after = modulated * jax.nn.sigmoid(modulated)
-            second[b, pl.ds(start, strip), :] = after.astype(BF16)
+            store_shifted(field, b, start, after)
             second_t[b, :, pl.ds(start, strip)] = after.T.astype(BF16)
         return carry
 
     lax.fori_loop(0, pixels // strip, modulate, 0)
-
-
-def kernel_second(
-    meta, second, image, pack, w0, w1, w2, w3, p0, p1, p2, p3,
-    middle, attn_t, qkv, field, weight, qkv_weight, attn, sems,
-):
-    pixels = image.shape[1]
-    me = meta[0]
-    weight_copies = fetch((w0, w1, w2, w3), weight, me, sems, 0)
-    qkv_copies = fetch((p0, p1, p2, p3), qkv_weight, me, sems, 4)
-    clear_padding(field, pixels)
-    strip = 128
-
-    def spread(index, carry):
-        start = pl.multiple_of(index * strip, strip)
-        for b in range(4):
-            store_shifted(field, b, start, second[b, pl.ds(start, strip), :].astype(F32))
-        return carry
-
-    lax.fori_loop(0, pixels // strip, spread, 0)
     wait_all(weight_copies)
 
     def write(start, tile):
@@ -540,8 +541,8 @@
 
 
 def kernel_back_attention(
-    meta, dqkv, mixed, attn_t, cot, middle, pack, dctx, p0, p1, p2, p3,
-    keep, send, dmiddle, field, sums, qkv_weight, cot_t, dattn, sems,
+    meta, dqkv, cot, middle, pack, dctx, p0, p1, p2, p3,
+    dmiddle, field, sums, d0, d1, d2, d3, qkv_weight, dattn, sems,
 ):
     pixels = cot.shape[1]
     me = meta[0]
@@ -549,52 +550,19 @@
     qkv_copies = fetch((p0, p1, p2, p3), qkv_weight, me, sems, 0)
     strip = 128
     clear_padding(field, pixels)
-
-    def turn(index, carry):
-        start = pl.multiple_of(index * strip, strip)
-        for b in range(4):
-            cot_t[b, :, pl.ds(start, strip)] = cot[b, pl.ds(start, strip), :].astype(F32).T.astype(BF16)
-        return carry
-
-    lax.fori_loop(0, pixels // strip, turn, 0)
+    means, inverses = norm_rows(pixels, strip, lambda b, start: middle[b, pl.ds(start, strip), :])
     wait_all(qkv_copies)
 
     def back(index, carry):
-        start = pl.multiple_of(index * 256, 256)
-        left = jnp.concatenate([dqkv[s, pl.ds(start, 256), :] for s in range(4)], axis=1)
+        start = pl.multiple_of(index * 512, 512)
+        left = jnp.concatenate([dqkv[s, pl.ds(start, 512), :] for s in range(4)], axis=1)
         right = jnp.concatenate([qkv_weight[s, kind] for s in range(4) for kind in range(3)], axis=1)
         tile = lax.dot_general(left, right, (((1,), (1,)), ((), ())), preferred_element_type=F32)
         for b in range(4):
-            dattn[b, pl.ds(start, 256), :] = tile[:, b * LANES : (b + 1) * LANES]
-        return carry
-
-    lax.fori_loop(0, pixels // 256, back, 0)
-
-    def weights(offset, carry):
-        s = jnp.bitwise_xor(me, offset)
-        place = offset // 2
-        attn_all = attn_t[...].reshape(C, pixels)
-        cot_all = cot_t[...].reshape(C, pixels)
-        grad = jnp.dot(attn_all, dqkv[s], preferred_element_type=F32).astype(BF16)
-        other = jnp.dot(cot_all, mixed[s], preferred_element_type=F32).astype(BF16)
-
-        def put(target):
-            for kind in range(3):
-                target[place, kind] = grad[:, kind * LANES : (kind + 1) * LANES]
-            target[place, 3] = other
-
-        @pl.when(offset % 2 == 0)
-        def _():
-            put(keep)
-
-        @pl.when(offset % 2 == 1)
-        def _():
-            put(send)
-
-        return carry
-
-    lax.fori_loop(0, 4, weights, 0)
-    means, inverses = norm_rows(pixels, strip, lambda b, start: middle[b, pl.ds(start, strip), :])
+            dattn[b, pl.ds(start, 512), :] = tile[:, b * LANES : (b + 1) * LANES]
+        return carry
+
+    lax.fori_loop(0, pixels // 512, back, 0)
     gains = [pack[b, E_G3 : E_G3 + 1, :] for b in range(4)]
 
     def read_normed(b, start):
@@ -623,52 +591,102 @@
         sums[b, S_CB2 : S_CB2 + 1, :] = column_sum(branch[b])
         sums[b, S_LIVE : S_LIVE + 1, :] = jnp.full((1, LANES), 1.0, F32) * alive
         sums[b, S_KEY : S_KEY + 8, :] = dctx[b]
-
-
-def kernel_weight_grad(meta, source_t, field, keep, send):
-    pixels = source_t.shape[2]
+    for offset, target in enumerate((d0, d1, d2, d3)):
+        target[...] = field[1, jnp.bitwise_xor(me, offset), PAD : PAD + pixels, :]
+
+
+def kernel_attention_grad(meta, dqkv, mixed, attn_t, cot, keep, send, cot_t):
+    pixels = cot.shape[1]
     me = meta[0]
-    left = source_t[...].reshape(C, pixels)
+    strip = 128
+
+    def turn(index, carry):
+        start = pl.multiple_of(index * strip, strip)
+        for b in range(4):
+            cot_t[b, :, pl.ds(start, strip)] = cot[b, pl.ds(start, strip), :].astype(F32).T.astype(BF16)
+        return carry
+
+    lax.fori_loop(0, pixels // strip, turn, 0)
+
+    def weights(offset, carry):
+        s = jnp.bitwise_xor(me, offset)
+        place = offset // 2
+        attn_all = attn_t[...].reshape(C, pixels)
+        cot_all = cot_t[...].reshape(C, pixels)
+        grad = jnp.dot(attn_all, dqkv[s], preferred_element_type=F32).astype(BF16)
+        other = jnp.dot(cot_all, mixed[s], preferred_element_type=F32).astype(BF16)
+
+        def put(target):
+            for kind in range(3):
+                target[place, kind] = grad[:, kind * LANES : (kind + 1) * LANES]
+            target[place, 3] = other
+
+        @pl.when(offset % 2 == 0)
+        def _():
+            put(keep)
+
+        @pl.when(offset % 2 == 1)
+        def _():
+            put(send)
+
+        return carry
+
+    lax.fori_loop(0, 4, weights, 0)
+
+
+def weight_taps(half, sources, field, target):
+    pixels = sources[0].shape[2]
 
     def body(index, carry):
-        tap = index // 2
-        side = index % 2
-        a = tap // 3
-        b = tap % 3
-        start = pl.multiple_of((2 - a) * SIDE, 32)
-        first = jnp.bitwise_xor(me, side)
-        right = jnp.concatenate(
-            [
-                field[2 - b, first, pl.ds(start, pixels), :],
-                field[2 - b, jnp.bitwise_xor(first, 2), pl.ds(start, pixels), :],
-            ],
-            axis=1,
+        left = jnp.concatenate(
+            [source[pl.ds(2 * half, 2)].reshape(2 * LANES, pixels) for source in sources], axis=1
         )
-        grad = jnp.dot(left, right, preferred_element_type=F32).astype(BF16)
-
-        @pl.when(side == 0)
+        columns = []
+        for tap in (2 * index, jnp.minimum(2 * index + 1, 8)):
+            start = pl.multiple_of((2 - tap // 3) * SIDE, 32)
+            side = 2 - lax.rem(tap, 3)
+            columns.append(
+                jnp.concatenate([field[side, k, pl.ds(start, pixels), :] for k in range(4)], axis=0)
+            )
+        grad = jnp.dot(left, jnp.concatenate(columns, axis=1), preferred_element_type=F32)
+        target[2 * index] = grad[:, :LANES].astype(target.dtype)
+
+        @pl.when(index < 4)
         def _():
-            keep[0, tap] = grad[:, :LANES]
-            keep[1, tap] = grad[:, LANES:]
-
-        @pl.when(side == 1)
-        def _():
-            send[0, tap] = grad[:, :LANES]
-            send[1, tap] = grad[:, LANES:]
-
-        return carry
-
-    lax.fori_loop(0, 18, body, 0)
+            target[2 * index + 1] = grad[:, LANES:].astype(target.dtype)
+
+        return carry
+
+    lax.fori_loop(0, 5, body, 0)
+
+
+def kernel_weight_send(digit, u0, u1, u2, u3, d0, d1, d2, d3, send, field):
+    pixels = u0.shape[2]
+    clear_padding(field, pixels)
+    strip = 128
+
+    def spread(index, carry):
+        start = pl.multiple_of(index * strip, strip)
+        for k, source in enumerate((d0, d1, d2, d3)):
+            store_shifted(field, k, start, source[pl.ds(start, strip), :].astype(F32))
+        return carry
+
+    lax.fori_loop(0, pixels // strip, spread, 0)
+    weight_taps(1 - digit[0], (u0, u1, u2, u3), field, send)
+
+
+def kernel_weight_own(digit, u0, u1, u2, u3, field, own):
+    weight_taps(digit[0], (u0, u1, u2, u3), field, own)
 
 
 def kernel_back_second(
-    meta, grad_field, inner, pack, sums_in, w0, w1, w2, w3,
-    field, s0, s1, s2, s3, weight, grad, sems,
+    meta, grad_field, inner, pack, sums_in, w0, w1, w2, w3, w4, w5, w6, w7,
+    field, sums, d0, d1, d2, d3, weight, grad, sems,
 ):
     pixels = inner.shape[1]
     me = meta[0]
     strip = 128
-    weight_copies = fetch((w0, w1, w2, w3), weight, me, sems, 0)
+    weight_copies = fetch_routed((w0, w1, w2, w3, w4, w5, w6, w7), weight, me, meta[2], sems, 0)
     clear_padding(field, pixels)
     means, inverses = norm_rows(pixels, strip, lambda b, start: inner[b, pl.ds(start, strip), :])
     wait_all(weight_copies)
@@ -706,39 +724,38 @@
     gain_sums, bias_sums = norm_back_strips(
         pixels, strip, read_normed, lambda b, start: grad[b, pl.ds(start, strip), :], gains, inverses, write
     )
-    for offset, target in enumerate((s0, s1, s2, s3)):
-        other = jnp.bitwise_xor(me, offset)
-        target[...] = sums_in[other]
-        for b in range(4):
-
-            @pl.when(other == b)
-            def _():
-                target[S_G2 : S_G2 + 1, :] = gain_sums[b]
-                target[S_B2 : S_B2 + 1, :] = bias_sums[b]
-                target[S_SCALE : S_SCALE + 1, :] = column_sum(modulation[2 * b])
-                target[S_SHIFT : S_SHIFT + 1, :] = column_sum(modulation[2 * b + 1])
+    for b in range(4):
+        sums[b] = sums_in[b]
+        sums[b, S_G2 : S_G2 + 1, :] = gain_sums[b]
+        sums[b, S_B2 : S_B2 + 1, :] = bias_sums[b]
+        sums[b, S_SCALE : S_SCALE + 1, :] = column_sum(modulation[2 * b])
+        sums[b, S_SHIFT : S_SHIFT + 1, :] = column_sum(modulation[2 * b + 1])
+    for offset, target in enumerate((d0, d1, d2, d3)):
+        target[...] = field[1, jnp.bitwise_xor(me, offset), PAD : PAD + pixels, :]
+
+
+def kernel_back_conv(meta, grad_field, w0, w1, w2, w3, w4, w5, w6, w7, grad, weight, sems):
+    pixels = grad.shape[1]
+    wait_all(fetch_routed((w0, w1, w2, w3, w4, w5, w6, w7), weight, meta[0], meta[2], sems, 0))
+
+    def write_grad(start, half, tile):
+        for b in range(2):
+            grad[2 * half + b, pl.ds(start, tile.shape[0]), :] = tile[:, b * LANES : (b + 1) * LANES]
+
+    conv_back_tiles(grad_field, weight, pixels, 512, write_grad)
 
 
 def kernel_back_first(
-    meta, grad_field, image, pack, dmiddle, w0, w1, w2, w3,
-    g0, g1, g2, g3, s0, s1, s2, s3, weight, grad, sems,
+    meta, grad_in, image, pack, dmiddle, sums_in, g0, g1, g2, g3, s0, s1, s2, s3, grad,
 ):
     pixels = image.shape[1]
     me = meta[0]
     strip = 128
-    weight_copies = fetch((w0, w1, w2, w3), weight, me, sems, 0)
 
     def read(b, start):
         return image[b, pl.ds(start, strip), :].astype(F32)
 
     means, inverses = norm_rows(pixels, strip, read)
-    wait_all(weight_copies)
-
-    def write_grad(start, half, tile):
-        for b in range(2):
-            grad[2 * half + b, pl.ds(start, tile.shape[0]), :] = tile[:, b * LANES : (b + 1) * LANES]
-
-    conv_back_tiles(grad_field, weight, pixels, 512, write_grad)
     gains = [pack[b, E_G1 : E_G1 + 1, :] for b in range(4)]
 
     def read_normed(b, start):
@@ -748,7 +765,7 @@
         start = pl.multiple_of(index * strip, strip)
         for b in range(4):
             before = read_normed(b, start) * gains[b] + pack[b, E_B1 : E_B1 + 1, :]
-            grad[b, pl.ds(start, strip), :] = silu_slope(before, grad[b, pl.ds(start, strip), :])
+            grad[b, pl.ds(start, strip), :] = silu_slope(before, grad_in[b, pl.ds(start, strip), :])
         return carry
 
     lax.fori_loop(0, pixels // strip, slope, 0)
@@ -762,18 +779,145 @@
     for offset, (target, small) in enumerate(zip((g0, g1, g2, g3), (s0, s1, s2, s3))):
         other = jnp.bitwise_xor(me, offset)
         target[...] = grad[other].astype(BF16)
-        small[...] = jnp.zeros((8, LANES), F32)
+        small[...] = sums_in[other]
         for b in range(4):
 
             @pl.when(other == b)
             def _():
-                small[0:1, :] = gain_sums[b]
-                small[1:2, :] = bias_sums[b]
+                small[S_G1 : S_G1 + 1, :] = gain_sums[b]
+                small[S_B1 : S_B1 + 1, :] = bias_sums[b]
+
+
+def kernel_factor_grads(
+    meta, factors, small0, small1, small2, small3, embed, context, vectors, scale
+):
+    me = meta[0]
+    groups = factors.shape[0]
+    smalls = (small0, small1, small2, small3)
+    total = jnp.zeros((S_ROWS, LANES), F32)
+    for g in range(groups):
+        for small in smalls:
+            total = total + small[g]
+    inverse = 1.0 / total[S_LIVE : S_LIVE + 1, :]
+    vectors[...] = total * inverse
+    scale[...] = jnp.broadcast_to(inverse, (8, LANES))
+    over_rows = (((0,), (0,)), ((), ()))
+    conditions, tokens, scales, shifts, keys, values = [], [], [], [], [], []
+    for g in range(groups):
+        for k, small in enumerate(smalls):
+            slot = jnp.bitwise_xor(me, k)
+            rows = factors[g, slot].astype(F32)
+            conditions.append(rows[0:1])
+            tokens.append(rows[CTX : 2 * CTX])
+            scales.append(small[g, S_SCALE : S_SCALE + 1, :])
+            shifts.append(small[g, S_SHIFT : S_SHIFT + 1, :])
+            keys.append(small[g, S_KEY : S_KEY + CTX, :])
+            values.append(small[g, S_VALUE : S_VALUE + CTX, :])
+    left = jnp.concatenate(conditions, axis=0)
+    for place, parts in enumerate((scales, shifts)):
+        right = jnp.concatenate(parts, axis=0) * inverse
+        embed[:, place, :] = lax.dot_general(
+            left, right, over_rows, precision=lax.Precision.HIGHEST, preferred_element_type=F32
+        )
+    left = jnp.concatenate(tokens, axis=0).astype(BF16)
+    for place, parts in enumerate((keys, values)):
+        right = jnp.concatenate(parts, axis=0).astype(BF16)
+        context[:, place, :] = (
+            lax.dot_general(left, right, over_rows, preferred_element_type=F32) * inverse
+        )
+
+
+def kernel_slots(meta, p0, p1, p2, p3, whole, sems):
+    wait_all(fetch((p0, p1, p2, p3), whole, meta[0], sems, 0))
+
+
+def kernel_split(counts, width, digit, *refs):
+    parts = refs[sum(counts) :]
+    rows = parts[0].shape[1]
+    for offset, part in enumerate(parts):
+        start = pl.multiple_of(jnp.bitwise_xor(digit[0], offset) * rows, rows)
+        position, base = 0, 0
+        for count in counts:
+            terms = refs[position : position + count]
+            total = terms[0][:, pl.ds(start, rows), :].astype(F32)
+            for term in terms[1:]:
+                total = total + term[:, pl.ds(start, rows), :].astype(F32)
+            part[base : base + total.shape[0]] = total.astype(part.dtype)
+            position += count
+            base += total.shape[0]
+
+
+def split_sum(groups, width, digit):
+    blocks = sum(terms[0].shape[0] for terms in groups)
+    rows = groups[0][0].shape[1]
+    flat = [term for terms in groups for term in terms]
+    shape = (blocks, rows // width, LANES)
+    return call(
+        functools.partial(kernel_split, tuple(len(terms) for terms in groups), width),
+        "split_sum",
+        [struct(shape, F32)] + [struct(shape, BF16)] * (width - 1),
+        [smem()] + [vmem()] * len(flat),
+        [],
+    )(digit, *flat)
+
+
+def kernel_total(*refs):
+    total = refs[0][...].astype(F32)
+    for term in refs[1:-1]:
+        total = total + term[...].astype(F32)
+    refs[-1][...] = total.astype(BF16)
+
+
+def total_sum(terms):
+    return call(
+        kernel_total, "total_sum", struct(terms[0].shape, BF16), [vmem()] * len(terms), []
+    )(*terms)
+
+
+def kernel_join(digit, *refs):
+    parts, whole = refs[:-1], refs[-1]
+    rows = parts[0].shape[1]
+    for offset, part in enumerate(parts):
+        start = pl.multiple_of(jnp.bitwise_xor(digit[0], offset) * rows, rows)
+        whole[:, pl.ds(start, rows), :] = part[...]
+
+
+def join(parts, digit):
+    blocks, rows, _ = parts[0].shape
+    return call(
+        kernel_join,
+        "join",
+        struct((blocks, rows * len(parts), LANES), BF16),
+        [smem()] + [vmem()] * len(parts),
+        [],
+    )(digit, *parts)
+
+
+def kernel_last(digit, scale, mine, other, whole):
+    rows = mine.shape[1]
+    for offset, part in enumerate((mine, other)):
+        start = pl.multiple_of(jnp.bitwise_xor(digit[0], offset) * rows, rows)
+        whole[:, pl.ds(start, rows), :] = part[...].astype(F32) * scale[0:1, :]
+
+
+def last_join(pair, digit, scale):
+    blocks, rows, _ = pair[0].shape
+    return call(
+        kernel_last,
+        "last_join",
+        struct((blocks, 2 * rows, LANES), F32),
+        [smem()] + [vmem()] * 3,
+        [],
+    )(digit, scale, *pair)
 
 
 def swap(value, axis, offset):
     size = lax.axis_size(axis)
     return lax.ppermute(value, axis, [(i, i ^ offset) for i in range(size)])
+
+
+def tie(*values):
+    return lax.optimization_barrier(values)
 
 
 def share(shard):
@@ -800,43 +944,12 @@
     return levels
 
 
-def gather_dp(value):
-    stacked = value[None]
-    for low, width in dp_levels(lax.axis_size("dp")):
-        stacked = jnp.concatenate(
-            [stacked] + [swap(stacked, "dp", low * k) for k in range(1, width)], axis=0
-        )
-    return stacked
-
-
-def reduce_grads(keep, send):
-    got = swap(send, "mp", 1)
-    far = keep[1].astype(F32) + got[1].astype(F32)
-    own = keep[0].astype(F32) + got[0].astype(F32)
-    value = (own + swap(far.astype(BF16), "mp", 2).astype(F32)).astype(BF16)
-    blocks = value.shape[0]
-    place = lax.axis_index("dp")
-    path = []
-    for low, width in dp_levels(lax.axis_size("dp")):
-        rows = value.shape[1] // width
-        digit = (place // low) % width
-        cut = value.reshape(blocks, width, rows, LANES)
-        parts = [
-            lax.dynamic_index_in_dim(cut, digit ^ k, 1, keepdims=False) for k in range(width)
-        ]
-        total = parts[0].astype(F32)
-        for k in range(1, width):
-            total = total + swap(parts[k], "dp", low * k).astype(F32)
-        value = total.astype(BF16)
-        path.append((low, width, digit))
-    for low, width, digit in reversed(path):
-        rows = value.shape[1]
-        whole = jnp.zeros((blocks, width, rows, LANES), BF16)
-        for k in range(width):
-            part = value if k == 0 else swap(value, "dp", low * k)
-            whole = lax.dynamic_update_index_in_dim(whole, part, digit ^ k, 1)
-        value = whole.reshape(blocks, width * rows, LANES)
-    return value
+def gather_step(stacked, low):
+    return jnp.concatenate([stacked, swap(stacked, "dp", low)], axis=0)
+
+
+def bits(size):
+    return [1 << k for k in range(size.bit_length() - 1)]
 
 
 def local(
@@ -862,13 +975,27 @@
 ):
     slots, pixels, width = image_in.shape
     me = lax.axis_index("mp")
-    meta = jnp.stack([me, (me < image_count[0]).astype(jnp.int32)]).astype(jnp.int32)
-
+    group = lax.axis_index("dp")
+    parity = (group ^ (group >> 1)) & 1
+    meta = jnp.stack([me, (me < image_count[0]).astype(jnp.int32), parity]).astype(jnp.int32)
+    levels = dp_levels(lax.axis_size("dp"))
+    digits = [((group // low) % wide).astype(jnp.int32)[None] for low, wide in levels]
+    steps = bits(lax.axis_size("dp"))
+
+    conv1_shard = conv1_weight.reshape(9, C, LANES)
+    conv2_shard = conv2_weight.reshape(9, C, LANES)
+    qkv_shard = jnp.transpose(qkv_weight, (1, 0, 2))
+
+    def half_of(shard):
+        rows = shard.shape[-2] // 2
+        return lax.dynamic_slice_in_dim(shard, parity * rows, rows, axis=shard.ndim - 2)
+
+    half1 = swap(half_of(conv1_shard), "mp", 2)
     images = exchange(pick(image_in, me))
-    conv1 = share(conv1_weight.reshape(9, C, LANES))
-
-    half = EMB // 2
-    frequency = jnp.exp(-math.log(10000.0) * jnp.arange(half, dtype=F32) / half)
+    near1 = swap(conv1_shard, "mp", 1)
+
+    half_width = EMB // 2
+    frequency = jnp.exp(-math.log(10000.0) * jnp.arange(half_width, dtype=F32) / half_width)
     angles = timesteps.astype(F32)[:, None] * frequency[None, :]
     condition = jax.nn.silu(
         jnp.concatenate([jnp.cos(angles), jnp.sin(angles)], axis=1) + clip_embed.astype(F32)
@@ -895,52 +1022,87 @@
         ],
         axis=1,
     )
+    early, near1 = tie(early, near1)
     packs = exchange(pick(early, me))
-    conv2 = share(conv2_weight.reshape(9, C, LANES))
-    qkv_w = share(jnp.transpose(qkv_weight, (1, 0, 2)))
-    proj_w = share(proj_weight)
-    cots = exchange(pick(out_cotangent, me))
-
-    factors = gather_dp(jnp.concatenate([condition, context_tokens.reshape(slots * CTX, EMB)], axis=0))
+    factors = jnp.concatenate(
+        [jnp.broadcast_to(condition[:, None], (slots, CTX, EMB)), context_tokens], axis=1
+    )[None]
+
+    def relayed(shard, near, half):
+        quarter = half.shape[-2] // 2
+        by_x = swap(half[:, :quarter], "dp", 1)
+        by_z = swap(half[:, quarter:], "dp", 2)
+        return (shard, near, half, by_x, by_z) + tuple(
+            swap(part, "mp", 1) for part in (half, by_x, by_z)
+        )
+
+    conv1 = relayed(conv1_shard, near1, half1)
+    half2 = half_of(conv2_shard)
+    half2, *tied = tie(half2, *images, *packs)
+    images, packs = tied[:4], tied[4:]
+    half2 = swap(half2, "mp", 2)
+    near2 = swap(conv2_shard, "mp", 1)
+    qkv_far = swap(qkv_shard, "mp", 2)
+    proj_far = swap(proj_weight, "mp", 2)
+    factors = gather_step(factors, steps[0])
 
     block = struct((4, pixels, LANES), BF16)
     block32 = struct((4, pixels, LANES), F32)
     turned = struct((4, LANES, pixels), BF16)
     fields = struct((3, 4, pixels + 2 * PAD, LANES), BF16)
+    piece = struct((pixels, LANES), BF16)
     field_scratch = pltpu.VMEM((3, 4, pixels + 2 * PAD, LANES), BF16)
     conv_scratch = pltpu.VMEM((4, 9, C, LANES), BF16)
     qkv_scratch = pltpu.VMEM((4, 3, C, LANES), BF16)
     grad_scratch = pltpu.VMEM((4, pixels, LANES), F32)
     conv_flops = 2 * pixels * 9 * C * C
 
-    image, pack, first_t, inner, second, second_t = call(
+    image, pack, first_t, inner = call(
         kernel_first,
         "first",
-        [block, struct((4, E_ROWS, LANES), F32), turned, block32, block, turned],
-        [smem()] + [anywhere()] * 12,
-        [field_scratch, conv_scratch, pltpu.SemaphoreType.DMA((12,))],
+        [block, struct((4, E_ROWS, LANES), F32), turned, block32],
+        [smem()] + [anywhere()] * 16,
+        [field_scratch, conv_scratch, pltpu.SemaphoreType.DMA((16,))],
         conv_flops,
-    )(meta, *images, *conv1, *packs)
-    middle, attn_t, qkv = call(
+    )(meta, *images, *packs, *conv1)
+
+    inner, half2, near2, qkv_far, proj_far, factors = tie(
+        inner, half2, near2, qkv_far, proj_far, factors
+    )
+    qkv_near = swap(qkv_shard, "mp", 1)
+    conv2 = relayed(conv2_shard, near2, half2)
+    qkv_w = (qkv_shard, qkv_near, qkv_far, swap(qkv_far, "mp", 1))
+    proj_w = (proj_weight, swap(proj_weight, "mp", 1), proj_far, swap(proj_far, "mp", 1))
+    inner, *conv2 = tie(inner, *conv2)
+    cots = exchange(pick(out_cotangent, me))
+    factors = gather_step(factors, steps[1])
+    middle, second_t, attn_t, qkv = call(
         kernel_second,
         "second",
-        [block32, turned, struct((4, pixels, 3 * LANES), BF16)],
-        [smem()] + [vmem()] * 3 + [anywhere()] * 8,
+        [block32, turned, turned, struct((4, pixels, 3 * LANES), BF16)],
+        [smem()] + [vmem()] * 3 + [anywhere()] * 12,
         [
             field_scratch,
             conv_scratch,
             qkv_scratch,
             pltpu.VMEM((4, pixels, LANES), BF16),
-            pltpu.SemaphoreType.DMA((8,)),
+            pltpu.SemaphoreType.DMA((12,)),
         ],
         conv_flops + 6 * pixels * C * C,
-    )(meta, second, image, pack, *conv2, *qkv_w)
+    )(meta, inner, image, pack, *qkv_w, *conv2)
     ctx_scratch = pltpu.VMEM((pixels, LANES), F32)
     turned_scratch = pltpu.VMEM((LANES, pixels), F32)
+    qkv, first_t, factors, *cots = tie(qkv, first_t, factors, *cots)
+    second_y = swap(second_t, "mp", 2)
+    first_y = swap(first_t, "mp", 2)
+    second_c = swap(second_t, "mp", 1)
+    first_c = swap(first_t, "mp", 1)
+    for low in steps[2:]:
+        factors = gather_step(factors, low)
     *outs, cot, mixed, dqkv, dctx = call(
         kernel_attention,
         "attention",
-        [struct((pixels, LANES), BF16)] * 4
+        [piece] * 4
         + [block, block, struct((4, pixels, 3 * LANES), BF16), struct((4, 2 * CTX, LANES), F32)],
         [smem()] + [vmem()] * 3 + [anywhere()] * 8,
         [
@@ -958,94 +1120,163 @@
         ],
         4 * 12 * pixels * pixels * C,
     )(meta, qkv, pack, middle, *cots, *proj_w)
-    att_keep, att_send, dmiddle, field2, sums = call(
+    dqkv, second_y, first_y, second_c, first_c, factors = tie(
+        dqkv, second_y, first_y, second_c, first_c, factors
+    )
+    second_d = swap(second_y, "mp", 1)
+    first_d = swap(first_y, "mp", 1)
+    dmiddle, field2, sums, *gradients2 = call(
         kernel_back_attention,
         "back_attention",
-        [struct((2, 4, C, LANES), BF16)] * 2 + [block32, fields, struct((4, S_ROWS, LANES), F32)],
-        [smem()] + [vmem()] * 7 + [anywhere()] * 4,
-        [
-            qkv_scratch,
-            pltpu.VMEM((4, LANES, pixels), BF16),
-            grad_scratch,
-            pltpu.SemaphoreType.DMA((4,)),
-        ],
-        14 * pixels * C * C,
-    )(meta, dqkv, mixed, attn_t, cot, middle, pack, dctx, *qkv_w)
-    weight_grad = call(
-        kernel_weight_grad,
-        "weight_grad",
-        [struct((2, 9, C, LANES), BF16)] * 2,
-        [smem()] + [vmem()] * 2,
-        [],
-        conv_flops,
-    )
-    conv2_keep, conv2_send = weight_grad(meta, second_t, field2)
-    field1, *terms = call(
+        [block32, fields, struct((4, S_ROWS, LANES), F32)] + [piece] * 4,
+        [smem()] + [vmem()] * 5 + [anywhere()] * 4,
+        [qkv_scratch, grad_scratch, pltpu.SemaphoreType.DMA((4,))],
+        8 * pixels * C * C,
+    )(meta, dqkv, cot, middle, pack, dctx, *qkv_w)
+    gradients2, second_d, first_d = tie(gradients2, second_d, first_d)
+    gradients2 = exchange(gradients2)
+    field1, sums, *gradients1 = call(
         kernel_back_second,
         "back_second",
-        [fields] + [struct((S_ROWS, LANES), F32)] * 4,
-        [smem()] + [vmem()] * 4 + [anywhere()] * 4,
-        [conv_scratch, grad_scratch, pltpu.SemaphoreType.DMA((4,))],
+        [fields, struct((4, S_ROWS, LANES), F32)] + [piece] * 4,
+        [smem()] + [vmem()] * 4 + [anywhere()] * 8,
+        [conv_scratch, grad_scratch, pltpu.SemaphoreType.DMA((8,))],
         conv_flops,
     )(meta, field2, inner, pack, sums, *conv2)
-    conv1_keep, conv1_send = weight_grad(meta, first_t, field1)
+
+    def weight_send(sources, gradients):
+        return call(
+            kernel_weight_send,
+            "weight_send",
+            [struct((9, C // 2, LANES), BF16), fields],
+            [smem()] + [vmem()] * 8,
+            [],
+            conv_flops // 2,
+        )(digits[0], *sources, *gradients)
+
+    def weight_own(sources, field):
+        return call(
+            kernel_weight_own,
+            "weight_own",
+            struct((9, C // 2, LANES), F32),
+            [smem()] + [vmem()] * 5,
+            [],
+            conv_flops // 2,
+        )(digits[0], *sources, field)
+
+    seconds = (second_t, second_c, second_y, second_d)
+    firsts = (first_t, first_c, first_y, first_d)
+    gradients1, gradients2 = tie(gradients1, gradients2)
+    gradients1 = exchange(gradients1)
+    send2, wide2 = weight_send(seconds, gradients2)
+    got2 = swap(send2, "dp", 1)
+    own2 = weight_own(seconds, wide2)
+    own2, gradients1, outs = tie(own2, gradients1, outs)
+    out_parts = exchange(outs)
+    send1, wide1 = weight_send(firsts, gradients1)
+    got1 = swap(send1, "dp", 1)
+    own1 = weight_own(firsts, wide1)
+    att_keep, att_send = call(
+        kernel_attention_grad,
+        "attention_grad",
+        [struct((2, 4, C, LANES), BF16)] * 2,
+        [smem()] + [vmem()] * 4,
+        [pltpu.VMEM((4, LANES, pixels), BF16)],
+        8 * pixels * C * C,
+    )(meta, dqkv, mixed, attn_t, cot)
+    own1, got2, out_parts = tie(own1, got2, out_parts)
+
+    def down(groups, level):
+        low, wide = levels[level]
+        parts = split_sum(groups, wide, digits[level])
+        return [parts[0]] + [swap(parts[k], "dp", low * k) for k in range(1, wide)]
+
+    def spread(value, level):
+        low, wide = levels[level]
+        return [value] + [swap(value, "dp", low * k) for k in range(1, wide)]
+
+    terms2 = down([[own2, got2]], 1)
+    att_got = swap(att_send, "mp", 1)
+    grad_first = call(
+        kernel_back_conv,
+        "back_conv",
+        block32,
+        [smem()] + [vmem()] + [anywhere()] * 8,
+        [conv_scratch, pltpu.SemaphoreType.DMA((8,))],
+        conv_flops,
+    )(meta, field1, *conv1)
+    grad_first, att_got, *terms2 = tie(grad_first, att_got, *terms2)
+    att_far = swap(total_sum([att_keep[1], att_got[1]]), "mp", 2)
+
+    def inner_levels(terms):
+        for level in range(2, len(levels)):
+            terms = down([terms], level)
+        value = total_sum(terms)
+        for level in range(len(levels) - 1, 1, -1):
+            value = join(spread(value, level), digits[level])
+        return value
+
+    value2 = inner_levels(terms2)
+    parts2 = spread(value2, 1)
+    terms1 = down([[own1, got1]], 1)
     back = call(
         kernel_back_first,
         "back_first",
-        [struct((pixels, LANES), BF16)] * 4 + [struct((8, LANES), F32)] * 4,
-        [smem()] + [vmem()] * 4 + [anywhere()] * 4,
-        [conv_scratch, grad_scratch, pltpu.SemaphoreType.DMA((4,))],
-        conv_flops,
-    )(meta, field1, image, pack, dmiddle, *conv1)
-    image_grads, last_terms = back[:4], back[4:]
-
-    order = me ^ jnp.arange(4)
+        [piece] * 4 + [struct((S_ROWS, LANES), F32)] * 4,
+        [smem()] + [vmem()] * 5,
+        [grad_scratch],
+        conv_flops // 4,
+    )(meta, grad_first, image, pack, dmiddle, sums)
+    image_grads, smalls = back[:4], back[4:]
+    half2_sum = join(parts2, digits[1])
+    pair2 = spread(half2_sum, 0)
+    value1 = inner_levels(terms1)
+    parts1 = spread(value1, 1)
+    half1_sum = join(parts1, digits[1])
+    pair1 = spread(half1_sum, 0)
+    att_terms = down([[att_keep[0], att_got[0], att_far]], 0)
+    att_terms = down([att_terms], 1)
+    att_value = inner_levels(att_terms)
+    att_pair = spread(join(spread(att_value, 1), digits[1]), 0)
+
+    image_parts = exchange(image_grads)
+    smalls = [small[None] for small in exchange(smalls)]
+    smalls = jnp.stack(smalls)
+    for low in steps:
+        smalls = jnp.concatenate([smalls, swap(smalls, "dp", low)], axis=1)
+    embed_grad, context_grad, vector_sums, scale = call(
+        kernel_factor_grads,
+        "factor_grads",
+        [
+            struct((EMB, 2, LANES), F32),
+            struct((EMB, 2, LANES), F32),
+            struct((S_ROWS, LANES), F32),
+            struct((8, LANES), F32),
+        ],
+        [smem()] + [vmem()] * 5,
+        [],
+    )(meta, factors, smalls[0], smalls[1], smalls[2], smalls[3])
 
     def in_slots(parts):
-        whole = jnp.zeros((4,) + parts[0].shape, parts[0].dtype)
-        for k in range(4):
-            whole = lax.dynamic_update_index_in_dim(whole, parts[k], me ^ k, 0)
-        return whole
-
-    del order
-    block_out = in_slots(exchange(outs))
-    image_grad = in_slots(exchange(image_grads))
-    small = gather_dp(in_slots(exchange(terms)))
-    last = gather_dp(sum(exchange(last_terms)))
-    groups = small.shape[0]
-    small = small.reshape(groups * slots, S_ROWS, LANES)
-    inverse_total = 1.0 / jnp.sum(small[:, S_LIVE, 0])
-    vector_sums = jnp.sum(small[:, :S_SCALE], axis=0) * inverse_total
-    last_sums = jnp.sum(last, axis=0) * inverse_total
-    all_condition = factors[:, :slots].reshape(groups * slots, EMB)
-    all_tokens = factors[:, slots:].reshape(groups * slots * CTX, EMB)
-    dscale_shift = small[:, S_SCALE : S_SHIFT + 1].reshape(groups * slots, 2 * LANES)
-    dcontext = jnp.concatenate(
-        [small[:, S_KEY : S_KEY + CTX], small[:, S_VALUE : S_VALUE + CTX]], axis=2
-    ).reshape(groups * slots * CTX, 2 * LANES)
-    over_rows = (((0,), (0,)), ((), ()))
-    embed_grad = (
-        lax.dot_general(
-            all_condition.astype(F32),
-            dscale_shift,
-            over_rows,
-            precision=lax.Precision.HIGHEST,
-            preferred_element_type=F32,
-        )
-        * inverse_total
-    ).reshape(EMB, 2, LANES)
-    context_grad = (
-        lax.dot_general(all_tokens, dcontext.astype(BF16), over_rows, preferred_element_type=F32)
-        * inverse_total
-    ).reshape(EMB, 2, LANES)
-    att = reduce_grads(att_keep, att_send).astype(F32) * inverse_total
-    conv2_grad = reduce_grads(conv2_keep, conv2_send).astype(F32) * inverse_total
-    conv1_grad = reduce_grads(conv1_keep, conv1_send).astype(F32) * inverse_total
+        return pl.pallas_call(
+            kernel_slots,
+            name="slots",
+            out_shape=struct((4, pixels, LANES), BF16),
+            in_specs=[smem()] + [anywhere()] * 4,
+            out_specs=vmem(),
+            scratch_shapes=[pltpu.SemaphoreType.DMA((4,))],
+        )(meta, *parts)
+
+    block_out = in_slots(out_parts)
+    image_grad = in_slots(image_parts)
+    conv2_grad = last_join(pair2, digits[0], scale)
+    conv1_grad = last_join(pair1, digits[0], scale)
+    att_grad = last_join(att_pair, digits[0], scale)
     return (
         block_out,
         image_grad,
-        last_sums[0],
-        last_sums[1],
+        vector_sums[S_G1],
+        vector_sums[S_B1],
         conv1_grad.reshape(3, 3, C, LANES),
         embed_grad,
         vector_sums[S_G2],
@@ -1054,9 +1285,9 @@
         vector_sums[S_CB2],
         vector_sums[S_G3],
         vector_sums[S_B3],
-        jnp.transpose(att[:3], (1, 0, 2)),
+        jnp.transpose(att_grad[:3], (1, 0, 2)),
         context_grad,
-        att[3].T,
+        att_grad[3].T,
     )
 
 

time: 473 us -> 344 us (0.73); the launches traced: 467 us -> 343 us
  waiting for transfers between devices: 176 us -> 72.3 us
  other arithmetic: 31.6 us -> 2.29 us
  local copies, waits for them, and re-layouts: 28.2 us -> 36.7 us
    ppermute x75 -> x82, waiting for transfers between devices: 176 us -> 72.3 us  [swap(): return lax.ppermute(value, axis, [(i, i ^ offset) for i in range(size)])]
    unnamed x92 -> x194, local copies, waits for them, and re-layouts: 8.72 us -> 25.1 us
    pallas_call x1 -> x0, other arithmetic: 12.4 us -> none  [local(): call(kernel_back_first, 'back_first', [struct((pixels, LANES), BF16)] * 4...]
    convert_element_type x9 -> x0, other arithmetic: 11.8 us -> none  [the longest x6 9.27 us: reduce_grads(): value = (own + swap(far.astype(BF16), 'mp', 2).astype(F32)).astype(BF16)]
    pallas_call x6 -> x28, Pallas kernels: 122 us -> 130 us  [the longest x1 40 us: local(): call(kernel_attention, 'attention', [piece] * 4 + [block, block, struct((...]
    dynamic_update_slice x26 -> x0, local copies, waits for them, and re-layouts: 7.53 us -> none  [the longest x11 6.95 us: in_slots(): whole = lax.dynamic_update_index_in_dim(whole, parts[k], me ^ k, 0)]
    pallas_call x1, Pallas kernels: 14.9 us -> 9.59 us  [local(): call(kernel_first, 'first', [block, struct((4, E_ROWS, LANES), F32), turn...]
    ppermute x75 -> x82, starting transfers between devices: 89.3 us -> 87.1 us  [swap(): return lax.ppermute(value, axis, [(i, i ^ offset) for i in range(size)])]
  transfers between devices with their start and end apart: 75 -> 82, of which waited for: 23 -> 23; matrix products, arithmetic and copies ran while one was open for 12% -> 5% of each run, Pallas kernels for 13% -> 41%
where the time goes in v2:
time: 344 us; the launch traced here: 343 us
  Pallas kernels  139 us (40%)
  starting transfers between devices  87.1 us (25%)
  waiting for transfers between devices  72.3 us (21%)
  local copies, waits for them, and re-layouts  36.7 us (11%)
    ppermute x82, starting transfers between devices, swap(): return lax.ppermute(value, axis, [(i, i ^ offset) for i in range(size)])  87.1 us
    ppermute x82, waiting for transfers between devices, swap(): return lax.ppermute(value, axis, [(i, i ^ offset) for i in range(size)])  72.3 us
    pallas_call x1, Pallas kernels, local(): call(kernel_attention, 'attention', [piece] * 4 + [block, block, struct((...  40 us
    unnamed x194, local copies, waits for them, and re-layouts  25.1 us
    pallas_call x1, Pallas kernels, local(): call(kernel_second, 'second', [block32, turned, turned, struct((4, pixels...  15.1 us
    pallas_call x2, Pallas kernels, weight_send(): call(kernel_weight_send, 'weight_send', [struct((9, C // 2, LANES), BF16)...  11.8 us
    pallas_call x1, Pallas kernels, local(): call(kernel_back_second, 'back_second', [fields, struct((4, S_ROWS, LANES...  11.3 us
    pallas_call x2, Pallas kernels, weight_own(): call(kernel_weight_own, 'weight_own', struct((9, C // 2, LANES), F32), [s...  10.7 us
  transfers between devices with their start and end apart: 82, of which 23 were waited for; matrix products, arithmetic and copies ran while one was open for 5% of the time, Pallas kernels for 41%

profile of v2, /device:TPU:0, one launch (start us, length us, event | category | flops | bytes accessed | tf_op | source)
XLA Modules:
  0.0 343.3 jit_solution(7409175455791743731)
XLA Ops:
  3.1 2.5 collective-permute-start.7
  17.2 2.9 collective-permute-done.7.w2
  28.2 2.9 collective-permute-done.1.i2
  51.2 9.6 %first.1 = (bf16[4,1024,128]{2,1,0:T(8,128)(2,1)S(1)}, f32[4,32,128]{2,1,0:T(8,128)S(1)}, bf16[4,128,1024]{2,1,0:T(8,128)(2,1)S(1)}, f32[4,1024,128]{2,1,0:T(8,128)S(1)}) custom-call(s32[3]{0:T(128)S(1)} %pad_add_fusion.meta, bf16[1024,128]{1,0:T(8,128)(2,1)S(1)} %get-tuple-element.151.i0, bf16[1024,128]{1,0:T(8,128)(2,1)S(1)} %copy-done.56, ...), custom_call_target="tpu_custom_call" | custom-call | flops 4831838208 | tf_op jit(solution)/shard_map/first/pallas_call | solution.py:1060
  60.9 7.0 %collective-permute-done.15.p2 = bf16[3,512,128]{2,1,0:T(8,128)(2,1)S(1)} collective-permute-done((bf16[3,512,128]{2,1,0:T(8,128)(2,1)}, bf16[3,512,128]{2,1,0:T(8,128)(2,1)S(1)}, u32[]{:S(2)}, u32[]{:S(2)}) %collective-permute-start.15) | collective-permute-done | bytes 393248 | tf_op jit(solution)/shard_map/ppermute | solution.py:916
  72.0 10.2 %collective-permute-done.25 = bf16[2,4,8,2048]{3,2,1,0:T(8,128)(2,1)S(1)} collective-permute-done((bf16[2,4,8,2048]{3,2,1,0:T(8,128)(2,1)S(1)}, bf16[2,4,8,2048]{3,2,1,0:T(8,128)(2,1)S(1)}, u32[]{:S(2)}, u32[]{:S(2)}) %collective-permute-start.25) | collective-permute-done | bytes 262176 | tf_op jit(solution)/shard_map/ppermute | solution.py:916
  86.9 15.1 %second.1 = (f32[4,1024,128]{2,1,0:T(8,128)S(1)}, bf16[4,128,1024]{2,1,0:T(8,128)(2,1)S(1)}, bf16[4,128,1024]{2,1,0:T(8,128)(2,1)S(1)}, bf16[4,1024,384]{2,1,0:T(8,128)(2,1)S(1)}) custom-call(s32[3]{0:T(128)S(1)} %pad_add_fusion.meta, f32[4,1024,128]{2,1,0:T(8,128)S(1)} %get-tuple-element.165.inner, bf16[4,1024,128]{2,1,0:T(8,128)(2,1)S(1)} %get-tuple-element.166.image, ...), custom_call_target="tpu_custom_call" | custom-call | flops 6442450944 | tf_op jit(solution)/shard_map/second/pallas_call | solution.py:1079
  105.7 2.6 collective-permute-start.35
  108.3 40.0 %attention.1 = (bf16[1024,128]{1,0:T(8,128)(2,1)S(1)}, bf16[1024,128]{1,0:T(8,128)(2,1)S(1)}, bf16[1024,128]{1,0:T(8,128)(2,1)S(1)}, bf16[1024,128]{1,0:T(8,128)...) custom-call(s32[3]{0:T(128)S(1)} %pad_add_fusion.meta, ...), custom_call_target="tpu_custom_call" | custom-call | flops 25769803776 | tf_op jit(solution)/shard_map/attention/pallas_call | solution.py:1102
  160.2 5.5 %attention_grad.1 = (bf16[2,4,512,128]{3,2,1,0:T(8,128)(2,1)S(1)}, bf16[2,4,512,128]{3,2,1,0:T(8,128)(2,1)S(1)}) custom-call(s32[3]{0:T(128)S(1)} %pad_add_fusion.meta, bf16[4,1024,384]{2,1,0:T(8,128)(2,1)S(1)} %copy-done.61, bf16[4,1024,128]{2,1,0:T(8,128)(2,1)S(1)} %copy-done.70, bf16[4,128,1024]{2,1,0:T(8,128)(2,1)S(1)} %copy-done.68, ...), custom_call_target="tpu_custom_call" | custom-call | flops 2147483648 | tf_op jit(solution)/shard_map/attention_grad/pallas_call | solution.py:1179
  166.0 6.3 %back_attention.1 = (f32[4,1024,128]{2,1,0:T(8,128)S(1)}, bf16[3,4,1088,128]{3,2,1,0:T(8,128)(2,1)S(1)}, f32[4,24,128]{2,1,0:T(8,128)S(1)}, bf16[1024,128]{1,0:T...) custom-call(s32[3]{0:T(128)S(1)} %pad_add_fusion.meta, ...), custom_call_target="tpu_custom_call" | custom-call | flops 2147483648 | tf_op jit(solution)/shard_map/back_attention/pallas_call | solution.py:1128
  172.4 11.3 %back_second.1 = (bf16[3,4,1088,128]{3,2,1,0:T(8,128)(2,1)S(1)}, f32[4,24,128]{2,1,0:T(8,128)S(1)}, bf16[1024,128]{1,0:T(8,128)(2,1)S(1)}, bf16[1024,128]{1,0:T(...) custom-call(s32[3]{0:T(128)S(1)} %pad_add_fusion.meta, ...), custom_call_target="tpu_custom_call" | custom-call | flops 4831838208 | tf_op jit(solution)/shard_map/back_second/pallas_call | solution.py:1138
  185.8 7.0 %back_conv.1.grad_in = f32[4,1024,128]{2,1,0:T(8,128)S(1)} custom-call(s32[3]{0:T(128)S(1)} %pad_add_fusion.meta, bf16[3,4,1088,128]{3,2,1,0:T(8,128)(2,1)S(1)} %get-tuple-element.241.grad_field, bf16[9,512,128]{2,1,0:T(8,128)(2,1)S(1)} %bitcast.120, bf16[9,512,128]{2,1,0:T(8,128)(2,1)S(1)} %copy-done.10, ...), custom_call_target="tpu_custom_call" | custom-call | flops 4831838208 | tf_op jit(solution)/shard_map/back_conv/pallas_call | solution.py:1200
  193.5 3.9 %collective-permute-done.40.d3 = bf16[1024,128]{1,0:T(8,128)(2,1)S(1)} collective-permute-done((bf16[1024,128]{1,0:T(8,128)(2,1)S(1)}, bf16[1024,128]{1,0:T(8,128)(2,1)S(1)}, u32[]{:S(2)}, u32[]{:S(2)}) %collective-permute-start.40) | collective-permute-done | bytes 262176 | tf_op jit(solution)/shard_map/ppermute | solution.py:916
  199.4 5.9 %weight_send.2 = (bf16[9,256,128]{2,1,0:T(8,128)(2,1)S(1)}, bf16[3,4,1088,128]{3,2,1,0:T(8,128)(2,1)S(1)}) custom-call(s32[1]{0:T(128)} %bitcast.4.digit, bf16[4,128,1024]{2,1,0:T(8,128)(2,1)S(1)} %copy-done.16, bf16[4,128,1024]{2,1,0:T(8,128)(2,1)S(1)} %copy-done.18, bf16[4,128,1024]{2,1,0:T(8,128)(2,1)} %collective-permute-done.31.u2, ...), custom_call_target="tpu_custom_call" | custom-call | flops 2415919104 | tf_op jit(solution)/shard_map/weight_send/pallas_call | solution.py:1148
  206.9 5.4 %weight_own.2.refs_0_ = f32[9,256,128]{2,1,0:T(8,128)S(1)} custom-call(s32[1]{0:T(128)} %bitcast.4.digit, bf16[4,128,1024]{2,1,0:T(8,128)(2,1)S(1)} %copy-done.16, bf16[4,128,1024]{2,1,0:T(8,128)(2,1)S(1)} %copy-done.18, bf16[4,128,1024]{2,1,0:T(8,128)(2,1)} %collective-permute-done.31.u2, bf16[4,128,1024]{2,1,0:T(8,128)(2,1)} %collective-permute-done.36.u3, ...), custom_call_target="tpu_custom_call" | custom-call | flops 2415919104 | tf_op jit(solution)/shard_map/weight_own/pallas_call | solution.py:1158
  214.4 5.9 %weight_send.3 = (bf16[9,256,128]{2,1,0:T(8,128)(2,1)S(1)}, bf16[3,4,1088,128]{3,2,1,0:T(8,128)(2,1)S(1)}) custom-call(s32[1]{0:T(128)} %bitcast.4.digit, bf16[4,128,1024]{2,1,0:T(8,128)(2,1)S(1)} %copy-done.12, bf16[4,128,1024]{2,1,0:T(8,128)(2,1)S(1)} %copy-done.14, bf16[4,128,1024]{2,1,0:T(8,128)(2,1)} %collective-permute-done.32.u2, ...), custom_call_target="tpu_custom_call" | custom-call | flops 2415919104 | tf_op jit(solution)/shard_map/weight_send/pallas_call | solution.py:1148
  220.3 5.3 %weight_own.3.refs_0_ = f32[9,256,128]{2,1,0:T(8,128)S(1)} custom-call(s32[1]{0:T(128)} %bitcast.4.digit, bf16[4,128,1024]{2,1,0:T(8,128)(2,1)S(1)} %copy-done.12, bf16[4,128,1024]{2,1,0:T(8,128)(2,1)S(1)} %copy-done.14, bf16[4,128,1024]{2,1,0:T(8,128)(2,1)} %collective-permute-done.32.u2, bf16[4,128,1024]{2,1,0:T(8,128)(2,1)} %collective-permute-done.37.u3, ...), custom_call_target="tpu_custom_call" | custom-call | flops 2415919104 | tf_op jit(solution)/shard_map/weight_own/pallas_call | solution.py:1158
  233.8 8.1 %collective-permute-done.50.refs_2_ = bf16[9,64,128]{2,1,0:T(8,128)(2,1)S(1)} collective-permute-done((bf16[9,64,128]{2,1,0:T(8,128)(2,1)S(1)}, bf16[9,64,128]{2,1,0:T(8,128)(2,1)S(1)}, u32[]{:S(2)}, u32[]{:S(2)}) %collective-permute-start.50) | collective-permute-done | bytes 147488 | tf_op jit(solution)/shard_map/ppermute | solution.py:916
  243.8 4.4 %back_first.1 = (bf16[1024,128]{1,0:T(8,128)(2,1)S(1)}, bf16[1024,128]{1,0:T(8,128)(2,1)S(1)}, bf16[1024,128]{1,0:T(8,128)(2,1)S(1)}, bf16[1024,128]{1,0:T(8,128...) custom-call(s32[3]{0:T(128)S(1)} %pad_add_fusion.meta, ...), custom_call_target="tpu_custom_call" | custom-call | flops 1207959552 | tf_op jit(solution)/shard_map/back_first/pallas_call | solution.py:1222
  250.2 6.7 %collective-permute-done.56 = f32[24,128]{1,0:T(8,128)S(1)} collective-permute-done((f32[24,128]{1,0:T(8,128)S(1)}, f32[24,128]{1,0:T(8,128)S(1)}, u32[]{:S(2)}, u32[]{:S(2)}) %collective-permute-start.56) | collective-permute-done | bytes 12320 | tf_op jit(solution)/shard_map/ppermute | solution.py:916
  259.1 3.8 %collective-permute-start.70 = (bf16[9,64,128]{2,1,0:T(8,128)(2,1)S(1)}, bf16[9,64,128]{2,1,0:T(8,128)(2,1)S(1)}, u32[]{:S(2)}, u32[]{:S(2)}) collective-permute-start(bf16[9,64,128]{2,1,0:T(8,128)(2,1)S(1)} %total_sum.5.refs_0_), channel_id=1, source_target_pairs={{0,16},{4,20},{8,24},{12,28},{16,0},{20,4},{24,8},{28,12},{1,17},{... | collective-permute-start | bytes 442376 | tf_op jit(solution)/shard_map/ppermute | solution.py:916
  265.9 6.0 %collective-permute-start.63 = (bf16[9,64,128]{2,1,0:T(8,128)(2,1)S(1)}, bf16[9,64,128]{2,1,0:T(8,128)(2,1)S(1)}, u32[]{:S(2)}, u32[]{:S(2)}) collective-permute-start(bf16[9,64,128]{2,1,0:T(8,128)(2,1)S(1)} %get-tuple-element.269), channel_id=1, source_target_pairs={{0,16},{4,20},{8,24},{12,28},{16,0},{20,4},{24,8},{28,12},{1,17},{... | collective-permute-start | bytes 442376 | tf_op jit(solution)/shard_map/ppermute | solution.py:916
  272.2 2.6 collective-permute-done.70.refs_2_
  277.9 6.3 %collective-permute-done.63.refs_2_ = bf16[9,64,128]{2,1,0:T(8,128)(2,1)S(1)} collective-permute-done((bf16[9,64,128]{2,1,0:T(8,128)(2,1)S(1)}, bf16[9,64,128]{2,1,0:T(8,128)(2,1)S(1)}, u32[]{:S(2)}, u32[]{:S(2)}) %collective-permute-start.63) | collective-permute-done | bytes 147488 | tf_op jit(solution)/shard_map/ppermute | solution.py:916
  284.2 4.5 %collective-permute-done.59 = f32[4,2,24,128]{3,2,1,0:T(8,128)S(1)} collective-permute-done((f32[4,2,24,128]{3,2,1,0:T(8,128)S(1)}, f32[4,2,24,128]{3,2,1,0:T(8,128)S(1)}, u32[]{:S(2)}, u32[]{:S(2)}) %collective-permute-start.59) | collective-permute-done | bytes 98336 | tf_op jit(solution)/shard_map/ppermute | solution.py:916
  291.2 2.6 collective-permute-start.60
  297.4 8.6 %collective-permute-start.76 = (bf16[4,64,128]{2,1,0:T(8,128)(2,1)}, bf16[4,64,128]{2,1,0:T(8,128)(2,1)}, u32[]{:S(2)}, u32[]{:S(2)}) collective-permute-start(bf16[4,64,128]{2,1,0:T(8,128)(2,1)} %get-tuple-element.282), channel_id=1, source_target_pairs={{0,16},{4,20},{8,24},{12,28},{16,0},{20,4},{24,8},{28,12},{1,17},{... | collective-permute-start | bytes 196616 | tf_op jit(solution)/shard_map/ppermute | solution.py:916
  306.0 3.3 collective-permute-done.66.refs_2_
  313.6 2.9 slots.2
  316.5 3.0 slots.3
  330.5 6.0 %factor_grads.1 = (f32[2048,2,128]{2,1,0:T(2,128)}, f32[2048,2,128]{2,1,0:T(2,128)}, f32[24,128]{1,0:T(8,128)S(1)}, f32[8,128]{1,0:T(8,128)S(1)}) custom-call(s32[3]{0:T(128)S(1)} %copy-done.7, bf16[8,4,8,2048]{3,2,1,0:T(8,128)(2,1)S(1)} %pad_maximum_fusion.factors, f32[8,24,128]{2,1,0:T(8,128)S(1)} %get-tuple-element.319.small0, ...), custom_call_target="tpu_custom_call" | custom-call | tf_op jit(solution)/shard_map/factor_grads/pallas_call | solution.py:1247
  (391 shorter events, 122.6 us)
Async XLA Ops:
  0.7 19.4 %collective-permute-start.3 = (bf16[9,512,128]{2,1,0:T(8,128)(2,1)}, bf16[9,512,128]{2,1,0:T(8,128)(2,1)S(1)}, u32[]{:S(2)}, u32[]{:S(2)}) collective-permute-start(bf16[9,512,128]{2,1,0:T(8,128)(2,1)} %bitcast.117), channel_id=1, source_target_pairs={{0,1},{1,0},{2,3},{3,2},{4,5},{5,4},{6,7},{7,6},{8,9},{9,8},{10,11... | collective-permute-start | bytes 3538952 | tf_op jit(solution)/shard_map/ppermute | solution.py:916
  7.9 19.5 %collective-permute-start = (bf16[1024,128]{1,0:T(8,128)(2,1)}, bf16[1024,128]{1,0:T(8,128)(2,1)S(1)}, u32[]{:S(2)}, u32[]{:S(2)}) collective-permute-start(bf16[1024,128]{1,0:T(8,128)(2,1)} %get-tuple-element.309), channel_id=1, source_target_pairs={{0,1},{1,0},{2,3},{3,2},{4,5},{5,4},{6,7},{7,6},{8,9},{9,8},{10,11... | collective-permute-start | bytes 786440 | tf_op jit(solution)/shard_map/ppermute | solution.py:916
  8.0 23.0 %collective-permute-start.1 = (bf16[1024,128]{1,0:T(8,128)(2,1)}, bf16[1024,128]{1,0:T(8,128)(2,1)S(1)}, u32[]{:S(2)}, u32[]{:S(2)}) collective-permute-start(bf16[1024,128]{1,0:T(8,128)(2,1)} %get-tuple-element.311), channel_id=1, source_target_pairs={{0,2},{1,3},{2,0},{3,1},{4,6},{5,7},{6,4},{7,5},{8,10},{9,11},{10,... | collective-permute-start | bytes 786440 | tf_op jit(solution)/shard_map/ppermute | solution.py:916
  20.0 47.8 %collective-permute-start.14 = (bf16[9,512,128]{2,1,0:T(8,128)(2,1)}, bf16[9,512,128]{2,1,0:T(8,128)(2,1)}, u32[]{:S(2)}, u32[]{:S(2)}) collective-permute-start(bf16[9,512,128]{2,1,0:T(8,128)(2,1)} %bitcast.5.w0), channel_id=1, source_target_pairs={{0,1},{1,0},{2,3},{3,2},{4,5},{5,4},{6,7},{7,6},{8,9},{9,8},{10,11... | collective-permute-start | bytes 3538952 | tf_op jit(solution)/shard_map/ppermute | solution.py:916
  40.7 27.2 %collective-permute-start.13 = (bf16[9,256,128]{2,1,0:T(8,128)(2,1)}, bf16[9,256,128]{2,1,0:T(8,128)(2,1)S(1)}, u32[]{:S(2)}, u32[]{:S(2)}) collective-permute-start(bf16[9,256,128]{2,1,0:T(8,128)(2,1)} %constant_dynamic-slice_fusion.1), channel_id=1, source_target_pairs={{0,2},{1,3},{2,0},{3,1},{4,6},{5,7},{6,4},{7,5},{8,10},{9,11},{10,... | collective-permute-start | bytes 1769480 | tf_op jit(solution)/shard_map/ppermute | solution.py:916
  41.8 19.1 %collective-permute-start.16 = (bf16[128,512]{1,0:T(8,128)(2,1)S(1)}, bf16[128,512]{1,0:T(8,128)(2,1)S(1)}, u32[]{:S(2)}, u32[]{:S(2)}) collective-permute-start(bf16[128,512]{1,0:T(8,128)(2,1)S(1)} %copy-done.59), channel_id=1, source_target_pairs={{0,2},{1,3},{2,0},{3,1},{4,6},{5,7},{6,4},{7,5},{8,10},{9,11},{10,... | collective-permute-start | bytes 393224 | tf_op jit(solution)/shard_map/ppermute | solution.py:916
  42.9 25.0 %collective-permute-start.15 = (bf16[3,512,128]{2,1,0:T(8,128)(2,1)}, bf16[3,512,128]{2,1,0:T(8,128)(2,1)S(1)}, u32[]{:S(2)}, u32[]{:S(2)}) collective-permute-start(bf16[3,512,128]{2,1,0:T(8,128)(2,1)} %bitcast.30.p0), channel_id=1, source_target_pairs={{0,2},{1,3},{2,0},{3,1},{4,6},{5,7},{6,4},{7,5},{8,10},{9,11},{10,... | collective-permute-start | bytes 1179656 | tf_op jit(solution)/shard_map/ppermute | solution.py:916
  84.3 19.5 %collective-permute-start.29 = (bf16[128,512]{1,0:T(8,128)(2,1)S(1)}, bf16[128,512]{1,0:T(8,128)(2,1)S(1)}, u32[]{:S(2)}, u32[]{:S(2)}) collective-permute-start(bf16[128,512]{1,0:T(8,128)(2,1)S(1)} %copy-done.59), channel_id=1, source_target_pairs={{0,1},{1,0},{2,3},{3,2},{4,5},{5,4},{6,7},{7,6},{8,9},{9,8},{10,11... | collective-permute-start | bytes 393224 | tf_op jit(solution)/shard_map/ppermute | solution.py:916
  84.7 18.4 %collective-permute-start.28 = (bf16[1024,128]{1,0:T(8,128)(2,1)S(1)}, bf16[1024,128]{1,0:T(8,128)(2,1)S(1)}, u32[]{:S(2)}, u32[]{:S(2)}) collective-permute-start(bf16[1024,128]{1,0:T(8,128)(2,1)S(1)} %get-tuple-element.304), channel_id=1, source_target_pairs={{0,3},{1,2},{2,1},{3,0},{4,7},{5,6},{6,5},{7,4},{8,11},{9,10},{10,... | collective-permute-start | bytes 786440 | tf_op jit(solution)/shard_map/ppermute | solution.py:916
  84.8 18.3 %collective-permute-start.26 = (bf16[1024,128]{1,0:T(8,128)(2,1)S(1)}, bf16[1024,128]{1,0:T(8,128)(2,1)S(1)}, u32[]{:S(2)}, u32[]{:S(2)}) collective-permute-start(bf16[1024,128]{1,0:T(8,128)(2,1)S(1)} %get-tuple-element.305), channel_id=1, source_target_pairs={{0,1},{1,0},{2,3},{3,2},{4,5},{5,4},{6,7},{7,6},{8,9},{9,8},{10,11... | collective-permute-start | bytes 786440 | tf_op jit(solution)/shard_map/ppermute | solution.py:916
  85.0 18.1 %collective-permute-start.27 = (bf16[1024,128]{1,0:T(8,128)(2,1)S(1)}, bf16[1024,128]{1,0:T(8,128)(2,1)S(1)}, u32[]{:S(2)}, u32[]{:S(2)}) collective-permute-start(bf16[1024,128]{1,0:T(8,128)(2,1)S(1)} %get-tuple-element.307), channel_id=1, source_target_pairs={{0,2},{1,3},{2,0},{3,1},{4,6},{5,7},{6,4},{7,5},{8,10},{9,11},{10,... | collective-permute-start | bytes 786440 | tf_op jit(solution)/shard_map/ppermute | solution.py:916
  86.9 18.8 %collective-permute-start.30 = (bf16[128,512]{1,0:T(8,128)(2,1)S(1)}, bf16[128,512]{1,0:T(8,128)(2,1)S(1)}, u32[]{:S(2)}, u32[]{:S(2)}) collective-permute-start(bf16[128,512]{1,0:T(8,128)(2,1)S(1)} %collective-permute-done.16.w2), channel_id=1, source_target_pairs={{0,1},{1,0},{2,3},{3,2},{4,5},{5,4},{6,7},{7,6},{8,9},{9,8},{10,11... | collective-permute-start | bytes 393224 | tf_op jit(solution)/shard_map/ppermute | solution.py:916
  103.1 48.7 %collective-permute-start.34 = (bf16[4,128,1024]{2,1,0:T(8,128)(2,1)S(1)}, bf16[4,128,1024]{2,1,0:T(8,128)(2,1)S(1)}, u32[]{:S(2)}, u32[]{:S(2)}) collective-permute-start(bf16[4,128,1024]{2,1,0:T(8,128)(2,1)S(1)} %get-tuple-element.180.u0), channel_id=1, source_target_pairs={{0,1},{1,0},{2,3},{3,2},{4,5},{5,4},{6,7},{7,6},{8,9},{9,8},{10,11... | collective-permute-start | bytes 3145736 | tf_op jit(solution)/shard_map/ppermute | solution.py:916
  103.7 49.3 %collective-permute-start.32 = (bf16[4,128,1024]{2,1,0:T(8,128)(2,1)S(1)}, bf16[4,128,1024]{2,1,0:T(8,128)(2,1)}, u32[]{:S(2)}, u32[]{:S(2)}) collective-permute-start(bf16[4,128,1024]{2,1,0:T(8,128)(2,1)S(1)} %get-tuple-element.180.u0), channel_id=1, source_target_pairs={{0,2},{1,3},{2,0},{3,1},{4,6},{5,7},{6,4},{7,5},{8,10},{9,11},{10,... | collective-permute-start | bytes 3145736 | tf_op jit(solution)/shard_map/ppermute | solution.py:916
  103.8 49.2 %collective-permute-start.33 = (bf16[4,128,1024]{2,1,0:T(8,128)(2,1)S(1)}, bf16[4,128,1024]{2,1,0:T(8,128)(2,1)S(1)}, u32[]{:S(2)}, u32[]{:S(2)}) collective-permute-start(bf16[4,128,1024]{2,1,0:T(8,128)(2,1)S(1)} %get-tuple-element.189.u0), channel_id=1, source_target_pairs={{0,1},{1,0},{2,3},{3,2},{4,5},{5,4},{6,7},{7,6},{8,9},{9,8},{10,11... | collective-permute-start | bytes 3145736 | tf_op jit(solution)/shard_map/ppermute | solution.py:916
  103.8 50.1 %collective-permute-start.31 = (bf16[4,128,1024]{2,1,0:T(8,128)(2,1)S(1)}, bf16[4,128,1024]{2,1,0:T(8,128)(2,1)}, u32[]{:S(2)}, u32[]{:S(2)}) collective-permute-start(bf16[4,128,1024]{2,1,0:T(8,128)(2,1)S(1)} %get-tuple-element.189.u0), channel_id=1, source_target_pairs={{0,2},{1,3},{2,0},{3,1},{4,6},{5,7},{6,4},{7,5},{8,10},{9,11},{10,... | collective-permute-start | bytes 3145736 | tf_op jit(solution)/shard_map/ppermute | solution.py:916
  105.7 46.0 %collective-permute-start.35 = (bf16[4,4,8,2048]{3,2,1,0:T(8,128)(2,1)S(1)}, bf16[4,4,8,2048]{3,2,1,0:T(8,128)(2,1)S(1)}, u32[]{:S(2)}, u32[]{:S(2)}) collective-permute-start(bf16[4,4,8,2048]{3,2,1,0:T(8,128)(2,1)S(1)} %pad_maximum_fusion.1), channel_id=1, source_target_pairs={{0,16},{4,20},{8,24},{12,28},{16,0},{20,4},{24,8},{28,12},{1,17},{... | collective-permute-start | bytes 1572872 | tf_op jit(solution)/shard_map/ppermute | solution.py:916
  154.0 29.8 %collective-permute-start.37 = (bf16[4,128,1024]{2,1,0:T(8,128)(2,1)}, bf16[4,128,1024]{2,1,0:T(8,128)(2,1)}, u32[]{:S(2)}, u32[]{:S(2)}) collective-permute-start(bf16[4,128,1024]{2,1,0:T(8,128)(2,1)} %collective-permute-done.32.u2), channel_id=1, source_target_pairs={{0,1},{1,0},{2,3},{3,2},{4,5},{5,4},{6,7},{7,6},{8,9},{9,8},{10,11... | collective-permute-start | bytes 3145736 | tf_op jit(solution)/shard_map/ppermute | solution.py:916
  154.1 29.7 %collective-permute-start.36 = (bf16[4,128,1024]{2,1,0:T(8,128)(2,1)}, bf16[4,128,1024]{2,1,0:T(8,128)(2,1)}, u32[]{:S(2)}, u32[]{:S(2)}) collective-permute-start(bf16[4,128,1024]{2,1,0:T(8,128)(2,1)} %collective-permute-done.31.u2), channel_id=1, source_target_pairs={{0,1},{1,0},{2,3},{3,2},{4,5},{5,4},{6,7},{7,6},{8,9},{9,8},{10,11... | collective-permute-start | bytes 3145736 | tf_op jit(solution)/shard_map/ppermute | solution.py:916
  165.7 65.9 %collective-permute-start.48 = (bf16[2,4,512,128]{3,2,1,0:T(8,128)(2,1)S(1)}, bf16[2,4,512,128]{3,2,1,0:T(8,128)(2,1)}, u32[]{:S(2)}, u32[]{:S(2)}) collective-permute-start(bf16[2,4,512,128]{3,2,1,0:T(8,128)(2,1)S(1)} %get-tuple-element.244), channel_id=1, source_target_pairs={{0,1},{1,0},{2,3},{3,2},{4,5},{5,4},{6,7},{7,6},{8,9},{9,8},{10,11... | collective-permute-start | bytes 3145736 | tf_op jit(solution)/shard_map/ppermute | solution.py:916
  205.3 20.7 %collective-permute-start.44 = (bf16[9,256,128]{2,1,0:T(8,128)(2,1)S(1)}, bf16[9,256,128]{2,1,0:T(8,128)(2,1)S(1)}, u32[]{:S(2)}, u32[]{:S(2)}) collective-permute-start(bf16[9,256,128]{2,1,0:T(8,128)(2,1)S(1)} %get-tuple-element.232), channel_id=1, source_target_pairs={{0,4},{4,0},{8,12},{12,8},{16,20},{20,16},{24,28},{28,24},{1,5},{5... | collective-permute-start | bytes 1769480 | tf_op jit(solution)/shard_map/ppermute | solution.py:916
  231.0 31.8 %collective-permute-start.61 = (bf16[9,256,128]{2,1,0:T(8,128)(2,1)S(1)}, bf16[9,256,128]{2,1,0:T(8,128)(2,1)S(1)}, u32[]{:S(2)}, u32[]{:S(2)}) collective-permute-start(bf16[9,256,128]{2,1,0:T(8,128)(2,1)S(1)} %get-tuple-element.266), channel_id=1, source_target_pairs={{0,4},{4,0},{8,12},{12,8},{16,20},{20,16},{24,28},{28,24},{1,5},{5... | collective-permute-start | bytes 1769480 | tf_op jit(solution)/shard_map/ppermute | solution.py:916
  243.4 22.6 %collective-permute-start.73 = (bf16[4,512,128]{2,1,0:T(8,128)(2,1)S(1)}, bf16[4,512,128]{2,1,0:T(8,128)(2,1)S(1)}, u32[]{:S(2)}, u32[]{:S(2)}) collective-permute-start(bf16[4,512,128]{2,1,0:T(8,128)(2,1)S(1)} %total_sum.6), channel_id=1, source_target_pairs={{0,2},{1,3},{2,0},{3,1},{4,6},{5,7},{6,4},{7,5},{8,10},{9,11},{10,... | collective-permute-start | bytes 1572872 | tf_op jit(solution)/shard_map/ppermute | solution.py:916
  265.9 24.3 %collective-permute-start.52 = (bf16[1024,128]{1,0:T(8,128)(2,1)S(1)}, bf16[1024,128]{1,0:T(8,128)(2,1)S(1)}, u32[]{:S(2)}, u32[]{:S(2)}) collective-permute-start(bf16[1024,128]{1,0:T(8,128)(2,1)S(1)} %get-tuple-element.255), channel_id=1, source_target_pairs={{0,1},{1,0},{2,3},{3,2},{4,5},{5,4},{6,7},{7,6},{8,9},{9,8},{10,11... | collective-permute-start | bytes 786440 | tf_op jit(solution)/shard_map/ppermute | solution.py:916
  265.9 18.2 %collective-permute-start.63 = (bf16[9,64,128]{2,1,0:T(8,128)(2,1)S(1)}, bf16[9,64,128]{2,1,0:T(8,128)(2,1)S(1)}, u32[]{:S(2)}, u32[]{:S(2)}) collective-permute-start(bf16[9,64,128]{2,1,0:T(8,128)(2,1)S(1)} %get-tuple-element.269), channel_id=1, source_target_pairs={{0,16},{4,20},{8,24},{12,28},{16,0},{20,4},{24,8},{28,12},{1,17},{... | collective-permute-start | bytes 442376 | tf_op jit(solution)/shard_map/ppermute | solution.py:916
  276.4 17.4 %collective-permute-start.74 = (bf16[4,256,128]{2,1,0:T(8,128)(2,1)S(1)}, bf16[4,256,128]{2,1,0:T(8,128)(2,1)S(1)}, u32[]{:S(2)}, u32[]{:S(2)}) collective-permute-start(bf16[4,256,128]{2,1,0:T(8,128)(2,1)S(1)} %get-tuple-element.279), channel_id=1, source_target_pairs={{0,4},{4,0},{8,12},{12,8},{16,20},{20,16},{24,28},{28,24},{1,5},{5... | collective-permute-start | bytes 786440 | tf_op jit(solution)/shard_map/ppermute | solution.py:916
  290.2 19.1 %collective-permute-start.66 = (bf16[9,64,128]{2,1,0:T(8,128)(2,1)S(1)}, bf16[9,64,128]{2,1,0:T(8,128)(2,1)S(1)}, u32[]{:S(2)}, u32[]{:S(2)}) collective-permute-start(bf16[9,64,128]{2,1,0:T(8,128)(2,1)S(1)} %total_sum.4.refs_0_), channel_id=1, source_target_pairs={{0,16},{4,20},{8,24},{12,28},{16,0},{20,4},{24,8},{28,12},{1,17},{... | collective-permute-start | bytes 442376 | tf_op jit(solution)/shard_map/ppermute | solution.py:916
  291.2 32.5 %collective-permute-start.60 = (f32[4,4,24,128]{3,2,1,0:T(8,128)}, f32[4,4,24,128]{3,2,1,0:T(8,128)}, u32[]{:S(2)}, u32[]{:S(2)}) collective-permute-start(f32[4,4,24,128]{3,2,1,0:T(8,128)} %pad_maximum_fusion.4), channel_id=1, source_target_pairs={{0,16},{4,20},{8,24},{12,28},{16,0},{20,4},{24,8},{28,12},{1,17},{... | collective-permute-start | bytes 589832 | tf_op jit(solution)/shard_map/ppermute | solution.py:916
  294.6 17.8 %collective-permute-start.75 = (bf16[4,64,128]{2,1,0:T(8,128)(2,1)S(1)}, bf16[4,64,128]{2,1,0:T(8,128)(2,1)S(1)}, u32[]{:S(2)}, u32[]{:S(2)}) collective-permute-start(bf16[4,64,128]{2,1,0:T(8,128)(2,1)S(1)} %get-tuple-element.281), channel_id=1, source_target_pairs={{0,8},{4,12},{8,0},{12,4},{16,24},{20,28},{24,16},{28,20},{1,9},{5... | collective-permute-start | bytes 196616 | tf_op jit(solution)/shard_map/ppermute | solution.py:916
  297.4 22.1 %collective-permute-start.76 = (bf16[4,64,128]{2,1,0:T(8,128)(2,1)}, bf16[4,64,128]{2,1,0:T(8,128)(2,1)}, u32[]{:S(2)}, u32[]{:S(2)}) collective-permute-start(bf16[4,64,128]{2,1,0:T(8,128)(2,1)} %get-tuple-element.282), channel_id=1, source_target_pairs={{0,16},{4,20},{8,24},{12,28},{16,0},{20,4},{24,8},{28,12},{1,17},{... | collective-permute-start | bytes 196616 | tf_op jit(solution)/shard_map/ppermute | solution.py:916
  310.8 26.2 %collective-permute-start.72 = (bf16[9,256,128]{2,1,0:T(8,128)(2,1)S(1)}, bf16[9,256,128]{2,1,0:T(8,128)(2,1)S(1)}, u32[]{:S(2)}, u32[]{:S(2)}) collective-permute-start(bf16[9,256,128]{2,1,0:T(8,128)(2,1)S(1)} %join.4.mine), channel_id=1, source_target_pairs={{0,4},{4,0},{8,12},{12,8},{16,20},{20,16},{24,28},{28,24},{1,5},{5... | collective-permute-start | bytes 1769480 | tf_op jit(solution)/shard_map/ppermute | solution.py:916
  313.1 25.6 %collective-permute-start.68 = (bf16[9,256,128]{2,1,0:T(8,128)(2,1)S(1)}, bf16[9,256,128]{2,1,0:T(8,128)(2,1)S(1)}, u32[]{:S(2)}, u32[]{:S(2)}) collective-permute-start(bf16[9,256,128]{2,1,0:T(8,128)(2,1)S(1)} %join.3.mine), channel_id=1, source_target_pairs={{0,4},{4,0},{8,12},{12,8},{16,20},{20,16},{24,28},{28,24},{1,5},{5... | collective-permute-start | bytes 1769480 | tf_op jit(solution)/shard_map/ppermute | solution.py:916
  (146 other events, 1773.7 us)

commit v3 on v2

--- a/solution.py
+++ b/solution.py
@@ -21,11 +21,13 @@
 BF16 = jnp.bfloat16
 NEG = -1e30
 
-E_SCALE, E_SHIFT, E_G1, E_B1, E_G2, E_B2, E_CB2, E_G3, E_B3 = range(9)
-E_KEY, E_VALUE, E_ROWS = 16, 24, 32
-S_G3, S_B3, S_CB2, S_G2, S_B2, S_SCALE, S_SHIFT, S_LIVE = range(8)
-S_KEY, S_VALUE, S_G1, S_B1, S_ROWS = 8, 12, 16, 17, 24
-VMEM_LIMIT = 30 << 20
+E_G1, E_B1, E_G2, E_B2, E_CB2, E_G3, E_B3 = range(7)
+E_ROWS = 8
+M_SCALE, M_SHIFT = range(2)
+M_KEY, M_VALUE, M_ROWS = 8, 16, 24
+S_G3, S_B3, S_CB2, S_G2, S_B2, S_SCALE, S_SHIFT = range(7)
+S_KEY, S_VALUE, S_G1, S_B1, S_ROWS = 8, 12, 16, 17, 32
+MIB = 1 << 20
 
 
 def vmem():
@@ -44,7 +46,7 @@
     return jax.ShapeDtypeStruct(shape, dtype)
 
 
-def call(body, name, out_shape, in_specs, scratch, flops=0, moved=0):
+def call(body, name, out_shape, in_specs, scratch, flops=0, limit=14):
     many = isinstance(out_shape, (list, tuple))
     return pl.pallas_call(
         body,
@@ -53,8 +55,8 @@
         in_specs=in_specs,
         out_specs=[vmem() for _ in out_shape] if many else vmem(),
         scratch_shapes=scratch,
-        compiler_params=pltpu.CompilerParams(vmem_limit_bytes=VMEM_LIMIT),
-        cost_estimate=pl.CostEstimate(flops=flops, transcendentals=0, bytes_accessed=moved),
+        compiler_params=pltpu.CompilerParams(vmem_limit_bytes=limit * MIB),
+        cost_estimate=pl.CostEstimate(flops=0, transcendentals=0, bytes_accessed=0),
     )
 
 
@@ -70,19 +72,16 @@
 
 
 def fetch_routed(sources, target, me, parity, sems, first):
-    quarter = target.shape[-2] // 4
+    quarter = target.shape[1] // 4
     copies = []
     for index, source in enumerate(sources):
-        slot = jnp.bitwise_xor(me, (0, 1, 2, 2, 2, 3, 3, 3)[index])
-        place = target.at[slot]
+        place = target.at[jnp.bitwise_xor(me, (0, 1, 2, 2, 2, 3, 3, 3)[index])]
         if index >= 2:
             kind = (index - 2) % 3
             rows = 2 * quarter if kind == 0 else quarter
             half = parity if kind == 0 else 1 - parity
             start = half * 2 * quarter + (quarter if kind == 2 else 0)
-            start = pl.multiple_of(start, quarter)
-            lead = (slice(None),) * (len(place.shape) - 2)
-            place = place.at[lead + (pl.ds(start, rows), slice(None))]
+            place = place.at[pl.ds(pl.multiple_of(start, quarter), rows), :]
         copy = pltpu.make_async_copy(source, place, sems.at[first + index])
         copy.start()
         copies.append(copy)
@@ -171,7 +170,7 @@
             ],
             axis=1,
         )
-        right = jnp.concatenate([weight[s].reshape(9 * C, LANES) for s in range(4)], axis=1)
+        right = jnp.concatenate([weight[s] for s in range(4)], axis=1)
         write(start, jnp.dot(left, right, preferred_element_type=F32))
         return carry
 
@@ -193,7 +192,7 @@
         )
         right = jnp.concatenate(
             [
-                weight[block, 3 * a + b, pl.ds(pl.multiple_of(half * 256, 256), 256), :]
+                weight[block, pl.ds(pl.multiple_of((3 * a + b) * C + half * 256, 256), 256), :]
                 for a in range(3)
                 for b in range(3)
                 for block in range(4)
@@ -256,24 +255,27 @@
 
 
 def kernel_second(
-    meta, inner, image, pack, p0, p1, p2, p3, w0, w1, w2, w3, w4, w5, w6, w7,
-    middle, second_t, attn_t, qkv, field, weight, qkv_weight, attn, sems,
+    meta, inner, image, pack, m0, m1, m2, m3, p0, p1, p2, p3, w0, w1, w2, w3, w4, w5, w6, w7,
+    middle, second_t, attn_t, qkv, mod, field, weight, qkv_weight, attn, sems,
 ):
     pixels = image.shape[1]
     me = meta[0]
     qkv_copies = fetch((p0, p1, p2, p3), qkv_weight, me, sems, 0)
     weight_copies = fetch_routed((w0, w1, w2, w3, w4, w5, w6, w7), weight, me, meta[2], sems, 4)
+    mod_copies = fetch((m0, m1, m2, m3), mod, me, sems, 12)
     clear_padding(field, pixels)
     strip = 128
     means2, inverses2 = norm_rows(pixels, strip, lambda b, start: inner[b, pl.ds(start, strip), :])
+
+    wait_all(mod_copies)
 
     def modulate(index, carry):
         start = pl.multiple_of(index * strip, strip)
         for b in range(4):
             gain = pack[b, E_G2 : E_G2 + 1, :]
             bias = pack[b, E_B2 : E_B2 + 1, :]
-            scale = pack[b, E_SCALE : E_SCALE + 1, :]
-            shift = pack[b, E_SHIFT : E_SHIFT + 1, :]
+            scale = mod[b, M_SCALE : M_SCALE + 1, :]
+            shift = mod[b, M_SHIFT : M_SHIFT + 1, :]
             normed = (inner[b, pl.ds(start, strip), :] - means2[b]) * inverses2[b]
             modulated = (normed * gain + bias) * (1.0 + scale) + shift
             after = modulated * jax.nn.sigmoid(modulated)
@@ -317,8 +319,8 @@
 
 
 def kernel_attention(
-    meta, qkv, pack, middle, c0, c1, c2, c3, w0, w1, w2, w3,
-    o0, o1, o2, o3, cot, mixed, dqkv, dctx,
+    meta, qkv, mod, middle, c0, c1, c2, c3, w0, w1, w2, w3,
+    o0, o1, o2, cot, mixed, dqkv, dctx,
     weight, grad_mixed, score_ctx, grad_ctx_prob, prob_ctx, dscore_ctx, out_pix, dquery, dkey_t, dvalue_t, sems,
 ):
     pixels = qkv.shape[1]
@@ -335,15 +337,15 @@
     def diagonal(kind):
         found = []
         for s in range(4):
-            rows8 = pack[s, kind : kind + 8, :]
+            rows8 = mod[s, kind : kind + 8, :]
             tiled = jnp.concatenate([rows8] * 4, axis=0)
             own = (row32 // 4) == (2 * s + lane32 // HEAD)
             kept = jnp.where(own, tiled, 0.0)
             found.append(jnp.concatenate([kept, jnp.zeros((96, LANES), F32)], axis=0).astype(BF16))
         return jnp.concatenate(found, axis=1)
 
-    keys_ctx = diagonal(E_KEY)
-    values_ctx = diagonal(E_VALUE)
+    keys_ctx = diagonal(M_KEY)
+    values_ctx = diagonal(M_VALUE)
     wait_all(cot_copies)
     wait_all(weight_copies)
 
@@ -483,7 +485,7 @@
         result = jnp.dot(
             jnp.concatenate(parts, axis=1), weight[...].reshape(C, C), preferred_element_type=F32
         )
-        for offset, target in enumerate((o0, o1, o2, o3)):
+        for offset, target in enumerate((o0, o1, o2.at[0], o2.at[1])):
             other = jnp.bitwise_xor(me, offset)
             value = jnp.zeros((block, LANES), F32)
             for s in range(4):
@@ -546,7 +548,6 @@
 ):
     pixels = cot.shape[1]
     me = meta[0]
-    alive = meta[1].astype(F32)
     qkv_copies = fetch((p0, p1, p2, p3), qkv_weight, me, sems, 0)
     strip = 128
     clear_padding(field, pixels)
@@ -589,7 +590,6 @@
         sums[b, S_G3 : S_G3 + 1, :] = gain_sums[b]
         sums[b, S_B3 : S_B3 + 1, :] = bias_sums[b]
         sums[b, S_CB2 : S_CB2 + 1, :] = column_sum(branch[b])
-        sums[b, S_LIVE : S_LIVE + 1, :] = jnp.full((1, LANES), 1.0, F32) * alive
         sums[b, S_KEY : S_KEY + 8, :] = dctx[b]
     for offset, target in enumerate((d0, d1, d2, d3)):
         target[...] = field[1, jnp.bitwise_xor(me, offset), PAD : PAD + pixels, :]
@@ -660,7 +660,7 @@
     lax.fori_loop(0, 5, body, 0)
 
 
-def kernel_weight_send(digit, u0, u1, u2, u3, d0, d1, d2, d3, send, field):
+def kernel_weight_send(meta, u0, u1, u2, u3, d0, d1, d2, d3, send, field):
     pixels = u0.shape[2]
     clear_padding(field, pixels)
     strip = 128
@@ -672,15 +672,15 @@
         return carry
 
     lax.fori_loop(0, pixels // strip, spread, 0)
-    weight_taps(1 - digit[0], (u0, u1, u2, u3), field, send)
-
-
-def kernel_weight_own(digit, u0, u1, u2, u3, field, own):
-    weight_taps(digit[0], (u0, u1, u2, u3), field, own)
+    weight_taps(1 - meta[3], (u0, u1, u2, u3), field, send)
+
+
+def kernel_weight_own(meta, u0, u1, u2, u3, field, own):
+    weight_taps(meta[3], (u0, u1, u2, u3), field, own)
 
 
 def kernel_back_second(
-    meta, grad_field, inner, pack, sums_in, w0, w1, w2, w3, w4, w5, w6, w7,
+    meta, grad_field, inner, pack, mod, sums_in, w0, w1, w2, w3, w4, w5, w6, w7,
     field, sums, d0, d1, d2, d3, weight, grad, sems,
 ):
     pixels = inner.shape[1]
@@ -706,8 +706,8 @@
         found = []
         for b in range(4):
             bias = pack[b, E_B2 : E_B2 + 1, :]
-            scale = pack[b, E_SCALE : E_SCALE + 1, :]
-            shift = pack[b, E_SHIFT : E_SHIFT + 1, :]
+            scale = mod[b, M_SCALE : M_SCALE + 1, :]
+            shift = mod[b, M_SHIFT : M_SHIFT + 1, :]
             shaped = read_normed(b, start) * gains[b] + bias
             modulated = shaped * (1.0 + scale) + shift
             dmod = silu_slope(modulated, grad[b, pl.ds(start, strip), :])
@@ -746,7 +746,7 @@
 
 
 def kernel_back_first(
-    meta, grad_in, image, pack, dmiddle, sums_in, g0, g1, g2, g3, s0, s1, s2, s3, grad,
+    meta, grad_in, image, pack, dmiddle, sums_in, g0, g1, g2, grad, sums,
 ):
     pixels = image.shape[1]
     me = meta[0]
@@ -776,69 +776,111 @@
     gain_sums, bias_sums = norm_back_strips(
         pixels, strip, read_normed, lambda b, start: grad[b, pl.ds(start, strip), :], gains, inverses, write
     )
-    for offset, (target, small) in enumerate(zip((g0, g1, g2, g3), (s0, s1, s2, s3))):
+    for b in range(4):
+        sums[b] = sums_in[b]
+        sums[b, S_G1 : S_G1 + 1, :] = gain_sums[b]
+        sums[b, S_B1 : S_B1 + 1, :] = bias_sums[b]
+    for offset, target in enumerate((g0, g1, g2.at[0], g2.at[1])):
         other = jnp.bitwise_xor(me, offset)
-        target[...] = grad[other].astype(BF16)
-        small[...] = sums_in[other]
-        for b in range(4):
-
-            @pl.when(other == b)
-            def _():
-                small[S_G1 : S_G1 + 1, :] = gain_sums[b]
-                small[S_B1 : S_B1 + 1, :] = bias_sums[b]
-
-
-def kernel_factor_grads(
-    meta, factors, small0, small1, small2, small3, embed, context, vectors, scale
-):
+        target[0:pixels, :] = grad[other].astype(BF16)
+        target[pixels : pixels + S_ROWS, :] = sums[other].astype(BF16)
+
+
+def kernel_scale(factors0, factors1, scale):
+    total = jnp.zeros((1, LANES), F32)
+    for factors in (factors0, factors1):
+        for g in range(factors.shape[0]):
+            total = total + factors[g, 0].astype(F32)[1:2, 0:LANES]
+    scale[...] = jnp.broadcast_to(1.0 / total, (8, LANES))
+
+
+def kernel_factor_grads(meta, scale, factors0, factors1, small0, small1, embed, context, vectors):
     me = meta[0]
-    groups = factors.shape[0]
-    smalls = (small0, small1, small2, small3)
+    groups = factors0.shape[0]
+    inverse = scale[0:1, :]
     total = jnp.zeros((S_ROWS, LANES), F32)
-    for g in range(groups):
-        for small in smalls:
-            total = total + small[g]
-    inverse = 1.0 / total[S_LIVE : S_LIVE + 1, :]
+    for small in (small0, small1):
+        for g in range(4 * groups):
+            total = total + small[g].astype(F32)
     vectors[...] = total * inverse
-    scale[...] = jnp.broadcast_to(inverse, (8, LANES))
     over_rows = (((0,), (0,)), ((), ()))
     conditions, tokens, scales, shifts, keys, values = [], [], [], [], [], []
-    for g in range(groups):
-        for k, small in enumerate(smalls):
-            slot = jnp.bitwise_xor(me, k)
-            rows = factors[g, slot].astype(F32)
-            conditions.append(rows[0:1])
-            tokens.append(rows[CTX : 2 * CTX])
-            scales.append(small[g, S_SCALE : S_SCALE + 1, :])
-            shifts.append(small[g, S_SHIFT : S_SHIFT + 1, :])
-            keys.append(small[g, S_KEY : S_KEY + CTX, :])
-            values.append(small[g, S_VALUE : S_VALUE + CTX, :])
-    left = jnp.concatenate(conditions, axis=0)
-    for place, parts in enumerate((scales, shifts)):
-        right = jnp.concatenate(parts, axis=0) * inverse
-        embed[:, place, :] = lax.dot_general(
-            left, right, over_rows, precision=lax.Precision.HIGHEST, preferred_element_type=F32
+    for factors, small in ((factors0, small0), (factors1, small1)):
+        for g in range(groups):
+            for k in range(4):
+                rows = factors[g, jnp.bitwise_xor(me, k)].astype(F32)
+                term = small[4 * g + k].astype(F32)
+                conditions.append(rows[0:1])
+                tokens.append(rows[CTX : 2 * CTX])
+                scales.append(term[S_SCALE : S_SCALE + 1])
+                shifts.append(term[S_SHIFT : S_SHIFT + 1])
+                keys.append(term[S_KEY : S_KEY + CTX])
+                values.append(term[S_VALUE : S_VALUE + CTX])
+    for lefts, pairs, target in (
+        (conditions, (scales, shifts), embed),
+        (tokens, (keys, values), context),
+    ):
+        left = jnp.concatenate(lefts, axis=0).astype(BF16)
+        right = jnp.concatenate(
+            [jnp.concatenate(parts, axis=0).astype(BF16) for parts in pairs], axis=1
         )
-    left = jnp.concatenate(tokens, axis=0).astype(BF16)
-    for place, parts in enumerate((keys, values)):
-        right = jnp.concatenate(parts, axis=0).astype(BF16)
-        context[:, place, :] = (
-            lax.dot_general(left, right, over_rows, preferred_element_type=F32) * inverse
-        )
-
-
-def kernel_slots(meta, p0, p1, p2, p3, whole, sems):
-    wait_all(fetch((p0, p1, p2, p3), whole, meta[0], sems, 0))
-
-
-def kernel_split(counts, width, digit, *refs):
+        grad = lax.dot_general(left, right, over_rows, preferred_element_type=F32)
+        for place in range(2):
+            target[:, place, :] = grad[:, place * LANES : (place + 1) * LANES] * inverse
+
+
+def kernel_stack(*refs):
+    whole = refs[-1]
+    base = 0
+    for ref in refs[:-1]:
+        count = ref.shape[0]
+        whole[base : base + count] = ref[...]
+        base += count
+
+
+def stack(parts):
+    shape = (sum(part.shape[0] for part in parts),) + parts[0].shape[1:]
+    return call(
+        kernel_stack, "stack", struct(shape, parts[0].dtype), [vmem()] * len(parts), [], limit=12
+    )(*parts)
+
+
+def kernel_slots(meta, own, near, far, across, whole, sems):
+    rows = pl.ds(0, whole.shape[1])
+    sources = (own.at[rows], near.at[rows], far.at[0, rows], across.at[1, rows])
+    wait_all(fetch(sources, whole, meta[0], sems, 0))
+
+
+def kernel_cut(source, first, second):
+    rows = first.shape[0]
+    first[...] = source[0:rows]
+    second[...] = source[rows : 2 * rows]
+
+
+def cut(source):
+    rows, lanes = source.shape
+    return call(
+        kernel_cut, "cut", [struct((rows // 2, lanes), BF16)] * 2, [vmem()], [], limit=8
+    )(source)
+
+
+def kernel_small_stack(own, near, far, across, whole):
+    rows = pl.ds(own.shape[0] - S_ROWS, S_ROWS)
+    whole[0] = own[rows, :]
+    whole[1] = near[rows, :]
+    whole[2] = far[0, rows, :]
+    whole[3] = across[1, rows, :]
+
+
+def kernel_split(counts, width, digit, meta, *refs):
     parts = refs[sum(counts) :]
     rows = parts[0].shape[1]
     for offset, part in enumerate(parts):
-        start = pl.multiple_of(jnp.bitwise_xor(digit[0], offset) * rows, rows)
+        start = pl.multiple_of(jnp.bitwise_xor(meta[digit], offset) * rows, rows)
         position, base = 0, 0
         for count in counts:
             terms = refs[position : position + count]
+            terms = [term.at[0] if len(term.shape) == 4 else term for term in terms]
             total = terms[0][:, pl.ds(start, rows), :].astype(F32)
             for term in terms[1:]:
                 total = total + term[:, pl.ds(start, rows), :].astype(F32)
@@ -847,18 +889,25 @@
             base += total.shape[0]
 
 
-def split_sum(groups, width, digit):
-    blocks = sum(terms[0].shape[0] for terms in groups)
-    rows = groups[0][0].shape[1]
+def split_sum(groups, width, digit, meta):
+    blocks = sum(terms[-1].shape[0] for terms in groups)
+    rows = groups[0][-1].shape[1]
     flat = [term for terms in groups for term in terms]
     shape = (blocks, rows // width, LANES)
     return call(
-        functools.partial(kernel_split, tuple(len(terms) for terms in groups), width),
+        functools.partial(kernel_split, tuple(len(terms) for terms in groups), width, digit),
         "split_sum",
         [struct(shape, F32)] + [struct(shape, BF16)] * (width - 1),
         [smem()] + [vmem()] * len(flat),
         [],
-    )(digit, *flat)
+        limit=12,
+    )(meta, *flat)
+
+
+def kernel_far(mine, got, own, far):
+    blocks = own.shape[0]
+    own[...] = mine[0:blocks] + got[0:blocks].astype(F32)
+    far[...] = (mine[blocks : 2 * blocks] + got[blocks : 2 * blocks].astype(F32)).astype(BF16)
 
 
 def kernel_total(*refs):
@@ -870,45 +919,53 @@
 
 def total_sum(terms):
     return call(
-        kernel_total, "total_sum", struct(terms[0].shape, BF16), [vmem()] * len(terms), []
+        kernel_total, "total_sum", struct(terms[0].shape, BF16), [vmem()] * len(terms), [], limit=12
     )(*terms)
 
 
-def kernel_join(digit, *refs):
+def kernel_join(digit, meta, *refs):
     parts, whole = refs[:-1], refs[-1]
     rows = parts[0].shape[1]
     for offset, part in enumerate(parts):
-        start = pl.multiple_of(jnp.bitwise_xor(digit[0], offset) * rows, rows)
+        start = pl.multiple_of(jnp.bitwise_xor(meta[digit], offset) * rows, rows)
         whole[:, pl.ds(start, rows), :] = part[...]
 
 
-def join(parts, digit):
+def join(parts, digit, meta):
     blocks, rows, _ = parts[0].shape
     return call(
-        kernel_join,
+        functools.partial(kernel_join, digit),
         "join",
         struct((blocks, rows * len(parts), LANES), BF16),
         [smem()] + [vmem()] * len(parts),
         [],
-    )(digit, *parts)
-
-
-def kernel_last(digit, scale, mine, other, whole):
+        limit=12,
+    )(meta, *parts)
+
+
+def kernel_last(digit, meta, scale, mine, other, conv, *more):
     rows = mine.shape[1]
     for offset, part in enumerate((mine, other)):
-        start = pl.multiple_of(jnp.bitwise_xor(digit[0], offset) * rows, rows)
-        whole[:, pl.ds(start, rows), :] = part[...].astype(F32) * scale[0:1, :]
-
-
-def last_join(pair, digit, scale):
+        start = pl.multiple_of(jnp.bitwise_xor(meta[digit], offset) * rows, rows)
+        count = conv.shape[0]
+        conv[:, pl.ds(start, rows), :] = part[0:count].astype(F32) * scale[0:1, :]
+        for proj in more:
+            proj[:, pl.ds(start, rows)] = (part[count].astype(F32) * scale[0:1, :]).T
+
+
+def last_join(pair, digit, meta, scale, more=False):
     blocks, rows, _ = pair[0].shape
+    shapes = [struct((3 if more else blocks, 2 * rows, LANES), F32)]
+    if more:
+        shapes.append(struct((LANES, 2 * rows), F32))
     return call(
-        kernel_last,
+        functools.partial(kernel_last, digit),
         "last_join",
-        struct((blocks, 2 * rows, LANES), F32),
+        shapes,
         [smem()] + [vmem()] * 3,
         [],
-    )(digit, scale, *pair)
+        limit=12,
+    )(meta, scale, *pair)
 
 
 def swap(value, axis, offset):
@@ -935,17 +992,7 @@
 
 
 def dp_levels(size):
-    levels = []
-    low = 1
-    while low < size:
-        width = 2 if low == 1 or size // low < 4 else 4
-        levels.append((low, width))
-        low *= width
-    return levels
-
-
-def gather_step(stacked, low):
-    return jnp.concatenate([stacked, swap(stacked, "dp", low)], axis=0)
+    return [(1 << k, 2) for k in range(size.bit_length() - 1)]
 
 
 def bits(size):
@@ -977,22 +1024,34 @@
     me = lax.axis_index("mp")
     group = lax.axis_index("dp")
     parity = (group ^ (group >> 1)) & 1
-    meta = jnp.stack([me, (me < image_count[0]).astype(jnp.int32), parity]).astype(jnp.int32)
     levels = dp_levels(lax.axis_size("dp"))
-    digits = [((group // low) % wide).astype(jnp.int32)[None] for low, wide in levels]
+    own_digits = [(group >> (low.bit_length() - 1)) & (wide - 1) for low, wide in levels]
+    meta = jnp.stack(
+        [me, (me < image_count[0]).astype(jnp.int32), parity] + own_digits
+    ).astype(jnp.int32)
+    digits = range(3, 3 + len(levels))
     steps = bits(lax.axis_size("dp"))
 
-    conv1_shard = conv1_weight.reshape(9, C, LANES)
-    conv2_shard = conv2_weight.reshape(9, C, LANES)
+    conv1_weight, conv2_weight, image_in, out_cotangent, meta = tie(
+        conv1_weight, conv2_weight, image_in, out_cotangent, meta
+    )
+
+    vectors = jnp.stack(
+        [norm1_gain, norm1_bias, norm2_gain, norm2_bias, conv2_bias, norm3_gain, norm3_bias, norm3_bias]
+    )
+    conv1_shard = conv1_weight.reshape(9 * C, LANES)
+    conv2_shard = conv2_weight.reshape(9 * C, LANES)
     qkv_shard = jnp.transpose(qkv_weight, (1, 0, 2))
 
     def half_of(shard):
-        rows = shard.shape[-2] // 2
-        return lax.dynamic_slice_in_dim(shard, parity * rows, rows, axis=shard.ndim - 2)
-
+        rows = shard.shape[0] // 2
+        return lax.dynamic_slice_in_dim(shard, parity * rows, rows, axis=0)
+
+    packs = share(vectors)
     half1 = swap(half_of(conv1_shard), "mp", 2)
-    images = exchange(pick(image_in, me))
     near1 = swap(conv1_shard, "mp", 1)
+    slices, *packs = tie(image_in, *packs)
+    images = exchange(pick(slices, me))
 
     half_width = EMB // 2
     frequency = jnp.exp(-math.log(10000.0) * jnp.arange(half_width, dtype=F32) / half_width)
@@ -1009,50 +1068,46 @@
         context_weight.reshape(EMB, 2 * LANES),
         preferred_element_type=F32,
     ).astype(BF16).astype(F32).reshape(slots, 2 * CTX, 2, LANES)
-    vectors = jnp.stack(
-        [norm1_gain, norm1_bias, norm2_gain, norm2_bias, conv2_bias, norm3_gain, norm3_bias]
+    early = jnp.concatenate(
+        [scale_shift, jnp.zeros((slots, 6, LANES), F32), context[:, :, 0], context[:, :, 1]], axis=1
     )
-    early = jnp.concatenate(
-        [
-            scale_shift,
-            jnp.broadcast_to(vectors[None], (slots, 7, LANES)),
-            jnp.zeros((slots, 7, LANES), F32),
-            context[:, :, 0],
-            context[:, :, 1],
-        ],
-        axis=1,
-    )
-    early, near1 = tie(early, near1)
-    packs = exchange(pick(early, me))
-    factors = jnp.concatenate(
-        [jnp.broadcast_to(condition[:, None], (slots, CTX, EMB)), context_tokens], axis=1
-    )[None]
+    count_rows = jnp.broadcast_to(image_count.astype(BF16)[:, None, None], (slots, CTX - 1, EMB))
+    factors = jnp.concatenate([condition[:, None], count_rows, context_tokens], axis=1)[None]
+    mods = pick(early, me)
+    half2 = half_of(conv2_shard)
 
     def relayed(shard, near, half):
-        quarter = half.shape[-2] // 2
-        by_x = swap(half[:, :quarter], "dp", 1)
-        by_z = swap(half[:, quarter:], "dp", 2)
+        by_x, by_z = cut(half)
+        by_x = swap(by_x, "dp", 1)
+        by_z = swap(by_z, "dp", 2)
         return (shard, near, half, by_x, by_z) + tuple(
             swap(part, "mp", 1) for part in (half, by_x, by_z)
         )
 
+    cots = pick(out_cotangent, me)
+    half1, near1, image_near, mods, half2, factors, cots = tie(
+        half1, near1, images[1], mods, half2, factors, cots
+    )
     conv1 = relayed(conv1_shard, near1, half1)
-    half2 = half_of(conv2_shard)
-    half2, *tied = tie(half2, *images, *packs)
-    images, packs = tied[:4], tied[4:]
+    far_images = images[2:]
+    mods, *conv1 = tie(mods, *conv1)
+    mods = exchange(mods)
+    conv1, far_images, mods, half2 = tie(conv1, far_images, mods, half2)
+    images = (images[0], image_near) + tuple(far_images)
     half2 = swap(half2, "mp", 2)
-    near2 = swap(conv2_shard, "mp", 1)
     qkv_far = swap(qkv_shard, "mp", 2)
     proj_far = swap(proj_weight, "mp", 2)
-    factors = gather_step(factors, steps[0])
+    near2 = swap(conv2_shard, "mp", 1)
+    factors = [factors, swap(factors, "dp", 1)]
 
     block = struct((4, pixels, LANES), BF16)
     block32 = struct((4, pixels, LANES), F32)
     turned = struct((4, LANES, pixels), BF16)
     fields = struct((3, 4, pixels + 2 * PAD, LANES), BF16)
     piece = struct((pixels, LANES), BF16)
+    pair_piece = struct((2, pixels, LANES), BF16)
     field_scratch = pltpu.VMEM((3, 4, pixels + 2 * PAD, LANES), BF16)
-    conv_scratch = pltpu.VMEM((4, 9, C, LANES), BF16)
+    conv_scratch = pltpu.VMEM((4, 9 * C, LANES), BF16)
     qkv_scratch = pltpu.VMEM((4, 3, C, LANES), BF16)
     grad_scratch = pltpu.VMEM((4, pixels, LANES), F32)
     conv_flops = 2 * pixels * 9 * C * C
@@ -1066,43 +1121,44 @@
         conv_flops,
     )(meta, *images, *packs, *conv1)
 
-    inner, half2, near2, qkv_far, proj_far, factors = tie(
-        inner, half2, near2, qkv_far, proj_far, factors
-    )
-    qkv_near = swap(qkv_shard, "mp", 1)
+    inner, half2, near2, factors = tie(inner, half2, near2, factors)
+    factors = stack(factors)
     conv2 = relayed(conv2_shard, near2, half2)
-    qkv_w = (qkv_shard, qkv_near, qkv_far, swap(qkv_far, "mp", 1))
-    proj_w = (proj_weight, swap(proj_weight, "mp", 1), proj_far, swap(proj_far, "mp", 1))
-    inner, *conv2 = tie(inner, *conv2)
-    cots = exchange(pick(out_cotangent, me))
-    factors = gather_step(factors, steps[1])
-    middle, second_t, attn_t, qkv = call(
+    inner, qkv_far, *conv2 = tie(inner, qkv_far, *conv2)
+    qkv_w = (qkv_shard, swap(qkv_shard, "mp", 1), qkv_far, swap(qkv_far, "mp", 1))
+    inner, *qkv_w = tie(inner, *qkv_w)
+    cots = exchange(cots)
+    factors = [factors, swap(factors, "dp", 2)]
+    middle, second_t, attn_t, qkv, mod = call(
         kernel_second,
         "second",
-        [block32, turned, turned, struct((4, pixels, 3 * LANES), BF16)],
-        [smem()] + [vmem()] * 3 + [anywhere()] * 12,
+        [block32, turned, turned, struct((4, pixels, 3 * LANES), BF16), struct((4, M_ROWS, LANES), F32)],
+        [smem()] + [vmem()] * 3 + [anywhere()] * 16,
         [
             field_scratch,
             conv_scratch,
             qkv_scratch,
             pltpu.VMEM((4, pixels, LANES), BF16),
-            pltpu.SemaphoreType.DMA((12,)),
+            pltpu.SemaphoreType.DMA((16,)),
         ],
         conv_flops + 6 * pixels * C * C,
-    )(meta, inner, image, pack, *qkv_w, *conv2)
+    )(meta, inner, image, pack, *mods, *qkv_w, *conv2)
     ctx_scratch = pltpu.VMEM((pixels, LANES), F32)
     turned_scratch = pltpu.VMEM((LANES, pixels), F32)
-    qkv, first_t, factors, *cots = tie(qkv, first_t, factors, *cots)
+    proj_w = (proj_weight, swap(proj_weight, "mp", 1), proj_far, swap(proj_far, "mp", 1))
+    qkv, first_t, factors, cots, proj_w = tie(qkv, first_t, factors, cots, proj_w)
+    factors = stack(factors)
     second_y = swap(second_t, "mp", 2)
     first_y = swap(first_t, "mp", 2)
     second_c = swap(second_t, "mp", 1)
     first_c = swap(first_t, "mp", 1)
-    for low in steps[2:]:
-        factors = gather_step(factors, low)
-    *outs, cot, mixed, dqkv, dctx = call(
+    for low in steps[2:-1]:
+        factors = stack([factors, swap(factors, "dp", low)])
+    factors = (factors, swap(factors, "dp", steps[-1]))
+    out_own, out_near, out_far, cot, mixed, dqkv, dctx = call(
         kernel_attention,
         "attention",
-        [piece] * 4
+        [piece, piece, pair_piece]
         + [block, block, struct((4, pixels, 3 * LANES), BF16), struct((4, 2 * CTX, LANES), F32)],
         [smem()] + [vmem()] * 3 + [anywhere()] * 8,
         [
@@ -1119,31 +1175,7 @@
             pltpu.SemaphoreType.DMA((8,)),
         ],
         4 * 12 * pixels * pixels * C,
-    )(meta, qkv, pack, middle, *cots, *proj_w)
-    dqkv, second_y, first_y, second_c, first_c, factors = tie(
-        dqkv, second_y, first_y, second_c, first_c, factors
-    )
-    second_d = swap(second_y, "mp", 1)
-    first_d = swap(first_y, "mp", 1)
-    dmiddle, field2, sums, *gradients2 = call(
-        kernel_back_attention,
-        "back_attention",
-        [block32, fields, struct((4, S_ROWS, LANES), F32)] + [piece] * 4,
-        [smem()] + [vmem()] * 5 + [anywhere()] * 4,
-        [qkv_scratch, grad_scratch, pltpu.SemaphoreType.DMA((4,))],
-        8 * pixels * C * C,
-    )(meta, dqkv, cot, middle, pack, dctx, *qkv_w)
-    gradients2, second_d, first_d = tie(gradients2, second_d, first_d)
-    gradients2 = exchange(gradients2)
-    field1, sums, *gradients1 = call(
-        kernel_back_second,
-        "back_second",
-        [fields, struct((4, S_ROWS, LANES), F32)] + [piece] * 4,
-        [smem()] + [vmem()] * 4 + [anywhere()] * 8,
-        [conv_scratch, grad_scratch, pltpu.SemaphoreType.DMA((8,))],
-        conv_flops,
-    )(meta, field2, inner, pack, sums, *conv2)
-
+    )(meta, qkv, mod, middle, *cots, *proj_w)
     def weight_send(sources, gradients):
         return call(
             kernel_weight_send,
@@ -1151,8 +1183,8 @@
             [struct((9, C // 2, LANES), BF16), fields],
             [smem()] + [vmem()] * 8,
             [],
-            conv_flops // 2,
-        )(digits[0], *sources, *gradients)
+            limit=16,
+        )(meta, *sources, *gradients)
 
     def weight_own(sources, field):
         return call(
@@ -1161,101 +1193,167 @@
             struct((9, C // 2, LANES), F32),
             [smem()] + [vmem()] * 5,
             [],
-            conv_flops // 2,
-        )(digits[0], *sources, field)
-
-    seconds = (second_t, second_c, second_y, second_d)
-    firsts = (first_t, first_c, first_y, first_d)
-    gradients1, gradients2 = tie(gradients1, gradients2)
-    gradients1 = exchange(gradients1)
-    send2, wide2 = weight_send(seconds, gradients2)
-    got2 = swap(send2, "dp", 1)
-    own2 = weight_own(seconds, wide2)
-    own2, gradients1, outs = tie(own2, gradients1, outs)
-    out_parts = exchange(outs)
-    send1, wide1 = weight_send(firsts, gradients1)
-    got1 = swap(send1, "dp", 1)
-    own1 = weight_own(firsts, wide1)
+            limit=16,
+        )(meta, *sources, field)
+
+    def down(terms, level):
+        own, send = split_sum([terms], 2, digits[level], meta)
+        return [own, swap(send, "dp", levels[level][0])]
+
+    def across(value, level):
+        return [value, swap(value, "dp", levels[level][0])]
+
+    def inner_levels(terms):
+        for level in range(3, len(levels)):
+            terms = down(terms, level)
+        value = total_sum(terms)
+        for level in range(len(levels) - 1, 2, -1):
+            value = join(across(value, level), digits[level], meta)
+        return value
+
     att_keep, att_send = call(
         kernel_attention_grad,
         "attention_grad",
         [struct((2, 4, C, LANES), BF16)] * 2,
         [smem()] + [vmem()] * 4,
         [pltpu.VMEM((4, LANES, pixels), BF16)],
-        8 * pixels * C * C,
     )(meta, dqkv, mixed, attn_t, cot)
-    own1, got2, out_parts = tie(own1, got2, out_parts)
-
-    def down(groups, level):
-        low, wide = levels[level]
-        parts = split_sum(groups, wide, digits[level])
-        return [parts[0]] + [swap(parts[k], "dp", low * k) for k in range(1, wide)]
-
-    def spread(value, level):
-        low, wide = levels[level]
-        return [value] + [swap(value, "dp", low * k) for k in range(1, wide)]
-
-    terms2 = down([[own2, got2]], 1)
-    att_got = swap(att_send, "mp", 1)
+    dqkv, att_send, second_y, first_y, second_c, first_c, factors = tie(
+        dqkv, att_send, second_y, first_y, second_c, first_c, factors
+    )
+    second_d = swap(second_y, "mp", 1)
+    first_d = swap(first_y, "mp", 1)
+    att = [att_keep.reshape(8, C, LANES), swap(att_send, "mp", 1).reshape(8, C, LANES)]
+    dmiddle, field2, sums, *gradients2 = call(
+        kernel_back_attention,
+        "back_attention",
+        [block32, fields, struct((4, S_ROWS, LANES), F32)] + [piece] * 4,
+        [smem()] + [vmem()] * 5 + [anywhere()] * 4,
+        [qkv_scratch, grad_scratch, pltpu.SemaphoreType.DMA((4,))],
+    )(meta, dqkv, cot, middle, pack, dctx, *qkv_w)
+    gradients2, second_d, first_d, att, field2 = tie(gradients2, second_d, first_d, att, field2)
+    seconds = (second_t, second_c, second_y, second_d)
+    firsts = (first_t, first_c, first_y, first_d)
+    gradients2 = exchange(gradients2)
+    att = down(att, 0)
+    field2, att[0] = tie(field2, att[0])
+    field1, sums, *gradients1 = call(
+        kernel_back_second,
+        "back_second",
+        [fields, struct((4, S_ROWS, LANES), F32)] + [piece] * 4,
+        [smem()] + [vmem()] * 5 + [anywhere()] * 8,
+        [conv_scratch, grad_scratch, pltpu.SemaphoreType.DMA((8,))],
+        limit=17,
+    )(meta, field2, inner, pack, mod, sums, *conv2)
+    gradients1, gradients2, att = tie(gradients1, gradients2, att)
+    gradients1 = exchange(gradients1)
+    att = down(att, 1)
+    gradients2, att[0] = tie(gradients2, att[0])
+    send2, wide2 = weight_send(seconds, gradients2)
+    got2 = swap(send2, "dp", 1)
+    wide2, att = tie(wide2, att)
+    att = down(att, 2)
+    wide2, att[0] = tie(wide2, att[0])
+    own2 = weight_own(seconds, wide2)
+    own2, att, field1 = tie(own2, att, field1)
+    for level in range(3, len(levels)):
+        att = down(att, level)
+    att_own, att_far = call(
+        kernel_far,
+        "att_far",
+        [struct((4,) + att[0].shape[1:], F32), struct((4,) + att[0].shape[1:], BF16)],
+        [vmem()] * 2,
+        [],
+        limit=12,
+    )(*att)
+    field1, att_own = tie(field1, att_own)
+    att = [att_own, swap(att_far, "mp", 2)]
     grad_first = call(
         kernel_back_conv,
         "back_conv",
         block32,
         [smem()] + [vmem()] + [anywhere()] * 8,
         [conv_scratch, pltpu.SemaphoreType.DMA((8,))],
-        conv_flops,
     )(meta, field1, *conv1)
-    grad_first, att_got, *terms2 = tie(grad_first, att_got, *terms2)
-    att_far = swap(total_sum([att_keep[1], att_got[1]]), "mp", 2)
-
-    def inner_levels(terms):
-        for level in range(2, len(levels)):
-            terms = down([terms], level)
-        value = total_sum(terms)
-        for level in range(len(levels) - 1, 1, -1):
-            value = join(spread(value, level), digits[level])
-        return value
-
-    value2 = inner_levels(terms2)
-    parts2 = spread(value2, 1)
-    terms1 = down([[own1, got1]], 1)
-    back = call(
+    grad_first, gradients1, att = tie(grad_first, gradients1, att)
+    att = total_sum(att)
+    for level in range(len(levels) - 1, 2, -1):
+        att = join(across(att, level), digits[level], meta)
+    gradients1, att, out_far = tie(gradients1, att, out_far)
+    att = across(att, 2)
+    send1, wide1 = weight_send(firsts, gradients1)
+    got1 = swap(send1, "dp", 1)
+    out_far = swap(out_far, "mp", 2)
+    wide1, got2, own2 = tie(wide1, got2, own2)
+    terms2 = down([own2, got2], 1)
+    wide1, terms2[0] = tie(wide1, terms2[0])
+    own1 = weight_own(firsts, wide1)
+    grad_first, own1, terms2, att = tie(grad_first, own1, terms2, att)
+    terms2 = down(terms2, 2)
+    att = across(join(att, digits[2], meta), 1)
+    grad_first, terms2[0], att[0] = tie(grad_first, terms2[0], att[0])
+    grad_own, grad_near, grad_far = call(
         kernel_back_first,
         "back_first",
-        [piece] * 4 + [struct((S_ROWS, LANES), F32)] * 4,
+        [
+            struct((pixels + S_ROWS, LANES), BF16),
+            struct((pixels + S_ROWS, LANES), BF16),
+            struct((2, pixels + S_ROWS, LANES), BF16),
+        ],
         [smem()] + [vmem()] * 5,
-        [grad_scratch],
-        conv_flops // 4,
+        [grad_scratch, pltpu.VMEM((4, S_ROWS, LANES), F32)],
     )(meta, grad_first, image, pack, dmiddle, sums)
-    image_grads, smalls = back[:4], back[4:]
-    half2_sum = join(parts2, digits[1])
-    pair2 = spread(half2_sum, 0)
-    value1 = inner_levels(terms1)
-    parts1 = spread(value1, 1)
-    half1_sum = join(parts1, digits[1])
-    pair1 = spread(half1_sum, 0)
-    att_terms = down([[att_keep[0], att_got[0], att_far]], 0)
-    att_terms = down([att_terms], 1)
-    att_value = inner_levels(att_terms)
-    att_pair = spread(join(spread(att_value, 1), digits[1]), 0)
-
-    image_parts = exchange(image_grads)
-    smalls = [small[None] for small in exchange(smalls)]
-    smalls = jnp.stack(smalls)
-    for low in steps:
-        smalls = jnp.concatenate([smalls, swap(smalls, "dp", low)], axis=1)
-    embed_grad, context_grad, vector_sums, scale = call(
+    grad_far, terms2, got1, own1 = tie(grad_far, terms2, got1, own1)
+    terms1 = down([own1, got1], 1)
+    ends2 = across(inner_levels(terms2), 2)
+    grad_far, ends2[0], terms1[0], att = tie(grad_far, ends2[0], terms1[0], att)
+    att = across(join(att, digits[1], meta), 0)
+    grad_far = swap(grad_far, "mp", 2)
+    ends2, terms1, grad_near, out_far = tie(ends2, terms1, grad_near, out_far)
+    terms1 = down(terms1, 2)
+    ends2 = across(join(ends2, digits[2], meta), 1)
+    scale = call(kernel_scale, "scale", struct((8, LANES), F32), [vmem()] * 2, [], limit=8)(*factors)
+    ends2, terms1, scale, att = tie(ends2, terms1, scale, att)
+    ends1 = across(inner_levels(terms1), 2)
+    ends2 = across(join(ends2, digits[1], meta), 0)
+    qkv_grad, proj_grad = last_join(att, digits[0], meta, scale, True)
+    ends1, qkv_grad, grad_near = tie(ends1, qkv_grad, grad_near)
+    ends1 = across(join(ends1, digits[2], meta), 1)
+    ends1[0], grad_near, grad_far = tie(ends1[0], grad_near, grad_far)
+    grad_near = swap(grad_near, "mp", 1)
+    grad_across = swap(grad_far, "mp", 1)
+    image_parts = (grad_own, grad_near, grad_far, grad_across)
+    ends1 = across(join(ends1, digits[1], meta), 0)
+    ends1[0], grad_across, grad_near, ends2 = tie(ends1[0], grad_across, grad_near, ends2)
+    smalls = call(
+        kernel_small_stack,
+        "stack",
+        struct((4, S_ROWS, LANES), BF16),
+        [vmem()] * 4,
+        [],
+        limit=8,
+    )(grad_own, grad_near, grad_far, grad_across)
+    small_got = swap(smalls, "dp", 1)
+    (conv2_grad,) = last_join(ends2, digits[0], meta, scale)
+    small_got, conv2_grad = tie(small_got, conv2_grad)
+    smalls = stack([smalls, small_got])
+    for low in steps[1:-1]:
+        smalls = stack([smalls, swap(smalls, "dp", low)])
+    small_got = swap(smalls, "dp", steps[-1])
+    smalls, out_far, out_near = tie(smalls, out_far, out_near)
+    out_parts = (out_own, swap(out_near, "mp", 1), out_far, swap(out_far, "mp", 1))
+    embed_grad, context_grad, vector_sums = call(
         kernel_factor_grads,
         "factor_grads",
         [
             struct((EMB, 2, LANES), F32),
             struct((EMB, 2, LANES), F32),
             struct((S_ROWS, LANES), F32),
-            struct((8, LANES), F32),
         ],
         [smem()] + [vmem()] * 5,
         [],
-    )(meta, factors, smalls[0], smalls[1], smalls[2], smalls[3])
+        limit=12 if len(steps) < 4 else 56,
+    )(meta, scale, *factors, smalls, small_got)
 
     def in_slots(parts):
         return pl.pallas_call(
@@ -1265,13 +1363,12 @@
             in_specs=[smem()] + [anywhere()] * 4,
             out_specs=vmem(),
             scratch_shapes=[pltpu.SemaphoreType.DMA((4,))],
+            compiler_params=pltpu.CompilerParams(vmem_limit_bytes=8 * MIB),
         )(meta, *parts)
 
     block_out = in_slots(out_parts)
     image_grad = in_slots(image_parts)
-    conv2_grad = last_join(pair2, digits[0], scale)
-    conv1_grad = last_join(pair1, digits[0], scale)
-    att_grad = last_join(att_pair, digits[0], scale)
+    (conv1_grad,) = last_join(ends1, digits[0], meta, scale)
     return (
         block_out,
         image_grad,
@@ -1285,9 +1382,9 @@
         vector_sums[S_CB2],
         vector_sums[S_G3],
         vector_sums[S_B3],
-        jnp.transpose(att_grad[:3], (1, 0, 2)),
+        jnp.transpose(qkv_grad, (1, 0, 2)),
         context_grad,
-        att_grad[3].T,
+        proj_grad,
     )
 
 

time: 344 us -> 301 us (0.88)
  starting transfers between devices: 87.1 us -> 48.6 us
  local copies, waits for them, and re-layouts: 36.7 us -> 7.55 us
  waiting for transfers between devices: 72.3 us -> 94.3 us
  Pallas kernels: 139 us -> 143 us
    ppermute x82 -> x76, starting transfers between devices: 87.1 us -> 48.6 us  [swap(): return lax.ppermute(value, axis, [(i, i ^ offset) for i in range(size)])]
    unnamed x194 -> x15, local copies, waits for them, and re-layouts: 25.1 us -> 1.14 us
    ppermute x82 -> x76, waiting for transfers between devices: 72.3 us -> 94.3 us  [swap(): return lax.ppermute(value, axis, [(i, i ^ offset) for i in range(size)])]
    pallas_call x8 -> x20, Pallas kernels: 47.7 us -> 54.9 us  [the longest x1 41.1 us: local(): call(kernel_attention, 'attention', [piece, piece, pair_piece] + [block,...]
  transfers between devices with their start and end apart: 82 -> 76, of which waited for: 23 -> 28; matrix products, arithmetic and copies ran while one was open for 5% -> 4% of each run, Pallas kernels for 41% -> 47%
where the time goes in v3:
time: 301 us; the launch traced here: 300 us
  Pallas kernels  143 us (48%)
  waiting for transfers between devices  94.3 us (31%)
  starting transfers between devices  48.6 us (16%)
  local copies, waits for them, and re-layouts  7.55 us (3%)
    ppermute x76, waiting for transfers between devices, swap(): return lax.ppermute(value, axis, [(i, i ^ offset) for i in range(size)])  94.3 us
    ppermute x76, starting transfers between devices, swap(): return lax.ppermute(value, axis, [(i, i ^ offset) for i in range(size)])  48.6 us
    pallas_call x1, Pallas kernels, local(): call(kernel_attention, 'attention', [piece, piece, pair_piece] + [block,...  41.1 us
    pallas_call x1, Pallas kernels, local(): call(kernel_second, 'second', [block32, turned, turned, struct((4, pixels...  16.3 us
    pallas_call x1, Pallas kernels, local(): call(kernel_back_second, 'back_second', [fields, struct((4, S_ROWS, LANES...  11.4 us
    pallas_call x1, Pallas kernels, local(): call(kernel_first, 'first', [block, struct((4, E_ROWS, LANES), F32), turn...  9.91 us
    pallas_call x2, Pallas kernels, weight_send(): call(kernel_weight_send, 'weight_send', [struct((9, C // 2, LANES), BF16)...  9.61 us
    pallas_call x2, Pallas kernels, weight_own(): call(kernel_weight_own, 'weight_own', struct((9, C // 2, LANES), F32), [s...  8.42 us
  transfers between devices with their start and end apart: 76, of which 28 were waited for; matrix products, arithmetic and copies ran while one was open for 4% of the time, Pallas kernels for 47%

profile of v3, /device:TPU:0, one launch (start us, length us, event | category | flops | bytes accessed | tf_op | source)
XLA Modules:
  0.0 300.4 jit_solution(5767455328873437740)
XLA Ops:
  1.5 3.0 %collective-permute-start.1 = (f32[8,128]{1,0:T(8,128)S(1)}, f32[8,128]{1,0:T(8,128)S(1)}, u32[]{:S(2)}, u32[]{:S(2)}) collective-permute-start(f32[8,128]{1,0:T(8,128)S(1)} %stack.69.e0), channel_id=1, source_target_pairs={{0,2},{1,3},{2,0},{3,1},{4,6},{5,7},{6,4},{7,5},{8,10},{9,11},{10,... | collective-permute-start | bytes 12296 | tf_op jit(solution)/shard_map/ppermute | solution.py:973
  19.4 2.8 collective-permute-done.3.source.w2
  25.9 4.5 %collective-permute-done.6.w3 = bf16[1152,128]{1,0:T(8,128)(2,1)S(1)} collective-permute-done((bf16[1152,128]{1,0:T(8,128)(2,1)S(1)}, bf16[1152,128]{1,0:T(8,128)(2,1)S(1)}, u32[]{:S(2)}, u32[]{:S(2)}) %collective-permute-start.6) | collective-permute-done | bytes 294944 | tf_op jit(solution)/shard_map/ppermute | solution.py:973
  34.4 5.2 %collective-permute-done.12.i3 = bf16[1024,128]{1,0:T(8,128)(2,1)S(1)} collective-permute-done((bf16[1024,128]{1,0:T(8,128)(2,1)S(1)}, bf16[1024,128]{1,0:T(8,128)(2,1)S(1)}, u32[]{:S(2)}, u32[]{:S(2)}) %collective-permute-start.12) | collective-permute-done | bytes 262176 | tf_op jit(solution)/shard_map/ppermute | solution.py:973
  40.9 5.3 %collective-permute-done.11.i2 = bf16[1024,128]{1,0:T(8,128)(2,1)S(1)} collective-permute-done((bf16[1024,128]{1,0:T(8,128)(2,1)S(1)}, bf16[1024,128]{1,0:T(8,128)(2,1)S(1)}, u32[]{:S(2)}, u32[]{:S(2)}) %collective-permute-start.11) | collective-permute-done | bytes 262176 | tf_op jit(solution)/shard_map/ppermute | solution.py:973
  47.6 9.9 %first.1 = (bf16[4,1024,128]{2,1,0:T(8,128)(2,1)S(1)}, f32[4,8,128]{2,1,0:T(8,128)S(1)}, bf16[4,128,1024]{2,1,0:T(8,128)(2,1)S(1)}, f32[4,1024,128]{2,1,0:T(8,128)S(1)}) custom-call(s32[6]{0:T(128)S(1)} %stack.61.meta, bf16[1024,128]{1,0:T(8,128)(2,1)S(1)} %get-tuple-element.532.i0, bf16[1024,128]{1,0:T(8,128)(2,1)S(1)} %collective-permute-done.5.i1, ...), custom_call_target="tpu_custom_call" | custom-call | tf_op jit(solution)/shard_map/first/pallas_call | solution.py:1115
  57.5 4.1 %collective-permute-done.16.source.w2 = bf16[2304,128]{1,0:T(8,128)(2,1)S(1)} collective-permute-done((bf16[2304,128]{1,0:T(8,128)(2,1)S(1)}, bf16[2304,128]{1,0:T(8,128)(2,1)S(1)}, u32[]{:S(2)}, u32[]{:S(2)}) %collective-permute-start.16) | collective-permute-done | bytes 589856 | tf_op jit(solution)/shard_map/ppermute | solution.py:973
  64.6 5.3 %collective-permute-done.20.w3 = bf16[1152,128]{1,0:T(8,128)(2,1)S(1)} collective-permute-done((bf16[1152,128]{1,0:T(8,128)(2,1)S(1)}, bf16[1152,128]{1,0:T(8,128)(2,1)S(1)}, u32[]{:S(2)}, u32[]{:S(2)}) %collective-permute-start.20) | collective-permute-done | bytes 294944 | tf_op jit(solution)/shard_map/ppermute | solution.py:973
  71.0 4.7 %collective-permute-done.19.p2 = bf16[3,512,128]{2,1,0:T(8,128)(2,1)S(1)} collective-permute-done((bf16[3,512,128]{2,1,0:T(8,128)(2,1)S(1)}, bf16[3,512,128]{2,1,0:T(8,128)(2,1)S(1)}, u32[]{:S(2)}, u32[]{:S(2)}) %collective-permute-start.19) | collective-permute-done | bytes 393248 | tf_op jit(solution)/shard_map/ppermute | solution.py:973
  78.4 4.2 %collective-permute-done.32.w2 = bf16[128,512]{1,0:T(8,128)(2,1)S(1)} collective-permute-done((bf16[128,512]{1,0:T(8,128)(2,1)S(1)}, bf16[128,512]{1,0:T(8,128)(2,1)S(1)}, u32[]{:S(2)}, u32[]{:S(2)}) %collective-permute-start.32) | collective-permute-done | bytes 131104 | tf_op jit(solution)/shard_map/ppermute | solution.py:973
  83.3 16.3 %second.1 = (f32[4,1024,128]{2,1,0:T(8,128)S(1)}, bf16[4,128,1024]{2,1,0:T(8,128)(2,1)S(1)}, bf16[4,128,1024]{2,1,0:T(8,128)(2,1)S(1)}, bf16[4,1024,384]{2,1,0:T(8,128)(2,1)S(1)}, f32[4,24,128]{2,1,0:T(8,128)S(1)}) custom-call(s32[6]{0:T(128)S(1)} %stack.61.meta, f32[4,1024,128]{2,1,0:T(8,128)S(1)} %get-tuple-element.324.inner, ...), custom_call_target="tpu_custom_call" | custom-call | tf_op jit(solution)/shard_map/second/pallas_call | solution.py:1132
  102.0 2.7 collective-permute-start.38
  104.7 41.1 %attention.1 = (bf16[1024,128]{1,0:T(8,128)(2,1)S(1)}, bf16[1024,128]{1,0:T(8,128)(2,1)S(1)}, bf16[2,1024,128]{2,1,0:T(8,128)(2,1)S(1)}, bf16[4,1024,128]{2,1,0:...) custom-call(s32[6]{0:T(128)S(1)} %stack.61.meta, ...), custom_call_target="tpu_custom_call" | custom-call | tf_op jit(solution)/shard_map/attention/pallas_call | solution.py:1158
  145.8 5.7 %attention_grad.1 = (bf16[2,4,512,128]{3,2,1,0:T(8,128)(2,1)S(1)}, bf16[2,4,512,128]{3,2,1,0:T(8,128)(2,1)S(1)}) custom-call(s32[6]{0:T(128)S(1)} %stack.61.meta, bf16[4,1024,384]{2,1,0:T(8,128)(2,1)S(1)} %get-tuple-element.374.dqkv, bf16[4,1024,128]{2,1,0:T(8,128)(2,1)S(1)} %get-tuple-element.365.mixed, ...), custom_call_target="tpu_custom_call" | custom-call | tf_op jit(solution)/shard_map/attention_grad/pallas_call | solution.py:1214
  152.2 6.5 %back_attention.1 = (f32[4,1024,128]{2,1,0:T(8,128)S(1)}, bf16[3,4,1088,128]{3,2,1,0:T(8,128)(2,1)S(1)}, f32[4,32,128]{2,1,0:T(8,128)S(1)}, bf16[1024,128]{1,0:T...) custom-call(s32[6]{0:T(128)S(1)} %stack.61.meta, ...), custom_call_target="tpu_custom_call" | custom-call | tf_op jit(solution)/shard_map/back_attention/pallas_call | solution.py:1227
  162.7 11.4 %back_second.1 = (bf16[3,4,1088,128]{3,2,1,0:T(8,128)(2,1)S(1)}, f32[4,32,128]{2,1,0:T(8,128)S(1)}, bf16[1024,128]{1,0:T(8,128)(2,1)S(1)}, bf16[1024,128]{1,0:T(...) custom-call(s32[6]{0:T(128)S(1)} %stack.61.meta, ...), custom_call_target="tpu_custom_call" | custom-call | tf_op jit(solution)/shard_map/back_second/pallas_call | solution.py:1240
  176.9 4.8 %weight_send.2 = (bf16[9,256,128]{2,1,0:T(8,128)(2,1)S(1)}, bf16[3,4,1088,128]{3,2,1,0:T(8,128)(2,1)S(1)}) custom-call(s32[6]{0:T(128)S(1)} %stack.61.meta, bf16[4,128,1024]{2,1,0:T(8,128)(2,1)S(1)} %get-tuple-element.363.u0, bf16[4,128,1024]{2,1,0:T(8,128)(2,1)S(1)} %collective-permute-done.36.u1, bf16[4,128,1024]{2,1,0:T(8,128)(2,1)S(1)} %collective-permute-done.34.u2, ...), custom_call_target="tpu_custom_call" | custom-call | tf_op jit(solution)/shard_map/weight_send/pallas_call | solution.py:1180
  185.4 4.2 %weight_own.2.refs_0_ = f32[9,256,128]{2,1,0:T(8,128)S(1)} custom-call(s32[6]{0:T(128)S(1)} %stack.61.meta, bf16[4,128,1024]{2,1,0:T(8,128)(2,1)S(1)} %get-tuple-element.363.u0, bf16[4,128,1024]{2,1,0:T(8,128)(2,1)S(1)} %collective-permute-done.36.u1, bf16[4,128,1024]{2,1,0:T(8,128)(2,1)S(1)} %collective-permute-done.34.u2, ...), custom_call_target="tpu_custom_call" | custom-call | tf_op jit(solution)/shard_map/weight_own/pallas_call | solution.py:1190
  189.7 4.7 %collective-permute-done.47.got = bf16[8,64,128]{2,1,0:T(8,128)(2,1)S(1)} collective-permute-done((bf16[8,64,128]{2,1,0:T(8,128)(2,1)S(1)}, bf16[8,64,128]{2,1,0:T(8,128)(2,1)S(1)}, u32[]{:S(2)}, u32[]{:S(2)}) %collective-permute-start.47) | collective-permute-done | bytes 131104 | tf_op jit(solution)/shard_map/ppermute | solution.py:973
  196.1 7.3 %back_conv.1.grad_in = f32[4,1024,128]{2,1,0:T(8,128)S(1)} custom-call(s32[6]{0:T(128)S(1)} %stack.61.meta, bf16[3,4,1088,128]{3,2,1,0:T(8,128)(2,1)S(1)} %get-tuple-element.427.grad_field, bf16[4608,128]{1,0:T(8,128)(2,1)S(1)} %bitcast.104, bf16[4608,128]{1,0:T(8,128)(2,1)S(1)} %collective-permute-done.4.w1, ...), custom_call_target="tpu_custom_call" | custom-call | tf_op jit(solution)/shard_map/back_conv/pallas_call | solution.py:1271
  203.4 4.8 %weight_send.3 = (bf16[9,256,128]{2,1,0:T(8,128)(2,1)S(1)}, bf16[3,4,1088,128]{3,2,1,0:T(8,128)(2,1)S(1)}) custom-call(s32[6]{0:T(128)S(1)} %stack.61.meta, bf16[4,128,1024]{2,1,0:T(8,128)(2,1)S(1)} %get-tuple-element.369.u0, bf16[4,128,1024]{2,1,0:T(8,128)(2,1)S(1)} %collective-permute-done.37.u1, bf16[4,128,1024]{2,1,0:T(8,128)(2,1)S(1)} %collective-permute-done.35.u2, ...), custom_call_target="tpu_custom_call" | custom-call | tf_op jit(solution)/shard_map/weight_send/pallas_call | solution.py:1180
  211.6 4.2 %weight_own.3.refs_0_ = f32[9,256,128]{2,1,0:T(8,128)S(1)} custom-call(s32[6]{0:T(128)S(1)} %stack.61.meta, bf16[4,128,1024]{2,1,0:T(8,128)(2,1)S(1)} %get-tuple-element.369.u0, bf16[4,128,1024]{2,1,0:T(8,128)(2,1)S(1)} %collective-permute-done.37.u1, bf16[4,128,1024]{2,1,0:T(8,128)(2,1)S(1)} %collective-permute-done.35.u2, ...), custom_call_target="tpu_custom_call" | custom-call | tf_op jit(solution)/shard_map/weight_own/pallas_call | solution.py:1190
  217.9 2.2 collective-permute-done.53.refs_1_
  222.5 4.3 %back_first.1 = (bf16[1056,128]{1,0:T(8,128)(2,1)S(1)}, bf16[1056,128]{1,0:T(8,128)(2,1)S(1)}, bf16[2,1056,128]{2,1,0:T(8,128)(2,1)S(1)}) custom-call(s32[6]{0:T(128)S(1)} %stack.61.meta, f32[4,1024,128]{2,1,0:T(8,128)S(1)} %back_conv.1.grad_in, bf16[4,1024,128]{2,1,0:T(8,128)(2,1)S(1)} %get-tuple-element.325.image, ...), custom_call_target="tpu_custom_call" | custom-call | tf_op jit(solution)/shard_map/back_first/pallas_call | solution.py:1295
  231.4 11.9 %collective-permute-done.57.refs_1_ = bf16[4,128,128]{2,1,0:T(8,128)(2,1)S(1)} collective-permute-done((bf16[4,128,128]{2,1,0:T(8,128)(2,1)S(1)}, bf16[4,128,128]{2,1,0:T(8,128)(2,1)S(1)}, u32[]{:S(2)}, u32[]{:S(2)}) %collective-permute-start.57) | collective-permute-done | bytes 131104 | tf_op jit(solution)/shard_map/ppermute | solution.py:973
  247.3 4.0 %collective-permute-done.63.other = bf16[4,256,128]{2,1,0:T(8,128)(2,1)S(1)} collective-permute-done((bf16[4,256,128]{2,1,0:T(8,128)(2,1)S(1)}, bf16[4,256,128]{2,1,0:T(8,128)(2,1)S(1)}, u32[]{:S(2)}, u32[]{:S(2)}) %collective-permute-start.63) | collective-permute-done | bytes 262176 | tf_op jit(solution)/shard_map/ppermute | solution.py:973
  251.2 2.2 collective-permute-done.62.refs_1_
  258.9 3.3 %collective-permute-done.64.refs_1_ = bf16[9,64,128]{2,1,0:T(8,128)(2,1)S(1)} collective-permute-done((bf16[9,64,128]{2,1,0:T(8,128)(2,1)S(1)}, bf16[9,64,128]{2,1,0:T(8,128)(2,1)S(1)}, u32[]{:S(2)}, u32[]{:S(2)}) %collective-permute-start.64) | collective-permute-done | bytes 147488 | tf_op jit(solution)/shard_map/ppermute | solution.py:973
  263.4 8.9 %collective-permute-done.66.refs_1_ = bf16[9,128,128]{2,1,0:T(8,128)(2,1)S(1)} collective-permute-done((bf16[9,128,128]{2,1,0:T(8,128)(2,1)S(1)}, bf16[9,128,128]{2,1,0:T(8,128)(2,1)S(1)}, u32[]{:S(2)}, u32[]{:S(2)}) %collective-permute-start.66) | collective-permute-done | bytes 294944 | tf_op jit(solution)/shard_map/ppermute | solution.py:973
  278.0 3.2 %collective-permute-done.71.refs_1_ = bf16[8,32,128]{2,1,0:T(8,128)(2,1)S(1)} collective-permute-done((bf16[8,32,128]{2,1,0:T(8,128)(2,1)S(1)}, bf16[8,32,128]{2,1,0:T(8,128)(2,1)S(1)}, u32[]{:S(2)}, u32[]{:S(2)}) %collective-permute-start.71) | collective-permute-done | bytes 65568 | tf_op jit(solution)/shard_map/ppermute | solution.py:973
  284.1 6.5 %collective-permute-done.74.small1 = bf16[16,32,128]{2,1,0:T(8,128)(2,1)S(1)} collective-permute-done((bf16[16,32,128]{2,1,0:T(8,128)(2,1)S(1)}, bf16[16,32,128]{2,1,0:T(8,128)(2,1)S(1)}, u32[]{:S(2)}, u32[]{:S(2)}) %collective-permute-start.74) | collective-permute-done | bytes 131104 | tf_op jit(solution)/shard_map/ppermute | solution.py:973
  290.6 5.4 %factor_grads.1 = (f32[2048,2,128]{2,1,0:T(2,128)}, f32[2048,2,128]{2,1,0:T(2,128)}, f32[32,128]{1,0:T(8,128)S(1)}) custom-call(s32[6]{0:T(128)S(1)} %stack.61.meta, f32[8,128]{1,0:T(8,128)S(1)} %scale.1, bf16[4,4,8,2048]{3,2,1,0:T(8,128)(2,1)S(1)} %stack.72.factors0, bf16[4,4,8,2048]{3,2,1,0:T(8,128)(2,1)S(1)} %collective-permute-done.38.factors1, ...), custom_call_target="tpu_custom_call" | custom-call | tf_op jit(solution)/shard_map/factor_grads/pallas_call | solution.py:1345
  (202 shorter events, 83.6 us)
Async XLA Ops:
  1.5 15.0 %collective-permute-start.1 = (f32[8,128]{1,0:T(8,128)S(1)}, f32[8,128]{1,0:T(8,128)S(1)}, u32[]{:S(2)}, u32[]{:S(2)}) collective-permute-start(f32[8,128]{1,0:T(8,128)S(1)} %stack.69.e0), channel_id=1, source_target_pairs={{0,2},{1,3},{2,0},{3,1},{4,6},{5,7},{6,4},{7,5},{8,10},{9,11},{10,... | collective-permute-start | bytes 12296 | tf_op jit(solution)/shard_map/ppermute | solution.py:973
  5.3 16.9 %collective-permute-start.4 = (bf16[4608,128]{1,0:T(8,128)(2,1)}, bf16[4608,128]{1,0:T(8,128)(2,1)S(1)}, u32[]{:S(2)}, u32[]{:S(2)}) collective-permute-start(bf16[4608,128]{1,0:T(8,128)(2,1)} %bitcast.101), channel_id=1, source_target_pairs={{0,1},{1,0},{2,3},{3,2},{4,5},{5,4},{6,7},{7,6},{8,9},{9,8},{10,11... | collective-permute-start | bytes 3538952 | tf_op jit(solution)/shard_map/ppermute | solution.py:973
  6.9 15.3 %collective-permute-start.3 = (bf16[2304,128]{1,0:T(8,128)(2,1)S(1)}, bf16[2304,128]{1,0:T(8,128)(2,1)S(1)}, u32[]{:S(2)}, u32[]{:S(2)}) collective-permute-start(bf16[2304,128]{1,0:T(8,128)(2,1)S(1)} %constant_dynamic-slice_fusion.1), channel_id=1, source_target_pairs={{0,2},{1,3},{2,0},{3,1},{4,6},{5,7},{6,4},{7,5},{8,10},{9,11},{10,... | collective-permute-start | bytes 1769480 | tf_op jit(solution)/shard_map/ppermute | solution.py:973
  25.4 32.1 %collective-permute-start.17 = (bf16[4608,128]{1,0:T(8,128)(2,1)S(1)}, bf16[4608,128]{1,0:T(8,128)(2,1)S(1)}, u32[]{:S(2)}, u32[]{:S(2)}) collective-permute-start(bf16[4608,128]{1,0:T(8,128)(2,1)S(1)} %bitcast.98), channel_id=1, source_target_pairs={{0,1},{1,0},{2,3},{3,2},{4,5},{5,4},{6,7},{7,6},{8,9},{9,8},{10,11... | collective-permute-start | bytes 3538952 | tf_op jit(solution)/shard_map/ppermute | solution.py:973
  32.3 13.9 %collective-permute-start.11 = (bf16[1024,128]{1,0:T(8,128)(2,1)S(1)}, bf16[1024,128]{1,0:T(8,128)(2,1)S(1)}, u32[]{:S(2)}, u32[]{:S(2)}) collective-permute-start(bf16[1024,128]{1,0:T(8,128)(2,1)S(1)} %get-tuple-element.530), channel_id=1, source_target_pairs={{0,2},{1,3},{2,0},{3,1},{4,6},{5,7},{6,4},{7,5},{8,10},{9,11},{10,... | collective-permute-start | bytes 786440 | tf_op jit(solution)/shard_map/ppermute | solution.py:973
  46.3 15.3 %collective-permute-start.16 = (bf16[2304,128]{1,0:T(8,128)(2,1)S(1)}, bf16[2304,128]{1,0:T(8,128)(2,1)S(1)}, u32[]{:S(2)}, u32[]{:S(2)}) collective-permute-start(bf16[2304,128]{1,0:T(8,128)(2,1)S(1)} %constant_dynamic-slice_fusion), channel_id=1, source_target_pairs={{0,2},{1,3},{2,0},{3,1},{4,6},{5,7},{6,4},{7,5},{8,10},{9,11},{10,... | collective-permute-start | bytes 1769480 | tf_op jit(solution)/shard_map/ppermute | solution.py:973
  76.7 22.8 %collective-permute-start.28 = (bf16[1024,128]{1,0:T(8,128)(2,1)S(1)}, bf16[1024,128]{1,0:T(8,128)(2,1)S(1)}, u32[]{:S(2)}, u32[]{:S(2)}) collective-permute-start(bf16[1024,128]{1,0:T(8,128)(2,1)S(1)} %get-tuple-element.348), channel_id=1, source_target_pairs={{0,1},{1,0},{2,3},{3,2},{4,5},{5,4},{6,7},{7,6},{8,9},{9,8},{10,11... | collective-permute-start | bytes 786440 | tf_op jit(solution)/shard_map/ppermute | solution.py:973
  77.6 21.9 %collective-permute-start.29 = (bf16[1024,128]{1,0:T(8,128)(2,1)S(1)}, bf16[1024,128]{1,0:T(8,128)(2,1)S(1)}, u32[]{:S(2)}, u32[]{:S(2)}) collective-permute-start(bf16[1024,128]{1,0:T(8,128)(2,1)S(1)} %get-tuple-element.349), channel_id=1, source_target_pairs={{0,2},{1,3},{2,0},{3,1},{4,6},{5,7},{6,4},{7,5},{8,10},{9,11},{10,... | collective-permute-start | bytes 786440 | tf_op jit(solution)/shard_map/ppermute | solution.py:973
  82.6 17.0 %collective-permute-start.30 = (bf16[1024,128]{1,0:T(8,128)(2,1)S(1)}, bf16[1024,128]{1,0:T(8,128)(2,1)S(1)}, u32[]{:S(2)}, u32[]{:S(2)}) collective-permute-start(bf16[1024,128]{1,0:T(8,128)(2,1)S(1)} %get-tuple-element.350), channel_id=1, source_target_pairs={{0,3},{1,2},{2,1},{3,0},{4,7},{5,6},{6,5},{7,4},{8,11},{9,10},{10,... | collective-permute-start | bytes 786440 | tf_op jit(solution)/shard_map/ppermute | solution.py:973
  82.6 17.0 %collective-permute-start.27 = (bf16[2,4,8,2048]{3,2,1,0:T(8,128)(2,1)S(1)}, bf16[2,4,8,2048]{3,2,1,0:T(8,128)(2,1)S(1)}, u32[]{:S(2)}, u32[]{:S(2)}) collective-permute-start(bf16[2,4,8,2048]{3,2,1,0:T(8,128)(2,1)S(1)} %stack.71.refs_0_), channel_id=1, source_target_pairs={{0,8},{4,12},{8,0},{12,4},{16,24},{20,28},{24,16},{28,20},{1,9},{5... | collective-permute-start | bytes 786440 | tf_op jit(solution)/shard_map/ppermute | solution.py:973
  83.1 16.5 %collective-permute-start.33 = (bf16[128,512]{1,0:T(8,128)(2,1)S(1)}, bf16[128,512]{1,0:T(8,128)(2,1)S(1)}, u32[]{:S(2)}, u32[]{:S(2)}) collective-permute-start(bf16[128,512]{1,0:T(8,128)(2,1)S(1)} %collective-permute-done.32.w2), channel_id=1, source_target_pairs={{0,1},{1,0},{2,3},{3,2},{4,5},{5,4},{6,7},{7,6},{8,9},{9,8},{10,11... | collective-permute-start | bytes 393224 | tf_op jit(solution)/shard_map/ppermute | solution.py:973
  99.6 51.9 %collective-permute-start.37 = (bf16[4,128,1024]{2,1,0:T(8,128)(2,1)S(1)}, bf16[4,128,1024]{2,1,0:T(8,128)(2,1)S(1)}, u32[]{:S(2)}, u32[]{:S(2)}) collective-permute-start(bf16[4,128,1024]{2,1,0:T(8,128)(2,1)S(1)} %get-tuple-element.369.u0), channel_id=1, source_target_pairs={{0,1},{1,0},{2,3},{3,2},{4,5},{5,4},{6,7},{7,6},{8,9},{9,8},{10,11... | collective-permute-start | bytes 3145736 | tf_op jit(solution)/shard_map/ppermute | solution.py:973
  100.0 51.6 %collective-permute-start.35 = (bf16[4,128,1024]{2,1,0:T(8,128)(2,1)S(1)}, bf16[4,128,1024]{2,1,0:T(8,128)(2,1)S(1)}, u32[]{:S(2)}, u32[]{:S(2)}) collective-permute-start(bf16[4,128,1024]{2,1,0:T(8,128)(2,1)S(1)} %get-tuple-element.369.u0), channel_id=1, source_target_pairs={{0,2},{1,3},{2,0},{3,1},{4,6},{5,7},{6,4},{7,5},{8,10},{9,11},{10,... | collective-permute-start | bytes 3145736 | tf_op jit(solution)/shard_map/ppermute | solution.py:973
  101.4 50.2 %collective-permute-start.36 = (bf16[4,128,1024]{2,1,0:T(8,128)(2,1)S(1)}, bf16[4,128,1024]{2,1,0:T(8,128)(2,1)S(1)}, u32[]{:S(2)}, u32[]{:S(2)}) collective-permute-start(bf16[4,128,1024]{2,1,0:T(8,128)(2,1)S(1)} %get-tuple-element.363.u0), channel_id=1, source_target_pairs={{0,1},{1,0},{2,3},{3,2},{4,5},{5,4},{6,7},{7,6},{8,9},{9,8},{10,11... | collective-permute-start | bytes 3145736 | tf_op jit(solution)/shard_map/ppermute | solution.py:973
  101.6 50.0 %collective-permute-start.34 = (bf16[4,128,1024]{2,1,0:T(8,128)(2,1)S(1)}, bf16[4,128,1024]{2,1,0:T(8,128)(2,1)S(1)}, u32[]{:S(2)}, u32[]{:S(2)}) collective-permute-start(bf16[4,128,1024]{2,1,0:T(8,128)(2,1)S(1)} %get-tuple-element.363.u0), channel_id=1, source_target_pairs={{0,2},{1,3},{2,0},{3,1},{4,6},{5,7},{6,4},{7,5},{8,10},{9,11},{10,... | collective-permute-start | bytes 3145736 | tf_op jit(solution)/shard_map/ppermute | solution.py:973
  102.0 49.5 %collective-permute-start.38 = (bf16[4,4,8,2048]{3,2,1,0:T(8,128)(2,1)S(1)}, bf16[4,4,8,2048]{3,2,1,0:T(8,128)(2,1)S(1)}, u32[]{:S(2)}, u32[]{:S(2)}) collective-permute-start(bf16[4,4,8,2048]{3,2,1,0:T(8,128)(2,1)S(1)} %stack.72.factors0), channel_id=1, source_target_pairs={{0,16},{4,20},{8,24},{12,28},{16,0},{20,4},{24,8},{28,12},{1,17},{... | collective-permute-start | bytes 1572872 | tf_op jit(solution)/shard_map/ppermute | solution.py:973
  159.5 15.1 %collective-permute-start.45 = (bf16[8,256,128]{2,1,0:T(8,128)(2,1)S(1)}, bf16[8,256,128]{2,1,0:T(8,128)(2,1)S(1)}, u32[]{:S(2)}, u32[]{:S(2)}) collective-permute-start(bf16[8,256,128]{2,1,0:T(8,128)(2,1)S(1)} %get-tuple-element.400), channel_id=1, source_target_pairs={{0,4},{4,0},{8,12},{12,8},{16,20},{20,16},{24,28},{28,24},{1,5},{5... | collective-permute-start | bytes 1572872 | tf_op jit(solution)/shard_map/ppermute | solution.py:973
  160.8 13.3 %collective-permute-start.42 = (bf16[1024,128]{1,0:T(8,128)(2,1)S(1)}, bf16[1024,128]{1,0:T(8,128)(2,1)S(1)}, u32[]{:S(2)}, u32[]{:S(2)}) collective-permute-start(bf16[1024,128]{1,0:T(8,128)(2,1)S(1)} %get-tuple-element.396), channel_id=1, source_target_pairs={{0,1},{1,0},{2,3},{3,2},{4,5},{5,4},{6,7},{7,6},{8,9},{9,8},{10,11... | collective-permute-start | bytes 786440 | tf_op jit(solution)/shard_map/ppermute | solution.py:973
  161.0 13.1 %collective-permute-start.43 = (bf16[1024,128]{1,0:T(8,128)(2,1)S(1)}, bf16[1024,128]{1,0:T(8,128)(2,1)S(1)}, u32[]{:S(2)}, u32[]{:S(2)}) collective-permute-start(bf16[1024,128]{1,0:T(8,128)(2,1)S(1)} %get-tuple-element.397), channel_id=1, source_target_pairs={{0,2},{1,3},{2,0},{3,1},{4,6},{5,7},{6,4},{7,5},{8,10},{9,11},{10,... | collective-permute-start | bytes 786440 | tf_op jit(solution)/shard_map/ppermute | solution.py:973
  181.7 27.8 %collective-permute-start.52 = (bf16[9,256,128]{2,1,0:T(8,128)(2,1)S(1)}, bf16[9,256,128]{2,1,0:T(8,128)(2,1)S(1)}, u32[]{:S(2)}, u32[]{:S(2)}) collective-permute-start(bf16[9,256,128]{2,1,0:T(8,128)(2,1)S(1)} %get-tuple-element.449), channel_id=1, source_target_pairs={{0,4},{4,0},{8,12},{12,8},{16,20},{20,16},{24,28},{28,24},{1,5},{5... | collective-permute-start | bytes 1769480 | tf_op jit(solution)/shard_map/ppermute | solution.py:973
  182.6 20.8 %collective-permute-start.48 = (bf16[1024,128]{1,0:T(8,128)(2,1)S(1)}, bf16[1024,128]{1,0:T(8,128)(2,1)S(1)}, u32[]{:S(2)}, u32[]{:S(2)}) collective-permute-start(bf16[1024,128]{1,0:T(8,128)(2,1)S(1)} %get-tuple-element.429), channel_id=1, source_target_pairs={{0,1},{1,0},{2,3},{3,2},{4,5},{5,4},{6,7},{7,6},{8,9},{9,8},{10,11... | collective-permute-start | bytes 786440 | tf_op jit(solution)/shard_map/ppermute | solution.py:973
  182.6 20.8 %collective-permute-start.49 = (bf16[1024,128]{1,0:T(8,128)(2,1)S(1)}, bf16[1024,128]{1,0:T(8,128)(2,1)S(1)}, u32[]{:S(2)}, u32[]{:S(2)}) collective-permute-start(bf16[1024,128]{1,0:T(8,128)(2,1)S(1)} %get-tuple-element.430), channel_id=1, source_target_pairs={{0,2},{1,3},{2,0},{3,1},{4,6},{5,7},{6,4},{7,5},{8,10},{9,11},{10,... | collective-permute-start | bytes 786440 | tf_op jit(solution)/shard_map/ppermute | solution.py:973
  184.2 19.2 %collective-permute-start.50 = (bf16[1024,128]{1,0:T(8,128)(2,1)S(1)}, bf16[1024,128]{1,0:T(8,128)(2,1)S(1)}, u32[]{:S(2)}, u32[]{:S(2)}) collective-permute-start(bf16[1024,128]{1,0:T(8,128)(2,1)S(1)} %get-tuple-element.431), channel_id=1, source_target_pairs={{0,3},{1,2},{2,1},{3,0},{4,7},{5,6},{6,5},{7,4},{8,11},{9,10},{10,... | collective-permute-start | bytes 786440 | tf_op jit(solution)/shard_map/ppermute | solution.py:973
  208.2 20.1 %collective-permute-start.56 = (bf16[9,256,128]{2,1,0:T(8,128)(2,1)S(1)}, bf16[9,256,128]{2,1,0:T(8,128)(2,1)S(1)}, u32[]{:S(2)}, u32[]{:S(2)}) collective-permute-start(bf16[9,256,128]{2,1,0:T(8,128)(2,1)S(1)} %get-tuple-element.472), channel_id=1, source_target_pairs={{0,4},{4,0},{8,12},{12,8},{16,20},{20,16},{24,28},{28,24},{1,5},{5... | collective-permute-start | bytes 1769480 | tf_op jit(solution)/shard_map/ppermute | solution.py:973
  210.3 33.0 %collective-permute-start.60 = (bf16[2,1024,128]{2,1,0:T(8,128)(2,1)S(1)}, bf16[2,1024,128]{2,1,0:T(8,128)(2,1)S(1)}, u32[]{:S(2)}, u32[]{:S(2)}) collective-permute-start(bf16[2,1024,128]{2,1,0:T(8,128)(2,1)S(1)} %get-tuple-element.485), channel_id=1, source_target_pairs={{0,2},{1,3},{2,0},{3,1},{4,6},{5,7},{6,4},{7,5},{8,10},{9,11},{10,... | collective-permute-start | bytes 1572872 | tf_op jit(solution)/shard_map/ppermute | solution.py:973
  229.0 14.3 %collective-permute-start.59 = (bf16[9,128,128]{2,1,0:T(8,128)(2,1)S(1)}, bf16[9,128,128]{2,1,0:T(8,128)(2,1)S(1)}, u32[]{:S(2)}, u32[]{:S(2)}) collective-permute-start(bf16[9,128,128]{2,1,0:T(8,128)(2,1)S(1)} %get-tuple-element.483), channel_id=1, source_target_pairs={{0,8},{4,12},{8,0},{12,4},{16,24},{20,28},{24,16},{28,20},{1,9},{5... | collective-permute-start | bytes 884744 | tf_op jit(solution)/shard_map/ppermute | solution.py:973
  229.1 14.2 %collective-permute-start.57 = (bf16[4,128,128]{2,1,0:T(8,128)(2,1)S(1)}, bf16[4,128,128]{2,1,0:T(8,128)(2,1)S(1)}, u32[]{:S(2)}, u32[]{:S(2)}) collective-permute-start(bf16[4,128,128]{2,1,0:T(8,128)(2,1)S(1)} %join.6.refs_0_), channel_id=1, source_target_pairs={{0,8},{4,12},{8,0},{12,4},{16,24},{20,28},{24,16},{28,20},{1,9},{5... | collective-permute-start | bytes 393224 | tf_op jit(solution)/shard_map/ppermute | solution.py:973
  243.3 19.5 %collective-permute-start.65 = (bf16[2,1056,128]{2,1,0:T(8,128)(2,1)S(1)}, bf16[2,1056,128]{2,1,0:T(8,128)(2,1)S(1)}, u32[]{:S(2)}, u32[]{:S(2)}) collective-permute-start(bf16[2,1056,128]{2,1,0:T(8,128)(2,1)S(1)} %get-tuple-element.506), channel_id=1, source_target_pairs={{0,2},{1,3},{2,0},{3,1},{4,6},{5,7},{6,4},{7,5},{8,10},{9,11},{10,... | collective-permute-start | bytes 1622024 | tf_op jit(solution)/shard_map/ppermute | solution.py:973
  256.4 16.5 %collective-permute-start.69 = (bf16[9,256,128]{2,1,0:T(8,128)(2,1)S(1)}, bf16[9,256,128]{2,1,0:T(8,128)(2,1)S(1)}, u32[]{:S(2)}, u32[]{:S(2)}) collective-permute-start(bf16[9,256,128]{2,1,0:T(8,128)(2,1)S(1)} %join.11.mine), channel_id=1, source_target_pairs={{0,4},{4,0},{8,12},{12,8},{16,20},{20,16},{24,28},{28,24},{1,5},{5... | collective-permute-start | bytes 1769480 | tf_op jit(solution)/shard_map/ppermute | solution.py:973
  277.2 19.3 %collective-permute-start.75 = (bf16[9,256,128]{2,1,0:T(8,128)(2,1)S(1)}, bf16[9,256,128]{2,1,0:T(8,128)(2,1)S(1)}, u32[]{:S(2)}, u32[]{:S(2)}) collective-permute-start(bf16[9,256,128]{2,1,0:T(8,128)(2,1)S(1)} %join.10.mine), channel_id=1, source_target_pairs={{0,4},{4,0},{8,12},{12,8},{16,20},{20,16},{24,28},{28,24},{1,5},{5... | collective-permute-start | bytes 1769480 | tf_op jit(solution)/shard_map/ppermute | solution.py:973
  281.2 17.4 %collective-permute-start.73 = (bf16[2,1024,128]{2,1,0:T(8,128)(2,1)S(1)}, bf16[2,1024,128]{2,1,0:T(8,128)(2,1)S(1)}, u32[]{:S(2)}, u32[]{:S(2)}) collective-permute-start(bf16[2,1024,128]{2,1,0:T(8,128)(2,1)S(1)} %collective-permute-done.60.far), channel_id=1, source_target_pairs={{0,1},{1,0},{2,3},{3,2},{4,5},{5,4},{6,7},{7,6},{8,9},{9,8},{10,11... | collective-permute-start | bytes 1572872 | tf_op jit(solution)/shard_map/ppermute | solution.py:973
  282.3 16.3 %collective-permute-start.72 = (bf16[1024,128]{1,0:T(8,128)(2,1)S(1)}, bf16[1024,128]{1,0:T(8,128)(2,1)S(1)}, u32[]{:S(2)}, u32[]{:S(2)}) collective-permute-start(bf16[1024,128]{1,0:T(8,128)(2,1)S(1)} %get-tuple-element.519), channel_id=1, source_target_pairs={{0,1},{1,0},{2,3},{3,2},{4,5},{5,4},{6,7},{7,6},{8,9},{9,8},{10,11... | collective-permute-start | bytes 786440 | tf_op jit(solution)/shard_map/ppermute | solution.py:973
  (51 other events, 443.7 us)

commit v4 on v3

--- a/solution.py
+++ b/solution.py
@@ -20,11 +20,11 @@
 F32 = jnp.float32
 BF16 = jnp.bfloat16
 NEG = -1e30
-
-E_G1, E_B1, E_G2, E_B2, E_CB2, E_G3, E_B3 = range(7)
-E_ROWS = 8
-M_SCALE, M_SHIFT = range(2)
-M_KEY, M_VALUE, M_ROWS = 8, 16, 24
+QKV_ROW = 9 * C
+PROJ_ROW = QKV_ROW + 3 * C
+
+E_G1, E_B1, E_G2, E_B2, E_CB2, E_G3, E_B3, M_SCALE, M_SHIFT = range(9)
+M_KEY, M_VALUE, E_ROWS = 16, 24, 32
 S_G3, S_B3, S_CB2, S_G2, S_B2, S_SCALE, S_SHIFT = range(7)
 S_KEY, S_VALUE, S_G1, S_B1, S_ROWS = 8, 12, 16, 17, 32
 MIB = 1 << 20
@@ -170,7 +170,7 @@
             ],
             axis=1,
         )
-        right = jnp.concatenate([weight[s] for s in range(4)], axis=1)
+        right = jnp.concatenate([weight[s, 0 : 9 * C, :] for s in range(4)], axis=1)
         write(start, jnp.dot(left, right, preferred_element_type=F32))
         return carry
 
@@ -214,16 +214,31 @@
     return grad_out * gate * (1.0 + before * (1.0 - gate))
 
 
+def kernel_early(meta, scale_shift, context, v0, v1, v2, v3, v4, v5, v6, own, near, far):
+    for offset, target in enumerate((own, near, far.at[0], far.at[1])):
+        slot = jnp.bitwise_xor(meta[0], offset)
+        target[...] = jnp.zeros((E_ROWS, LANES), F32)
+        for row, vector in enumerate((v0, v1, v2, v3, v4, v5, v6)):
+            target[row : row + 1, :] = vector[...]
+        scales = scale_shift[slot]
+        target[M_SCALE : M_SCALE + 1, :] = scales[:, :LANES]
+        target[M_SHIFT : M_SHIFT + 1, :] = scales[:, LANES:]
+        tokens = context[slot]
+        target[M_KEY : M_KEY + 8, :] = tokens[:, :LANES]
+        target[M_VALUE : M_VALUE + 8, :] = tokens[:, LANES:]
+
+
 def kernel_first(
     meta, i0, i1, i2, i3, e0, e1, e2, e3, w0, w1, w2, w3, w4, w5, w6, w7,
-    image, pack, first_t, inner, field, weight, sems,
+    image, pack, first_t, inner, second_t, second, field, weight, sems,
 ):
     pixels = image.shape[1]
     me = meta[0]
-    image_copies = fetch((i0, i1, i2, i3), image, me, sems, 0)
-    pack_copies = fetch((e0, e1, e2, e3), pack, me, sems, 4)
+    image_copies = fetch((i0, i1, i2.at[0], i3.at[1]), image, me, sems, 0)
+    pack_copies = fetch((e0, e1, e2.at[0], e3.at[1]), pack, me, sems, 4)
     weight_copies = fetch_routed((w0, w1, w2, w3, w4, w5, w6, w7), weight, me, meta[2], sems, 8)
     clear_padding(field, pixels)
+    clear_padding(second, pixels)
     wait_all(image_copies)
     wait_all(pack_copies)
     strip = 128
@@ -252,39 +267,33 @@
             inner[b, pl.ds(start, tile.shape[0]), :] = tile[:, b * LANES : (b + 1) * LANES]
 
     conv_tiles(field, weight, pixels, 512, write)
-
-
-def kernel_second(
-    meta, inner, image, pack, m0, m1, m2, m3, p0, p1, p2, p3, w0, w1, w2, w3, w4, w5, w6, w7,
-    middle, second_t, attn_t, qkv, mod, field, weight, qkv_weight, attn, sems,
-):
-    pixels = image.shape[1]
-    me = meta[0]
-    qkv_copies = fetch((p0, p1, p2, p3), qkv_weight, me, sems, 0)
-    weight_copies = fetch_routed((w0, w1, w2, w3, w4, w5, w6, w7), weight, me, meta[2], sems, 4)
-    mod_copies = fetch((m0, m1, m2, m3), mod, me, sems, 12)
-    clear_padding(field, pixels)
-    strip = 128
     means2, inverses2 = norm_rows(pixels, strip, lambda b, start: inner[b, pl.ds(start, strip), :])
-
-    wait_all(mod_copies)
 
     def modulate(index, carry):
         start = pl.multiple_of(index * strip, strip)
         for b in range(4):
             gain = pack[b, E_G2 : E_G2 + 1, :]
             bias = pack[b, E_B2 : E_B2 + 1, :]
-            scale = mod[b, M_SCALE : M_SCALE + 1, :]
-            shift = mod[b, M_SHIFT : M_SHIFT + 1, :]
+            scale = pack[b, M_SCALE : M_SCALE + 1, :]
+            shift = pack[b, M_SHIFT : M_SHIFT + 1, :]
             normed = (inner[b, pl.ds(start, strip), :] - means2[b]) * inverses2[b]
             modulated = (normed * gain + bias) * (1.0 + scale) + shift
             after = modulated * jax.nn.sigmoid(modulated)
-            store_shifted(field, b, start, after)
+            store_shifted(second, b, start, after)
             second_t[b, :, pl.ds(start, strip)] = after.T.astype(BF16)
         return carry
 
     lax.fori_loop(0, pixels // strip, modulate, 0)
-    wait_all(weight_copies)
+
+
+def kernel_second(
+    meta, second, image, pack, w0, w1, w2, w3, w4, w5, w6, w7,
+    middle, attn_t, qkv, qkv_weight, proj_weight, weight, attn, sems,
+):
+    pixels = image.shape[1]
+    me = meta[0]
+    wait_all(fetch_routed((w0, w1, w2, w3, w4, w5, w6, w7), weight, me, meta[2], sems, 0))
+    strip = 128
 
     def write(start, tile):
         rows = tile.shape[0]
@@ -292,7 +301,7 @@
             branch = tile[:, b * LANES : (b + 1) * LANES] + pack[b, E_CB2 : E_CB2 + 1, :]
             middle[b, pl.ds(start, rows), :] = image[b, pl.ds(start, rows), :].astype(F32) + branch
 
-    conv_tiles(field, weight, pixels, 512, write)
+    conv_tiles(second, weight, pixels, 512, write)
     means, inverses = norm_rows(pixels, strip, lambda b, start: middle[b, pl.ds(start, strip), :])
 
     def normalise(index, carry):
@@ -305,13 +314,17 @@
         return carry
 
     lax.fori_loop(0, pixels // strip, normalise, 0)
-    wait_all(qkv_copies)
+    for s in range(4):
+        qkv_weight[s] = weight[s, QKV_ROW:PROJ_ROW, :]
+        proj_weight[s] = weight[s, PROJ_ROW : PROJ_ROW + C, :]
 
     def project(index, carry):
         s = index // 2
         start = pl.multiple_of((index % 2) * 512, 512)
         left = jnp.concatenate([attn[b, pl.ds(start, 512), :] for b in range(4)], axis=1)
-        right = jnp.concatenate([qkv_weight[s, kind] for kind in range(3)], axis=1)
+        right = jnp.concatenate(
+            [weight[s, QKV_ROW + kind * C : QKV_ROW + (kind + 1) * C, :] for kind in range(3)], axis=1
+        )
         qkv[s, pl.ds(start, 512), :] = jnp.dot(left, right, preferred_element_type=F32).astype(BF16)
         return carry
 
@@ -319,15 +332,14 @@
 
 
 def kernel_attention(
-    meta, qkv, mod, middle, c0, c1, c2, c3, w0, w1, w2, w3,
+    meta, qkv, pack, middle, weight, c0, c1, c2, c3,
     o0, o1, o2, cot, mixed, dqkv, dctx,
-    weight, grad_mixed, score_ctx, grad_ctx_prob, prob_ctx, dscore_ctx, out_pix, dquery, dkey_t, dvalue_t, sems,
+    grad_mixed, score_ctx, grad_ctx_prob, prob_ctx, dscore_ctx, out_pix, dquery, dkey_t, dvalue_t, sems,
 ):
     pixels = qkv.shape[1]
     me = meta[0]
     alive = meta[1].astype(F32)
     cot_copies = fetch((c0, c1, c2, c3), cot, me, sems, 0)
-    weight_copies = fetch((w0, w1, w2, w3), weight, me, sems, 4)
     scale = 1.0 / math.sqrt(HEAD)
     block = 256
 
@@ -337,7 +349,7 @@
     def diagonal(kind):
         found = []
         for s in range(4):
-            rows8 = mod[s, kind : kind + 8, :]
+            rows8 = pack[s, kind : kind + 8, :]
             tiled = jnp.concatenate([rows8] * 4, axis=0)
             own = (row32 // 4) == (2 * s + lane32 // HEAD)
             kept = jnp.where(own, tiled, 0.0)
@@ -347,7 +359,15 @@
     keys_ctx = diagonal(M_KEY)
     values_ctx = diagonal(M_VALUE)
     wait_all(cot_copies)
-    wait_all(weight_copies)
+
+    def projection():
+        return jnp.concatenate(
+            [
+                jnp.concatenate([weight[s, o * LANES : (o + 1) * LANES, :] for o in range(4)], axis=1)
+                for s in range(4)
+            ],
+            axis=0,
+        )
 
     def prepare(index, carry):
         start = pl.multiple_of(index * block, block)
@@ -355,7 +375,7 @@
         for s in range(4):
             cot[s, rows, :] = (cot[s, rows, :].astype(F32) * alive).astype(BF16)
         all_cot = jnp.concatenate([cot[s, rows, :] for s in range(4)], axis=1)
-        all_weight = weight[...].reshape(C, C)
+        all_weight = projection()
         grad = lax.dot_general(
             all_cot, all_weight, (((1,), (1,)), ((), ())), preferred_element_type=F32
         ).astype(BF16)
@@ -483,7 +503,7 @@
             parts.append(both)
             dqkv[s, rows, 0:LANES] = (dquery[s, rows, :] + dquery_ctx[:, cut]).astype(BF16)
         result = jnp.dot(
-            jnp.concatenate(parts, axis=1), weight[...].reshape(C, C), preferred_element_type=F32
+            jnp.concatenate(parts, axis=1), projection(), preferred_element_type=F32
         )
         for offset, target in enumerate((o0, o1, o2.at[0], o2.at[1])):
             other = jnp.bitwise_xor(me, offset)
@@ -543,21 +563,21 @@
 
 
 def kernel_back_attention(
-    meta, dqkv, cot, middle, pack, dctx, p0, p1, p2, p3,
-    dmiddle, field, sums, d0, d1, d2, d3, qkv_weight, dattn, sems,
+    meta, dqkv, cot, middle, pack, dctx, qkv_weight,
+    dmiddle, field, sums, d0, d1, d2, d3, dattn,
 ):
     pixels = cot.shape[1]
     me = meta[0]
-    qkv_copies = fetch((p0, p1, p2, p3), qkv_weight, me, sems, 0)
     strip = 128
     clear_padding(field, pixels)
     means, inverses = norm_rows(pixels, strip, lambda b, start: middle[b, pl.ds(start, strip), :])
-    wait_all(qkv_copies)
 
     def back(index, carry):
         start = pl.multiple_of(index * 512, 512)
         left = jnp.concatenate([dqkv[s, pl.ds(start, 512), :] for s in range(4)], axis=1)
-        right = jnp.concatenate([qkv_weight[s, kind] for s in range(4) for kind in range(3)], axis=1)
+        right = jnp.concatenate(
+            [qkv_weight[s, kind * C : (kind + 1) * C, :] for s in range(4) for kind in range(3)], axis=1
+        )
         tile = lax.dot_general(left, right, (((1,), (1,)), ((), ())), preferred_element_type=F32)
         for b in range(4):
             dattn[b, pl.ds(start, 512), :] = tile[:, b * LANES : (b + 1) * LANES]
@@ -680,7 +700,7 @@
 
 
 def kernel_back_second(
-    meta, grad_field, inner, pack, mod, sums_in, w0, w1, w2, w3, w4, w5, w6, w7,
+    meta, grad_field, inner, pack, sums_in, w0, w1, w2, w3, w4, w5, w6, w7,
     field, sums, d0, d1, d2, d3, weight, grad, sems,
 ):
     pixels = inner.shape[1]
@@ -706,8 +726,8 @@
         found = []
         for b in range(4):
             bias = pack[b, E_B2 : E_B2 + 1, :]
-            scale = mod[b, M_SCALE : M_SCALE + 1, :]
-            shift = mod[b, M_SHIFT : M_SHIFT + 1, :]
+            scale = pack[b, M_SCALE : M_SCALE + 1, :]
+            shift = pack[b, M_SHIFT : M_SHIFT + 1, :]
             shaped = read_normed(b, start) * gains[b] + bias
             modulated = shaped * (1.0 + scale) + shift
             dmod = silu_slope(modulated, grad[b, pl.ds(start, strip), :])
@@ -991,6 +1011,13 @@
     return [lax.dynamic_index_in_dim(stack, me ^ k, 0, keepdims=False) for k in range(4)]
 
 
+def pick_pair(stack, me):
+    own = lax.dynamic_index_in_dim(stack, me, 0, keepdims=False)
+    near = lax.dynamic_index_in_dim(stack, me ^ 1, 0, keepdims=False)
+    far = [lax.dynamic_index_in_dim(stack, me ^ k, 0, keepdims=True) for k in (2, 3)]
+    return own, near, jnp.concatenate(far, axis=0)
+
+
 def dp_levels(size):
     return [(1 << k, 2) for k in range(size.bit_length() - 1)]
 
@@ -1036,22 +1063,18 @@
         conv1_weight, conv2_weight, image_in, out_cotangent, meta
     )
 
-    vectors = jnp.stack(
-        [norm1_gain, norm1_bias, norm2_gain, norm2_bias, conv2_bias, norm3_gain, norm3_bias, norm3_bias]
-    )
     conv1_shard = conv1_weight.reshape(9 * C, LANES)
-    conv2_shard = conv2_weight.reshape(9 * C, LANES)
-    qkv_shard = jnp.transpose(qkv_weight, (1, 0, 2))
 
     def half_of(shard):
         rows = shard.shape[0] // 2
         return lax.dynamic_slice_in_dim(shard, parity * rows, rows, axis=0)
 
-    packs = share(vectors)
-    half1 = swap(half_of(conv1_shard), "mp", 2)
+    half1, image_in = tie(half_of(conv1_shard), image_in)
+    half1 = swap(half1, "mp", 2)
     near1 = swap(conv1_shard, "mp", 1)
-    slices, *packs = tie(image_in, *packs)
-    images = exchange(pick(slices, me))
+    images = pick_pair(image_in, me)
+    image_near = swap(images[1], "mp", 1)
+    image_far = swap(images[2], "mp", 2)
 
     half_width = EMB // 2
     frequency = jnp.exp(-math.log(10000.0) * jnp.arange(half_width, dtype=F32) / half_width)
@@ -1061,20 +1084,35 @@
     ).astype(BF16)
     scale_shift = jnp.dot(
         condition, embed_weight.reshape(EMB, 2 * LANES), preferred_element_type=F32
-    ).reshape(slots, 2, LANES)
+    ).reshape(slots, 1, 2 * LANES)
     doubled = jnp.concatenate([context_tokens, context_tokens], axis=1)
     context = jnp.dot(
         doubled.reshape(slots * 2 * CTX, EMB),
         context_weight.reshape(EMB, 2 * LANES),
         preferred_element_type=F32,
-    ).astype(BF16).astype(F32).reshape(slots, 2 * CTX, 2, LANES)
-    early = jnp.concatenate(
-        [scale_shift, jnp.zeros((slots, 6, LANES), F32), context[:, :, 0], context[:, :, 1]], axis=1
-    )
+    ).astype(BF16).astype(F32).reshape(slots, 2 * CTX, 2 * LANES)
+    vectors = [norm1_gain, norm1_bias, norm2_gain, norm2_bias, conv2_bias, norm3_gain, norm3_bias]
+    early = struct((E_ROWS, LANES), F32)
+    packs = call(
+        kernel_early,
+        "early",
+        [early, early, struct((2, E_ROWS, LANES), F32)],
+        [smem()] + [vmem()] * 9,
+        [],
+        limit=8,
+    )(meta, scale_shift, context, *[vector[None] for vector in vectors])
     count_rows = jnp.broadcast_to(image_count.astype(BF16)[:, None, None], (slots, CTX - 1, EMB))
     factors = jnp.concatenate([condition[:, None], count_rows, context_tokens], axis=1)[None]
-    mods = pick(early, me)
-    half2 = half_of(conv2_shard)
+    cots = pick(out_cotangent, me)
+    rest_shard = jnp.concatenate(
+        [
+            conv2_weight.reshape(9 * C, LANES),
+            jnp.transpose(qkv_weight, (1, 0, 2)).reshape(3 * C, LANES),
+            jnp.transpose(proj_weight.reshape(LANES, 4, LANES), (1, 0, 2)).reshape(C, LANES),
+        ],
+        axis=0,
+    )
+    rest_half = half_of(rest_shard)
 
     def relayed(shard, near, half):
         by_x, by_z = cut(half)
@@ -1084,20 +1122,17 @@
             swap(part, "mp", 1) for part in (half, by_x, by_z)
         )
 
-    cots = pick(out_cotangent, me)
-    half1, near1, image_near, mods, half2, factors, cots = tie(
-        half1, near1, images[1], mods, half2, factors, cots
+    near1, image_near, packs, half1 = tie(near1, image_near, packs, half1)
+    pack_near = swap(packs[1], "mp", 1)
+    pack_far = swap(packs[2], "mp", 2)
+    conv1 = relayed(conv1_shard, near1, half1)
+    image_far, pack_near, pack_far, rest_shard, rest_half, factors, cots, *conv1 = tie(
+        image_far, pack_near, pack_far, rest_shard, rest_half, factors, cots, *conv1
     )
-    conv1 = relayed(conv1_shard, near1, half1)
-    far_images = images[2:]
-    mods, *conv1 = tie(mods, *conv1)
-    mods = exchange(mods)
-    conv1, far_images, mods, half2 = tie(conv1, far_images, mods, half2)
-    images = (images[0], image_near) + tuple(far_images)
-    half2 = swap(half2, "mp", 2)
-    qkv_far = swap(qkv_shard, "mp", 2)
-    proj_far = swap(proj_weight, "mp", 2)
-    near2 = swap(conv2_shard, "mp", 1)
+    images = (images[0], image_near, image_far, swap(image_far, "mp", 1))
+    packs = (packs[0], pack_near, pack_far, swap(pack_far, "mp", 1))
+    rest_half = swap(rest_half, "mp", 2)
+    rest_near = swap(rest_shard, "mp", 1)
     factors = [factors, swap(factors, "dp", 1)]
 
     block = struct((4, pixels, LANES), BF16)
@@ -1108,45 +1143,41 @@
     pair_piece = struct((2, pixels, LANES), BF16)
     field_scratch = pltpu.VMEM((3, 4, pixels + 2 * PAD, LANES), BF16)
     conv_scratch = pltpu.VMEM((4, 9 * C, LANES), BF16)
-    qkv_scratch = pltpu.VMEM((4, 3, C, LANES), BF16)
+    rest_scratch = pltpu.VMEM((4, PROJ_ROW + C, LANES), BF16)
     grad_scratch = pltpu.VMEM((4, pixels, LANES), F32)
-    conv_flops = 2 * pixels * 9 * C * C
-
-    image, pack, first_t, inner = call(
+
+    image, pack, first_t, inner, second_t, second = call(
         kernel_first,
         "first",
-        [block, struct((4, E_ROWS, LANES), F32), turned, block32],
+        [block, struct((4, E_ROWS, LANES), F32), turned, block32, turned, fields],
         [smem()] + [anywhere()] * 16,
         [field_scratch, conv_scratch, pltpu.SemaphoreType.DMA((16,))],
-        conv_flops,
+        limit=17,
     )(meta, *images, *packs, *conv1)
 
-    inner, half2, near2, factors = tie(inner, half2, near2, factors)
+    second, rest_half, rest_near, factors = tie(second, rest_half, rest_near, factors)
+    rest = relayed(rest_shard, rest_near, rest_half)
+    cots = exchange(cots)
+    second, *rest = tie(second, *rest)
     factors = stack(factors)
-    conv2 = relayed(conv2_shard, near2, half2)
-    inner, qkv_far, *conv2 = tie(inner, qkv_far, *conv2)
-    qkv_w = (qkv_shard, swap(qkv_shard, "mp", 1), qkv_far, swap(qkv_far, "mp", 1))
-    inner, *qkv_w = tie(inner, *qkv_w)
-    cots = exchange(cots)
     factors = [factors, swap(factors, "dp", 2)]
-    middle, second_t, attn_t, qkv, mod = call(
+    middle, attn_t, qkv, qkv_w, proj_w = call(
         kernel_second,
         "second",
-        [block32, turned, turned, struct((4, pixels, 3 * LANES), BF16), struct((4, M_ROWS, LANES), F32)],
-        [smem()] + [vmem()] * 3 + [anywhere()] * 16,
         [
-            field_scratch,
-            conv_scratch,
-            qkv_scratch,
-            pltpu.VMEM((4, pixels, LANES), BF16),
-            pltpu.SemaphoreType.DMA((16,)),
+            block32,
+            turned,
+            struct((4, pixels, 3 * LANES), BF16),
+            struct((4, 3 * C, LANES), BF16),
+            struct((4, C, LANES), BF16),
         ],
-        conv_flops + 6 * pixels * C * C,
-    )(meta, inner, image, pack, *mods, *qkv_w, *conv2)
+        [smem()] + [vmem()] * 3 + [anywhere()] * 8,
+        [rest_scratch, pltpu.VMEM((4, pixels, LANES), BF16), pltpu.SemaphoreType.DMA((8,))],
+        limit=17,
+    )(meta, second, image, pack, *rest)
     ctx_scratch = pltpu.VMEM((pixels, LANES), F32)
     turned_scratch = pltpu.VMEM((LANES, pixels), F32)
-    proj_w = (proj_weight, swap(proj_weight, "mp", 1), proj_far, swap(proj_far, "mp", 1))
-    qkv, first_t, factors, cots, proj_w = tie(qkv, first_t, factors, cots, proj_w)
+    qkv, first_t, second_t, factors, cots = tie(qkv, first_t, second_t, factors, cots)
     factors = stack(factors)
     second_y = swap(second_t, "mp", 2)
     first_y = swap(first_t, "mp", 2)
@@ -1160,9 +1191,8 @@
         "attention",
         [piece, piece, pair_piece]
         + [block, block, struct((4, pixels, 3 * LANES), BF16), struct((4, 2 * CTX, LANES), F32)],
-        [smem()] + [vmem()] * 3 + [anywhere()] * 8,
+        [smem()] + [vmem()] * 4 + [anywhere()] * 4,
         [
-            pltpu.VMEM((4, LANES, C), BF16),
             pltpu.VMEM((4, pixels, LANES), BF16),
             ctx_scratch,
             ctx_scratch,
@@ -1172,10 +1202,10 @@
             grad_scratch,
             turned_scratch,
             turned_scratch,
-            pltpu.SemaphoreType.DMA((8,)),
+            pltpu.SemaphoreType.DMA((4,)),
         ],
-        4 * 12 * pixels * pixels * C,
-    )(meta, qkv, mod, middle, *cots, *proj_w)
+    )(meta, qkv, pack, middle, proj_w, *cots)
+
     def weight_send(sources, gradients):
         return call(
             kernel_weight_send,
@@ -1228,9 +1258,9 @@
         kernel_back_attention,
         "back_attention",
         [block32, fields, struct((4, S_ROWS, LANES), F32)] + [piece] * 4,
-        [smem()] + [vmem()] * 5 + [anywhere()] * 4,
-        [qkv_scratch, grad_scratch, pltpu.SemaphoreType.DMA((4,))],
-    )(meta, dqkv, cot, middle, pack, dctx, *qkv_w)
+        [smem()] + [vmem()] * 6,
+        [grad_scratch],
+    )(meta, dqkv, cot, middle, pack, dctx, qkv_w)
     gradients2, second_d, first_d, att, field2 = tie(gradients2, second_d, first_d, att, field2)
     seconds = (second_t, second_c, second_y, second_d)
     firsts = (first_t, first_c, first_y, first_d)
@@ -1241,10 +1271,10 @@
         kernel_back_second,
         "back_second",
         [fields, struct((4, S_ROWS, LANES), F32)] + [piece] * 4,
-        [smem()] + [vmem()] * 5 + [anywhere()] * 8,
-        [conv_scratch, grad_scratch, pltpu.SemaphoreType.DMA((8,))],
-        limit=17,
-    )(meta, field2, inner, pack, mod, sums, *conv2)
+        [smem()] + [vmem()] * 4 + [anywhere()] * 8,
+        [rest_scratch, grad_scratch, pltpu.SemaphoreType.DMA((8,))],
+        limit=20,
+    )(meta, field2, inner, pack, sums, *rest)
     gradients1, gradients2, att = tie(gradients1, gradients2, att)
     gradients1 = exchange(gradients1)
     att = down(att, 1)

time: 301 us -> 286 us (0.950)
  waiting for transfers between devices: 94.3 us -> 78.5 us
  starting transfers between devices: 48.6 us -> 51.7 us
    ppermute x76 -> x67, waiting for transfers between devices: 94.3 us -> 78.5 us  [swap(): return lax.ppermute(value, axis, [(i, i ^ offset) for i in range(size)])]
    ppermute x76 -> x67, starting transfers between devices: 48.6 us -> 51.7 us  [swap(): return lax.ppermute(value, axis, [(i, i ^ offset) for i in range(size)])]
    pallas_call x1 -> x2, Pallas kernels: 16.3 us -> 13.9 us  [the longest x1 13.3 us: local(): call(kernel_second, 'second', [block32, turned, struct((4, pixels, 3 * LA...]
  transfers between devices with their start and end apart: 76 -> 67, of which waited for: 28 -> 21; matrix products, arithmetic and copies ran while one was open for 4% -> 3% of each run, Pallas kernels for 47% -> 49%
where the time goes in v4:
time: 286 us; the launch traced here: 285 us
  Pallas kernels  143 us (50%)
  waiting for transfers between devices  78.5 us (27%)
  starting transfers between devices  51.7 us (18%)
  local copies, waits for them, and re-layouts  5.03 us (2%)
    ppermute x67, waiting for transfers between devices, swap(): return lax.ppermute(value, axis, [(i, i ^ offset) for i in range(size)])  78.5 us
    ppermute x67, starting transfers between devices, swap(): return lax.ppermute(value, axis, [(i, i ^ offset) for i in range(size)])  51.7 us
    pallas_call x1, Pallas kernels, local(): call(kernel_attention, 'attention', [piece, piece, pair_piece] + [block,...  40 us
    pallas_call x1, Pallas kernels, local(): call(kernel_second, 'second', [block32, turned, struct((4, pixels, 3 * LA...  13.3 us
    pallas_call x1, Pallas kernels, local(): call(kernel_first, 'first', [block, struct((4, E_ROWS, LANES), F32), turn...  12.9 us
    pallas_call x1, Pallas kernels, local(): call(kernel_back_second, 'back_second', [fields, struct((4, S_ROWS, LANES...  12.5 us
    pallas_call x2, Pallas kernels, weight_send(): call(kernel_weight_send, 'weight_send', [struct((9, C // 2, LANES), BF16)...  9.62 us
    pallas_call x2, Pallas kernels, weight_own(): call(kernel_weight_own, 'weight_own', struct((9, C // 2, LANES), F32), [s...  8.42 us
  transfers between devices with their start and end apart: 67, of which 21 were waited for; matrix products, arithmetic and copies ran while one was open for 3% of the time, Pallas kernels for 49%

profile of v4, /device:TPU:0, one launch (start us, length us, event | category | flops | bytes accessed | tf_op | source)
XLA Modules:
  0.0 285.4 jit_solution(9207000999932617914)
XLA Ops:
  3.8 2.5 collective-permute-start.2
  14.3 6.4 %collective-permute-done.2.source.w2 = bf16[2304,128]{1,0:T(8,128)(2,1)S(1)} collective-permute-done((bf16[2304,128]{1,0:T(8,128)(2,1)}, bf16[2304,128]{1,0:T(8,128)(2,1)S(1)}, u32[]{:S(2)}, u32[]{:S(2)}) %collective-permute-start.2) | collective-permute-done | bytes 589856 | tf_op jit(solution)/shard_map/ppermute | solution.py:993
  24.6 4.9 %collective-permute-done.6.w3 = bf16[1152,128]{1,0:T(8,128)(2,1)S(1)} collective-permute-done((bf16[1152,128]{1,0:T(8,128)(2,1)S(1)}, bf16[1152,128]{1,0:T(8,128)(2,1)S(1)}, u32[]{:S(2)}, u32[]{:S(2)}) %collective-permute-start.6) | collective-permute-done | bytes 294944 | tf_op jit(solution)/shard_map/ppermute | solution.py:993
  33.7 2.1 collective-permute-done.5.e2
  40.6 12.9 %first.1 = (bf16[4,1024,128]{2,1,0:T(8,128)(2,1)S(1)}, f32[4,32,128]{2,1,0:T(8,128)S(1)}, bf16[4,128,1024]{2,1,0:T(8,128)(2,1)S(1)}, f32[4,1024,128]{2,1,0:T(8,1...) custom-call(s32[6]{0:T(128)S(1)} %stack.36.meta, bf16[1024,128]{1,0:T(8,128)(2,1)S(1)} %copy-done.11, ...), custom_call_target="tpu_custom_call" | custom-call | tf_op jit(solution)/shard_map/first/pallas_call | solution.py:1149
  53.5 3.7 %collective-permute-done.13.source.w2 = bf16[3328,128]{1,0:T(8,128)(2,1)S(1)} collective-permute-done((bf16[3328,128]{1,0:T(8,128)(2,1)S(1)}, bf16[3328,128]{1,0:T(8,128)(2,1)S(1)}, u32[]{:S(2)}, u32[]{:S(2)}) %collective-permute-start.13) | collective-permute-done | bytes 852000 | tf_op jit(solution)/shard_map/ppermute | solution.py:993
  60.7 8.1 %collective-permute-done.16.w3 = bf16[1664,128]{1,0:T(8,128)(2,1)S(1)} collective-permute-done((bf16[1664,128]{1,0:T(8,128)(2,1)S(1)}, bf16[1664,128]{1,0:T(8,128)(2,1)S(1)}, u32[]{:S(2)}, u32[]{:S(2)}) %collective-permute-start.16) | collective-permute-done | bytes 426016 | tf_op jit(solution)/shard_map/ppermute | solution.py:993
  74.0 13.3 %second.1 = (f32[4,1024,128]{2,1,0:T(8,128)S(1)}, bf16[4,128,1024]{2,1,0:T(8,128)(2,1)S(1)}, bf16[4,1024,384]{2,1,0:T(8,128)(2,1)S(1)}, bf16[4,1536,128]{2,1,0:T(8,128)(2,1)S(1)}, bf16[4,512,128]{2,1,0:T(8,128)(2,1)S(1)}) custom-call(s32[6]{0:T(128)S(1)} %stack.36.meta, bf16[3,4,1088,128]{3,2,1,0:T(8,128)(2,1)S(1)} %get-tuple-element.287.second, ...), custom_call_target="tpu_custom_call" | custom-call | tf_op jit(solution)/shard_map/second/pallas_call | solution.py:1164
  89.8 2.7 collective-permute-start.29
  92.4 40.0 %attention.1 = (bf16[1024,128]{1,0:T(8,128)(2,1)S(1)}, bf16[1024,128]{1,0:T(8,128)(2,1)S(1)}, bf16[2,1024,128]{2,1,0:T(8,128)(2,1)S(1)}, bf16[4,1024,128]{2,1,0:...) custom-call(s32[6]{0:T(128)S(1)} %stack.36.meta, ...), custom_call_target="tpu_custom_call" | custom-call | tf_op jit(solution)/shard_map/attention/pallas_call | solution.py:1189
  132.5 5.6 %attention_grad.1 = (bf16[2,4,512,128]{3,2,1,0:T(8,128)(2,1)S(1)}, bf16[2,4,512,128]{3,2,1,0:T(8,128)(2,1)S(1)}) custom-call(s32[6]{0:T(128)S(1)} %stack.36.meta, bf16[4,1024,384]{2,1,0:T(8,128)(2,1)S(1)} %get-tuple-element.326.dqkv, bf16[4,1024,128]{2,1,0:T(8,128)(2,1)S(1)} %get-tuple-element.317.mixed, ...), custom_call_target="tpu_custom_call" | custom-call | tf_op jit(solution)/shard_map/attention_grad/pallas_call | solution.py:1244
  138.8 5.7 %back_attention.1 = (f32[4,1024,128]{2,1,0:T(8,128)S(1)}, bf16[3,4,1088,128]{3,2,1,0:T(8,128)(2,1)S(1)}, f32[4,32,128]{2,1,0:T(8,128)S(1)}, bf16[1024,128]{1,0:T...) custom-call(s32[6]{0:T(128)S(1)} %stack.36.meta, ...), custom_call_target="tpu_custom_call" | custom-call | tf_op jit(solution)/shard_map/back_attention/pallas_call | solution.py:1257
  148.3 12.5 %back_second.1 = (bf16[3,4,1088,128]{3,2,1,0:T(8,128)(2,1)S(1)}, f32[4,32,128]{2,1,0:T(8,128)S(1)}, bf16[1024,128]{1,0:T(8,128)(2,1)S(1)}, bf16[1024,128]{1,0:T(...) custom-call(s32[6]{0:T(128)S(1)} %stack.36.meta, ...), custom_call_target="tpu_custom_call" | custom-call | tf_op jit(solution)/shard_map/back_second/pallas_call | solution.py:1270
  162.0 4.8 %weight_send.2 = (bf16[9,256,128]{2,1,0:T(8,128)(2,1)S(1)}, bf16[3,4,1088,128]{3,2,1,0:T(8,128)(2,1)S(1)}) custom-call(s32[6]{0:T(128)S(1)} %stack.36.meta, bf16[4,128,1024]{2,1,0:T(8,128)(2,1)S(1)} %get-tuple-element.315.u0, bf16[4,128,1024]{2,1,0:T(8,128)(2,1)S(1)} %collective-permute-done.27.u1, bf16[4,128,1024]{2,1,0:T(8,128)(2,1)S(1)} %collective-permute-done.25.u2, ...), custom_call_target="tpu_custom_call" | custom-call | tf_op jit(solution)/shard_map/weight_send/pallas_call | solution.py:1210
  171.3 4.2 %weight_own.2.refs_0_ = f32[9,256,128]{2,1,0:T(8,128)S(1)} custom-call(s32[6]{0:T(128)S(1)} %stack.36.meta, bf16[4,128,1024]{2,1,0:T(8,128)(2,1)S(1)} %get-tuple-element.315.u0, bf16[4,128,1024]{2,1,0:T(8,128)(2,1)S(1)} %collective-permute-done.27.u1, bf16[4,128,1024]{2,1,0:T(8,128)(2,1)S(1)} %collective-permute-done.25.u2, ...), custom_call_target="tpu_custom_call" | custom-call | tf_op jit(solution)/shard_map/weight_own/pallas_call | solution.py:1220
  175.5 4.3 %collective-permute-done.38.got = bf16[8,64,128]{2,1,0:T(8,128)(2,1)S(1)} collective-permute-done((bf16[8,64,128]{2,1,0:T(8,128)(2,1)S(1)}, bf16[8,64,128]{2,1,0:T(8,128)(2,1)S(1)}, u32[]{:S(2)}, u32[]{:S(2)}) %collective-permute-start.38) | collective-permute-done | bytes 131104 | tf_op jit(solution)/shard_map/ppermute | solution.py:993
  181.4 7.3 %back_conv.1.grad_in = f32[4,1024,128]{2,1,0:T(8,128)S(1)} custom-call(s32[6]{0:T(128)S(1)} %stack.36.meta, bf16[3,4,1088,128]{3,2,1,0:T(8,128)(2,1)S(1)} %get-tuple-element.381.grad_field, bf16[4608,128]{1,0:T(8,128)(2,1)S(1)} %bitcast.83, bf16[4608,128]{1,0:T(8,128)(2,1)S(1)} %collective-permute-done.w1, ...), custom_call_target="tpu_custom_call" | custom-call | tf_op jit(solution)/shard_map/back_conv/pallas_call | solution.py:1301
  188.8 4.8 %weight_send.3 = (bf16[9,256,128]{2,1,0:T(8,128)(2,1)S(1)}, bf16[3,4,1088,128]{3,2,1,0:T(8,128)(2,1)S(1)}) custom-call(s32[6]{0:T(128)S(1)} %stack.36.meta, bf16[4,128,1024]{2,1,0:T(8,128)(2,1)S(1)} %get-tuple-element.321.u0, bf16[4,128,1024]{2,1,0:T(8,128)(2,1)S(1)} %collective-permute-done.28.u1, bf16[4,128,1024]{2,1,0:T(8,128)(2,1)S(1)} %collective-permute-done.26.u2, ...), custom_call_target="tpu_custom_call" | custom-call | tf_op jit(solution)/shard_map/weight_send/pallas_call | solution.py:1210
  197.8 4.2 %weight_own.3.refs_0_ = f32[9,256,128]{2,1,0:T(8,128)S(1)} custom-call(s32[6]{0:T(128)S(1)} %stack.36.meta, bf16[4,128,1024]{2,1,0:T(8,128)(2,1)S(1)} %get-tuple-element.321.u0, bf16[4,128,1024]{2,1,0:T(8,128)(2,1)S(1)} %collective-permute-done.28.u1, bf16[4,128,1024]{2,1,0:T(8,128)(2,1)S(1)} %collective-permute-done.26.u2, ...), custom_call_target="tpu_custom_call" | custom-call | tf_op jit(solution)/shard_map/weight_own/pallas_call | solution.py:1220
  202.0 2.2 collective-permute-done.44.refs_1_
  206.6 4.2 %back_first.1 = (bf16[1056,128]{1,0:T(8,128)(2,1)S(1)}, bf16[1056,128]{1,0:T(8,128)(2,1)S(1)}, bf16[2,1056,128]{2,1,0:T(8,128)(2,1)S(1)}) custom-call(s32[6]{0:T(128)S(1)} %stack.36.meta, f32[4,1024,128]{2,1,0:T(8,128)S(1)} %back_conv.1.grad_in, bf16[4,1024,128]{2,1,0:T(8,128)(2,1)S(1)} %get-tuple-element.288.image, ...), custom_call_target="tpu_custom_call" | custom-call | tf_op jit(solution)/shard_map/back_first/pallas_call | solution.py:1325
  210.8 2.2 collective-permute-done.46.refs_1_
  215.9 11.6 %collective-permute-done.48.refs_1_ = bf16[4,128,128]{2,1,0:T(8,128)(2,1)S(1)} collective-permute-done((bf16[4,128,128]{2,1,0:T(8,128)(2,1)S(1)}, bf16[4,128,128]{2,1,0:T(8,128)(2,1)S(1)}, u32[]{:S(2)}, u32[]{:S(2)}) %collective-permute-start.48) | collective-permute-done | bytes 131104 | tf_op jit(solution)/shard_map/ppermute | solution.py:993
  233.2 2.7 collective-permute-done.54.other
  235.9 5.0 %collective-permute-done.53.refs_1_ = bf16[9,64,128]{2,1,0:T(8,128)(2,1)S(1)} collective-permute-done((bf16[9,64,128]{2,1,0:T(8,128)(2,1)S(1)}, bf16[9,64,128]{2,1,0:T(8,128)(2,1)S(1)}, u32[]{:S(2)}, u32[]{:S(2)}) %collective-permute-start.53) | collective-permute-done | bytes 147488 | tf_op jit(solution)/shard_map/ppermute | solution.py:993
  244.4 2.6 collective-permute-done.55.refs_1_
  248.2 8.9 %collective-permute-done.57.refs_1_ = bf16[9,128,128]{2,1,0:T(8,128)(2,1)S(1)} collective-permute-done((bf16[9,128,128]{2,1,0:T(8,128)(2,1)S(1)}, bf16[9,128,128]{2,1,0:T(8,128)(2,1)S(1)}, u32[]{:S(2)}, u32[]{:S(2)}) %collective-permute-start.57) | collective-permute-done | bytes 294944 | tf_op jit(solution)/shard_map/ppermute | solution.py:993
  259.3 2.1 last_join.4
  263.5 2.5 collective-permute-done.62.refs_1_
  269.5 6.0 %collective-permute-done.65.small1 = bf16[16,32,128]{2,1,0:T(8,128)(2,1)S(1)} collective-permute-done((bf16[16,32,128]{2,1,0:T(8,128)(2,1)S(1)}, bf16[16,32,128]{2,1,0:T(8,128)(2,1)S(1)}, u32[]{:S(2)}, u32[]{:S(2)}) %collective-permute-start.65) | collective-permute-done | bytes 131104 | tf_op jit(solution)/shard_map/ppermute | solution.py:993
  275.6 5.4 %factor_grads.1 = (f32[2048,2,128]{2,1,0:T(2,128)}, f32[2048,2,128]{2,1,0:T(2,128)}, f32[32,128]{1,0:T(8,128)S(1)}) custom-call(s32[6]{0:T(128)S(1)} %stack.36.meta, f32[8,128]{1,0:T(8,128)S(1)} %scale.1, bf16[4,4,8,2048]{3,2,1,0:T(8,128)(2,1)S(1)} %stack.39.factors0, bf16[4,4,8,2048]{3,2,1,0:T(8,128)(2,1)S(1)} %collective-permute-done.29.factors1, ...), custom_call_target="tpu_custom_call" | custom-call | tf_op jit(solution)/shard_map/factor_grads/pallas_call | solution.py:1375
  281.5 2.1 last_join.5
  (226 shorter events, 75.4 us)
Async XLA Ops:
  1.4 19.3 %collective-permute-start = (bf16[4608,128]{1,0:T(8,128)(2,1)}, bf16[4608,128]{1,0:T(8,128)(2,1)S(1)}, u32[]{:S(2)}, u32[]{:S(2)}) collective-permute-start(bf16[4608,128]{1,0:T(8,128)(2,1)} %bitcast.80), channel_id=1, source_target_pairs={{0,1},{1,0},{2,3},{3,2},{4,5},{5,4},{6,7},{7,6},{8,9},{9,8},{10,11... | collective-permute-start | bytes 3538952 | tf_op jit(solution)/shard_map/ppermute | solution.py:993
  3.8 16.9 %collective-permute-start.2 = (bf16[2304,128]{1,0:T(8,128)(2,1)}, bf16[2304,128]{1,0:T(8,128)(2,1)S(1)}, u32[]{:S(2)}, u32[]{:S(2)}) collective-permute-start(bf16[2304,128]{1,0:T(8,128)(2,1)} %constant_dynamic-slice_fusion.3), channel_id=1, source_target_pairs={{0,2},{1,3},{2,0},{3,1},{4,6},{5,7},{6,4},{7,5},{8,10},{9,11},{10,... | collective-permute-start | bytes 1769480 | tf_op jit(solution)/shard_map/ppermute | solution.py:993
  9.5 22.4 %collective-permute-start.3 = (bf16[2,1024,128]{2,1,0:T(8,128)(2,1)}, bf16[2,1024,128]{2,1,0:T(8,128)(2,1)}, u32[]{:S(2)}, u32[]{:S(2)}) collective-permute-start(bf16[2,1024,128]{2,1,0:T(8,128)(2,1)} %pad_maximum_fusion.1), channel_id=1, source_target_pairs={{0,2},{1,3},{2,0},{3,1},{4,6},{5,7},{6,4},{7,5},{8,10},{9,11},{10,... | collective-permute-start | bytes 1572872 | tf_op jit(solution)/shard_map/ppermute | solution.py:993
  35.8 21.4 %collective-permute-start.14 = (bf16[6656,128]{1,0:T(8,128)(2,1)S(1)}, bf16[6656,128]{1,0:T(8,128)(2,1)S(1)}, u32[]{:S(2)}, u32[]{:S(2)}) collective-permute-start(bf16[6656,128]{1,0:T(8,128)(2,1)S(1)} %pad_maximum_fusion.w0), channel_id=1, source_target_pairs={{0,1},{1,0},{2,3},{3,2},{4,5},{5,4},{6,7},{7,6},{8,9},{9,8},{10,11... | collective-permute-start | bytes 5111816 | tf_op jit(solution)/shard_map/ppermute | solution.py:993
  35.9 21.4 %collective-permute-start.13 = (bf16[3328,128]{1,0:T(8,128)(2,1)S(1)}, bf16[3328,128]{1,0:T(8,128)(2,1)S(1)}, u32[]{:S(2)}, u32[]{:S(2)}) collective-permute-start(bf16[3328,128]{1,0:T(8,128)(2,1)S(1)} %constant_dynamic-slice_fusion), channel_id=1, source_target_pairs={{0,2},{1,3},{2,0},{3,1},{4,6},{5,7},{6,4},{7,5},{8,10},{9,11},{10,... | collective-permute-start | bytes 2555912 | tf_op jit(solution)/shard_map/ppermute | solution.py:993
  37.9 15.6 %collective-permute-start.15 = (bf16[1,4,8,2048]{3,2,1,0:T(8,128)(2,1)S(1)}, bf16[1,4,8,2048]{3,2,1,0:T(8,128)(2,1)S(1)}, u32[]{:S(2)}, u32[]{:S(2)}) collective-permute-start(bf16[1,4,8,2048]{3,2,1,0:T(8,128)(2,1)S(1)} %fusion.9.refs_0_), channel_id=1, source_target_pairs={{0,4},{4,0},{8,12},{12,8},{16,20},{20,16},{24,28},{28,24},{1,5},{5... | collective-permute-start | bytes 393224 | tf_op jit(solution)/shard_map/ppermute | solution.py:993
  60.7 13.3 %collective-permute-start.18 = (bf16[3328,128]{1,0:T(8,128)(2,1)S(1)}, bf16[3328,128]{1,0:T(8,128)(2,1)S(1)}, u32[]{:S(2)}, u32[]{:S(2)}) collective-permute-start(bf16[3328,128]{1,0:T(8,128)(2,1)S(1)} %collective-permute-done.13.source.w2), channel_id=1, source_target_pairs={{0,1},{1,0},{2,3},{3,2},{4,5},{5,4},{6,7},{7,6},{8,9},{9,8},{10,11... | collective-permute-start | bytes 2555912 | tf_op jit(solution)/shard_map/ppermute | solution.py:993
  70.2 17.1 %collective-permute-start.22 = (bf16[1024,128]{1,0:T(8,128)(2,1)S(1)}, bf16[1024,128]{1,0:T(8,128)(2,1)S(1)}, u32[]{:S(2)}, u32[]{:S(2)}) collective-permute-start(bf16[1024,128]{1,0:T(8,128)(2,1)S(1)} %get-tuple-element.304), channel_id=1, source_target_pairs={{0,1},{1,0},{2,3},{3,2},{4,5},{5,4},{6,7},{7,6},{8,9},{9,8},{10,11... | collective-permute-start | bytes 786440 | tf_op jit(solution)/shard_map/ppermute | solution.py:993
  70.7 16.6 %collective-permute-start.23 = (bf16[1024,128]{1,0:T(8,128)(2,1)S(1)}, bf16[1024,128]{1,0:T(8,128)(2,1)S(1)}, u32[]{:S(2)}, u32[]{:S(2)}) collective-permute-start(bf16[1024,128]{1,0:T(8,128)(2,1)S(1)} %get-tuple-element.305), channel_id=1, source_target_pairs={{0,2},{1,3},{2,0},{3,1},{4,6},{5,7},{6,4},{7,5},{8,10},{9,11},{10,... | collective-permute-start | bytes 786440 | tf_op jit(solution)/shard_map/ppermute | solution.py:993
  72.3 15.1 %collective-permute-start.24 = (bf16[1024,128]{1,0:T(8,128)(2,1)S(1)}, bf16[1024,128]{1,0:T(8,128)(2,1)S(1)}, u32[]{:S(2)}, u32[]{:S(2)}) collective-permute-start(bf16[1024,128]{1,0:T(8,128)(2,1)S(1)} %get-tuple-element.306), channel_id=1, source_target_pairs={{0,3},{1,2},{2,1},{3,0},{4,7},{5,6},{6,5},{7,4},{8,11},{9,10},{10,... | collective-permute-start | bytes 786440 | tf_op jit(solution)/shard_map/ppermute | solution.py:993
  72.4 15.0 %collective-permute-start.21 = (bf16[2,4,8,2048]{3,2,1,0:T(8,128)(2,1)S(1)}, bf16[2,4,8,2048]{3,2,1,0:T(8,128)(2,1)S(1)}, u32[]{:S(2)}, u32[]{:S(2)}) collective-permute-start(bf16[2,4,8,2048]{3,2,1,0:T(8,128)(2,1)S(1)} %stack.38.refs_0_), channel_id=1, source_target_pairs={{0,8},{4,12},{8,0},{12,4},{16,24},{20,28},{24,16},{28,20},{1,9},{5... | collective-permute-start | bytes 786440 | tf_op jit(solution)/shard_map/ppermute | solution.py:993
  87.4 50.7 %collective-permute-start.27 = (bf16[4,128,1024]{2,1,0:T(8,128)(2,1)S(1)}, bf16[4,128,1024]{2,1,0:T(8,128)(2,1)S(1)}, u32[]{:S(2)}, u32[]{:S(2)}) collective-permute-start(bf16[4,128,1024]{2,1,0:T(8,128)(2,1)S(1)} %get-tuple-element.315.u0), channel_id=1, source_target_pairs={{0,1},{1,0},{2,3},{3,2},{4,5},{5,4},{6,7},{7,6},{8,9},{9,8},{10,11... | collective-permute-start | bytes 3145736 | tf_op jit(solution)/shard_map/ppermute | solution.py:993
  87.7 50.4 %collective-permute-start.25 = (bf16[4,128,1024]{2,1,0:T(8,128)(2,1)S(1)}, bf16[4,128,1024]{2,1,0:T(8,128)(2,1)S(1)}, u32[]{:S(2)}, u32[]{:S(2)}) collective-permute-start(bf16[4,128,1024]{2,1,0:T(8,128)(2,1)S(1)} %get-tuple-element.315.u0), channel_id=1, source_target_pairs={{0,2},{1,3},{2,0},{3,1},{4,6},{5,7},{6,4},{7,5},{8,10},{9,11},{10,... | collective-permute-start | bytes 3145736 | tf_op jit(solution)/shard_map/ppermute | solution.py:993
  89.2 48.9 %collective-permute-start.28 = (bf16[4,128,1024]{2,1,0:T(8,128)(2,1)S(1)}, bf16[4,128,1024]{2,1,0:T(8,128)(2,1)S(1)}, u32[]{:S(2)}, u32[]{:S(2)}) collective-permute-start(bf16[4,128,1024]{2,1,0:T(8,128)(2,1)S(1)} %get-tuple-element.321.u0), channel_id=1, source_target_pairs={{0,1},{1,0},{2,3},{3,2},{4,5},{5,4},{6,7},{7,6},{8,9},{9,8},{10,11... | collective-permute-start | bytes 3145736 | tf_op jit(solution)/shard_map/ppermute | solution.py:993
  89.2 48.9 %collective-permute-start.26 = (bf16[4,128,1024]{2,1,0:T(8,128)(2,1)S(1)}, bf16[4,128,1024]{2,1,0:T(8,128)(2,1)S(1)}, u32[]{:S(2)}, u32[]{:S(2)}) collective-permute-start(bf16[4,128,1024]{2,1,0:T(8,128)(2,1)S(1)} %get-tuple-element.321.u0), channel_id=1, source_target_pairs={{0,2},{1,3},{2,0},{3,1},{4,6},{5,7},{6,4},{7,5},{8,10},{9,11},{10,... | collective-permute-start | bytes 3145736 | tf_op jit(solution)/shard_map/ppermute | solution.py:993
  89.8 48.3 %collective-permute-start.29 = (bf16[4,4,8,2048]{3,2,1,0:T(8,128)(2,1)S(1)}, bf16[4,4,8,2048]{3,2,1,0:T(8,128)(2,1)S(1)}, u32[]{:S(2)}, u32[]{:S(2)}) collective-permute-start(bf16[4,4,8,2048]{3,2,1,0:T(8,128)(2,1)S(1)} %stack.39.factors0), channel_id=1, source_target_pairs={{0,16},{4,20},{8,24},{12,28},{16,0},{20,4},{24,8},{28,12},{1,17},{... | collective-permute-start | bytes 1572872 | tf_op jit(solution)/shard_map/ppermute | solution.py:993
  145.3 15.6 %collective-permute-start.36 = (bf16[8,256,128]{2,1,0:T(8,128)(2,1)S(1)}, bf16[8,256,128]{2,1,0:T(8,128)(2,1)S(1)}, u32[]{:S(2)}, u32[]{:S(2)}) collective-permute-start(bf16[8,256,128]{2,1,0:T(8,128)(2,1)S(1)} %get-tuple-element.354), channel_id=1, source_target_pairs={{0,4},{4,0},{8,12},{12,8},{16,20},{20,16},{24,28},{28,24},{1,5},{5... | collective-permute-start | bytes 1572872 | tf_op jit(solution)/shard_map/ppermute | solution.py:993
  146.5 14.4 %collective-permute-start.33 = (bf16[1024,128]{1,0:T(8,128)(2,1)S(1)}, bf16[1024,128]{1,0:T(8,128)(2,1)S(1)}, u32[]{:S(2)}, u32[]{:S(2)}) collective-permute-start(bf16[1024,128]{1,0:T(8,128)(2,1)S(1)} %get-tuple-element.350), channel_id=1, source_target_pairs={{0,1},{1,0},{2,3},{3,2},{4,5},{5,4},{6,7},{7,6},{8,9},{9,8},{10,11... | collective-permute-start | bytes 786440 | tf_op jit(solution)/shard_map/ppermute | solution.py:993
  146.6 14.2 %collective-permute-start.34 = (bf16[1024,128]{1,0:T(8,128)(2,1)S(1)}, bf16[1024,128]{1,0:T(8,128)(2,1)S(1)}, u32[]{:S(2)}, u32[]{:S(2)}) collective-permute-start(bf16[1024,128]{1,0:T(8,128)(2,1)S(1)} %get-tuple-element.351), channel_id=1, source_target_pairs={{0,2},{1,3},{2,0},{3,1},{4,6},{5,7},{6,4},{7,5},{8,10},{9,11},{10,... | collective-permute-start | bytes 786440 | tf_op jit(solution)/shard_map/ppermute | solution.py:993
  166.9 27.6 %collective-permute-start.43 = (bf16[9,256,128]{2,1,0:T(8,128)(2,1)S(1)}, bf16[9,256,128]{2,1,0:T(8,128)(2,1)S(1)}, u32[]{:S(2)}, u32[]{:S(2)}) collective-permute-start(bf16[9,256,128]{2,1,0:T(8,128)(2,1)S(1)} %get-tuple-element.403), channel_id=1, source_target_pairs={{0,4},{4,0},{8,12},{12,8},{16,20},{20,16},{24,28},{28,24},{1,5},{5... | collective-permute-start | bytes 1769480 | tf_op jit(solution)/shard_map/ppermute | solution.py:993
  167.8 20.8 %collective-permute-start.39 = (bf16[1024,128]{1,0:T(8,128)(2,1)S(1)}, bf16[1024,128]{1,0:T(8,128)(2,1)S(1)}, u32[]{:S(2)}, u32[]{:S(2)}) collective-permute-start(bf16[1024,128]{1,0:T(8,128)(2,1)S(1)} %get-tuple-element.383), channel_id=1, source_target_pairs={{0,1},{1,0},{2,3},{3,2},{4,5},{5,4},{6,7},{7,6},{8,9},{9,8},{10,11... | collective-permute-start | bytes 786440 | tf_op jit(solution)/shard_map/ppermute | solution.py:993
  167.8 20.8 %collective-permute-start.40 = (bf16[1024,128]{1,0:T(8,128)(2,1)S(1)}, bf16[1024,128]{1,0:T(8,128)(2,1)S(1)}, u32[]{:S(2)}, u32[]{:S(2)}) collective-permute-start(bf16[1024,128]{1,0:T(8,128)(2,1)S(1)} %get-tuple-element.384), channel_id=1, source_target_pairs={{0,2},{1,3},{2,0},{3,1},{4,6},{5,7},{6,4},{7,5},{8,10},{9,11},{10,... | collective-permute-start | bytes 786440 | tf_op jit(solution)/shard_map/ppermute | solution.py:993
  169.4 19.3 %collective-permute-start.41 = (bf16[1024,128]{1,0:T(8,128)(2,1)S(1)}, bf16[1024,128]{1,0:T(8,128)(2,1)S(1)}, u32[]{:S(2)}, u32[]{:S(2)}) collective-permute-start(bf16[1024,128]{1,0:T(8,128)(2,1)S(1)} %get-tuple-element.385), channel_id=1, source_target_pairs={{0,3},{1,2},{2,1},{3,0},{4,7},{5,6},{6,5},{7,4},{8,11},{9,10},{10,... | collective-permute-start | bytes 786440 | tf_op jit(solution)/shard_map/ppermute | solution.py:993
  193.6 19.4 %collective-permute-start.47 = (bf16[9,256,128]{2,1,0:T(8,128)(2,1)S(1)}, bf16[9,256,128]{2,1,0:T(8,128)(2,1)S(1)}, u32[]{:S(2)}, u32[]{:S(2)}) collective-permute-start(bf16[9,256,128]{2,1,0:T(8,128)(2,1)S(1)} %get-tuple-element.426), channel_id=1, source_target_pairs={{0,4},{4,0},{8,12},{12,8},{16,20},{20,16},{24,28},{28,24},{1,5},{5... | collective-permute-start | bytes 1769480 | tf_op jit(solution)/shard_map/ppermute | solution.py:993
  195.2 32.3 %collective-permute-start.51 = (bf16[2,1024,128]{2,1,0:T(8,128)(2,1)S(1)}, bf16[2,1024,128]{2,1,0:T(8,128)(2,1)S(1)}, u32[]{:S(2)}, u32[]{:S(2)}) collective-permute-start(bf16[2,1024,128]{2,1,0:T(8,128)(2,1)S(1)} %copy-done.22), channel_id=1, source_target_pairs={{0,2},{1,3},{2,0},{3,1},{4,6},{5,7},{6,4},{7,5},{8,10},{9,11},{10,... | collective-permute-start | bytes 1572872 | tf_op jit(solution)/shard_map/ppermute | solution.py:993
  213.6 13.9 %collective-permute-start.50 = (bf16[9,128,128]{2,1,0:T(8,128)(2,1)S(1)}, bf16[9,128,128]{2,1,0:T(8,128)(2,1)S(1)}, u32[]{:S(2)}, u32[]{:S(2)}) collective-permute-start(bf16[9,128,128]{2,1,0:T(8,128)(2,1)S(1)} %get-tuple-element.437), channel_id=1, source_target_pairs={{0,8},{4,12},{8,0},{12,4},{16,24},{20,28},{24,16},{28,20},{1,9},{5... | collective-permute-start | bytes 884744 | tf_op jit(solution)/shard_map/ppermute | solution.py:993
  213.7 13.8 %collective-permute-start.48 = (bf16[4,128,128]{2,1,0:T(8,128)(2,1)S(1)}, bf16[4,128,128]{2,1,0:T(8,128)(2,1)S(1)}, u32[]{:S(2)}, u32[]{:S(2)}) collective-permute-start(bf16[4,128,128]{2,1,0:T(8,128)(2,1)S(1)} %join.6.refs_0_), channel_id=1, source_target_pairs={{0,8},{4,12},{8,0},{12,4},{16,24},{20,28},{24,16},{28,20},{1,9},{5... | collective-permute-start | bytes 393224 | tf_op jit(solution)/shard_map/ppermute | solution.py:993
  227.5 20.1 %collective-permute-start.56 = (bf16[2,1056,128]{2,1,0:T(8,128)(2,1)S(1)}, bf16[2,1056,128]{2,1,0:T(8,128)(2,1)S(1)}, u32[]{:S(2)}, u32[]{:S(2)}) collective-permute-start(bf16[2,1056,128]{2,1,0:T(8,128)(2,1)S(1)} %get-tuple-element.460), channel_id=1, source_target_pairs={{0,2},{1,3},{2,0},{3,1},{4,6},{5,7},{6,4},{7,5},{8,10},{9,11},{10,... | collective-permute-start | bytes 1622024 | tf_op jit(solution)/shard_map/ppermute | solution.py:993
  241.6 16.1 %collective-permute-start.60 = (bf16[9,256,128]{2,1,0:T(8,128)(2,1)S(1)}, bf16[9,256,128]{2,1,0:T(8,128)(2,1)S(1)}, u32[]{:S(2)}, u32[]{:S(2)}) collective-permute-start(bf16[9,256,128]{2,1,0:T(8,128)(2,1)S(1)} %join.11.mine), channel_id=1, source_target_pairs={{0,4},{4,0},{8,12},{12,8},{16,20},{20,16},{24,28},{28,24},{1,5},{5... | collective-permute-start | bytes 1769480 | tf_op jit(solution)/shard_map/ppermute | solution.py:993
  262.0 19.5 %collective-permute-start.66 = (bf16[9,256,128]{2,1,0:T(8,128)(2,1)S(1)}, bf16[9,256,128]{2,1,0:T(8,128)(2,1)S(1)}, u32[]{:S(2)}, u32[]{:S(2)}) collective-permute-start(bf16[9,256,128]{2,1,0:T(8,128)(2,1)S(1)} %join.10.mine), channel_id=1, source_target_pairs={{0,4},{4,0},{8,12},{12,8},{16,20},{20,16},{24,28},{28,24},{1,5},{5... | collective-permute-start | bytes 1769480 | tf_op jit(solution)/shard_map/ppermute | solution.py:993
  266.0 17.6 %collective-permute-start.64 = (bf16[2,1024,128]{2,1,0:T(8,128)(2,1)S(1)}, bf16[2,1024,128]{2,1,0:T(8,128)(2,1)S(1)}, u32[]{:S(2)}, u32[]{:S(2)}) collective-permute-start(bf16[2,1024,128]{2,1,0:T(8,128)(2,1)S(1)} %collective-permute-done.51.far), channel_id=1, source_target_pairs={{0,1},{1,0},{2,3},{3,2},{4,5},{5,4},{6,7},{7,6},{8,9},{9,8},{10,11... | collective-permute-start | bytes 1572872 | tf_op jit(solution)/shard_map/ppermute | solution.py:993
  267.5 16.1 %collective-permute-start.63 = (bf16[1024,128]{1,0:T(8,128)(2,1)S(1)}, bf16[1024,128]{1,0:T(8,128)(2,1)S(1)}, u32[]{:S(2)}, u32[]{:S(2)}) collective-permute-start(bf16[1024,128]{1,0:T(8,128)(2,1)S(1)} %copy-done.24), channel_id=1, source_target_pairs={{0,1},{1,0},{2,3},{3,2},{4,5},{5,4},{6,7},{7,6},{8,9},{9,8},{10,11... | collective-permute-start | bytes 786440 | tf_op jit(solution)/shard_map/ppermute | solution.py:993
  (65 other events, 533.6 us)

commit v5 on v4

--- a/solution.py
+++ b/solution.py
@@ -341,7 +341,7 @@
     alive = meta[1].astype(F32)
     cot_copies = fetch((c0, c1, c2, c3), cot, me, sems, 0)
     scale = 1.0 / math.sqrt(HEAD)
-    block = 256
+    block = 1024
 
     row32 = lax.broadcasted_iota(jnp.int32, (32, LANES), 0)
     lane32 = lax.broadcasted_iota(jnp.int32, (32, LANES), 1)
@@ -814,39 +814,51 @@
     scale[...] = jnp.broadcast_to(1.0 / total, (8, LANES))
 
 
-def kernel_factor_grads(meta, scale, factors0, factors1, small0, small1, embed, context, vectors):
-    me = meta[0]
-    groups = factors0.shape[0]
+def kernel_factors(meta, factors0, factors1, left):
+    conditions, tokens = [], []
+    for factors in (factors0, factors1):
+        for g in range(factors.shape[0]):
+            for k in range(4):
+                rows = factors[g, jnp.bitwise_xor(meta[0], k)].astype(F32)
+                conditions.append(rows[0:1])
+                tokens.append(rows[CTX : 2 * CTX])
+    rest = left.shape[1] - 5 * len(conditions)
+    rows = tokens + conditions
+    if rest:
+        rows.append(jnp.zeros((rest, EMB), F32))
+    left[...] = jnp.concatenate(rows, axis=0).T.astype(BF16)
+
+
+def kernel_factor_grads(scale, left, small0, small1, embed, context, vectors):
     inverse = scale[0:1, :]
     total = jnp.zeros((S_ROWS, LANES), F32)
+    scales, shifts, keys, values = [], [], [], []
     for small in (small0, small1):
-        for g in range(4 * groups):
-            total = total + small[g].astype(F32)
+        for k in range(small.shape[0]):
+            term = small[k].astype(F32)
+            total = total + term
+            scales.append(term[S_SCALE : S_SCALE + 1])
+            shifts.append(term[S_SHIFT : S_SHIFT + 1])
+            keys.append(term[S_KEY : S_KEY + CTX])
+            values.append(term[S_VALUE : S_VALUE + CTX])
     vectors[...] = total * inverse
-    over_rows = (((0,), (0,)), ((), ()))
-    conditions, tokens, scales, shifts, keys, values = [], [], [], [], [], []
-    for factors, small in ((factors0, small0), (factors1, small1)):
-        for g in range(groups):
-            for k in range(4):
-                rows = factors[g, jnp.bitwise_xor(me, k)].astype(F32)
-                term = small[4 * g + k].astype(F32)
-                conditions.append(rows[0:1])
-                tokens.append(rows[CTX : 2 * CTX])
-                scales.append(term[S_SCALE : S_SCALE + 1])
-                shifts.append(term[S_SHIFT : S_SHIFT + 1])
-                keys.append(term[S_KEY : S_KEY + CTX])
-                values.append(term[S_VALUE : S_VALUE + CTX])
-    for lefts, pairs, target in (
-        (conditions, (scales, shifts), embed),
-        (tokens, (keys, values), context),
-    ):
-        left = jnp.concatenate(lefts, axis=0).astype(BF16)
-        right = jnp.concatenate(
-            [jnp.concatenate(parts, axis=0).astype(BF16) for parts in pairs], axis=1
-        )
-        grad = lax.dot_general(left, right, over_rows, preferred_element_type=F32)
-        for place in range(2):
-            target[:, place, :] = grad[:, place * LANES : (place + 1) * LANES] * inverse
+    images = len(scales)
+    rest = left.shape[1] - 5 * images
+    none = jnp.zeros((4 * images, LANES), F32)
+    columns = []
+    for parts in (keys, values):
+        whole = [jnp.concatenate(parts, axis=0), jnp.zeros((images + rest, LANES), F32)]
+        columns.append(jnp.concatenate(whole, axis=0))
+    for parts in (scales, shifts):
+        whole = [none] + parts
+        if rest:
+            whole.append(jnp.zeros((rest, LANES), F32))
+        columns.append(jnp.concatenate(whole, axis=0))
+    right = jnp.concatenate(columns, axis=1).astype(BF16)
+    grad = jnp.dot(left[...], right, preferred_element_type=F32)
+    for place in range(2):
+        context[:, place, :] = grad[:, place * LANES : (place + 1) * LANES] * inverse
+        embed[:, place, :] = grad[:, (place + 2) * LANES : (place + 3) * LANES] * inverse
 
 
 def kernel_stack(*refs):
@@ -1204,6 +1216,7 @@
             turned_scratch,
             pltpu.SemaphoreType.DMA((4,)),
         ],
+        limit=30,
     )(meta, qkv, pack, middle, proj_w, *cots)
 
     def weight_send(sources, gradients):
@@ -1248,11 +1261,8 @@
         [smem()] + [vmem()] * 4,
         [pltpu.VMEM((4, LANES, pixels), BF16)],
     )(meta, dqkv, mixed, attn_t, cot)
-    dqkv, att_send, second_y, first_y, second_c, first_c, factors = tie(
-        dqkv, att_send, second_y, first_y, second_c, first_c, factors
-    )
+    dqkv, att_send, second_y, second_c, factors = tie(dqkv, att_send, second_y, second_c, factors)
     second_d = swap(second_y, "mp", 1)
-    first_d = swap(first_y, "mp", 1)
     att = [att_keep.reshape(8, C, LANES), swap(att_send, "mp", 1).reshape(8, C, LANES)]
     dmiddle, field2, sums, *gradients2 = call(
         kernel_back_attention,
@@ -1261,9 +1271,11 @@
         [smem()] + [vmem()] * 6,
         [grad_scratch],
     )(meta, dqkv, cot, middle, pack, dctx, qkv_w)
-    gradients2, second_d, first_d, att, field2 = tie(gradients2, second_d, first_d, att, field2)
+    gradients2, second_d, first_y, first_c, att, field2 = tie(
+        gradients2, second_d, first_y, first_c, att, field2
+    )
+    first_d = swap(first_y, "mp", 1)
     seconds = (second_t, second_c, second_y, second_d)
-    firsts = (first_t, first_c, first_y, first_d)
     gradients2 = exchange(gradients2)
     att = down(att, 0)
     field2, att[0] = tie(field2, att[0])
@@ -1275,7 +1287,8 @@
         [rest_scratch, grad_scratch, pltpu.SemaphoreType.DMA((8,))],
         limit=20,
     )(meta, field2, inner, pack, sums, *rest)
-    gradients1, gradients2, att = tie(gradients1, gradients2, att)
+    gradients1, gradients2, att, first_d = tie(gradients1, gradients2, att, first_d)
+    firsts = (first_t, first_c, first_y, first_d)
     gradients1 = exchange(gradients1)
     att = down(att, 1)
     gradients2, att[0] = tie(gradients2, att[0])
@@ -1336,7 +1349,17 @@
     grad_far, terms2, got1, own1 = tie(grad_far, terms2, got1, own1)
     terms1 = down([own1, got1], 1)
     ends2 = across(inner_levels(terms2), 2)
-    grad_far, ends2[0], terms1[0], att = tie(grad_far, ends2[0], terms1[0], att)
+    factors, ends2[0], terms1[0] = tie(factors, ends2[0], terms1[0])
+    columns = -(-5 * slots * lax.axis_size("dp") // LANES) * LANES
+    left = call(
+        kernel_factors,
+        "factors",
+        struct((EMB, columns), BF16),
+        [smem()] + [vmem()] * 2,
+        [],
+        limit=12 if len(steps) < 4 else 56,
+    )(meta, *factors)
+    grad_far, ends2[0], terms1[0], att, left = tie(grad_far, ends2[0], terms1[0], att, left)
     att = across(join(att, digits[1], meta), 0)
     grad_far = swap(grad_far, "mp", 2)
     ends2, terms1, grad_near, out_far = tie(ends2, terms1, grad_near, out_far)
@@ -1353,8 +1376,6 @@
     grad_near = swap(grad_near, "mp", 1)
     grad_across = swap(grad_far, "mp", 1)
     image_parts = (grad_own, grad_near, grad_far, grad_across)
-    ends1 = across(join(ends1, digits[1], meta), 0)
-    ends1[0], grad_across, grad_near, ends2 = tie(ends1[0], grad_across, grad_near, ends2)
     smalls = call(
         kernel_small_stack,
         "stack",
@@ -1364,27 +1385,15 @@
         limit=8,
     )(grad_own, grad_near, grad_far, grad_across)
     small_got = swap(smalls, "dp", 1)
-    (conv2_grad,) = last_join(ends2, digits[0], meta, scale)
-    small_got, conv2_grad = tie(small_got, conv2_grad)
+    ends1 = across(join(ends1, digits[1], meta), 0)
+    ends1[0], small_got, ends2 = tie(ends1[0], small_got, ends2)
     smalls = stack([smalls, small_got])
     for low in steps[1:-1]:
         smalls = stack([smalls, swap(smalls, "dp", low)])
     small_got = swap(smalls, "dp", steps[-1])
-    smalls, out_far, out_near = tie(smalls, out_far, out_near)
+    (conv2_grad,) = last_join(ends2, digits[0], meta, scale)
+    smalls, out_far, out_near, conv2_grad = tie(smalls, out_far, out_near, conv2_grad)
     out_parts = (out_own, swap(out_near, "mp", 1), out_far, swap(out_far, "mp", 1))
-    embed_grad, context_grad, vector_sums = call(
-        kernel_factor_grads,
-        "factor_grads",
-        [
-            struct((EMB, 2, LANES), F32),
-            struct((EMB, 2, LANES), F32),
-            struct((S_ROWS, LANES), F32),
-        ],
-        [smem()] + [vmem()] * 5,
-        [],
-        limit=12 if len(steps) < 4 else 56,
-    )(meta, scale, *factors, smalls, small_got)
-
     def in_slots(parts):
         return pl.pallas_call(
             kernel_slots,
@@ -1398,6 +1407,21 @@
 
     block_out = in_slots(out_parts)
     image_grad = in_slots(image_parts)
+    small_got, block_out, image_grad = tie(small_got, block_out, image_grad)
+    embed_grad, context_grad, vector_sums = call(
+        kernel_factor_grads,
+        "factor_grads",
+        [
+            struct((EMB, 2, LANES), F32),
+            struct((EMB, 2, LANES), F32),
+            struct((S_ROWS, LANES), F32),
+        ],
+        [vmem()] * 4,
+        [],
+        limit=14 if len(steps) < 4 else 56,
+    )(scale, left, smalls, small_got)
+
+    ends1, embed_grad = tie(ends1, embed_grad)
     (conv1_grad,) = last_join(ends1, digits[0], meta, scale)
     return (
         block_out,

time: 286 us -> 275 us (0.962)
  Pallas kernels: 143 us -> 137 us
  starting transfers between devices: 51.7 us -> 45.9 us
    pallas_call x1, Pallas kernels: 40 us -> 33.8 us  [local(): call(kernel_attention, 'attention', [piece, piece, pair_piece] + [block,...]
    ppermute x67, starting transfers between devices: 51.7 us -> 45.9 us  [swap(): return lax.ppermute(value, axis, [(i, i ^ offset) for i in range(size)])]
  transfers between devices with their start and end apart: 67 -> 67, of which waited for: 21 -> 22; matrix products, arithmetic and copies ran while one was open for 3% -> 3% of each run, Pallas kernels for 49% -> 49%
where the time goes in v5:
time: 275 us
  Pallas kernels  137 us (50%)
  waiting for transfers between devices  78.7 us (29%)
  starting transfers between devices  45.9 us (17%)
  local copies, waits for them, and re-layouts  6.53 us (2%)
  other arithmetic  2.77 us (1%)
    ppermute x67, waiting for transfers between devices, swap(): return lax.ppermute(value, axis, [(i, i ^ offset) for i in range(size)])  78.7 us
    ppermute x67, starting transfers between devices, swap(): return lax.ppermute(value, axis, [(i, i ^ offset) for i in range(size)])  45.9 us
    pallas_call x1, Pallas kernels, local(): call(kernel_attention, 'attention', [piece, piece, pair_piece] + [block,...  33.8 us
    pallas_call x1, Pallas kernels, local(): call(kernel_second, 'second', [block32, turned, struct((4, pixels, 3 * LA...  13.3 us
    pallas_call x1, Pallas kernels, local(): call(kernel_first, 'first', [block, struct((4, E_ROWS, LANES), F32), turn...  12.7 us
    pallas_call x1, Pallas kernels, local(): call(kernel_back_second, 'back_second', [fields, struct((4, S_ROWS, LANES...  12.5 us
    pallas_call x2, Pallas kernels, weight_send(): call(kernel_weight_send, 'weight_send', [struct((9, C // 2, LANES), BF16)...  9.61 us
    pallas_call x2, Pallas kernels, weight_own(): call(kernel_weight_own, 'weight_own', struct((9, C // 2, LANES), F32), [s...  8.42 us
  transfers between devices with their start and end apart: 67, of which 22 were waited for; matrix products, arithmetic and copies ran while one was open for 3% of the time, Pallas kernels for 49%

profile of v5, /device:TPU:0, one launch (start us, length us, event | category | flops | bytes accessed | tf_op | source)
XLA Modules:
  0.0 275.1 jit_solution(9969645368921894965)
XLA Ops:
  3.8 2.1 constant_dynamic-slice_fusion.2
  5.9 3.0 %collective-permute-start.2 = (bf16[2304,128]{1,0:T(8,128)(2,1)}, bf16[2304,128]{1,0:T(8,128)(2,1)S(1)}, u32[]{:S(2)}, u32[]{:S(2)}) collective-permute-start(bf16[2304,128]{1,0:T(8,128)(2,1)} %constant_dynamic-slice_fusion.3), channel_id=1, source_target_pairs={{0,2},{1,3},{2,0},{3,1},{4,6},{5,7},{6,4},{7,5},{8,10},{9,11},{10,... | collective-permute-start | bytes 1769480 | tf_op jit(solution)/shard_map/ppermute | solution.py:1005
  14.7 8.5 %collective-permute-done.2.source.w2 = bf16[2304,128]{1,0:T(8,128)(2,1)S(1)} collective-permute-done((bf16[2304,128]{1,0:T(8,128)(2,1)}, bf16[2304,128]{1,0:T(8,128)(2,1)S(1)}, u32[]{:S(2)}, u32[]{:S(2)}) %collective-permute-start.2) | collective-permute-done | bytes 589856 | tf_op jit(solution)/shard_map/ppermute | solution.py:1005
  23.3 2.2 collective-permute-start.7
  27.2 4.0 %collective-permute-done.7.w4 = bf16[1152,128]{1,0:T(8,128)(2,1)S(1)} collective-permute-done((bf16[1152,128]{1,0:T(8,128)(2,1)S(1)}, bf16[1152,128]{1,0:T(8,128)(2,1)S(1)}, u32[]{:S(2)}, u32[]{:S(2)}) %collective-permute-start.7) | collective-permute-done | bytes 294944 | tf_op jit(solution)/shard_map/ppermute | solution.py:1005
  41.1 12.7 %first.1 = (bf16[4,1024,128]{2,1,0:T(8,128)(2,1)S(1)}, f32[4,32,128]{2,1,0:T(8,128)S(1)}, bf16[4,128,1024]{2,1,0:T(8,128)(2,1)S(1)}, f32[4,1024,128]{2,1,0:T(8,1...) custom-call(s32[6]{0:T(128)S(1)} %stack.36.meta, bf16[1024,128]{1,0:T(8,128)(2,1)S(1)} %copy-done.23, ...), custom_call_target="tpu_custom_call" | custom-call | tf_op jit(solution)/shard_map/first/pallas_call | solution.py:1161
  53.9 4.1 %collective-permute-done.13.source.w2 = bf16[3328,128]{1,0:T(8,128)(2,1)S(1)} collective-permute-done((bf16[3328,128]{1,0:T(8,128)(2,1)S(1)}, bf16[3328,128]{1,0:T(8,128)(2,1)S(1)}, u32[]{:S(2)}, u32[]{:S(2)}) %collective-permute-start.13) | collective-permute-done | bytes 852000 | tf_op jit(solution)/shard_map/ppermute | solution.py:1005
  60.4 9.1 %collective-permute-done.16.w3 = bf16[1664,128]{1,0:T(8,128)(2,1)S(1)} collective-permute-done((bf16[1664,128]{1,0:T(8,128)(2,1)S(1)}, bf16[1664,128]{1,0:T(8,128)(2,1)S(1)}, u32[]{:S(2)}, u32[]{:S(2)}) %collective-permute-start.16) | collective-permute-done | bytes 426016 | tf_op jit(solution)/shard_map/ppermute | solution.py:1005
  73.7 13.3 %second.1 = (f32[4,1024,128]{2,1,0:T(8,128)S(1)}, bf16[4,128,1024]{2,1,0:T(8,128)(2,1)S(1)}, bf16[4,1024,384]{2,1,0:T(8,128)(2,1)S(1)}, bf16[4,1536,128]{2,1,0:T(8,128)(2,1)S(1)}, bf16[4,512,128]{2,1,0:T(8,128)(2,1)S(1)}) custom-call(s32[6]{0:T(128)S(1)} %stack.36.meta, bf16[3,4,1088,128]{3,2,1,0:T(8,128)(2,1)S(1)} %get-tuple-element.296.second, ...), custom_call_target="tpu_custom_call" | custom-call | tf_op jit(solution)/shard_map/second/pallas_call | solution.py:1176
  89.9 2.7 collective-permute-start.27
  93.1 33.8 %attention.1 = (bf16[1024,128]{1,0:T(8,128)(2,1)S(1)}, bf16[1024,128]{1,0:T(8,128)(2,1)S(1)}, bf16[2,1024,128]{2,1,0:T(8,128)(2,1)S(1)}, bf16[4,1024,128]{2,1,0:...) custom-call(s32[6]{0:T(128)S(1)} %stack.36.meta, ...), custom_call_target="tpu_custom_call" | custom-call | tf_op jit(solution)/shard_map/attention/pallas_call | solution.py:1201
  126.9 5.6 %attention_grad.1 = (bf16[2,4,512,128]{3,2,1,0:T(8,128)(2,1)S(1)}, bf16[2,4,512,128]{3,2,1,0:T(8,128)(2,1)S(1)}) custom-call(s32[6]{0:T(128)S(1)} %stack.36.meta, bf16[4,1024,384]{2,1,0:T(8,128)(2,1)S(1)} %get-tuple-element.333.dqkv, bf16[4,1024,128]{2,1,0:T(8,128)(2,1)S(1)} %get-tuple-element.325.mixed, ...), custom_call_target="tpu_custom_call" | custom-call | tf_op jit(solution)/shard_map/attention_grad/pallas_call | solution.py:1257
  133.2 5.7 %back_attention.1 = (f32[4,1024,128]{2,1,0:T(8,128)S(1)}, bf16[3,4,1088,128]{3,2,1,0:T(8,128)(2,1)S(1)}, f32[4,32,128]{2,1,0:T(8,128)S(1)}, bf16[1024,128]{1,0:T...) custom-call(s32[6]{0:T(128)S(1)} %stack.36.meta, ...), custom_call_target="tpu_custom_call" | custom-call | tf_op jit(solution)/shard_map/back_attention/pallas_call | solution.py:1267
  143.3 12.5 %back_second.1 = (bf16[3,4,1088,128]{3,2,1,0:T(8,128)(2,1)S(1)}, f32[4,32,128]{2,1,0:T(8,128)S(1)}, bf16[1024,128]{1,0:T(8,128)(2,1)S(1)}, bf16[1024,128]{1,0:T(...) custom-call(s32[6]{0:T(128)S(1)} %stack.36.meta, ...), custom_call_target="tpu_custom_call" | custom-call | tf_op jit(solution)/shard_map/back_second/pallas_call | solution.py:1282
  157.8 4.8 %weight_send.2 = (bf16[9,256,128]{2,1,0:T(8,128)(2,1)S(1)}, bf16[3,4,1088,128]{3,2,1,0:T(8,128)(2,1)S(1)}) custom-call(s32[6]{0:T(128)S(1)} %stack.36.meta, bf16[4,128,1024]{2,1,0:T(8,128)(2,1)S(1)} %get-tuple-element.316.u0, bf16[4,128,1024]{2,1,0:T(8,128)(2,1)S(1)} %collective-permute-done.26.u1, bf16[4,128,1024]{2,1,0:T(8,128)(2,1)S(1)} %collective-permute-done.25.u2, ...), custom_call_target="tpu_custom_call" | custom-call | tf_op jit(solution)/shard_map/weight_send/pallas_call | solution.py:1223
  166.5 4.2 %weight_own.2.refs_0_ = f32[9,256,128]{2,1,0:T(8,128)S(1)} custom-call(s32[6]{0:T(128)S(1)} %stack.36.meta, bf16[4,128,1024]{2,1,0:T(8,128)(2,1)S(1)} %get-tuple-element.316.u0, bf16[4,128,1024]{2,1,0:T(8,128)(2,1)S(1)} %collective-permute-done.26.u1, bf16[4,128,1024]{2,1,0:T(8,128)(2,1)S(1)} %collective-permute-done.25.u2, ...), custom_call_target="tpu_custom_call" | custom-call | tf_op jit(solution)/shard_map/weight_own/pallas_call | solution.py:1233
  170.7 4.8 %collective-permute-done.38.got = bf16[8,64,128]{2,1,0:T(8,128)(2,1)S(1)} collective-permute-done((bf16[8,64,128]{2,1,0:T(8,128)(2,1)S(1)}, bf16[8,64,128]{2,1,0:T(8,128)(2,1)S(1)}, u32[]{:S(2)}, u32[]{:S(2)}) %collective-permute-start.38) | collective-permute-done | bytes 131104 | tf_op jit(solution)/shard_map/ppermute | solution.py:1005
  177.1 7.3 %back_conv.1.grad_in = f32[4,1024,128]{2,1,0:T(8,128)S(1)} custom-call(s32[6]{0:T(128)S(1)} %stack.36.meta, bf16[3,4,1088,128]{3,2,1,0:T(8,128)(2,1)S(1)} %get-tuple-element.389.grad_field, bf16[4608,128]{1,0:T(8,128)(2,1)S(1)} %bitcast.83, bf16[4608,128]{1,0:T(8,128)(2,1)S(1)} %collective-permute-done.w1, ...), custom_call_target="tpu_custom_call" | custom-call | tf_op jit(solution)/shard_map/back_conv/pallas_call | solution.py:1314
  184.5 4.8 %weight_send.3 = (bf16[9,256,128]{2,1,0:T(8,128)(2,1)S(1)}, bf16[3,4,1088,128]{3,2,1,0:T(8,128)(2,1)S(1)}) custom-call(s32[6]{0:T(128)S(1)} %stack.36.meta, bf16[4,128,1024]{2,1,0:T(8,128)(2,1)S(1)} %get-tuple-element.340.u0, bf16[4,128,1024]{2,1,0:T(8,128)(2,1)S(1)} %collective-permute-done.30.u1, bf16[4,128,1024]{2,1,0:T(8,128)(2,1)S(1)} %collective-permute-done.29.u2, ...), custom_call_target="tpu_custom_call" | custom-call | tf_op jit(solution)/shard_map/weight_send/pallas_call | solution.py:1223
  192.9 4.2 %weight_own.3.refs_0_ = f32[9,256,128]{2,1,0:T(8,128)S(1)} custom-call(s32[6]{0:T(128)S(1)} %stack.36.meta, bf16[4,128,1024]{2,1,0:T(8,128)(2,1)S(1)} %get-tuple-element.340.u0, bf16[4,128,1024]{2,1,0:T(8,128)(2,1)S(1)} %collective-permute-done.30.u1, bf16[4,128,1024]{2,1,0:T(8,128)(2,1)S(1)} %collective-permute-done.29.u2, ...), custom_call_target="tpu_custom_call" | custom-call | tf_op jit(solution)/shard_map/weight_own/pallas_call | solution.py:1233
  198.0 2.2 collective-permute-done.44.refs_1_
  202.7 4.2 %back_first.1 = (bf16[1056,128]{1,0:T(8,128)(2,1)S(1)}, bf16[1056,128]{1,0:T(8,128)(2,1)S(1)}, bf16[2,1056,128]{2,1,0:T(8,128)(2,1)S(1)}) custom-call(s32[6]{0:T(128)S(1)} %stack.36.meta, f32[4,1024,128]{2,1,0:T(8,128)S(1)} %back_conv.1.grad_in, bf16[4,1024,128]{2,1,0:T(8,128)(2,1)S(1)} %get-tuple-element.297.image, ...), custom_call_target="tpu_custom_call" | custom-call | tf_op jit(solution)/shard_map/back_first/pallas_call | solution.py:1338
  208.6 2.0 collective-permute-start.48
  212.4 9.7 %collective-permute-done.48.refs_1_ = bf16[4,128,128]{2,1,0:T(8,128)(2,1)S(1)} collective-permute-done((bf16[4,128,128]{2,1,0:T(8,128)(2,1)S(1)}, bf16[4,128,128]{2,1,0:T(8,128)(2,1)S(1)}, u32[]{:S(2)}, u32[]{:S(2)}) %collective-permute-start.48) | collective-permute-done | bytes 131104 | tf_op jit(solution)/shard_map/ppermute | solution.py:1005
  227.8 3.4 %collective-permute-done.54.other = bf16[4,256,128]{2,1,0:T(8,128)(2,1)S(1)} collective-permute-done((bf16[4,256,128]{2,1,0:T(8,128)(2,1)S(1)}, bf16[4,256,128]{2,1,0:T(8,128)(2,1)S(1)}, u32[]{:S(2)}, u32[]{:S(2)}) %collective-permute-start.54) | collective-permute-done | bytes 262176 | tf_op jit(solution)/shard_map/ppermute | solution.py:1005
  231.2 5.9 %collective-permute-done.53.refs_1_ = bf16[9,64,128]{2,1,0:T(8,128)(2,1)S(1)} collective-permute-done((bf16[9,64,128]{2,1,0:T(8,128)(2,1)S(1)}, bf16[9,64,128]{2,1,0:T(8,128)(2,1)S(1)}, u32[]{:S(2)}, u32[]{:S(2)}) %collective-permute-start.53) | collective-permute-done | bytes 147488 | tf_op jit(solution)/shard_map/ppermute | solution.py:1005
  239.5 3.7 %collective-permute-done.55.refs_1_ = bf16[9,64,128]{2,1,0:T(8,128)(2,1)S(1)} collective-permute-done((bf16[9,64,128]{2,1,0:T(8,128)(2,1)S(1)}, bf16[9,64,128]{2,1,0:T(8,128)(2,1)S(1)}, u32[]{:S(2)}, u32[]{:S(2)}) %collective-permute-start.55) | collective-permute-done | bytes 147488 | tf_op jit(solution)/shard_map/ppermute | solution.py:1005
  246.4 6.9 %collective-permute-done.59.refs_1_ = bf16[9,128,128]{2,1,0:T(8,128)(2,1)S(1)} collective-permute-done((bf16[9,128,128]{2,1,0:T(8,128)(2,1)S(1)}, bf16[9,128,128]{2,1,0:T(8,128)(2,1)S(1)}, u32[]{:S(2)}, u32[]{:S(2)}) %collective-permute-start.59) | collective-permute-done | bytes 294944 | tf_op jit(solution)/shard_map/ppermute | solution.py:1005
  254.6 2.1 last_join.4
  262.8 5.1 %collective-permute-done.63.small1 = bf16[16,32,128]{2,1,0:T(8,128)(2,1)S(1)} collective-permute-done((bf16[16,32,128]{2,1,0:T(8,128)(2,1)S(1)}, bf16[16,32,128]{2,1,0:T(8,128)(2,1)S(1)}, u32[]{:S(2)}, u32[]{:S(2)}) %collective-permute-start.63) | collective-permute-done | bytes 131104 | tf_op jit(solution)/shard_map/ppermute | solution.py:1005
  267.8 4.6 %factor_grads.1 = (f32[2048,2,128]{2,1,0:T(2,128)}, f32[2048,2,128]{2,1,0:T(2,128)}, f32[32,128]{1,0:T(8,128)S(1)}) custom-call(f32[8,128]{1,0:T(8,128)S(1)} %scale.1, bf16[2048,256]{1,0:T(8,128)(2,1)S(1)} %factors.1.left, bf16[16,32,128]{2,1,0:T(8,128)(2,1)S(1)} %stack.42.small0, bf16[16,32,128]{2,1,0:T(8,128)(2,1)S(1)} %collective-permute-done.63.small1), custom_call_target="tpu_custom_call" | custom-call | tf_op jit(solution)/shard_map/factor_grads/pallas_call | solution.py:1411
  273.0 2.1 last_join.5
  (255 shorter events, 71.5 us)
Async XLA Ops:
  1.4 21.8 %collective-permute-start = (bf16[4608,128]{1,0:T(8,128)(2,1)}, bf16[4608,128]{1,0:T(8,128)(2,1)S(1)}, u32[]{:S(2)}, u32[]{:S(2)}) collective-permute-start(bf16[4608,128]{1,0:T(8,128)(2,1)} %bitcast.80), channel_id=1, source_target_pairs={{0,1},{1,0},{2,3},{3,2},{4,5},{5,4},{6,7},{7,6},{8,9},{9,8},{10,11... | collective-permute-start | bytes 3538952 | tf_op jit(solution)/shard_map/ppermute | solution.py:1005
  5.9 17.3 %collective-permute-start.2 = (bf16[2304,128]{1,0:T(8,128)(2,1)}, bf16[2304,128]{1,0:T(8,128)(2,1)S(1)}, u32[]{:S(2)}, u32[]{:S(2)}) collective-permute-start(bf16[2304,128]{1,0:T(8,128)(2,1)} %constant_dynamic-slice_fusion.3), channel_id=1, source_target_pairs={{0,2},{1,3},{2,0},{3,1},{4,6},{5,7},{6,4},{7,5},{8,10},{9,11},{10,... | collective-permute-start | bytes 1769480 | tf_op jit(solution)/shard_map/ppermute | solution.py:1005
  9.7 24.4 %collective-permute-start.3 = (bf16[2,1024,128]{2,1,0:T(8,128)(2,1)}, bf16[2,1024,128]{2,1,0:T(8,128)(2,1)}, u32[]{:S(2)}, u32[]{:S(2)}) collective-permute-start(bf16[2,1024,128]{2,1,0:T(8,128)(2,1)} %pad_maximum_fusion.1), channel_id=1, source_target_pairs={{0,2},{1,3},{2,0},{3,1},{4,6},{5,7},{6,4},{7,5},{8,10},{9,11},{10,... | collective-permute-start | bytes 1572872 | tf_op jit(solution)/shard_map/ppermute | solution.py:1005
  36.5 21.4 %collective-permute-start.14 = (bf16[6656,128]{1,0:T(8,128)(2,1)S(1)}, bf16[6656,128]{1,0:T(8,128)(2,1)S(1)}, u32[]{:S(2)}, u32[]{:S(2)}) collective-permute-start(bf16[6656,128]{1,0:T(8,128)(2,1)S(1)} %pad_maximum_fusion.w0), channel_id=1, source_target_pairs={{0,1},{1,0},{2,3},{3,2},{4,5},{5,4},{6,7},{7,6},{8,9},{9,8},{10,11... | collective-permute-start | bytes 5111816 | tf_op jit(solution)/shard_map/ppermute | solution.py:1005
  36.6 21.4 %collective-permute-start.13 = (bf16[3328,128]{1,0:T(8,128)(2,1)S(1)}, bf16[3328,128]{1,0:T(8,128)(2,1)S(1)}, u32[]{:S(2)}, u32[]{:S(2)}) collective-permute-start(bf16[3328,128]{1,0:T(8,128)(2,1)S(1)} %constant_dynamic-slice_fusion), channel_id=1, source_target_pairs={{0,2},{1,3},{2,0},{3,1},{4,6},{5,7},{6,4},{7,5},{8,10},{9,11},{10,... | collective-permute-start | bytes 2555912 | tf_op jit(solution)/shard_map/ppermute | solution.py:1005
  38.4 15.6 %collective-permute-start.15 = (bf16[1,4,8,2048]{3,2,1,0:T(8,128)(2,1)S(1)}, bf16[1,4,8,2048]{3,2,1,0:T(8,128)(2,1)S(1)}, u32[]{:S(2)}, u32[]{:S(2)}) collective-permute-start(bf16[1,4,8,2048]{3,2,1,0:T(8,128)(2,1)S(1)} %fusion.9.refs_0_), channel_id=1, source_target_pairs={{0,4},{4,0},{8,12},{12,8},{16,20},{20,16},{24,28},{28,24},{1,5},{5... | collective-permute-start | bytes 393224 | tf_op jit(solution)/shard_map/ppermute | solution.py:1005
  60.4 13.3 %collective-permute-start.18 = (bf16[3328,128]{1,0:T(8,128)(2,1)S(1)}, bf16[3328,128]{1,0:T(8,128)(2,1)S(1)}, u32[]{:S(2)}, u32[]{:S(2)}) collective-permute-start(bf16[3328,128]{1,0:T(8,128)(2,1)S(1)} %collective-permute-done.13.source.w2), channel_id=1, source_target_pairs={{0,1},{1,0},{2,3},{3,2},{4,5},{5,4},{6,7},{7,6},{8,9},{9,8},{10,11... | collective-permute-start | bytes 2555912 | tf_op jit(solution)/shard_map/ppermute | solution.py:1005
  70.7 17.6 %collective-permute-start.22 = (bf16[1024,128]{1,0:T(8,128)(2,1)S(1)}, bf16[1024,128]{1,0:T(8,128)(2,1)S(1)}, u32[]{:S(2)}, u32[]{:S(2)}) collective-permute-start(bf16[1024,128]{1,0:T(8,128)(2,1)S(1)} %get-tuple-element.313), channel_id=1, source_target_pairs={{0,1},{1,0},{2,3},{3,2},{4,5},{5,4},{6,7},{7,6},{8,9},{9,8},{10,11... | collective-permute-start | bytes 786440 | tf_op jit(solution)/shard_map/ppermute | solution.py:1005
  71.2 17.1 %collective-permute-start.23 = (bf16[1024,128]{1,0:T(8,128)(2,1)S(1)}, bf16[1024,128]{1,0:T(8,128)(2,1)S(1)}, u32[]{:S(2)}, u32[]{:S(2)}) collective-permute-start(bf16[1024,128]{1,0:T(8,128)(2,1)S(1)} %get-tuple-element.314), channel_id=1, source_target_pairs={{0,2},{1,3},{2,0},{3,1},{4,6},{5,7},{6,4},{7,5},{8,10},{9,11},{10,... | collective-permute-start | bytes 786440 | tf_op jit(solution)/shard_map/ppermute | solution.py:1005
  72.8 15.5 %collective-permute-start.24 = (bf16[1024,128]{1,0:T(8,128)(2,1)S(1)}, bf16[1024,128]{1,0:T(8,128)(2,1)S(1)}, u32[]{:S(2)}, u32[]{:S(2)}) collective-permute-start(bf16[1024,128]{1,0:T(8,128)(2,1)S(1)} %get-tuple-element.315), channel_id=1, source_target_pairs={{0,3},{1,2},{2,1},{3,0},{4,7},{5,6},{6,5},{7,4},{8,11},{9,10},{10,... | collective-permute-start | bytes 786440 | tf_op jit(solution)/shard_map/ppermute | solution.py:1005
  72.9 15.4 %collective-permute-start.21 = (bf16[2,4,8,2048]{3,2,1,0:T(8,128)(2,1)S(1)}, bf16[2,4,8,2048]{3,2,1,0:T(8,128)(2,1)S(1)}, u32[]{:S(2)}, u32[]{:S(2)}) collective-permute-start(bf16[2,4,8,2048]{3,2,1,0:T(8,128)(2,1)S(1)} %stack.38.refs_0_), channel_id=1, source_target_pairs={{0,8},{4,12},{8,0},{12,4},{16,24},{20,28},{24,16},{28,20},{1,9},{5... | collective-permute-start | bytes 786440 | tf_op jit(solution)/shard_map/ppermute | solution.py:1005
  88.3 44.2 %collective-permute-start.25 = (bf16[4,128,1024]{2,1,0:T(8,128)(2,1)S(1)}, bf16[4,128,1024]{2,1,0:T(8,128)(2,1)S(1)}, u32[]{:S(2)}, u32[]{:S(2)}) collective-permute-start(bf16[4,128,1024]{2,1,0:T(8,128)(2,1)S(1)} %get-tuple-element.316.u0), channel_id=1, source_target_pairs={{0,2},{1,3},{2,0},{3,1},{4,6},{5,7},{6,4},{7,5},{8,10},{9,11},{10,... | collective-permute-start | bytes 3145736 | tf_op jit(solution)/shard_map/ppermute | solution.py:1005
  89.6 42.9 %collective-permute-start.26 = (bf16[4,128,1024]{2,1,0:T(8,128)(2,1)S(1)}, bf16[4,128,1024]{2,1,0:T(8,128)(2,1)S(1)}, u32[]{:S(2)}, u32[]{:S(2)}) collective-permute-start(bf16[4,128,1024]{2,1,0:T(8,128)(2,1)S(1)} %get-tuple-element.316.u0), channel_id=1, source_target_pairs={{0,1},{1,0},{2,3},{3,2},{4,5},{5,4},{6,7},{7,6},{8,9},{9,8},{10,11... | collective-permute-start | bytes 3145736 | tf_op jit(solution)/shard_map/ppermute | solution.py:1005
  89.9 42.6 %collective-permute-start.27 = (bf16[4,4,8,2048]{3,2,1,0:T(8,128)(2,1)S(1)}, bf16[4,4,8,2048]{3,2,1,0:T(8,128)(2,1)S(1)}, u32[]{:S(2)}, u32[]{:S(2)}) collective-permute-start(bf16[4,4,8,2048]{3,2,1,0:T(8,128)(2,1)S(1)} %stack.39.factors0), channel_id=1, source_target_pairs={{0,16},{4,20},{8,24},{12,28},{16,0},{20,4},{24,8},{28,12},{1,17},{... | collective-permute-start | bytes 1572872 | tf_op jit(solution)/shard_map/ppermute | solution.py:1005
  92.5 46.4 %collective-permute-start.29 = (bf16[4,128,1024]{2,1,0:T(8,128)(2,1)S(1)}, bf16[4,128,1024]{2,1,0:T(8,128)(2,1)S(1)}, u32[]{:S(2)}, u32[]{:S(2)}) collective-permute-start(bf16[4,128,1024]{2,1,0:T(8,128)(2,1)S(1)} %get-tuple-element.340.u0), channel_id=1, source_target_pairs={{0,2},{1,3},{2,0},{3,1},{4,6},{5,7},{6,4},{7,5},{8,10},{9,11},{10,... | collective-permute-start | bytes 3145736 | tf_op jit(solution)/shard_map/ppermute | solution.py:1005
  93.1 45.9 %collective-permute-start.30 = (bf16[4,128,1024]{2,1,0:T(8,128)(2,1)S(1)}, bf16[4,128,1024]{2,1,0:T(8,128)(2,1)S(1)}, u32[]{:S(2)}, u32[]{:S(2)}) collective-permute-start(bf16[4,128,1024]{2,1,0:T(8,128)(2,1)S(1)} %get-tuple-element.340.u0), channel_id=1, source_target_pairs={{0,1},{1,0},{2,3},{3,2},{4,5},{5,4},{6,7},{7,6},{8,9},{9,8},{10,11... | collective-permute-start | bytes 3145736 | tf_op jit(solution)/shard_map/ppermute | solution.py:1005
  139.0 16.9 %collective-permute-start.36 = (bf16[4,128,1024]{2,1,0:T(8,128)(2,1)S(1)}, bf16[4,128,1024]{2,1,0:T(8,128)(2,1)S(1)}, u32[]{:S(2)}, u32[]{:S(2)}) collective-permute-start(bf16[4,128,1024]{2,1,0:T(8,128)(2,1)S(1)} %collective-permute-done.29.u2), channel_id=1, source_target_pairs={{0,1},{1,0},{2,3},{3,2},{4,5},{5,4},{6,7},{7,6},{8,9},{9,8},{10,11... | collective-permute-start | bytes 3145736 | tf_op jit(solution)/shard_map/ppermute | solution.py:1005
  140.3 15.6 %collective-permute-start.35 = (bf16[8,256,128]{2,1,0:T(8,128)(2,1)S(1)}, bf16[8,256,128]{2,1,0:T(8,128)(2,1)S(1)}, u32[]{:S(2)}, u32[]{:S(2)}) collective-permute-start(bf16[8,256,128]{2,1,0:T(8,128)(2,1)S(1)} %get-tuple-element.361), channel_id=1, source_target_pairs={{0,4},{4,0},{8,12},{12,8},{16,20},{20,16},{24,28},{28,24},{1,5},{5... | collective-permute-start | bytes 1572872 | tf_op jit(solution)/shard_map/ppermute | solution.py:1005
  141.4 14.4 %collective-permute-start.32 = (bf16[1024,128]{1,0:T(8,128)(2,1)S(1)}, bf16[1024,128]{1,0:T(8,128)(2,1)S(1)}, u32[]{:S(2)}, u32[]{:S(2)}) collective-permute-start(bf16[1024,128]{1,0:T(8,128)(2,1)S(1)} %get-tuple-element.357), channel_id=1, source_target_pairs={{0,1},{1,0},{2,3},{3,2},{4,5},{5,4},{6,7},{7,6},{8,9},{9,8},{10,11... | collective-permute-start | bytes 786440 | tf_op jit(solution)/shard_map/ppermute | solution.py:1005
  141.4 14.4 %collective-permute-start.33 = (bf16[1024,128]{1,0:T(8,128)(2,1)S(1)}, bf16[1024,128]{1,0:T(8,128)(2,1)S(1)}, u32[]{:S(2)}, u32[]{:S(2)}) collective-permute-start(bf16[1024,128]{1,0:T(8,128)(2,1)S(1)} %get-tuple-element.358), channel_id=1, source_target_pairs={{0,2},{1,3},{2,0},{3,1},{4,6},{5,7},{6,4},{7,5},{8,10},{9,11},{10,... | collective-permute-start | bytes 786440 | tf_op jit(solution)/shard_map/ppermute | solution.py:1005
  142.4 13.5 %collective-permute-start.34 = (bf16[1024,128]{1,0:T(8,128)(2,1)S(1)}, bf16[1024,128]{1,0:T(8,128)(2,1)S(1)}, u32[]{:S(2)}, u32[]{:S(2)}) collective-permute-start(bf16[1024,128]{1,0:T(8,128)(2,1)S(1)} %get-tuple-element.359), channel_id=1, source_target_pairs={{0,3},{1,2},{2,1},{3,0},{4,7},{5,6},{6,5},{7,4},{8,11},{9,10},{10,... | collective-permute-start | bytes 786440 | tf_op jit(solution)/shard_map/ppermute | solution.py:1005
  162.6 27.3 %collective-permute-start.43 = (bf16[9,256,128]{2,1,0:T(8,128)(2,1)S(1)}, bf16[9,256,128]{2,1,0:T(8,128)(2,1)S(1)}, u32[]{:S(2)}, u32[]{:S(2)}) collective-permute-start(bf16[9,256,128]{2,1,0:T(8,128)(2,1)S(1)} %get-tuple-element.411), channel_id=1, source_target_pairs={{0,4},{4,0},{8,12},{12,8},{16,20},{20,16},{24,28},{28,24},{1,5},{5... | collective-permute-start | bytes 1769480 | tf_op jit(solution)/shard_map/ppermute | solution.py:1005
  163.6 20.8 %collective-permute-start.39 = (bf16[1024,128]{1,0:T(8,128)(2,1)S(1)}, bf16[1024,128]{1,0:T(8,128)(2,1)S(1)}, u32[]{:S(2)}, u32[]{:S(2)}) collective-permute-start(bf16[1024,128]{1,0:T(8,128)(2,1)S(1)} %get-tuple-element.391), channel_id=1, source_target_pairs={{0,1},{1,0},{2,3},{3,2},{4,5},{5,4},{6,7},{7,6},{8,9},{9,8},{10,11... | collective-permute-start | bytes 786440 | tf_op jit(solution)/shard_map/ppermute | solution.py:1005
  163.6 20.8 %collective-permute-start.40 = (bf16[1024,128]{1,0:T(8,128)(2,1)S(1)}, bf16[1024,128]{1,0:T(8,128)(2,1)S(1)}, u32[]{:S(2)}, u32[]{:S(2)}) collective-permute-start(bf16[1024,128]{1,0:T(8,128)(2,1)S(1)} %get-tuple-element.392), channel_id=1, source_target_pairs={{0,2},{1,3},{2,0},{3,1},{4,6},{5,7},{6,4},{7,5},{8,10},{9,11},{10,... | collective-permute-start | bytes 786440 | tf_op jit(solution)/shard_map/ppermute | solution.py:1005
  165.1 19.3 %collective-permute-start.41 = (bf16[1024,128]{1,0:T(8,128)(2,1)S(1)}, bf16[1024,128]{1,0:T(8,128)(2,1)S(1)}, u32[]{:S(2)}, u32[]{:S(2)}) collective-permute-start(bf16[1024,128]{1,0:T(8,128)(2,1)S(1)} %get-tuple-element.393), channel_id=1, source_target_pairs={{0,3},{1,2},{2,1},{3,0},{4,7},{5,6},{6,5},{7,4},{8,11},{9,10},{10,... | collective-permute-start | bytes 786440 | tf_op jit(solution)/shard_map/ppermute | solution.py:1005
  189.3 18.5 %collective-permute-start.47 = (bf16[9,256,128]{2,1,0:T(8,128)(2,1)S(1)}, bf16[9,256,128]{2,1,0:T(8,128)(2,1)S(1)}, u32[]{:S(2)}, u32[]{:S(2)}) collective-permute-start(bf16[9,256,128]{2,1,0:T(8,128)(2,1)S(1)} %get-tuple-element.434), channel_id=1, source_target_pairs={{0,4},{4,0},{8,12},{12,8},{16,20},{20,16},{24,28},{28,24},{1,5},{5... | collective-permute-start | bytes 1769480 | tf_op jit(solution)/shard_map/ppermute | solution.py:1005
  190.7 32.8 %collective-permute-start.51 = (bf16[2,1024,128]{2,1,0:T(8,128)(2,1)S(1)}, bf16[2,1024,128]{2,1,0:T(8,128)(2,1)S(1)}, u32[]{:S(2)}, u32[]{:S(2)}) collective-permute-start(bf16[2,1024,128]{2,1,0:T(8,128)(2,1)S(1)} %copy-done.34), channel_id=1, source_target_pairs={{0,2},{1,3},{2,0},{3,1},{4,6},{5,7},{6,4},{7,5},{8,10},{9,11},{10,... | collective-permute-start | bytes 1572872 | tf_op jit(solution)/shard_map/ppermute | solution.py:1005
  208.5 15.0 %collective-permute-start.50 = (bf16[9,128,128]{2,1,0:T(8,128)(2,1)S(1)}, bf16[9,128,128]{2,1,0:T(8,128)(2,1)S(1)}, u32[]{:S(2)}, u32[]{:S(2)}) collective-permute-start(bf16[9,128,128]{2,1,0:T(8,128)(2,1)S(1)} %get-tuple-element.451), channel_id=1, source_target_pairs={{0,8},{4,12},{8,0},{12,4},{16,24},{20,28},{24,16},{28,20},{1,9},{5... | collective-permute-start | bytes 884744 | tf_op jit(solution)/shard_map/ppermute | solution.py:1005
  208.6 13.6 %collective-permute-start.48 = (bf16[4,128,128]{2,1,0:T(8,128)(2,1)S(1)}, bf16[4,128,128]{2,1,0:T(8,128)(2,1)S(1)}, u32[]{:S(2)}, u32[]{:S(2)}) collective-permute-start(bf16[4,128,128]{2,1,0:T(8,128)(2,1)S(1)} %join.6.refs_0_), channel_id=1, source_target_pairs={{0,8},{4,12},{8,0},{12,4},{16,24},{20,28},{24,16},{28,20},{1,9},{5... | collective-permute-start | bytes 393224 | tf_op jit(solution)/shard_map/ppermute | solution.py:1005
  222.2 21.6 %collective-permute-start.56 = (bf16[2,1056,128]{2,1,0:T(8,128)(2,1)S(1)}, bf16[2,1056,128]{2,1,0:T(8,128)(2,1)S(1)}, u32[]{:S(2)}, u32[]{:S(2)}) collective-permute-start(bf16[2,1056,128]{2,1,0:T(8,128)(2,1)S(1)} %get-tuple-element.472), channel_id=1, source_target_pairs={{0,2},{1,3},{2,0},{3,1},{4,6},{5,7},{6,4},{7,5},{8,10},{9,11},{10,... | collective-permute-start | bytes 1622024 | tf_op jit(solution)/shard_map/ppermute | solution.py:1005
  237.8 16.2 %collective-permute-start.61 = (bf16[9,256,128]{2,1,0:T(8,128)(2,1)S(1)}, bf16[9,256,128]{2,1,0:T(8,128)(2,1)S(1)}, u32[]{:S(2)}, u32[]{:S(2)}) collective-permute-start(bf16[9,256,128]{2,1,0:T(8,128)(2,1)S(1)} %join.11.mine), channel_id=1, source_target_pairs={{0,4},{4,0},{8,12},{12,8},{16,20},{20,16},{24,28},{28,24},{1,5},{5... | collective-permute-start | bytes 1769480 | tf_op jit(solution)/shard_map/ppermute | solution.py:1005
  254.3 18.1 %collective-permute-start.66 = (bf16[9,256,128]{2,1,0:T(8,128)(2,1)S(1)}, bf16[9,256,128]{2,1,0:T(8,128)(2,1)S(1)}, u32[]{:S(2)}, u32[]{:S(2)}) collective-permute-start(bf16[9,256,128]{2,1,0:T(8,128)(2,1)S(1)} %join.10.mine), channel_id=1, source_target_pairs={{0,4},{4,0},{8,12},{12,8},{16,20},{20,16},{24,28},{28,24},{1,5},{5... | collective-permute-start | bytes 1769480 | tf_op jit(solution)/shard_map/ppermute | solution.py:1005
  (79 other events, 665.6 us)

commit v6 on v5

--- a/solution.py
+++ b/solution.py
@@ -230,7 +230,7 @@
 
 def kernel_first(
     meta, i0, i1, i2, i3, e0, e1, e2, e3, w0, w1, w2, w3, w4, w5, w6, w7,
-    image, pack, first_t, inner, second_t, second, field, weight, sems,
+    image, pack, first_t, inner, second_t, second, weight, stats, field, sems,
 ):
     pixels = image.shape[1]
     me = meta[0]
@@ -284,11 +284,14 @@
         return carry
 
     lax.fori_loop(0, pixels // strip, modulate, 0)
+    for b in range(4):
+        for row, value in enumerate((means[b], inverses[b], means2[b], inverses2[b])):
+            stats[b, row : row + 1, :] = value
 
 
 def kernel_second(
     meta, second, image, pack, w0, w1, w2, w3, w4, w5, w6, w7,
-    middle, attn_t, qkv, qkv_weight, proj_weight, weight, attn, sems,
+    middle, attn_t, qkv, qkv_weight, proj_weight, weight, stats, attn, sems,
 ):
     pixels = image.shape[1]
     me = meta[0]
@@ -329,6 +332,9 @@
         return carry
 
     lax.fori_loop(0, 4 * (pixels // 512), project, 0)
+    for b in range(4):
+        for row, value in enumerate((means[b], inverses[b])):
+            stats[b, row : row + 1, :] = value
 
 
 def kernel_attention(
@@ -528,49 +534,44 @@
             dctx[s, position * CTX : (position + 1) * CTX, :] = folded[0:CTX]
 
 
-def norm_back_strips(pixels, strip, read_normed, read_grad, gains, inverses, write):
+def saved(stats, row):
+    return [stats[b, row : row + 1, :] for b in range(4)]
+
+
+def norm_back_strips(pixels, strip, read_normed, read_grad, gains, inverses, gain_sums, bias_sums, write):
     count = pixels * (C // GROUPS)
-
-    def terms(start):
-        found = []
-        for b in range(4):
-            grad = read_grad(b, start)
-            found += [grad, grad * read_normed(b, start)]
-        return found
-
-    sums = sum_strips(pixels, strip, 8, terms)
-    bias_sums = [column_sum(sums[2 * b]) for b in range(4)]
-    gain_sums = [column_sum(sums[2 * b + 1]) for b in range(4)]
-    firsts = [
-        group_sum(jnp.broadcast_to(bias_sums[b] * gains[b], (8, LANES)) * (1.0 / 8)) * (1.0 / count)
-        for b in range(4)
-    ]
-    seconds = [
-        group_sum(jnp.broadcast_to(gain_sums[b] * gains[b], (8, LANES)) * (1.0 / 8)) * (1.0 / count)
-        for b in range(4)
-    ]
+    firsts, seconds = (
+        [
+            group_sum(jnp.broadcast_to(sums[b] * gains[b], (8, LANES)) * (1.0 / 8)) * (1.0 / count)
+            for b in range(4)
+        ]
+        for sums in (bias_sums, gain_sums)
+    )
 
     def body(index, carry):
         start = pl.multiple_of(index * strip, strip)
+        found = []
         for b in range(4):
             normed = read_normed(b, start)
             grad = read_grad(b, start) * gains[b]
-            write(b, start, inverses[b] * (grad - firsts[b] - normed * seconds[b]))
-        return carry
-
-    lax.fori_loop(0, pixels // strip, body, 0)
-    return gain_sums, bias_sums
+            found.append(write(b, start, inverses[b] * (grad - firsts[b] - normed * seconds[b])))
+        if found[0] is None:
+            return carry
+        return tuple(old + fold(new) for old, new in zip(carry, found))
+
+    zero = tuple(jnp.zeros((8, LANES), F32) for _ in range(4))
+    return lax.fori_loop(0, pixels // strip, body, zero)
 
 
 def kernel_back_attention(
-    meta, dqkv, cot, middle, pack, dctx, qkv_weight,
+    meta, dqkv, cot, middle, pack, stats, dctx, qkv_weight,
     dmiddle, field, sums, d0, d1, d2, d3, dattn,
 ):
     pixels = cot.shape[1]
     me = meta[0]
     strip = 128
     clear_padding(field, pixels)
-    means, inverses = norm_rows(pixels, strip, lambda b, start: middle[b, pl.ds(start, strip), :])
+    means, inverses = saved(stats, 0), saved(stats, 1)
 
     def back(index, carry):
         start = pl.multiple_of(index * 512, 512)
@@ -592,18 +593,29 @@
     def write(b, start, value):
         total = cot[b, pl.ds(start, strip), :].astype(F32) + value
         dmiddle[b, pl.ds(start, strip), :] = total
-        store_shifted(field, b, start, total.astype(BF16).astype(F32))
-
-    gain_sums, bias_sums = norm_back_strips(
-        pixels, strip, read_normed, lambda b, start: dattn[b, pl.ds(start, strip), :], gains, inverses, write
-    )
-    branch = sum_strips(
+        rounded = total.astype(BF16).astype(F32)
+        store_shifted(field, b, start, rounded)
+        return rounded
+
+    def terms(start):
+        found = []
+        for b in range(4):
+            grad = dattn[b, pl.ds(start, strip), :]
+            found += [grad, grad * read_normed(b, start)]
+        return found
+
+    totals = [column_sum(rows8) for rows8 in sum_strips(pixels, strip, 8, terms)]
+    bias_sums, gain_sums = totals[0::2], totals[1::2]
+    branch = norm_back_strips(
         pixels,
         strip,
-        4,
-        lambda start: [
-            field[1, b, pl.ds(pl.multiple_of(PAD + start, 32), strip), :].astype(F32) for b in range(4)
-        ],
+        read_normed,
+        lambda b, start: dattn[b, pl.ds(start, strip), :],
+        gains,
+        inverses,
+        gain_sums,
+        bias_sums,
+        write,
     )
     for b in range(4):
         sums[b] = jnp.zeros((S_ROWS, LANES), F32)
@@ -628,30 +640,20 @@
 
     lax.fori_loop(0, pixels // strip, turn, 0)
 
-    def weights(offset, carry):
+    attn_all = attn_t[...].reshape(C, pixels)
+    cot_all = cot_t[...].reshape(C, pixels)
+    for offset, target in enumerate((keep, send)):
         s = jnp.bitwise_xor(me, offset)
-        place = offset // 2
-        attn_all = attn_t[...].reshape(C, pixels)
-        cot_all = cot_t[...].reshape(C, pixels)
-        grad = jnp.dot(attn_all, dqkv[s], preferred_element_type=F32).astype(BF16)
-        other = jnp.dot(cot_all, mixed[s], preferred_element_type=F32).astype(BF16)
-
-        def put(target):
+        pair = (s, jnp.bitwise_xor(s, 2))
+        right = jnp.concatenate([dqkv[p] for p in pair], axis=1)
+        grad = jnp.dot(attn_all, right, preferred_element_type=F32).astype(BF16)
+        right = jnp.concatenate([mixed[p] for p in pair], axis=1)
+        other = jnp.dot(cot_all, right, preferred_element_type=F32).astype(BF16)
+        for place in range(2):
             for kind in range(3):
-                target[place, kind] = grad[:, kind * LANES : (kind + 1) * LANES]
-            target[place, 3] = other
-
-        @pl.when(offset % 2 == 0)
-        def _():
-            put(keep)
-
-        @pl.when(offset % 2 == 1)
-        def _():
-            put(send)
-
-        return carry
-
-    lax.fori_loop(0, 4, weights, 0)
+                column = (3 * place + kind) * LANES
+                target[place, kind] = grad[:, column : column + LANES]
+            target[place, 3] = other[:, place * LANES : (place + 1) * LANES]
 
 
 def weight_taps(half, sources, field, target):
@@ -700,16 +702,14 @@
 
 
 def kernel_back_second(
-    meta, grad_field, inner, pack, sums_in, w0, w1, w2, w3, w4, w5, w6, w7,
-    field, sums, d0, d1, d2, d3, weight, grad, sems,
+    meta, grad_field, inner, pack, stats, sums_in, weight,
+    field, sums, d0, d1, d2, d3, grad,
 ):
     pixels = inner.shape[1]
     me = meta[0]
     strip = 128
-    weight_copies = fetch_routed((w0, w1, w2, w3, w4, w5, w6, w7), weight, me, meta[2], sems, 0)
     clear_padding(field, pixels)
-    means, inverses = norm_rows(pixels, strip, lambda b, start: inner[b, pl.ds(start, strip), :])
-    wait_all(weight_copies)
+    means, inverses = saved(stats, 2), saved(stats, 3)
 
     def write_grad(start, half, tile):
         for b in range(2):
@@ -728,35 +728,48 @@
             bias = pack[b, E_B2 : E_B2 + 1, :]
             scale = pack[b, M_SCALE : M_SCALE + 1, :]
             shift = pack[b, M_SHIFT : M_SHIFT + 1, :]
-            shaped = read_normed(b, start) * gains[b] + bias
-            modulated = shaped * (1.0 + scale) + shift
+            normed = read_normed(b, start)
+            modulated = (normed * gains[b] + bias) * (1.0 + scale) + shift
             dmod = silu_slope(modulated, grad[b, pl.ds(start, strip), :])
             grad[b, pl.ds(start, strip), :] = dmod * (1.0 + scale)
-            found += [dmod * shaped, dmod]
+            found += [dmod, dmod * normed]
         return tuple(old + fold(new) for old, new in zip(carry, found))
 
     zero = tuple(jnp.zeros((8, LANES), F32) for _ in range(8))
-    modulation = lax.fori_loop(0, pixels // strip, slope, zero)
+    totals = [column_sum(rows8) for rows8 in lax.fori_loop(0, pixels // strip, slope, zero)]
+    plain, scaled = totals[0::2], totals[1::2]
+    factors = [1.0 + pack[b, M_SCALE : M_SCALE + 1, :] for b in range(4)]
+    bias_sums = [plain[b] * factors[b] for b in range(4)]
+    gain_sums = [scaled[b] * factors[b] for b in range(4)]
 
     def write(b, start, value):
         store_shifted(field, b, start, value)
 
-    gain_sums, bias_sums = norm_back_strips(
-        pixels, strip, read_normed, lambda b, start: grad[b, pl.ds(start, strip), :], gains, inverses, write
+    norm_back_strips(
+        pixels,
+        strip,
+        read_normed,
+        lambda b, start: grad[b, pl.ds(start, strip), :],
+        gains,
+        inverses,
+        gain_sums,
+        bias_sums,
+        write,
     )
     for b in range(4):
         sums[b] = sums_in[b]
         sums[b, S_G2 : S_G2 + 1, :] = gain_sums[b]
         sums[b, S_B2 : S_B2 + 1, :] = bias_sums[b]
-        sums[b, S_SCALE : S_SCALE + 1, :] = column_sum(modulation[2 * b])
-        sums[b, S_SHIFT : S_SHIFT + 1, :] = column_sum(modulation[2 * b + 1])
+        sums[b, S_SCALE : S_SCALE + 1, :] = (
+            scaled[b] * gains[b] + plain[b] * pack[b, E_B2 : E_B2 + 1, :]
+        )
+        sums[b, S_SHIFT : S_SHIFT + 1, :] = plain[b]
     for offset, target in enumerate((d0, d1, d2, d3)):
         target[...] = field[1, jnp.bitwise_xor(me, offset), PAD : PAD + pixels, :]
 
 
-def kernel_back_conv(meta, grad_field, w0, w1, w2, w3, w4, w5, w6, w7, grad, weight, sems):
+def kernel_back_conv(grad_field, weight, grad):
     pixels = grad.shape[1]
-    wait_all(fetch_routed((w0, w1, w2, w3, w4, w5, w6, w7), weight, meta[0], meta[2], sems, 0))
 
     def write_grad(start, half, tile):
         for b in range(2):
@@ -766,7 +779,7 @@
 
 
 def kernel_back_first(
-    meta, grad_in, image, pack, dmiddle, sums_in, g0, g1, g2, grad, sums,
+    meta, grad_in, image, pack, stats, dmiddle, sums_in, g0, g1, g2, grad, sums,
 ):
     pixels = image.shape[1]
     me = meta[0]
@@ -775,7 +788,7 @@
     def read(b, start):
         return image[b, pl.ds(start, strip), :].astype(F32)
 
-    means, inverses = norm_rows(pixels, strip, read)
+    means, inverses = saved(stats, 0), saved(stats, 1)
     gains = [pack[b, E_G1 : E_G1 + 1, :] for b in range(4)]
 
     def read_normed(b, start):
@@ -783,18 +796,32 @@
 
     def slope(index, carry):
         start = pl.multiple_of(index * strip, strip)
+        found = []
         for b in range(4):
-            before = read_normed(b, start) * gains[b] + pack[b, E_B1 : E_B1 + 1, :]
-            grad[b, pl.ds(start, strip), :] = silu_slope(before, grad_in[b, pl.ds(start, strip), :])
-        return carry
-
-    lax.fori_loop(0, pixels // strip, slope, 0)
+            normed = read_normed(b, start)
+            before = normed * gains[b] + pack[b, E_B1 : E_B1 + 1, :]
+            value = silu_slope(before, grad_in[b, pl.ds(start, strip), :])
+            grad[b, pl.ds(start, strip), :] = value
+            found += [value, value * normed]
+        return tuple(old + fold(new) for old, new in zip(carry, found))
+
+    zero = tuple(jnp.zeros((8, LANES), F32) for _ in range(8))
+    totals = [column_sum(rows8) for rows8 in lax.fori_loop(0, pixels // strip, slope, zero)]
+    bias_sums, gain_sums = totals[0::2], totals[1::2]
 
     def write(b, start, value):
         grad[b, pl.ds(start, strip), :] = dmiddle[b, pl.ds(start, strip), :] + value
 
-    gain_sums, bias_sums = norm_back_strips(
-        pixels, strip, read_normed, lambda b, start: grad[b, pl.ds(start, strip), :], gains, inverses, write
+    norm_back_strips(
+        pixels,
+        strip,
+        read_normed,
+        lambda b, start: grad[b, pl.ds(start, strip), :],
+        gains,
+        inverses,
+        gain_sums,
+        bias_sums,
+        write,
     )
     for b in range(4):
         sums[b] = sums_in[b]
@@ -1154,17 +1181,24 @@
     piece = struct((pixels, LANES), BF16)
     pair_piece = struct((2, pixels, LANES), BF16)
     field_scratch = pltpu.VMEM((3, 4, pixels + 2 * PAD, LANES), BF16)
-    conv_scratch = pltpu.VMEM((4, 9 * C, LANES), BF16)
-    rest_scratch = pltpu.VMEM((4, PROJ_ROW + C, LANES), BF16)
     grad_scratch = pltpu.VMEM((4, pixels, LANES), F32)
 
-    image, pack, first_t, inner, second_t, second = call(
+    image, pack, first_t, inner, second_t, second, conv1_all, stats1 = call(
         kernel_first,
         "first",
-        [block, struct((4, E_ROWS, LANES), F32), turned, block32, turned, fields],
+        [
+            block,
+            struct((4, E_ROWS, LANES), F32),
+            turned,
+            block32,
+            turned,
+            fields,
+            struct((4, 9 * C, LANES), BF16),
+            struct((4, 8, LANES), F32),
+        ],
         [smem()] + [anywhere()] * 16,
-        [field_scratch, conv_scratch, pltpu.SemaphoreType.DMA((16,))],
-        limit=17,
+        [field_scratch, pltpu.SemaphoreType.DMA((16,))],
+        limit=12,
     )(meta, *images, *packs, *conv1)
 
     second, rest_half, rest_near, factors = tie(second, rest_half, rest_near, factors)
@@ -1173,7 +1207,7 @@
     second, *rest = tie(second, *rest)
     factors = stack(factors)
     factors = [factors, swap(factors, "dp", 2)]
-    middle, attn_t, qkv, qkv_w, proj_w = call(
+    middle, attn_t, qkv, qkv_w, proj_w, rest_all, stats2 = call(
         kernel_second,
         "second",
         [
@@ -1182,10 +1216,12 @@
             struct((4, pixels, 3 * LANES), BF16),
             struct((4, 3 * C, LANES), BF16),
             struct((4, C, LANES), BF16),
+            struct((4, PROJ_ROW + C, LANES), BF16),
+            struct((4, 8, LANES), F32),
         ],
         [smem()] + [vmem()] * 3 + [anywhere()] * 8,
-        [rest_scratch, pltpu.VMEM((4, pixels, LANES), BF16), pltpu.SemaphoreType.DMA((8,))],
-        limit=17,
+        [pltpu.VMEM((4, pixels, LANES), BF16), pltpu.SemaphoreType.DMA((8,))],
+        limit=12,
     )(meta, second, image, pack, *rest)
     ctx_scratch = pltpu.VMEM((pixels, LANES), F32)
     turned_scratch = pltpu.VMEM((LANES, pixels), F32)
@@ -1216,7 +1252,7 @@
             turned_scratch,
             pltpu.SemaphoreType.DMA((4,)),
         ],
-        limit=30,
+        limit=24,
     )(meta, qkv, pack, middle, proj_w, *cots)
 
     def weight_send(sources, gradients):
@@ -1268,9 +1304,9 @@
         kernel_back_attention,
         "back_attention",
         [block32, fields, struct((4, S_ROWS, LANES), F32)] + [piece] * 4,
-        [smem()] + [vmem()] * 6,
+        [smem()] + [vmem()] * 7,
         [grad_scratch],
-    )(meta, dqkv, cot, middle, pack, dctx, qkv_w)
+    )(meta, dqkv, cot, middle, pack, stats2, dctx, qkv_w)
     gradients2, second_d, first_y, first_c, att, field2 = tie(
         gradients2, second_d, first_y, first_c, att, field2
     )
@@ -1283,10 +1319,10 @@
         kernel_back_second,
         "back_second",
         [fields, struct((4, S_ROWS, LANES), F32)] + [piece] * 4,
-        [smem()] + [vmem()] * 4 + [anywhere()] * 8,
-        [rest_scratch, grad_scratch, pltpu.SemaphoreType.DMA((8,))],
-        limit=20,
-    )(meta, field2, inner, pack, sums, *rest)
+        [smem()] + [vmem()] * 6,
+        [grad_scratch],
+        limit=12,
+    )(meta, field2, inner, pack, stats1, sums, rest_all)
     gradients1, gradients2, att, first_d = tie(gradients1, gradients2, att, first_d)
     firsts = (first_t, first_c, first_y, first_d)
     gradients1 = exchange(gradients1)
@@ -1315,9 +1351,9 @@
         kernel_back_conv,
         "back_conv",
         block32,
-        [smem()] + [vmem()] + [anywhere()] * 8,
-        [conv_scratch, pltpu.SemaphoreType.DMA((8,))],
-    )(meta, field1, *conv1)
+        [vmem()] * 2,
+        [],
+    )(field1, conv1_all)
     grad_first, gradients1, att = tie(grad_first, gradients1, att)
     att = total_sum(att)
     for level in range(len(levels) - 1, 2, -1):
@@ -1343,9 +1379,9 @@
             struct((pixels + S_ROWS, LANES), BF16),
             struct((2, pixels + S_ROWS, LANES), BF16),
         ],
-        [smem()] + [vmem()] * 5,
+        [smem()] + [vmem()] * 6,
         [grad_scratch, pltpu.VMEM((4, S_ROWS, LANES), F32)],
-    )(meta, grad_first, image, pack, dmiddle, sums)
+    )(meta, grad_first, image, pack, stats1, dmiddle, sums)
     grad_far, terms2, got1, own1 = tie(grad_far, terms2, got1, own1)
     terms1 = down([own1, got1], 1)
     ends2 = across(inner_levels(terms2), 2)

time: 275 us -> 269 us (0.978)
  starting transfers between devices: 45.9 us -> 55.9 us
  Pallas kernels: 137 us -> 128 us
  waiting for transfers between devices: 78.7 us -> 71.9 us
    ppermute x67, starting transfers between devices: 45.9 us -> 55.9 us  [swap(): return lax.ppermute(value, axis, [(i, i ^ offset) for i in range(size)])]
    ppermute x67, waiting for transfers between devices: 78.7 us -> 71.9 us  [swap(): return lax.ppermute(value, axis, [(i, i ^ offset) for i in range(size)])]
    pallas_call x1, Pallas kernels: 12.5 us -> 9.08 us  [local(): call(kernel_back_second, 'back_second', [fields, struct((4, S_ROWS, LANES...]
  transfers between devices with their start and end apart: 67 -> 67, of which waited for: 22 -> 23; matrix products, arithmetic and copies ran while one was open for 3% -> 3% of each run, Pallas kernels for 49% -> 46%
where the time goes in v6:
time: 269 us
  Pallas kernels  128 us (48%)
  waiting for transfers between devices  71.9 us (27%)
  starting transfers between devices  55.9 us (21%)
  local copies, waits for them, and re-layouts  6.29 us (2%)
  other arithmetic  2.77 us (1%)
    ppermute x67, waiting for transfers between devices, swap(): return lax.ppermute(value, axis, [(i, i ^ offset) for i in range(size)])  71.9 us
    ppermute x67, starting transfers between devices, swap(): return lax.ppermute(value, axis, [(i, i ^ offset) for i in range(size)])  55.9 us
    pallas_call x1, Pallas kernels, local(): call(kernel_attention, 'attention', [piece, piece, pair_piece] + [block,...  33.8 us
    pallas_call x1, Pallas kernels, local(): call(kernel_second, 'second', [block32, turned, struct((4, pixels, 3 * LA...  13.3 us
    pallas_call x1, Pallas kernels, local(): call(kernel_first, 'first', [block, struct((4, E_ROWS, LANES), F32), turn...  12.7 us
    pallas_call x2, Pallas kernels, weight_send(): call(kernel_weight_send, 'weight_send', [struct((9, C // 2, LANES), BF16)...  9.61 us
    pallas_call x1, Pallas kernels, local(): call(kernel_back_second, 'back_second', [fields, struct((4, S_ROWS, LANES...  9.08 us
    pallas_call x2, Pallas kernels, weight_own(): call(kernel_weight_own, 'weight_own', struct((9, C // 2, LANES), F32), [s...  8.42 us
  transfers between devices with their start and end apart: 67, of which 23 were waited for; matrix products, arithmetic and copies ran while one was open for 3% of the time, Pallas kernels for 46%

profile of v6, /device:TPU:0, one launch (start us, length us, event | category | flops | bytes accessed | tf_op | source)
XLA Modules:
  0.0 268.6 jit_solution(5223968279518409362)
XLA Ops:
  5.9 3.0 %collective-permute-start.2 = (bf16[2304,128]{1,0:T(8,128)(2,1)}, bf16[2304,128]{1,0:T(8,128)(2,1)S(1)}, u32[]{:S(2)}, u32[]{:S(2)}) collective-permute-start(bf16[2304,128]{1,0:T(8,128)(2,1)} %constant_dynamic-slice_fusion.3), channel_id=1, source_target_pairs={{0,2},{1,3},{2,0},{3,1},{4,6},{5,7},{6,4},{7,5},{8,10},{9,11},{10,... | collective-permute-start | bytes 1769480 | tf_op jit(solution)/shard_map/ppermute | solution.py:1032
  14.4 8.9 %collective-permute-done.2.source.w2 = bf16[2304,128]{1,0:T(8,128)(2,1)S(1)} collective-permute-done((bf16[2304,128]{1,0:T(8,128)(2,1)}, bf16[2304,128]{1,0:T(8,128)(2,1)S(1)}, u32[]{:S(2)}, u32[]{:S(2)}) %collective-permute-start.2) | collective-permute-done | bytes 589856 | tf_op jit(solution)/shard_map/ppermute | solution.py:1032
  23.3 2.2 collective-permute-start.7
  27.2 4.0 %collective-permute-done.7.w4 = bf16[1152,128]{1,0:T(8,128)(2,1)S(1)} collective-permute-done((bf16[1152,128]{1,0:T(8,128)(2,1)S(1)}, bf16[1152,128]{1,0:T(8,128)(2,1)S(1)}, u32[]{:S(2)}, u32[]{:S(2)}) %collective-permute-start.7) | collective-permute-done | bytes 294944 | tf_op jit(solution)/shard_map/ppermute | solution.py:1032
  41.1 12.7 %first.1 = (bf16[4,1024,128]{2,1,0:T(8,128)(2,1)S(1)}, f32[4,32,128]{2,1,0:T(8,128)S(1)}, bf16[4,128,1024]{2,1,0:T(8,128)(2,1)S(1)}, f32[4,1024,128]{2,1,0:T(8,1...) custom-call(s32[6]{0:T(128)S(1)} %stack.36.meta, ...), custom_call_target="tpu_custom_call" | custom-call | tf_op jit(solution)/shard_map/first/pallas_call | solution.py:1186
  55.2 2.8 %collective-permute-done.13.source.w2 = bf16[3328,128]{1,0:T(8,128)(2,1)S(1)} collective-permute-done((bf16[3328,128]{1,0:T(8,128)(2,1)S(1)}, bf16[3328,128]{1,0:T(8,128)(2,1)S(1)}, u32[]{:S(2)}, u32[]{:S(2)}) %collective-permute-start.13) | collective-permute-done | bytes 852000 | tf_op jit(solution)/shard_map/ppermute | solution.py:1032
  60.4 9.1 %collective-permute-done.16.w3 = bf16[1664,128]{1,0:T(8,128)(2,1)S(1)} collective-permute-done((bf16[1664,128]{1,0:T(8,128)(2,1)S(1)}, bf16[1664,128]{1,0:T(8,128)(2,1)S(1)}, u32[]{:S(2)}, u32[]{:S(2)}) %collective-permute-start.16) | collective-permute-done | bytes 426016 | tf_op jit(solution)/shard_map/ppermute | solution.py:1032
  73.7 13.3 %second.1 = (f32[4,1024,128]{2,1,0:T(8,128)S(1)}, bf16[4,128,1024]{2,1,0:T(8,128)(2,1)S(1)}, bf16[4,1024,384]{2,1,0:T(8,128)(2,1)S(1)}, bf16[4,1536,128]{2,1,0:T...) custom-call(s32[6]{0:T(128)S(1)} %stack.36.meta, ...), custom_call_target="tpu_custom_call" | custom-call | tf_op jit(solution)/shard_map/second/pallas_call | solution.py:1210
  88.7 2.7 collective-permute-start.27
  91.8 33.8 %attention.1 = (bf16[1024,128]{1,0:T(8,128)(2,1)S(1)}, bf16[1024,128]{1,0:T(8,128)(2,1)S(1)}, bf16[2,1024,128]{2,1,0:T(8,128)(2,1)S(1)}, bf16[4,1024,128]{2,1,0:...) custom-call(s32[6]{0:T(128)S(1)} %stack.36.meta, ...), custom_call_target="tpu_custom_call" | custom-call | tf_op jit(solution)/shard_map/attention/pallas_call | solution.py:1237
  125.7 3.8 %attention_grad.1 = (bf16[2,4,512,128]{3,2,1,0:T(8,128)(2,1)S(1)}, bf16[2,4,512,128]{3,2,1,0:T(8,128)(2,1)S(1)}) custom-call(s32[6]{0:T(128)S(1)} %stack.36.meta, bf16[4,1024,384]{2,1,0:T(8,128)(2,1)S(1)} %get-tuple-element.337.dqkv, bf16[4,1024,128]{2,1,0:T(8,128)(2,1)S(1)} %get-tuple-element.329.mixed, ...), custom_call_target="tpu_custom_call" | custom-call | tf_op jit(solution)/shard_map/attention_grad/pallas_call | solution.py:1293
  130.1 4.6 %back_attention.1 = (f32[4,1024,128]{2,1,0:T(8,128)S(1)}, bf16[3,4,1088,128]{3,2,1,0:T(8,128)(2,1)S(1)}, f32[4,32,128]{2,1,0:T(8,128)S(1)}, bf16[1024,128]{1,0:T...) custom-call(s32[6]{0:T(128)S(1)} %stack.36.meta, ...), custom_call_target="tpu_custom_call" | custom-call | tf_op jit(solution)/shard_map/back_attention/pallas_call | solution.py:1303
  139.1 9.1 %back_second.1 = (bf16[3,4,1088,128]{3,2,1,0:T(8,128)(2,1)S(1)}, f32[4,32,128]{2,1,0:T(8,128)S(1)}, bf16[1024,128]{1,0:T(8,128)(2,1)S(1)}, bf16[1024,128]{1,0:T(...) custom-call(s32[6]{0:T(128)S(1)} %stack.36.meta, ...), custom_call_target="tpu_custom_call" | custom-call | tf_op jit(solution)/shard_map/back_second/pallas_call | solution.py:1318
  148.3 3.0 %collective-permute-done.34.d3 = bf16[1024,128]{1,0:T(8,128)(2,1)S(1)} collective-permute-done((bf16[1024,128]{1,0:T(8,128)(2,1)S(1)}, bf16[1024,128]{1,0:T(8,128)(2,1)S(1)}, u32[]{:S(2)}, u32[]{:S(2)}) %collective-permute-start.34) | collective-permute-done | bytes 262176 | tf_op jit(solution)/shard_map/ppermute | solution.py:1032
  153.2 4.8 %weight_send.2 = (bf16[9,256,128]{2,1,0:T(8,128)(2,1)S(1)}, bf16[3,4,1088,128]{3,2,1,0:T(8,128)(2,1)S(1)}) custom-call(s32[6]{0:T(128)S(1)} %stack.36.meta, bf16[4,128,1024]{2,1,0:T(8,128)(2,1)S(1)} %get-tuple-element.320.u0, bf16[4,128,1024]{2,1,0:T(8,128)(2,1)S(1)} %collective-permute-done.26.u1, bf16[4,128,1024]{2,1,0:T(8,128)(2,1)S(1)} %collective-permute-done.25.u2, ...), custom_call_target="tpu_custom_call" | custom-call | tf_op jit(solution)/shard_map/weight_send/pallas_call | solution.py:1259
  163.5 4.2 %weight_own.2.refs_0_ = f32[9,256,128]{2,1,0:T(8,128)S(1)} custom-call(s32[6]{0:T(128)S(1)} %stack.36.meta, bf16[4,128,1024]{2,1,0:T(8,128)(2,1)S(1)} %get-tuple-element.320.u0, bf16[4,128,1024]{2,1,0:T(8,128)(2,1)S(1)} %collective-permute-done.26.u1, bf16[4,128,1024]{2,1,0:T(8,128)(2,1)S(1)} %collective-permute-done.25.u2, ...), custom_call_target="tpu_custom_call" | custom-call | tf_op jit(solution)/shard_map/weight_own/pallas_call | solution.py:1269
  167.8 3.2 %collective-permute-done.38.got = bf16[8,64,128]{2,1,0:T(8,128)(2,1)S(1)} collective-permute-done((bf16[8,64,128]{2,1,0:T(8,128)(2,1)S(1)}, bf16[8,64,128]{2,1,0:T(8,128)(2,1)S(1)}, u32[]{:S(2)}, u32[]{:S(2)}) %collective-permute-start.38) | collective-permute-done | bytes 131104 | tf_op jit(solution)/shard_map/ppermute | solution.py:1032
  172.5 5.7 %back_conv.1.grad_in = f32[4,1024,128]{2,1,0:T(8,128)S(1)} custom-call(bf16[3,4,1088,128]{3,2,1,0:T(8,128)(2,1)S(1)} %get-tuple-element.396.grad_field, bf16[4,4608,128]{2,1,0:T(8,128)(2,1)S(1)} %get-tuple-element.397.weight), custom_call_target="tpu_custom_call" | custom-call | tf_op jit(solution)/shard_map/back_conv/pallas_call | solution.py:1350
  178.2 4.8 %weight_send.3 = (bf16[9,256,128]{2,1,0:T(8,128)(2,1)S(1)}, bf16[3,4,1088,128]{3,2,1,0:T(8,128)(2,1)S(1)}) custom-call(s32[6]{0:T(128)S(1)} %stack.36.meta, bf16[4,128,1024]{2,1,0:T(8,128)(2,1)S(1)} %get-tuple-element.345.u0, bf16[4,128,1024]{2,1,0:T(8,128)(2,1)S(1)} %collective-permute-done.30.u1, bf16[4,128,1024]{2,1,0:T(8,128)(2,1)S(1)} %collective-permute-done.29.u2, ...), custom_call_target="tpu_custom_call" | custom-call | tf_op jit(solution)/shard_map/weight_send/pallas_call | solution.py:1259
  185.6 2.6 collective-permute-start.45
  188.1 4.2 %weight_own.3.refs_0_ = f32[9,256,128]{2,1,0:T(8,128)S(1)} custom-call(s32[6]{0:T(128)S(1)} %stack.36.meta, bf16[4,128,1024]{2,1,0:T(8,128)(2,1)S(1)} %get-tuple-element.345.u0, bf16[4,128,1024]{2,1,0:T(8,128)(2,1)S(1)} %collective-permute-done.30.u1, bf16[4,128,1024]{2,1,0:T(8,128)(2,1)S(1)} %collective-permute-done.29.u2, ...), custom_call_target="tpu_custom_call" | custom-call | tf_op jit(solution)/shard_map/weight_own/pallas_call | solution.py:1269
  196.4 2.9 %back_first.1 = (bf16[1056,128]{1,0:T(8,128)(2,1)S(1)}, bf16[1056,128]{1,0:T(8,128)(2,1)S(1)}, bf16[2,1056,128]{2,1,0:T(8,128)(2,1)S(1)}) custom-call(s32[6]{0:T(128)S(1)} %stack.36.meta, f32[4,1024,128]{2,1,0:T(8,128)S(1)} %back_conv.1.grad_in, bf16[4,1024,128]{2,1,0:T(8,128)(2,1)S(1)} %get-tuple-element.301.image, ...), custom_call_target="tpu_custom_call" | custom-call | tf_op jit(solution)/shard_map/back_first/pallas_call | solution.py:1374
  199.2 3.1 %collective-permute-done.46.refs_1_ = bf16[9,64,128]{2,1,0:T(8,128)(2,1)S(1)} collective-permute-done((bf16[9,64,128]{2,1,0:T(8,128)(2,1)S(1)}, bf16[9,64,128]{2,1,0:T(8,128)(2,1)S(1)}, u32[]{:S(2)}, u32[]{:S(2)}) %collective-permute-start.46) | collective-permute-done | bytes 147488 | tf_op jit(solution)/shard_map/ppermute | solution.py:1032
  207.1 7.9 %collective-permute-done.48.refs_1_ = bf16[4,128,128]{2,1,0:T(8,128)(2,1)S(1)} collective-permute-done((bf16[4,128,128]{2,1,0:T(8,128)(2,1)S(1)}, bf16[4,128,128]{2,1,0:T(8,128)(2,1)S(1)}, u32[]{:S(2)}, u32[]{:S(2)}) %collective-permute-start.48) | collective-permute-done | bytes 131104 | tf_op jit(solution)/shard_map/ppermute | solution.py:1032
  216.2 2.5 collective-permute-start.52
  223.5 2.2 collective-permute-done.54.other
  225.7 3.7 %collective-permute-done.53.refs_1_ = bf16[9,64,128]{2,1,0:T(8,128)(2,1)S(1)} collective-permute-done((bf16[9,64,128]{2,1,0:T(8,128)(2,1)S(1)}, bf16[9,64,128]{2,1,0:T(8,128)(2,1)S(1)}, u32[]{:S(2)}, u32[]{:S(2)}) %collective-permute-start.53) | collective-permute-done | bytes 147488 | tf_op jit(solution)/shard_map/ppermute | solution.py:1032
  234.1 2.6 collective-permute-done.55.refs_1_
  240.1 6.7 %collective-permute-done.59.refs_1_ = bf16[9,128,128]{2,1,0:T(8,128)(2,1)S(1)} collective-permute-done((bf16[9,128,128]{2,1,0:T(8,128)(2,1)S(1)}, bf16[9,128,128]{2,1,0:T(8,128)(2,1)S(1)}, u32[]{:S(2)}, u32[]{:S(2)}) %collective-permute-start.59) | collective-permute-done | bytes 294944 | tf_op jit(solution)/shard_map/ppermute | solution.py:1032
  257.3 4.1 %collective-permute-done.63.small1 = bf16[16,32,128]{2,1,0:T(8,128)(2,1)S(1)} collective-permute-done((bf16[16,32,128]{2,1,0:T(8,128)(2,1)S(1)}, bf16[16,32,128]{2,1,0:T(8,128)(2,1)S(1)}, u32[]{:S(2)}, u32[]{:S(2)}) %collective-permute-start.63) | collective-permute-done | bytes 131104 | tf_op jit(solution)/shard_map/ppermute | solution.py:1032
  261.4 4.6 %factor_grads.1 = (f32[2048,2,128]{2,1,0:T(2,128)}, f32[2048,2,128]{2,1,0:T(2,128)}, f32[32,128]{1,0:T(8,128)S(1)}) custom-call(f32[8,128]{1,0:T(8,128)S(1)} %scale.1, bf16[2048,256]{1,0:T(8,128)(2,1)S(1)} %factors.1.left, bf16[16,32,128]{2,1,0:T(8,128)(2,1)S(1)} %stack.42.small0, bf16[16,32,128]{2,1,0:T(8,128)(2,1)S(1)} %collective-permute-done.63.small1), custom_call_target="tpu_custom_call" | custom-call | tf_op jit(solution)/shard_map/factor_grads/pallas_call | solution.py:1447
  266.5 2.1 last_join.5
  (211 shorter events, 81.8 us)
Async XLA Ops:
  1.4 21.8 %collective-permute-start = (bf16[4608,128]{1,0:T(8,128)(2,1)}, bf16[4608,128]{1,0:T(8,128)(2,1)S(1)}, u32[]{:S(2)}, u32[]{:S(2)}) collective-permute-start(bf16[4608,128]{1,0:T(8,128)(2,1)} %bitcast.80), channel_id=1, source_target_pairs={{0,1},{1,0},{2,3},{3,2},{4,5},{5,4},{6,7},{7,6},{8,9},{9,8},{10,11... | collective-permute-start | bytes 3538952 | tf_op jit(solution)/shard_map/ppermute | solution.py:1032
  5.9 17.3 %collective-permute-start.2 = (bf16[2304,128]{1,0:T(8,128)(2,1)}, bf16[2304,128]{1,0:T(8,128)(2,1)S(1)}, u32[]{:S(2)}, u32[]{:S(2)}) collective-permute-start(bf16[2304,128]{1,0:T(8,128)(2,1)} %constant_dynamic-slice_fusion.3), channel_id=1, source_target_pairs={{0,2},{1,3},{2,0},{3,1},{4,6},{5,7},{6,4},{7,5},{8,10},{9,11},{10,... | collective-permute-start | bytes 1769480 | tf_op jit(solution)/shard_map/ppermute | solution.py:1032
  9.7 24.4 %collective-permute-start.3 = (bf16[2,1024,128]{2,1,0:T(8,128)(2,1)}, bf16[2,1024,128]{2,1,0:T(8,128)(2,1)}, u32[]{:S(2)}, u32[]{:S(2)}) collective-permute-start(bf16[2,1024,128]{2,1,0:T(8,128)(2,1)} %pad_maximum_fusion.1), channel_id=1, source_target_pairs={{0,2},{1,3},{2,0},{3,1},{4,6},{5,7},{6,4},{7,5},{8,10},{9,11},{10,... | collective-permute-start | bytes 1572872 | tf_op jit(solution)/shard_map/ppermute | solution.py:1032
  36.5 21.4 %collective-permute-start.14 = (bf16[6656,128]{1,0:T(8,128)(2,1)S(1)}, bf16[6656,128]{1,0:T(8,128)(2,1)S(1)}, u32[]{:S(2)}, u32[]{:S(2)}) collective-permute-start(bf16[6656,128]{1,0:T(8,128)(2,1)S(1)} %pad_maximum_fusion.w0), channel_id=1, source_target_pairs={{0,1},{1,0},{2,3},{3,2},{4,5},{5,4},{6,7},{7,6},{8,9},{9,8},{10,11... | collective-permute-start | bytes 5111816 | tf_op jit(solution)/shard_map/ppermute | solution.py:1032
  36.6 21.4 %collective-permute-start.13 = (bf16[3328,128]{1,0:T(8,128)(2,1)S(1)}, bf16[3328,128]{1,0:T(8,128)(2,1)S(1)}, u32[]{:S(2)}, u32[]{:S(2)}) collective-permute-start(bf16[3328,128]{1,0:T(8,128)(2,1)S(1)} %constant_dynamic-slice_fusion), channel_id=1, source_target_pairs={{0,2},{1,3},{2,0},{3,1},{4,6},{5,7},{6,4},{7,5},{8,10},{9,11},{10,... | collective-permute-start | bytes 2555912 | tf_op jit(solution)/shard_map/ppermute | solution.py:1032
  38.3 16.8 %collective-permute-start.15 = (bf16[1,4,8,2048]{3,2,1,0:T(8,128)(2,1)S(1)}, bf16[1,4,8,2048]{3,2,1,0:T(8,128)(2,1)S(1)}, u32[]{:S(2)}, u32[]{:S(2)}) collective-permute-start(bf16[1,4,8,2048]{3,2,1,0:T(8,128)(2,1)S(1)} %fusion.9.refs_0_), channel_id=1, source_target_pairs={{0,4},{4,0},{8,12},{12,8},{16,20},{20,16},{24,28},{28,24},{1,5},{5... | collective-permute-start | bytes 393224 | tf_op jit(solution)/shard_map/ppermute | solution.py:1032
  58.0 11.4 %collective-permute-start.16 = (bf16[1664,128]{1,0:T(8,128)(2,1)S(1)}, bf16[1664,128]{1,0:T(8,128)(2,1)S(1)}, u32[]{:S(2)}, u32[]{:S(2)}) collective-permute-start(bf16[1664,128]{1,0:T(8,128)(2,1)S(1)} %get-tuple-element.298), channel_id=1, source_target_pairs={{0,4},{4,0},{8,12},{12,8},{16,20},{20,16},{24,28},{28,24},{1,5},{5... | collective-permute-start | bytes 1277960 | tf_op jit(solution)/shard_map/ppermute | solution.py:1032
  60.4 13.3 %collective-permute-start.18 = (bf16[3328,128]{1,0:T(8,128)(2,1)S(1)}, bf16[3328,128]{1,0:T(8,128)(2,1)S(1)}, u32[]{:S(2)}, u32[]{:S(2)}) collective-permute-start(bf16[3328,128]{1,0:T(8,128)(2,1)S(1)} %collective-permute-done.13.source.w2), channel_id=1, source_target_pairs={{0,1},{1,0},{2,3},{3,2},{4,5},{5,4},{6,7},{7,6},{8,9},{9,8},{10,11... | collective-permute-start | bytes 2555912 | tf_op jit(solution)/shard_map/ppermute | solution.py:1032
  70.7 16.4 %collective-permute-start.22 = (bf16[1024,128]{1,0:T(8,128)(2,1)S(1)}, bf16[1024,128]{1,0:T(8,128)(2,1)S(1)}, u32[]{:S(2)}, u32[]{:S(2)}) collective-permute-start(bf16[1024,128]{1,0:T(8,128)(2,1)S(1)} %get-tuple-element.317), channel_id=1, source_target_pairs={{0,1},{1,0},{2,3},{3,2},{4,5},{5,4},{6,7},{7,6},{8,9},{9,8},{10,11... | collective-permute-start | bytes 786440 | tf_op jit(solution)/shard_map/ppermute | solution.py:1032
  71.2 15.9 %collective-permute-start.23 = (bf16[1024,128]{1,0:T(8,128)(2,1)S(1)}, bf16[1024,128]{1,0:T(8,128)(2,1)S(1)}, u32[]{:S(2)}, u32[]{:S(2)}) collective-permute-start(bf16[1024,128]{1,0:T(8,128)(2,1)S(1)} %get-tuple-element.318), channel_id=1, source_target_pairs={{0,2},{1,3},{2,0},{3,1},{4,6},{5,7},{6,4},{7,5},{8,10},{9,11},{10,... | collective-permute-start | bytes 786440 | tf_op jit(solution)/shard_map/ppermute | solution.py:1032
  72.7 14.3 %collective-permute-start.24 = (bf16[1024,128]{1,0:T(8,128)(2,1)S(1)}, bf16[1024,128]{1,0:T(8,128)(2,1)S(1)}, u32[]{:S(2)}, u32[]{:S(2)}) collective-permute-start(bf16[1024,128]{1,0:T(8,128)(2,1)S(1)} %get-tuple-element.319), channel_id=1, source_target_pairs={{0,3},{1,2},{2,1},{3,0},{4,7},{5,6},{6,5},{7,4},{8,11},{9,10},{10,... | collective-permute-start | bytes 786440 | tf_op jit(solution)/shard_map/ppermute | solution.py:1032
  72.8 14.2 %collective-permute-start.21 = (bf16[2,4,8,2048]{3,2,1,0:T(8,128)(2,1)S(1)}, bf16[2,4,8,2048]{3,2,1,0:T(8,128)(2,1)S(1)}, u32[]{:S(2)}, u32[]{:S(2)}) collective-permute-start(bf16[2,4,8,2048]{3,2,1,0:T(8,128)(2,1)S(1)} %stack.38.refs_0_), channel_id=1, source_target_pairs={{0,8},{4,12},{8,0},{12,4},{16,24},{20,28},{24,16},{28,20},{1,9},{5... | collective-permute-start | bytes 786440 | tf_op jit(solution)/shard_map/ppermute | solution.py:1032
  87.1 42.4 %collective-permute-start.25 = (bf16[4,128,1024]{2,1,0:T(8,128)(2,1)S(1)}, bf16[4,128,1024]{2,1,0:T(8,128)(2,1)S(1)}, u32[]{:S(2)}, u32[]{:S(2)}) collective-permute-start(bf16[4,128,1024]{2,1,0:T(8,128)(2,1)S(1)} %get-tuple-element.320.u0), channel_id=1, source_target_pairs={{0,2},{1,3},{2,0},{3,1},{4,6},{5,7},{6,4},{7,5},{8,10},{9,11},{10,... | collective-permute-start | bytes 3145736 | tf_op jit(solution)/shard_map/ppermute | solution.py:1032
  88.4 41.1 %collective-permute-start.26 = (bf16[4,128,1024]{2,1,0:T(8,128)(2,1)S(1)}, bf16[4,128,1024]{2,1,0:T(8,128)(2,1)S(1)}, u32[]{:S(2)}, u32[]{:S(2)}) collective-permute-start(bf16[4,128,1024]{2,1,0:T(8,128)(2,1)S(1)} %get-tuple-element.320.u0), channel_id=1, source_target_pairs={{0,1},{1,0},{2,3},{3,2},{4,5},{5,4},{6,7},{7,6},{8,9},{9,8},{10,11... | collective-permute-start | bytes 3145736 | tf_op jit(solution)/shard_map/ppermute | solution.py:1032
  88.7 40.8 %collective-permute-start.27 = (bf16[4,4,8,2048]{3,2,1,0:T(8,128)(2,1)S(1)}, bf16[4,4,8,2048]{3,2,1,0:T(8,128)(2,1)S(1)}, u32[]{:S(2)}, u32[]{:S(2)}) collective-permute-start(bf16[4,4,8,2048]{3,2,1,0:T(8,128)(2,1)S(1)} %stack.39.factors0), channel_id=1, source_target_pairs={{0,16},{4,20},{8,24},{12,28},{16,0},{20,4},{24,8},{28,12},{1,17},{... | collective-permute-start | bytes 1572872 | tf_op jit(solution)/shard_map/ppermute | solution.py:1032
  91.3 43.6 %collective-permute-start.29 = (bf16[4,128,1024]{2,1,0:T(8,128)(2,1)S(1)}, bf16[4,128,1024]{2,1,0:T(8,128)(2,1)S(1)}, u32[]{:S(2)}, u32[]{:S(2)}) collective-permute-start(bf16[4,128,1024]{2,1,0:T(8,128)(2,1)S(1)} %get-tuple-element.345.u0), channel_id=1, source_target_pairs={{0,2},{1,3},{2,0},{3,1},{4,6},{5,7},{6,4},{7,5},{8,10},{9,11},{10,... | collective-permute-start | bytes 3145736 | tf_op jit(solution)/shard_map/ppermute | solution.py:1032
  91.8 43.1 %collective-permute-start.30 = (bf16[4,128,1024]{2,1,0:T(8,128)(2,1)S(1)}, bf16[4,128,1024]{2,1,0:T(8,128)(2,1)S(1)}, u32[]{:S(2)}, u32[]{:S(2)}) collective-permute-start(bf16[4,128,1024]{2,1,0:T(8,128)(2,1)S(1)} %get-tuple-element.345.u0), channel_id=1, source_target_pairs={{0,1},{1,0},{2,3},{3,2},{4,5},{5,4},{6,7},{7,6},{8,9},{9,8},{10,11... | collective-permute-start | bytes 3145736 | tf_op jit(solution)/shard_map/ppermute | solution.py:1032
  134.9 16.3 %collective-permute-start.36 = (bf16[4,128,1024]{2,1,0:T(8,128)(2,1)S(1)}, bf16[4,128,1024]{2,1,0:T(8,128)(2,1)S(1)}, u32[]{:S(2)}, u32[]{:S(2)}) collective-permute-start(bf16[4,128,1024]{2,1,0:T(8,128)(2,1)S(1)} %collective-permute-done.29.u2), channel_id=1, source_target_pairs={{0,1},{1,0},{2,3},{3,2},{4,5},{5,4},{6,7},{7,6},{8,9},{9,8},{10,11... | collective-permute-start | bytes 3145736 | tf_op jit(solution)/shard_map/ppermute | solution.py:1032
  136.1 15.1 %collective-permute-start.35 = (bf16[8,256,128]{2,1,0:T(8,128)(2,1)S(1)}, bf16[8,256,128]{2,1,0:T(8,128)(2,1)S(1)}, u32[]{:S(2)}, u32[]{:S(2)}) collective-permute-start(bf16[8,256,128]{2,1,0:T(8,128)(2,1)S(1)} %get-tuple-element.368), channel_id=1, source_target_pairs={{0,4},{4,0},{8,12},{12,8},{16,20},{20,16},{24,28},{28,24},{1,5},{5... | collective-permute-start | bytes 1572872 | tf_op jit(solution)/shard_map/ppermute | solution.py:1032
  138.2 13.0 %collective-permute-start.34 = (bf16[1024,128]{1,0:T(8,128)(2,1)S(1)}, bf16[1024,128]{1,0:T(8,128)(2,1)S(1)}, u32[]{:S(2)}, u32[]{:S(2)}) collective-permute-start(bf16[1024,128]{1,0:T(8,128)(2,1)S(1)} %get-tuple-element.366), channel_id=1, source_target_pairs={{0,3},{1,2},{2,1},{3,0},{4,7},{5,6},{6,5},{7,4},{8,11},{9,10},{10,... | collective-permute-start | bytes 786440 | tf_op jit(solution)/shard_map/ppermute | solution.py:1032
  158.0 25.7 %collective-permute-start.43 = (bf16[9,256,128]{2,1,0:T(8,128)(2,1)S(1)}, bf16[9,256,128]{2,1,0:T(8,128)(2,1)S(1)}, u32[]{:S(2)}, u32[]{:S(2)}) collective-permute-start(bf16[9,256,128]{2,1,0:T(8,128)(2,1)S(1)} %get-tuple-element.419), channel_id=1, source_target_pairs={{0,4},{4,0},{8,12},{12,8},{16,20},{20,16},{24,28},{28,24},{1,5},{5... | collective-permute-start | bytes 1769480 | tf_op jit(solution)/shard_map/ppermute | solution.py:1032
  159.0 19.2 %collective-permute-start.39 = (bf16[1024,128]{1,0:T(8,128)(2,1)S(1)}, bf16[1024,128]{1,0:T(8,128)(2,1)S(1)}, u32[]{:S(2)}, u32[]{:S(2)}) collective-permute-start(bf16[1024,128]{1,0:T(8,128)(2,1)S(1)} %get-tuple-element.399), channel_id=1, source_target_pairs={{0,1},{1,0},{2,3},{3,2},{4,5},{5,4},{6,7},{7,6},{8,9},{9,8},{10,11... | collective-permute-start | bytes 786440 | tf_op jit(solution)/shard_map/ppermute | solution.py:1032
  159.0 19.2 %collective-permute-start.40 = (bf16[1024,128]{1,0:T(8,128)(2,1)S(1)}, bf16[1024,128]{1,0:T(8,128)(2,1)S(1)}, u32[]{:S(2)}, u32[]{:S(2)}) collective-permute-start(bf16[1024,128]{1,0:T(8,128)(2,1)S(1)} %get-tuple-element.400), channel_id=1, source_target_pairs={{0,2},{1,3},{2,0},{3,1},{4,6},{5,7},{6,4},{7,5},{8,10},{9,11},{10,... | collective-permute-start | bytes 786440 | tf_op jit(solution)/shard_map/ppermute | solution.py:1032
  160.5 17.7 %collective-permute-start.41 = (bf16[1024,128]{1,0:T(8,128)(2,1)S(1)}, bf16[1024,128]{1,0:T(8,128)(2,1)S(1)}, u32[]{:S(2)}, u32[]{:S(2)}) collective-permute-start(bf16[1024,128]{1,0:T(8,128)(2,1)S(1)} %get-tuple-element.401), channel_id=1, source_target_pairs={{0,3},{1,2},{2,1},{3,0},{4,7},{5,6},{6,5},{7,4},{8,11},{9,10},{10,... | collective-permute-start | bytes 786440 | tf_op jit(solution)/shard_map/ppermute | solution.py:1032
  183.1 19.3 %collective-permute-start.47 = (bf16[9,256,128]{2,1,0:T(8,128)(2,1)S(1)}, bf16[9,256,128]{2,1,0:T(8,128)(2,1)S(1)}, u32[]{:S(2)}, u32[]{:S(2)}) collective-permute-start(bf16[9,256,128]{2,1,0:T(8,128)(2,1)S(1)} %get-tuple-element.442), channel_id=1, source_target_pairs={{0,4},{4,0},{8,12},{12,8},{16,20},{20,16},{24,28},{28,24},{1,5},{5... | collective-permute-start | bytes 1769480 | tf_op jit(solution)/shard_map/ppermute | solution.py:1032
  184.4 31.2 %collective-permute-start.51 = (bf16[2,1024,128]{2,1,0:T(8,128)(2,1)S(1)}, bf16[2,1024,128]{2,1,0:T(8,128)(2,1)S(1)}, u32[]{:S(2)}, u32[]{:S(2)}) collective-permute-start(bf16[2,1024,128]{2,1,0:T(8,128)(2,1)S(1)} %copy-done.14), channel_id=1, source_target_pairs={{0,2},{1,3},{2,0},{3,1},{4,6},{5,7},{6,4},{7,5},{8,10},{9,11},{10,... | collective-permute-start | bytes 1572872 | tf_op jit(solution)/shard_map/ppermute | solution.py:1032
  203.0 12.6 %collective-permute-start.50 = (bf16[9,128,128]{2,1,0:T(8,128)(2,1)S(1)}, bf16[9,128,128]{2,1,0:T(8,128)(2,1)S(1)}, u32[]{:S(2)}, u32[]{:S(2)}) collective-permute-start(bf16[9,128,128]{2,1,0:T(8,128)(2,1)S(1)} %get-tuple-element.459), channel_id=1, source_target_pairs={{0,8},{4,12},{8,0},{12,4},{16,24},{20,28},{24,16},{28,20},{1,9},{5... | collective-permute-start | bytes 884744 | tf_op jit(solution)/shard_map/ppermute | solution.py:1032
  203.1 11.9 %collective-permute-start.48 = (bf16[4,128,128]{2,1,0:T(8,128)(2,1)S(1)}, bf16[4,128,128]{2,1,0:T(8,128)(2,1)S(1)}, u32[]{:S(2)}, u32[]{:S(2)}) collective-permute-start(bf16[4,128,128]{2,1,0:T(8,128)(2,1)S(1)} %join.6.refs_0_), channel_id=1, source_target_pairs={{0,8},{4,12},{8,0},{12,4},{16,24},{20,28},{24,16},{28,20},{1,9},{5... | collective-permute-start | bytes 393224 | tf_op jit(solution)/shard_map/ppermute | solution.py:1032
  215.0 22.3 %collective-permute-start.56 = (bf16[2,1056,128]{2,1,0:T(8,128)(2,1)S(1)}, bf16[2,1056,128]{2,1,0:T(8,128)(2,1)S(1)}, u32[]{:S(2)}, u32[]{:S(2)}) collective-permute-start(bf16[2,1056,128]{2,1,0:T(8,128)(2,1)S(1)} %get-tuple-element.480), channel_id=1, source_target_pairs={{0,2},{1,3},{2,0},{3,1},{4,6},{5,7},{6,4},{7,5},{8,10},{9,11},{10,... | collective-permute-start | bytes 1622024 | tf_op jit(solution)/shard_map/ppermute | solution.py:1032
  216.2 13.2 %collective-permute-start.52 = (bf16[9,128,128]{2,1,0:T(8,128)(2,1)S(1)}, bf16[9,128,128]{2,1,0:T(8,128)(2,1)S(1)}, u32[]{:S(2)}, u32[]{:S(2)}) collective-permute-start(bf16[9,128,128]{2,1,0:T(8,128)(2,1)S(1)} %join.7.refs_0_), channel_id=1, source_target_pairs={{0,8},{4,12},{8,0},{12,4},{16,24},{20,28},{24,16},{28,20},{1,9},{5... | collective-permute-start | bytes 884744 | tf_op jit(solution)/shard_map/ppermute | solution.py:1032
  230.5 16.9 %collective-permute-start.61 = (bf16[9,256,128]{2,1,0:T(8,128)(2,1)S(1)}, bf16[9,256,128]{2,1,0:T(8,128)(2,1)S(1)}, u32[]{:S(2)}, u32[]{:S(2)}) collective-permute-start(bf16[9,256,128]{2,1,0:T(8,128)(2,1)S(1)} %join.11.mine), channel_id=1, source_target_pairs={{0,4},{4,0},{8,12},{12,8},{16,20},{20,16},{24,28},{28,24},{1,5},{5... | collective-permute-start | bytes 1769480 | tf_op jit(solution)/shard_map/ppermute | solution.py:1032
  247.8 18.2 %collective-permute-start.66 = (bf16[9,256,128]{2,1,0:T(8,128)(2,1)S(1)}, bf16[9,256,128]{2,1,0:T(8,128)(2,1)S(1)}, u32[]{:S(2)}, u32[]{:S(2)}) collective-permute-start(bf16[9,256,128]{2,1,0:T(8,128)(2,1)S(1)} %join.10.mine), channel_id=1, source_target_pairs={{0,4},{4,0},{8,12},{12,8},{16,20},{20,16},{24,28},{28,24},{1,5},{5... | collective-permute-start | bytes 1769480 | tf_op jit(solution)/shard_map/ppermute | solution.py:1032
  (57 other events, 364.3 us)

commit v7 on v6

--- a/solution.py
+++ b/solution.py
@@ -1382,8 +1382,9 @@
         [smem()] + [vmem()] * 6,
         [grad_scratch, pltpu.VMEM((4, S_ROWS, LANES), F32)],
     )(meta, grad_first, image, pack, stats1, dmiddle, sums)
-    grad_far, terms2, got1, own1 = tie(grad_far, terms2, got1, own1)
+    grad_far, got1, own1 = tie(grad_far, got1, own1)
     terms1 = down([own1, got1], 1)
+    terms1[0], terms2 = tie(terms1[0], terms2)
     ends2 = across(inner_levels(terms2), 2)
     factors, ends2[0], terms1[0] = tie(factors, ends2[0], terms1[0])
     columns = -(-5 * slots * lax.axis_size("dp") // LANES) * LANES
@@ -1395,20 +1396,17 @@
         [],
         limit=12 if len(steps) < 4 else 56,
     )(meta, *factors)
-    grad_far, ends2[0], terms1[0], att, left = tie(grad_far, ends2[0], terms1[0], att, left)
-    att = across(join(att, digits[1], meta), 0)
-    grad_far = swap(grad_far, "mp", 2)
-    ends2, terms1, grad_near, out_far = tie(ends2, terms1, grad_near, out_far)
+    grad_far, ends2, terms1, left, out_far = tie(grad_far, ends2, terms1, left, out_far)
     terms1 = down(terms1, 2)
     ends2 = across(join(ends2, digits[2], meta), 1)
+    grad_far = swap(grad_far, "mp", 2)
     scale = call(kernel_scale, "scale", struct((8, LANES), F32), [vmem()] * 2, [], limit=8)(*factors)
-    ends2, terms1, scale, att = tie(ends2, terms1, scale, att)
+    ends2, terms1, scale = tie(ends2, terms1, scale)
     ends1 = across(inner_levels(terms1), 2)
     ends2 = across(join(ends2, digits[1], meta), 0)
-    qkv_grad, proj_grad = last_join(att, digits[0], meta, scale, True)
-    ends1, qkv_grad, grad_near = tie(ends1, qkv_grad, grad_near)
+    ends1, grad_near, grad_far, att = tie(ends1, grad_near, grad_far, att)
     ends1 = across(join(ends1, digits[2], meta), 1)
-    ends1[0], grad_near, grad_far = tie(ends1[0], grad_near, grad_far)
+    att = across(join(att, digits[1], meta), 0)
     grad_near = swap(grad_near, "mp", 1)
     grad_across = swap(grad_far, "mp", 1)
     image_parts = (grad_own, grad_near, grad_far, grad_across)
@@ -1422,14 +1420,13 @@
     )(grad_own, grad_near, grad_far, grad_across)
     small_got = swap(smalls, "dp", 1)
     ends1 = across(join(ends1, digits[1], meta), 0)
-    ends1[0], small_got, ends2 = tie(ends1[0], small_got, ends2)
+    ends1[0], small_got, ends2, att = tie(ends1[0], small_got, ends2, att)
     smalls = stack([smalls, small_got])
     for low in steps[1:-1]:
         smalls = stack([smalls, swap(smalls, "dp", low)])
     small_got = swap(smalls, "dp", steps[-1])
     (conv2_grad,) = last_join(ends2, digits[0], meta, scale)
-    smalls, out_far, out_near, conv2_grad = tie(smalls, out_far, out_near, conv2_grad)
-    out_parts = (out_own, swap(out_near, "mp", 1), out_far, swap(out_far, "mp", 1))
+    qkv_grad, proj_grad = last_join(att, digits[0], meta, scale, True)
     def in_slots(parts):
         return pl.pallas_call(
             kernel_slots,
@@ -1441,9 +1438,11 @@
             compiler_params=pltpu.CompilerParams(vmem_limit_bytes=8 * MIB),
         )(meta, *parts)
 
-    block_out = in_slots(out_parts)
     image_grad = in_slots(image_parts)
-    small_got, block_out, image_grad = tie(small_got, block_out, image_grad)
+    small_got, image_grad, conv2_grad, qkv_grad, out_far, out_near = tie(
+        small_got, image_grad, conv2_grad, qkv_grad, out_far, out_near
+    )
+    out_parts = (out_own, swap(out_near, "mp", 1), out_far, swap(out_far, "mp", 1))
     embed_grad, context_grad, vector_sums = call(
         kernel_factor_grads,
         "factor_grads",
@@ -1457,7 +1456,9 @@
         limit=14 if len(steps) < 4 else 56,
     )(scale, left, smalls, small_got)
 
-    ends1, embed_grad = tie(ends1, embed_grad)
+    out_parts, embed_grad = tie(out_parts, embed_grad)
+    block_out = in_slots(out_parts)
+    ends1, block_out = tie(ends1, block_out)
     (conv1_grad,) = last_join(ends1, digits[0], meta, scale)
     return (
         block_out,

time: 269 us -> 268 us (level)
  transfers between devices with their start and end apart: 67 -> 67, of which waited for: 23 -> 25; matrix products, arithmetic and copies ran while one was open for 3% -> 4% of each run, Pallas kernels for 46% -> 47%
where the time goes in v7:
time: 268 us
  Pallas kernels  127 us (47%)
  waiting for transfers between devices  71.1 us (27%)
  starting transfers between devices  55.9 us (21%)
  local copies, waits for them, and re-layouts  6.29 us (2%)
  other arithmetic  2.77 us (1%)
    ppermute x67, waiting for transfers between devices, swap(): return lax.ppermute(value, axis, [(i, i ^ offset) for i in range(size)])  71.1 us
    ppermute x67, starting transfers between devices, swap(): return lax.ppermute(value, axis, [(i, i ^ offset) for i in range(size)])  55.9 us
    pallas_call x1, Pallas kernels, local(): call(kernel_attention, 'attention', [piece, piece, pair_piece] + [block,...  33.8 us
    pallas_call x1, Pallas kernels, local(): call(kernel_second, 'second', [block32, turned, struct((4, pixels, 3 * LA...  13.3 us
    pallas_call x1, Pallas kernels, local(): call(kernel_first, 'first', [block, struct((4, E_ROWS, LANES), F32), turn...  12.7 us
    pallas_call x2, Pallas kernels, weight_send(): call(kernel_weight_send, 'weight_send', [struct((9, C // 2, LANES), BF16)...  9.61 us
    pallas_call x1, Pallas kernels, local(): call(kernel_back_second, 'back_second', [fields, struct((4, S_ROWS, LANES...  9.08 us
    pallas_call x2, Pallas kernels, weight_own(): call(kernel_weight_own, 'weight_own', struct((9, C // 2, LANES), F32), [s...  8.42 us
  transfers between devices with their start and end apart: 67, of which 25 were waited for; matrix products, arithmetic and copies ran while one was open for 4% of the time, Pallas kernels for 47%

profile of v7, /device:TPU:0, one launch (start us, length us, event | category | flops | bytes accessed | tf_op | source)
XLA Modules:
  0.0 267.5 jit_solution(1260178530452096481)
XLA Ops:
  5.9 3.0 %collective-permute-start.2 = (bf16[2304,128]{1,0:T(8,128)(2,1)}, bf16[2304,128]{1,0:T(8,128)(2,1)S(1)}, u32[]{:S(2)}, u32[]{:S(2)}) collective-permute-start(bf16[2304,128]{1,0:T(8,128)(2,1)} %constant_dynamic-slice_fusion.3), channel_id=1, source_target_pairs={{0,2},{1,3},{2,0},{3,1},{4,6},{5,7},{6,4},{7,5},{8,10},{9,11},{10,... | collective-permute-start | bytes 1769480 | tf_op jit(solution)/shard_map/ppermute | solution.py:1032
  14.4 8.9 %collective-permute-done.2.source.w2 = bf16[2304,128]{1,0:T(8,128)(2,1)S(1)} collective-permute-done((bf16[2304,128]{1,0:T(8,128)(2,1)}, bf16[2304,128]{1,0:T(8,128)(2,1)S(1)}, u32[]{:S(2)}, u32[]{:S(2)}) %collective-permute-start.2) | collective-permute-done | bytes 589856 | tf_op jit(solution)/shard_map/ppermute | solution.py:1032
  23.3 2.2 collective-permute-start.7
  27.2 4.0 %collective-permute-done.7.w4 = bf16[1152,128]{1,0:T(8,128)(2,1)S(1)} collective-permute-done((bf16[1152,128]{1,0:T(8,128)(2,1)S(1)}, bf16[1152,128]{1,0:T(8,128)(2,1)S(1)}, u32[]{:S(2)}, u32[]{:S(2)}) %collective-permute-start.7) | collective-permute-done | bytes 294944 | tf_op jit(solution)/shard_map/ppermute | solution.py:1032
  41.1 12.7 %first.1 = (bf16[4,1024,128]{2,1,0:T(8,128)(2,1)S(1)}, f32[4,32,128]{2,1,0:T(8,128)S(1)}, bf16[4,128,1024]{2,1,0:T(8,128)(2,1)S(1)}, f32[4,1024,128]{2,1,0:T(8,1...) custom-call(s32[6]{0:T(128)S(1)} %stack.36.meta, ...), custom_call_target="tpu_custom_call" | custom-call | tf_op jit(solution)/shard_map/first/pallas_call | solution.py:1186
  55.2 2.8 %collective-permute-done.13.source.w2 = bf16[3328,128]{1,0:T(8,128)(2,1)S(1)} collective-permute-done((bf16[3328,128]{1,0:T(8,128)(2,1)S(1)}, bf16[3328,128]{1,0:T(8,128)(2,1)S(1)}, u32[]{:S(2)}, u32[]{:S(2)}) %collective-permute-start.13) | collective-permute-done | bytes 852000 | tf_op jit(solution)/shard_map/ppermute | solution.py:1032
  60.4 9.1 %collective-permute-done.16.w3 = bf16[1664,128]{1,0:T(8,128)(2,1)S(1)} collective-permute-done((bf16[1664,128]{1,0:T(8,128)(2,1)S(1)}, bf16[1664,128]{1,0:T(8,128)(2,1)S(1)}, u32[]{:S(2)}, u32[]{:S(2)}) %collective-permute-start.16) | collective-permute-done | bytes 426016 | tf_op jit(solution)/shard_map/ppermute | solution.py:1032
  73.7 13.3 %second.1 = (f32[4,1024,128]{2,1,0:T(8,128)S(1)}, bf16[4,128,1024]{2,1,0:T(8,128)(2,1)S(1)}, bf16[4,1024,384]{2,1,0:T(8,128)(2,1)S(1)}, bf16[4,1536,128]{2,1,0:T...) custom-call(s32[6]{0:T(128)S(1)} %stack.36.meta, ...), custom_call_target="tpu_custom_call" | custom-call | tf_op jit(solution)/shard_map/second/pallas_call | solution.py:1210
  88.7 2.7 collective-permute-start.27
  91.8 33.8 %attention.1 = (bf16[1024,128]{1,0:T(8,128)(2,1)S(1)}, bf16[1024,128]{1,0:T(8,128)(2,1)S(1)}, bf16[2,1024,128]{2,1,0:T(8,128)(2,1)S(1)}, bf16[4,1024,128]{2,1,0:...) custom-call(s32[6]{0:T(128)S(1)} %stack.36.meta, ...), custom_call_target="tpu_custom_call" | custom-call | tf_op jit(solution)/shard_map/attention/pallas_call | solution.py:1237
  125.7 3.8 %attention_grad.1 = (bf16[2,4,512,128]{3,2,1,0:T(8,128)(2,1)S(1)}, bf16[2,4,512,128]{3,2,1,0:T(8,128)(2,1)S(1)}) custom-call(s32[6]{0:T(128)S(1)} %stack.36.meta, bf16[4,1024,384]{2,1,0:T(8,128)(2,1)S(1)} %get-tuple-element.336.dqkv, bf16[4,1024,128]{2,1,0:T(8,128)(2,1)S(1)} %get-tuple-element.328.mixed, ...), custom_call_target="tpu_custom_call" | custom-call | tf_op jit(solution)/shard_map/attention_grad/pallas_call | solution.py:1293
  130.1 4.6 %back_attention.1 = (f32[4,1024,128]{2,1,0:T(8,128)S(1)}, bf16[3,4,1088,128]{3,2,1,0:T(8,128)(2,1)S(1)}, f32[4,32,128]{2,1,0:T(8,128)S(1)}, bf16[1024,128]{1,0:T...) custom-call(s32[6]{0:T(128)S(1)} %stack.36.meta, ...), custom_call_target="tpu_custom_call" | custom-call | tf_op jit(solution)/shard_map/back_attention/pallas_call | solution.py:1303
  139.1 9.1 %back_second.1 = (bf16[3,4,1088,128]{3,2,1,0:T(8,128)(2,1)S(1)}, f32[4,32,128]{2,1,0:T(8,128)S(1)}, bf16[1024,128]{1,0:T(8,128)(2,1)S(1)}, bf16[1024,128]{1,0:T(...) custom-call(s32[6]{0:T(128)S(1)} %stack.36.meta, ...), custom_call_target="tpu_custom_call" | custom-call | tf_op jit(solution)/shard_map/back_second/pallas_call | solution.py:1318
  148.3 3.0 %collective-permute-done.34.d3 = bf16[1024,128]{1,0:T(8,128)(2,1)S(1)} collective-permute-done((bf16[1024,128]{1,0:T(8,128)(2,1)S(1)}, bf16[1024,128]{1,0:T(8,128)(2,1)S(1)}, u32[]{:S(2)}, u32[]{:S(2)}) %collective-permute-start.34) | collective-permute-done | bytes 262176 | tf_op jit(solution)/shard_map/ppermute | solution.py:1032
  153.2 4.8 %weight_send.2 = (bf16[9,256,128]{2,1,0:T(8,128)(2,1)S(1)}, bf16[3,4,1088,128]{3,2,1,0:T(8,128)(2,1)S(1)}) custom-call(s32[6]{0:T(128)S(1)} %stack.36.meta, bf16[4,128,1024]{2,1,0:T(8,128)(2,1)S(1)} %get-tuple-element.319.u0, bf16[4,128,1024]{2,1,0:T(8,128)(2,1)S(1)} %collective-permute-done.26.u1, bf16[4,128,1024]{2,1,0:T(8,128)(2,1)S(1)} %collective-permute-done.25.u2, ...), custom_call_target="tpu_custom_call" | custom-call | tf_op jit(solution)/shard_map/weight_send/pallas_call | solution.py:1259
  163.5 4.2 %weight_own.2.refs_0_ = f32[9,256,128]{2,1,0:T(8,128)S(1)} custom-call(s32[6]{0:T(128)S(1)} %stack.36.meta, bf16[4,128,1024]{2,1,0:T(8,128)(2,1)S(1)} %get-tuple-element.319.u0, bf16[4,128,1024]{2,1,0:T(8,128)(2,1)S(1)} %collective-permute-done.26.u1, bf16[4,128,1024]{2,1,0:T(8,128)(2,1)S(1)} %collective-permute-done.25.u2, ...), custom_call_target="tpu_custom_call" | custom-call | tf_op jit(solution)/shard_map/weight_own/pallas_call | solution.py:1269
  167.8 3.2 %collective-permute-done.38.got = bf16[8,64,128]{2,1,0:T(8,128)(2,1)S(1)} collective-permute-done((bf16[8,64,128]{2,1,0:T(8,128)(2,1)S(1)}, bf16[8,64,128]{2,1,0:T(8,128)(2,1)S(1)}, u32[]{:S(2)}, u32[]{:S(2)}) %collective-permute-start.38) | collective-permute-done | bytes 131104 | tf_op jit(solution)/shard_map/ppermute | solution.py:1032
  172.5 5.7 %back_conv.1.grad_in = f32[4,1024,128]{2,1,0:T(8,128)S(1)} custom-call(bf16[3,4,1088,128]{3,2,1,0:T(8,128)(2,1)S(1)} %get-tuple-element.395.grad_field, bf16[4,4608,128]{2,1,0:T(8,128)(2,1)S(1)} %get-tuple-element.396.weight), custom_call_target="tpu_custom_call" | custom-call | tf_op jit(solution)/shard_map/back_conv/pallas_call | solution.py:1350
  178.2 4.8 %weight_send.3 = (bf16[9,256,128]{2,1,0:T(8,128)(2,1)S(1)}, bf16[3,4,1088,128]{3,2,1,0:T(8,128)(2,1)S(1)}) custom-call(s32[6]{0:T(128)S(1)} %stack.36.meta, bf16[4,128,1024]{2,1,0:T(8,128)(2,1)S(1)} %get-tuple-element.344.u0, bf16[4,128,1024]{2,1,0:T(8,128)(2,1)S(1)} %collective-permute-done.30.u1, bf16[4,128,1024]{2,1,0:T(8,128)(2,1)S(1)} %collective-permute-done.29.u2, ...), custom_call_target="tpu_custom_call" | custom-call | tf_op jit(solution)/shard_map/weight_send/pallas_call | solution.py:1259
  185.6 2.6 collective-permute-start.45
  188.1 4.2 %weight_own.3.refs_0_ = f32[9,256,128]{2,1,0:T(8,128)S(1)} custom-call(s32[6]{0:T(128)S(1)} %stack.36.meta, bf16[4,128,1024]{2,1,0:T(8,128)(2,1)S(1)} %get-tuple-element.344.u0, bf16[4,128,1024]{2,1,0:T(8,128)(2,1)S(1)} %collective-permute-done.30.u1, bf16[4,128,1024]{2,1,0:T(8,128)(2,1)S(1)} %collective-permute-done.29.u2, ...), custom_call_target="tpu_custom_call" | custom-call | tf_op jit(solution)/shard_map/weight_own/pallas_call | solution.py:1269
  196.4 2.9 %back_first.1 = (bf16[1056,128]{1,0:T(8,128)(2,1)S(1)}, bf16[1056,128]{1,0:T(8,128)(2,1)S(1)}, bf16[2,1056,128]{2,1,0:T(8,128)(2,1)S(1)}) custom-call(s32[6]{0:T(128)S(1)} %stack.36.meta, f32[4,1024,128]{2,1,0:T(8,128)S(1)} %back_conv.1.grad_in, bf16[4,1024,128]{2,1,0:T(8,128)(2,1)S(1)} %get-tuple-element.300.image, ...), custom_call_target="tpu_custom_call" | custom-call | tf_op jit(solution)/shard_map/back_first/pallas_call | solution.py:1374
  204.2 5.5 %collective-permute-done.48.refs_1_ = bf16[9,64,128]{2,1,0:T(8,128)(2,1)S(1)} collective-permute-done((bf16[9,64,128]{2,1,0:T(8,128)(2,1)S(1)}, bf16[9,64,128]{2,1,0:T(8,128)(2,1)S(1)}, u32[]{:S(2)}, u32[]{:S(2)}) %collective-permute-start.48) | collective-permute-done | bytes 147488 | tf_op jit(solution)/shard_map/ppermute | solution.py:1032
  216.2 5.7 %collective-permute-done.52.refs_1_ = bf16[9,64,128]{2,1,0:T(8,128)(2,1)S(1)} collective-permute-done((bf16[9,64,128]{2,1,0:T(8,128)(2,1)S(1)}, bf16[9,64,128]{2,1,0:T(8,128)(2,1)S(1)}, u32[]{:S(2)}, u32[]{:S(2)}) %collective-permute-start.52) | collective-permute-done | bytes 147488 | tf_op jit(solution)/shard_map/ppermute | solution.py:1032
  221.9 2.2 collective-permute-done.51.refs_1_
  227.3 4.7 %collective-permute-done.55.refs_1_ = bf16[4,128,128]{2,1,0:T(8,128)(2,1)S(1)} collective-permute-done((bf16[4,128,128]{2,1,0:T(8,128)(2,1)S(1)}, bf16[4,128,128]{2,1,0:T(8,128)(2,1)S(1)}, u32[]{:S(2)}, u32[]{:S(2)}) %collective-permute-start.55) | collective-permute-done | bytes 131104 | tf_op jit(solution)/shard_map/ppermute | solution.py:1032
  235.9 6.1 %collective-permute-done.56.refs_1_ = bf16[9,128,128]{2,1,0:T(8,128)(2,1)S(1)} collective-permute-done((bf16[9,128,128]{2,1,0:T(8,128)(2,1)S(1)}, bf16[9,128,128]{2,1,0:T(8,128)(2,1)S(1)}, u32[]{:S(2)}, u32[]{:S(2)}) %collective-permute-start.56) | collective-permute-done | bytes 294944 | tf_op jit(solution)/shard_map/ppermute | solution.py:1032
  246.6 2.5 collective-permute-done.63.refs_1_
  249.2 2.9 %collective-permute-start.64 = (bf16[16,32,128]{2,1,0:T(8,128)(2,1)S(1)}, bf16[16,32,128]{2,1,0:T(8,128)(2,1)S(1)}, u32[]{:S(2)}, u32[]{:S(2)}) collective-permute-start(bf16[16,32,128]{2,1,0:T(8,128)(2,1)S(1)} %stack.42.small0), channel_id=1, source_target_pairs={{0,16},{4,20},{8,24},{12,28},{16,0},{20,4},{24,8},{28,12},{1,17},{... | collective-permute-start | bytes 393224 | tf_op jit(solution)/shard_map/ppermute | solution.py:1032
  256.0 2.1 last_join.3
  258.6 4.6 %factor_grads.1 = (f32[2048,2,128]{2,1,0:T(2,128)}, f32[2048,2,128]{2,1,0:T(2,128)}, f32[32,128]{1,0:T(8,128)S(1)}) custom-call(f32[8,128]{1,0:T(8,128)S(1)} %scale.1, bf16[2048,256]{1,0:T(8,128)(2,1)S(1)} %factors.1.left, bf16[16,32,128]{2,1,0:T(8,128)(2,1)S(1)} %stack.42.small0, bf16[16,32,128]{2,1,0:T(8,128)(2,1)S(1)} %collective-permute-done.64.small1), custom_call_target="tpu_custom_call" | custom-call | tf_op jit(solution)/shard_map/factor_grads/pallas_call | solution.py:1446
  265.4 2.1 last_join.5
  (211 shorter events, 81.7 us)
Async XLA Ops:
  1.4 21.8 %collective-permute-start = (bf16[4608,128]{1,0:T(8,128)(2,1)}, bf16[4608,128]{1,0:T(8,128)(2,1)S(1)}, u32[]{:S(2)}, u32[]{:S(2)}) collective-permute-start(bf16[4608,128]{1,0:T(8,128)(2,1)} %bitcast.80), channel_id=1, source_target_pairs={{0,1},{1,0},{2,3},{3,2},{4,5},{5,4},{6,7},{7,6},{8,9},{9,8},{10,11... | collective-permute-start | bytes 3538952 | tf_op jit(solution)/shard_map/ppermute | solution.py:1032
  5.9 17.3 %collective-permute-start.2 = (bf16[2304,128]{1,0:T(8,128)(2,1)}, bf16[2304,128]{1,0:T(8,128)(2,1)S(1)}, u32[]{:S(2)}, u32[]{:S(2)}) collective-permute-start(bf16[2304,128]{1,0:T(8,128)(2,1)} %constant_dynamic-slice_fusion.3), channel_id=1, source_target_pairs={{0,2},{1,3},{2,0},{3,1},{4,6},{5,7},{6,4},{7,5},{8,10},{9,11},{10,... | collective-permute-start | bytes 1769480 | tf_op jit(solution)/shard_map/ppermute | solution.py:1032
  9.7 24.4 %collective-permute-start.3 = (bf16[2,1024,128]{2,1,0:T(8,128)(2,1)}, bf16[2,1024,128]{2,1,0:T(8,128)(2,1)}, u32[]{:S(2)}, u32[]{:S(2)}) collective-permute-start(bf16[2,1024,128]{2,1,0:T(8,128)(2,1)} %pad_maximum_fusion.1), channel_id=1, source_target_pairs={{0,2},{1,3},{2,0},{3,1},{4,6},{5,7},{6,4},{7,5},{8,10},{9,11},{10,... | collective-permute-start | bytes 1572872 | tf_op jit(solution)/shard_map/ppermute | solution.py:1032
  36.5 21.4 %collective-permute-start.14 = (bf16[6656,128]{1,0:T(8,128)(2,1)S(1)}, bf16[6656,128]{1,0:T(8,128)(2,1)S(1)}, u32[]{:S(2)}, u32[]{:S(2)}) collective-permute-start(bf16[6656,128]{1,0:T(8,128)(2,1)S(1)} %pad_maximum_fusion.w0), channel_id=1, source_target_pairs={{0,1},{1,0},{2,3},{3,2},{4,5},{5,4},{6,7},{7,6},{8,9},{9,8},{10,11... | collective-permute-start | bytes 5111816 | tf_op jit(solution)/shard_map/ppermute | solution.py:1032
  36.6 21.4 %collective-permute-start.13 = (bf16[3328,128]{1,0:T(8,128)(2,1)S(1)}, bf16[3328,128]{1,0:T(8,128)(2,1)S(1)}, u32[]{:S(2)}, u32[]{:S(2)}) collective-permute-start(bf16[3328,128]{1,0:T(8,128)(2,1)S(1)} %constant_dynamic-slice_fusion), channel_id=1, source_target_pairs={{0,2},{1,3},{2,0},{3,1},{4,6},{5,7},{6,4},{7,5},{8,10},{9,11},{10,... | collective-permute-start | bytes 2555912 | tf_op jit(solution)/shard_map/ppermute | solution.py:1032
  38.3 16.8 %collective-permute-start.15 = (bf16[1,4,8,2048]{3,2,1,0:T(8,128)(2,1)S(1)}, bf16[1,4,8,2048]{3,2,1,0:T(8,128)(2,1)S(1)}, u32[]{:S(2)}, u32[]{:S(2)}) collective-permute-start(bf16[1,4,8,2048]{3,2,1,0:T(8,128)(2,1)S(1)} %fusion.9.refs_0_), channel_id=1, source_target_pairs={{0,4},{4,0},{8,12},{12,8},{16,20},{20,16},{24,28},{28,24},{1,5},{5... | collective-permute-start | bytes 393224 | tf_op jit(solution)/shard_map/ppermute | solution.py:1032
  58.0 11.4 %collective-permute-start.16 = (bf16[1664,128]{1,0:T(8,128)(2,1)S(1)}, bf16[1664,128]{1,0:T(8,128)(2,1)S(1)}, u32[]{:S(2)}, u32[]{:S(2)}) collective-permute-start(bf16[1664,128]{1,0:T(8,128)(2,1)S(1)} %get-tuple-element.297), channel_id=1, source_target_pairs={{0,4},{4,0},{8,12},{12,8},{16,20},{20,16},{24,28},{28,24},{1,5},{5... | collective-permute-start | bytes 1277960 | tf_op jit(solution)/shard_map/ppermute | solution.py:1032
  59.6 11.1 %collective-permute-start.17 = (bf16[1664,128]{1,0:T(8,128)(2,1)S(1)}, bf16[1664,128]{1,0:T(8,128)(2,1)S(1)}, u32[]{:S(2)}, u32[]{:S(2)}) collective-permute-start(bf16[1664,128]{1,0:T(8,128)(2,1)S(1)} %get-tuple-element.298), channel_id=1, source_target_pairs={{0,8},{4,12},{8,0},{12,4},{16,24},{20,28},{24,16},{28,20},{1,9},{5... | collective-permute-start | bytes 1277960 | tf_op jit(solution)/shard_map/ppermute | solution.py:1032
  60.4 13.3 %collective-permute-start.18 = (bf16[3328,128]{1,0:T(8,128)(2,1)S(1)}, bf16[3328,128]{1,0:T(8,128)(2,1)S(1)}, u32[]{:S(2)}, u32[]{:S(2)}) collective-permute-start(bf16[3328,128]{1,0:T(8,128)(2,1)S(1)} %collective-permute-done.13.source.w2), channel_id=1, source_target_pairs={{0,1},{1,0},{2,3},{3,2},{4,5},{5,4},{6,7},{7,6},{8,9},{9,8},{10,11... | collective-permute-start | bytes 2555912 | tf_op jit(solution)/shard_map/ppermute | solution.py:1032
  70.7 16.4 %collective-permute-start.22 = (bf16[1024,128]{1,0:T(8,128)(2,1)S(1)}, bf16[1024,128]{1,0:T(8,128)(2,1)S(1)}, u32[]{:S(2)}, u32[]{:S(2)}) collective-permute-start(bf16[1024,128]{1,0:T(8,128)(2,1)S(1)} %get-tuple-element.316), channel_id=1, source_target_pairs={{0,1},{1,0},{2,3},{3,2},{4,5},{5,4},{6,7},{7,6},{8,9},{9,8},{10,11... | collective-permute-start | bytes 786440 | tf_op jit(solution)/shard_map/ppermute | solution.py:1032
  71.2 15.9 %collective-permute-start.23 = (bf16[1024,128]{1,0:T(8,128)(2,1)S(1)}, bf16[1024,128]{1,0:T(8,128)(2,1)S(1)}, u32[]{:S(2)}, u32[]{:S(2)}) collective-permute-start(bf16[1024,128]{1,0:T(8,128)(2,1)S(1)} %get-tuple-element.317), channel_id=1, source_target_pairs={{0,2},{1,3},{2,0},{3,1},{4,6},{5,7},{6,4},{7,5},{8,10},{9,11},{10,... | collective-permute-start | bytes 786440 | tf_op jit(solution)/shard_map/ppermute | solution.py:1032
  72.7 14.3 %collective-permute-start.24 = (bf16[1024,128]{1,0:T(8,128)(2,1)S(1)}, bf16[1024,128]{1,0:T(8,128)(2,1)S(1)}, u32[]{:S(2)}, u32[]{:S(2)}) collective-permute-start(bf16[1024,128]{1,0:T(8,128)(2,1)S(1)} %get-tuple-element.318), channel_id=1, source_target_pairs={{0,3},{1,2},{2,1},{3,0},{4,7},{5,6},{6,5},{7,4},{8,11},{9,10},{10,... | collective-permute-start | bytes 786440 | tf_op jit(solution)/shard_map/ppermute | solution.py:1032
  72.8 14.2 %collective-permute-start.21 = (bf16[2,4,8,2048]{3,2,1,0:T(8,128)(2,1)S(1)}, bf16[2,4,8,2048]{3,2,1,0:T(8,128)(2,1)S(1)}, u32[]{:S(2)}, u32[]{:S(2)}) collective-permute-start(bf16[2,4,8,2048]{3,2,1,0:T(8,128)(2,1)S(1)} %stack.38.refs_0_), channel_id=1, source_target_pairs={{0,8},{4,12},{8,0},{12,4},{16,24},{20,28},{24,16},{28,20},{1,9},{5... | collective-permute-start | bytes 786440 | tf_op jit(solution)/shard_map/ppermute | solution.py:1032
  87.1 42.4 %collective-permute-start.25 = (bf16[4,128,1024]{2,1,0:T(8,128)(2,1)S(1)}, bf16[4,128,1024]{2,1,0:T(8,128)(2,1)S(1)}, u32[]{:S(2)}, u32[]{:S(2)}) collective-permute-start(bf16[4,128,1024]{2,1,0:T(8,128)(2,1)S(1)} %get-tuple-element.319.u0), channel_id=1, source_target_pairs={{0,2},{1,3},{2,0},{3,1},{4,6},{5,7},{6,4},{7,5},{8,10},{9,11},{10,... | collective-permute-start | bytes 3145736 | tf_op jit(solution)/shard_map/ppermute | solution.py:1032
  88.4 41.1 %collective-permute-start.26 = (bf16[4,128,1024]{2,1,0:T(8,128)(2,1)S(1)}, bf16[4,128,1024]{2,1,0:T(8,128)(2,1)S(1)}, u32[]{:S(2)}, u32[]{:S(2)}) collective-permute-start(bf16[4,128,1024]{2,1,0:T(8,128)(2,1)S(1)} %get-tuple-element.319.u0), channel_id=1, source_target_pairs={{0,1},{1,0},{2,3},{3,2},{4,5},{5,4},{6,7},{7,6},{8,9},{9,8},{10,11... | collective-permute-start | bytes 3145736 | tf_op jit(solution)/shard_map/ppermute | solution.py:1032
  88.7 40.8 %collective-permute-start.27 = (bf16[4,4,8,2048]{3,2,1,0:T(8,128)(2,1)S(1)}, bf16[4,4,8,2048]{3,2,1,0:T(8,128)(2,1)S(1)}, u32[]{:S(2)}, u32[]{:S(2)}) collective-permute-start(bf16[4,4,8,2048]{3,2,1,0:T(8,128)(2,1)S(1)} %stack.39.factors0), channel_id=1, source_target_pairs={{0,16},{4,20},{8,24},{12,28},{16,0},{20,4},{24,8},{28,12},{1,17},{... | collective-permute-start | bytes 1572872 | tf_op jit(solution)/shard_map/ppermute | solution.py:1032
  91.3 43.6 %collective-permute-start.29 = (bf16[4,128,1024]{2,1,0:T(8,128)(2,1)S(1)}, bf16[4,128,1024]{2,1,0:T(8,128)(2,1)S(1)}, u32[]{:S(2)}, u32[]{:S(2)}) collective-permute-start(bf16[4,128,1024]{2,1,0:T(8,128)(2,1)S(1)} %get-tuple-element.344.u0), channel_id=1, source_target_pairs={{0,2},{1,3},{2,0},{3,1},{4,6},{5,7},{6,4},{7,5},{8,10},{9,11},{10,... | collective-permute-start | bytes 3145736 | tf_op jit(solution)/shard_map/ppermute | solution.py:1032
  91.8 43.1 %collective-permute-start.30 = (bf16[4,128,1024]{2,1,0:T(8,128)(2,1)S(1)}, bf16[4,128,1024]{2,1,0:T(8,128)(2,1)S(1)}, u32[]{:S(2)}, u32[]{:S(2)}) collective-permute-start(bf16[4,128,1024]{2,1,0:T(8,128)(2,1)S(1)} %get-tuple-element.344.u0), channel_id=1, source_target_pairs={{0,1},{1,0},{2,3},{3,2},{4,5},{5,4},{6,7},{7,6},{8,9},{9,8},{10,11... | collective-permute-start | bytes 3145736 | tf_op jit(solution)/shard_map/ppermute | solution.py:1032
  134.9 16.3 %collective-permute-start.36 = (bf16[4,128,1024]{2,1,0:T(8,128)(2,1)S(1)}, bf16[4,128,1024]{2,1,0:T(8,128)(2,1)S(1)}, u32[]{:S(2)}, u32[]{:S(2)}) collective-permute-start(bf16[4,128,1024]{2,1,0:T(8,128)(2,1)S(1)} %collective-permute-done.29.u2), channel_id=1, source_target_pairs={{0,1},{1,0},{2,3},{3,2},{4,5},{5,4},{6,7},{7,6},{8,9},{9,8},{10,11... | collective-permute-start | bytes 3145736 | tf_op jit(solution)/shard_map/ppermute | solution.py:1032
  136.1 15.1 %collective-permute-start.35 = (bf16[8,256,128]{2,1,0:T(8,128)(2,1)S(1)}, bf16[8,256,128]{2,1,0:T(8,128)(2,1)S(1)}, u32[]{:S(2)}, u32[]{:S(2)}) collective-permute-start(bf16[8,256,128]{2,1,0:T(8,128)(2,1)S(1)} %get-tuple-element.367), channel_id=1, source_target_pairs={{0,4},{4,0},{8,12},{12,8},{16,20},{20,16},{24,28},{28,24},{1,5},{5... | collective-permute-start | bytes 1572872 | tf_op jit(solution)/shard_map/ppermute | solution.py:1032
  137.3 11.0 %collective-permute-start.33 = (bf16[1024,128]{1,0:T(8,128)(2,1)S(1)}, bf16[1024,128]{1,0:T(8,128)(2,1)S(1)}, u32[]{:S(2)}, u32[]{:S(2)}) collective-permute-start(bf16[1024,128]{1,0:T(8,128)(2,1)S(1)} %get-tuple-element.364), channel_id=1, source_target_pairs={{0,2},{1,3},{2,0},{3,1},{4,6},{5,7},{6,4},{7,5},{8,10},{9,11},{10,... | collective-permute-start | bytes 786440 | tf_op jit(solution)/shard_map/ppermute | solution.py:1032
  138.2 13.0 %collective-permute-start.34 = (bf16[1024,128]{1,0:T(8,128)(2,1)S(1)}, bf16[1024,128]{1,0:T(8,128)(2,1)S(1)}, u32[]{:S(2)}, u32[]{:S(2)}) collective-permute-start(bf16[1024,128]{1,0:T(8,128)(2,1)S(1)} %get-tuple-element.365), channel_id=1, source_target_pairs={{0,3},{1,2},{2,1},{3,0},{4,7},{5,6},{6,5},{7,4},{8,11},{9,10},{10,... | collective-permute-start | bytes 786440 | tf_op jit(solution)/shard_map/ppermute | solution.py:1032
  158.0 25.7 %collective-permute-start.43 = (bf16[9,256,128]{2,1,0:T(8,128)(2,1)S(1)}, bf16[9,256,128]{2,1,0:T(8,128)(2,1)S(1)}, u32[]{:S(2)}, u32[]{:S(2)}) collective-permute-start(bf16[9,256,128]{2,1,0:T(8,128)(2,1)S(1)} %get-tuple-element.418), channel_id=1, source_target_pairs={{0,4},{4,0},{8,12},{12,8},{16,20},{20,16},{24,28},{28,24},{1,5},{5... | collective-permute-start | bytes 1769480 | tf_op jit(solution)/shard_map/ppermute | solution.py:1032
  159.0 19.2 %collective-permute-start.39 = (bf16[1024,128]{1,0:T(8,128)(2,1)S(1)}, bf16[1024,128]{1,0:T(8,128)(2,1)S(1)}, u32[]{:S(2)}, u32[]{:S(2)}) collective-permute-start(bf16[1024,128]{1,0:T(8,128)(2,1)S(1)} %get-tuple-element.398), channel_id=1, source_target_pairs={{0,1},{1,0},{2,3},{3,2},{4,5},{5,4},{6,7},{7,6},{8,9},{9,8},{10,11... | collective-permute-start | bytes 786440 | tf_op jit(solution)/shard_map/ppermute | solution.py:1032
  159.0 19.2 %collective-permute-start.40 = (bf16[1024,128]{1,0:T(8,128)(2,1)S(1)}, bf16[1024,128]{1,0:T(8,128)(2,1)S(1)}, u32[]{:S(2)}, u32[]{:S(2)}) collective-permute-start(bf16[1024,128]{1,0:T(8,128)(2,1)S(1)} %get-tuple-element.399), channel_id=1, source_target_pairs={{0,2},{1,3},{2,0},{3,1},{4,6},{5,7},{6,4},{7,5},{8,10},{9,11},{10,... | collective-permute-start | bytes 786440 | tf_op jit(solution)/shard_map/ppermute | solution.py:1032
  160.5 17.7 %collective-permute-start.41 = (bf16[1024,128]{1,0:T(8,128)(2,1)S(1)}, bf16[1024,128]{1,0:T(8,128)(2,1)S(1)}, u32[]{:S(2)}, u32[]{:S(2)}) collective-permute-start(bf16[1024,128]{1,0:T(8,128)(2,1)S(1)} %get-tuple-element.400), channel_id=1, source_target_pairs={{0,3},{1,2},{2,1},{3,0},{4,7},{5,6},{6,5},{7,4},{8,11},{9,10},{10,... | collective-permute-start | bytes 786440 | tf_op jit(solution)/shard_map/ppermute | solution.py:1032
  183.1 16.2 %collective-permute-start.46 = (bf16[9,256,128]{2,1,0:T(8,128)(2,1)S(1)}, bf16[9,256,128]{2,1,0:T(8,128)(2,1)S(1)}, u32[]{:S(2)}, u32[]{:S(2)}) collective-permute-start(bf16[9,256,128]{2,1,0:T(8,128)(2,1)S(1)} %get-tuple-element.438), channel_id=1, source_target_pairs={{0,4},{4,0},{8,12},{12,8},{16,20},{20,16},{24,28},{28,24},{1,5},{5... | collective-permute-start | bytes 1769480 | tf_op jit(solution)/shard_map/ppermute | solution.py:1032
  184.4 19.7 %collective-permute-start.50 = (bf16[2,1024,128]{2,1,0:T(8,128)(2,1)S(1)}, bf16[2,1024,128]{2,1,0:T(8,128)(2,1)S(1)}, u32[]{:S(2)}, u32[]{:S(2)}) collective-permute-start(bf16[2,1024,128]{2,1,0:T(8,128)(2,1)S(1)} %copy-done.14), channel_id=1, source_target_pairs={{0,2},{1,3},{2,0},{3,1},{4,6},{5,7},{6,4},{7,5},{8,10},{9,11},{10,... | collective-permute-start | bytes 1572872 | tf_op jit(solution)/shard_map/ppermute | solution.py:1032
  199.9 11.6 %collective-permute-start.49 = (bf16[9,128,128]{2,1,0:T(8,128)(2,1)S(1)}, bf16[9,128,128]{2,1,0:T(8,128)(2,1)S(1)}, u32[]{:S(2)}, u32[]{:S(2)}) collective-permute-start(bf16[9,128,128]{2,1,0:T(8,128)(2,1)S(1)} %get-tuple-element.453), channel_id=1, source_target_pairs={{0,8},{4,12},{8,0},{12,4},{16,24},{20,28},{24,16},{28,20},{1,9},{5... | collective-permute-start | bytes 884744 | tf_op jit(solution)/shard_map/ppermute | solution.py:1032
  211.5 20.4 %collective-permute-start.54 = (bf16[2,1056,128]{2,1,0:T(8,128)(2,1)S(1)}, bf16[2,1056,128]{2,1,0:T(8,128)(2,1)S(1)}, u32[]{:S(2)}, u32[]{:S(2)}) collective-permute-start(bf16[2,1056,128]{2,1,0:T(8,128)(2,1)S(1)} %get-tuple-element.466), channel_id=1, source_target_pairs={{0,2},{1,3},{2,0},{3,1},{4,6},{5,7},{6,4},{7,5},{8,10},{9,11},{10,... | collective-permute-start | bytes 1622024 | tf_op jit(solution)/shard_map/ppermute | solution.py:1032
  226.1 18.5 %collective-permute-start.60 = (bf16[9,256,128]{2,1,0:T(8,128)(2,1)S(1)}, bf16[9,256,128]{2,1,0:T(8,128)(2,1)S(1)}, u32[]{:S(2)}, u32[]{:S(2)}) collective-permute-start(bf16[9,256,128]{2,1,0:T(8,128)(2,1)S(1)} %join.10.mine), channel_id=1, source_target_pairs={{0,4},{4,0},{8,12},{12,8},{16,20},{20,16},{24,28},{28,24},{1,5},{5... | collective-permute-start | bytes 1769480 | tf_op jit(solution)/shard_map/ppermute | solution.py:1032
  252.1 13.3 %collective-permute-start.62 = (bf16[9,256,128]{2,1,0:T(8,128)(2,1)S(1)}, bf16[9,256,128]{2,1,0:T(8,128)(2,1)S(1)}, u32[]{:S(2)}, u32[]{:S(2)}) collective-permute-start(bf16[9,256,128]{2,1,0:T(8,128)(2,1)S(1)} %join.9.mine), channel_id=1, source_target_pairs={{0,4},{4,0},{8,12},{12,8},{16,20},{20,16},{24,28},{28,24},{1,5},{5... | collective-permute-start | bytes 1769480 | tf_op jit(solution)/shard_map/ppermute | solution.py:1032
  (57 other events, 363.5 us)

commit v8 on v7

--- a/solution.py
+++ b/solution.py
@@ -1332,9 +1332,15 @@
     got2 = swap(send2, "dp", 1)
     wide2, att = tie(wide2, att)
     att = down(att, 2)
-    wide2, att[0] = tie(wide2, att[0])
-    own2 = weight_own(seconds, wide2)
-    own2, att, field1 = tie(own2, att, field1)
+    field1, wide2, att[0] = tie(field1, wide2, att[0])
+    grad_first = call(
+        kernel_back_conv,
+        "back_conv",
+        block32,
+        [vmem()] * 2,
+        [],
+    )(field1, conv1_all)
+    grad_first, att, wide2 = tie(grad_first, att, wide2)
     for level in range(3, len(levels)):
         att = down(att, level)
     att_own, att_far = call(
@@ -1345,16 +1351,10 @@
         [],
         limit=12,
     )(*att)
-    field1, att_own = tie(field1, att_own)
+    wide2, att_own = tie(wide2, att_own)
     att = [att_own, swap(att_far, "mp", 2)]
-    grad_first = call(
-        kernel_back_conv,
-        "back_conv",
-        block32,
-        [vmem()] * 2,
-        [],
-    )(field1, conv1_all)
-    grad_first, gradients1, att = tie(grad_first, gradients1, att)
+    own2 = weight_own(seconds, wide2)
+    own2, gradients1, att = tie(own2, gradients1, att)
     att = total_sum(att)
     for level in range(len(levels) - 1, 2, -1):
         att = join(across(att, level), digits[level], meta)

time: 268 us -> 267 us (level)
  transfers between devices with their start and end apart: 67 -> 67, of which waited for: 25 -> 24; matrix products, arithmetic and copies ran while one was open for 4% -> 4% of each run, Pallas kernels for 47% -> 47%
where the time goes in v8:
time: 267 us; the launch traced here: 266 us
  Pallas kernels  127 us (48%)
  waiting for transfers between devices  71.5 us (27%)
  starting transfers between devices  54.3 us (20%)
  local copies, waits for them, and re-layouts  6.29 us (2%)
  other arithmetic  2.77 us (1%)
    ppermute x67, waiting for transfers between devices, swap(): return lax.ppermute(value, axis, [(i, i ^ offset) for i in range(size)])  71.5 us
    ppermute x67, starting transfers between devices, swap(): return lax.ppermute(value, axis, [(i, i ^ offset) for i in range(size)])  54.3 us
    pallas_call x1, Pallas kernels, local(): call(kernel_attention, 'attention', [piece, piece, pair_piece] + [block,...  33.8 us
    pallas_call x1, Pallas kernels, local(): call(kernel_second, 'second', [block32, turned, struct((4, pixels, 3 * LA...  13.3 us
    pallas_call x1, Pallas kernels, local(): call(kernel_first, 'first', [block, struct((4, E_ROWS, LANES), F32), turn...  12.7 us
    pallas_call x2, Pallas kernels, weight_send(): call(kernel_weight_send, 'weight_send', [struct((9, C // 2, LANES), BF16)...  9.62 us
    pallas_call x1, Pallas kernels, local(): call(kernel_back_second, 'back_second', [fields, struct((4, S_ROWS, LANES...  9.08 us
    pallas_call x2, Pallas kernels, weight_own(): call(kernel_weight_own, 'weight_own', struct((9, C // 2, LANES), F32), [s...  8.42 us
  transfers between devices with their start and end apart: 67, of which 24 were waited for; matrix products, arithmetic and copies ran while one was open for 4% of the time, Pallas kernels for 47%

profile of v8, /device:TPU:0, one launch (start us, length us, event | category | flops | bytes accessed | tf_op | source)
XLA Modules:
  0.0 266.4 jit_solution(16173155212216754704)
XLA Ops:
  5.9 3.0 %collective-permute-start.2 = (bf16[2304,128]{1,0:T(8,128)(2,1)}, bf16[2304,128]{1,0:T(8,128)(2,1)S(1)}, u32[]{:S(2)}, u32[]{:S(2)}) collective-permute-start(bf16[2304,128]{1,0:T(8,128)(2,1)} %constant_dynamic-slice_fusion.3), channel_id=1, source_target_pairs={{0,2},{1,3},{2,0},{3,1},{4,6},{5,7},{6,4},{7,5},{8,10},{9,11},{10,... | collective-permute-start | bytes 1769480 | tf_op jit(solution)/shard_map/ppermute | solution.py:1032
  14.4 8.9 %collective-permute-done.2.source.w2 = bf16[2304,128]{1,0:T(8,128)(2,1)S(1)} collective-permute-done((bf16[2304,128]{1,0:T(8,128)(2,1)}, bf16[2304,128]{1,0:T(8,128)(2,1)S(1)}, u32[]{:S(2)}, u32[]{:S(2)}) %collective-permute-start.2) | collective-permute-done | bytes 589856 | tf_op jit(solution)/shard_map/ppermute | solution.py:1032
  23.3 2.2 collective-permute-start.7
  27.2 4.0 %collective-permute-done.7.w4 = bf16[1152,128]{1,0:T(8,128)(2,1)S(1)} collective-permute-done((bf16[1152,128]{1,0:T(8,128)(2,1)S(1)}, bf16[1152,128]{1,0:T(8,128)(2,1)S(1)}, u32[]{:S(2)}, u32[]{:S(2)}) %collective-permute-start.7) | collective-permute-done | bytes 294944 | tf_op jit(solution)/shard_map/ppermute | solution.py:1032
  41.1 12.7 %first.1 = (bf16[4,1024,128]{2,1,0:T(8,128)(2,1)S(1)}, f32[4,32,128]{2,1,0:T(8,128)S(1)}, bf16[4,128,1024]{2,1,0:T(8,128)(2,1)S(1)}, f32[4,1024,128]{2,1,0:T(8,1...) custom-call(s32[6]{0:T(128)S(1)} %stack.36.meta, ...), custom_call_target="tpu_custom_call" | custom-call | tf_op jit(solution)/shard_map/first/pallas_call | solution.py:1186
  55.2 2.8 %collective-permute-done.13.source.w2 = bf16[3328,128]{1,0:T(8,128)(2,1)S(1)} collective-permute-done((bf16[3328,128]{1,0:T(8,128)(2,1)S(1)}, bf16[3328,128]{1,0:T(8,128)(2,1)S(1)}, u32[]{:S(2)}, u32[]{:S(2)}) %collective-permute-start.13) | collective-permute-done | bytes 852000 | tf_op jit(solution)/shard_map/ppermute | solution.py:1032
  60.4 9.1 %collective-permute-done.16.w3 = bf16[1664,128]{1,0:T(8,128)(2,1)S(1)} collective-permute-done((bf16[1664,128]{1,0:T(8,128)(2,1)S(1)}, bf16[1664,128]{1,0:T(8,128)(2,1)S(1)}, u32[]{:S(2)}, u32[]{:S(2)}) %collective-permute-start.16) | collective-permute-done | bytes 426016 | tf_op jit(solution)/shard_map/ppermute | solution.py:1032
  73.7 13.3 %second.1 = (f32[4,1024,128]{2,1,0:T(8,128)S(1)}, bf16[4,128,1024]{2,1,0:T(8,128)(2,1)S(1)}, bf16[4,1024,384]{2,1,0:T(8,128)(2,1)S(1)}, bf16[4,1536,128]{2,1,0:T...) custom-call(s32[6]{0:T(128)S(1)} %stack.36.meta, ...), custom_call_target="tpu_custom_call" | custom-call | tf_op jit(solution)/shard_map/second/pallas_call | solution.py:1210
  88.7 2.7 collective-permute-start.27
  91.8 33.8 %attention.1 = (bf16[1024,128]{1,0:T(8,128)(2,1)S(1)}, bf16[1024,128]{1,0:T(8,128)(2,1)S(1)}, bf16[2,1024,128]{2,1,0:T(8,128)(2,1)S(1)}, bf16[4,1024,128]{2,1,0:...) custom-call(s32[6]{0:T(128)S(1)} %stack.36.meta, ...), custom_call_target="tpu_custom_call" | custom-call | tf_op jit(solution)/shard_map/attention/pallas_call | solution.py:1237
  125.7 3.8 %attention_grad.1 = (bf16[2,4,512,128]{3,2,1,0:T(8,128)(2,1)S(1)}, bf16[2,4,512,128]{3,2,1,0:T(8,128)(2,1)S(1)}) custom-call(s32[6]{0:T(128)S(1)} %stack.36.meta, bf16[4,1024,384]{2,1,0:T(8,128)(2,1)S(1)} %get-tuple-element.335.dqkv, bf16[4,1024,128]{2,1,0:T(8,128)(2,1)S(1)} %get-tuple-element.328.mixed, ...), custom_call_target="tpu_custom_call" | custom-call | tf_op jit(solution)/shard_map/attention_grad/pallas_call | solution.py:1293
  130.1 4.6 %back_attention.1 = (f32[4,1024,128]{2,1,0:T(8,128)S(1)}, bf16[3,4,1088,128]{3,2,1,0:T(8,128)(2,1)S(1)}, f32[4,32,128]{2,1,0:T(8,128)S(1)}, bf16[1024,128]{1,0:T...) custom-call(s32[6]{0:T(128)S(1)} %stack.36.meta, ...), custom_call_target="tpu_custom_call" | custom-call | tf_op jit(solution)/shard_map/back_attention/pallas_call | solution.py:1303
  139.1 9.1 %back_second.1 = (bf16[3,4,1088,128]{3,2,1,0:T(8,128)(2,1)S(1)}, f32[4,32,128]{2,1,0:T(8,128)S(1)}, bf16[1024,128]{1,0:T(8,128)(2,1)S(1)}, bf16[1024,128]{1,0:T(...) custom-call(s32[6]{0:T(128)S(1)} %stack.36.meta, ...), custom_call_target="tpu_custom_call" | custom-call | tf_op jit(solution)/shard_map/back_second/pallas_call | solution.py:1318
  148.3 3.0 %collective-permute-done.34.d3 = bf16[1024,128]{1,0:T(8,128)(2,1)S(1)} collective-permute-done((bf16[1024,128]{1,0:T(8,128)(2,1)S(1)}, bf16[1024,128]{1,0:T(8,128)(2,1)S(1)}, u32[]{:S(2)}, u32[]{:S(2)}) %collective-permute-start.34) | collective-permute-done | bytes 262176 | tf_op jit(solution)/shard_map/ppermute | solution.py:1032
  153.2 4.8 %weight_send.2 = (bf16[9,256,128]{2,1,0:T(8,128)(2,1)S(1)}, bf16[3,4,1088,128]{3,2,1,0:T(8,128)(2,1)S(1)}) custom-call(s32[6]{0:T(128)S(1)} %stack.36.meta, bf16[4,128,1024]{2,1,0:T(8,128)(2,1)S(1)} %get-tuple-element.332.u0, bf16[4,128,1024]{2,1,0:T(8,128)(2,1)S(1)} %collective-permute-done.26.u1, bf16[4,128,1024]{2,1,0:T(8,128)(2,1)S(1)} %collective-permute-done.25.u2, ...), custom_call_target="tpu_custom_call" | custom-call | tf_op jit(solution)/shard_map/weight_send/pallas_call | solution.py:1259
  163.5 5.7 %back_conv.1.grad_in = f32[4,1024,128]{2,1,0:T(8,128)S(1)} custom-call(bf16[3,4,1088,128]{3,2,1,0:T(8,128)(2,1)S(1)} %get-tuple-element.389.grad_field, bf16[4,4608,128]{2,1,0:T(8,128)(2,1)S(1)} %get-tuple-element.390.weight), custom_call_target="tpu_custom_call" | custom-call | tf_op jit(solution)/shard_map/back_conv/pallas_call | solution.py:1336
  172.5 4.2 %weight_own.2.refs_0_ = f32[9,256,128]{2,1,0:T(8,128)S(1)} custom-call(s32[6]{0:T(128)S(1)} %stack.36.meta, bf16[4,128,1024]{2,1,0:T(8,128)(2,1)S(1)} %get-tuple-element.332.u0, bf16[4,128,1024]{2,1,0:T(8,128)(2,1)S(1)} %collective-permute-done.26.u1, bf16[4,128,1024]{2,1,0:T(8,128)(2,1)S(1)} %collective-permute-done.25.u2, ...), custom_call_target="tpu_custom_call" | custom-call | tf_op jit(solution)/shard_map/weight_own/pallas_call | solution.py:1269
  176.8 4.8 %weight_send.3 = (bf16[9,256,128]{2,1,0:T(8,128)(2,1)S(1)}, bf16[3,4,1088,128]{3,2,1,0:T(8,128)(2,1)S(1)}) custom-call(s32[6]{0:T(128)S(1)} %stack.36.meta, bf16[4,128,1024]{2,1,0:T(8,128)(2,1)S(1)} %get-tuple-element.344.u0, bf16[4,128,1024]{2,1,0:T(8,128)(2,1)S(1)} %collective-permute-done.30.u1, bf16[4,128,1024]{2,1,0:T(8,128)(2,1)S(1)} %collective-permute-done.29.u2, ...), custom_call_target="tpu_custom_call" | custom-call | tf_op jit(solution)/shard_map/weight_send/pallas_call | solution.py:1259
  184.1 2.6 collective-permute-start.45
  186.7 4.2 %weight_own.3.refs_0_ = f32[9,256,128]{2,1,0:T(8,128)S(1)} custom-call(s32[6]{0:T(128)S(1)} %stack.36.meta, bf16[4,128,1024]{2,1,0:T(8,128)(2,1)S(1)} %get-tuple-element.344.u0, bf16[4,128,1024]{2,1,0:T(8,128)(2,1)S(1)} %collective-permute-done.30.u1, bf16[4,128,1024]{2,1,0:T(8,128)(2,1)S(1)} %collective-permute-done.29.u2, ...), custom_call_target="tpu_custom_call" | custom-call | tf_op jit(solution)/shard_map/weight_own/pallas_call | solution.py:1269
  194.9 2.9 %back_first.1 = (bf16[1056,128]{1,0:T(8,128)(2,1)S(1)}, bf16[1056,128]{1,0:T(8,128)(2,1)S(1)}, bf16[2,1056,128]{2,1,0:T(8,128)(2,1)S(1)}) custom-call(s32[6]{0:T(128)S(1)} %stack.36.meta, f32[4,1024,128]{2,1,0:T(8,128)S(1)} %back_conv.1.grad_in, bf16[4,1024,128]{2,1,0:T(8,128)(2,1)S(1)} %get-tuple-element.301.image, ...), custom_call_target="tpu_custom_call" | custom-call | tf_op jit(solution)/shard_map/back_first/pallas_call | solution.py:1374
  202.7 5.4 %collective-permute-done.48.refs_1_ = bf16[9,64,128]{2,1,0:T(8,128)(2,1)S(1)} collective-permute-done((bf16[9,64,128]{2,1,0:T(8,128)(2,1)S(1)}, bf16[9,64,128]{2,1,0:T(8,128)(2,1)S(1)}, u32[]{:S(2)}, u32[]{:S(2)}) %collective-permute-start.48) | collective-permute-done | bytes 147488 | tf_op jit(solution)/shard_map/ppermute | solution.py:1032
  214.6 5.4 %collective-permute-done.52.refs_1_ = bf16[9,64,128]{2,1,0:T(8,128)(2,1)S(1)} collective-permute-done((bf16[9,64,128]{2,1,0:T(8,128)(2,1)S(1)}, bf16[9,64,128]{2,1,0:T(8,128)(2,1)S(1)}, u32[]{:S(2)}, u32[]{:S(2)}) %collective-permute-start.52) | collective-permute-done | bytes 147488 | tf_op jit(solution)/shard_map/ppermute | solution.py:1032
  220.1 2.2 collective-permute-done.51.refs_1_
  224.2 2.6 collective-permute-start.60
  226.9 3.1 %collective-permute-done.55.refs_1_ = bf16[4,128,128]{2,1,0:T(8,128)(2,1)S(1)} collective-permute-done((bf16[4,128,128]{2,1,0:T(8,128)(2,1)S(1)}, bf16[4,128,128]{2,1,0:T(8,128)(2,1)S(1)}, u32[]{:S(2)}, u32[]{:S(2)}) %collective-permute-start.55) | collective-permute-done | bytes 131104 | tf_op jit(solution)/shard_map/ppermute | solution.py:1032
  234.1 6.0 %collective-permute-done.56.refs_1_ = bf16[9,128,128]{2,1,0:T(8,128)(2,1)S(1)} collective-permute-done((bf16[9,128,128]{2,1,0:T(8,128)(2,1)S(1)}, bf16[9,128,128]{2,1,0:T(8,128)(2,1)S(1)}, u32[]{:S(2)}, u32[]{:S(2)}) %collective-permute-start.56) | collective-permute-done | bytes 294944 | tf_op jit(solution)/shard_map/ppermute | solution.py:1032
  240.7 3.4 %collective-permute-done.61.other = bf16[4,256,128]{2,1,0:T(8,128)(2,1)S(1)} collective-permute-done((bf16[4,256,128]{2,1,0:T(8,128)(2,1)S(1)}, bf16[4,256,128]{2,1,0:T(8,128)(2,1)S(1)}, u32[]{:S(2)}, u32[]{:S(2)}) %collective-permute-start.61) | collective-permute-done | bytes 262176 | tf_op jit(solution)/shard_map/ppermute | solution.py:1032
  244.8 4.9 %collective-permute-done.63.refs_1_ = bf16[8,32,128]{2,1,0:T(8,128)(2,1)S(1)} collective-permute-done((bf16[8,32,128]{2,1,0:T(8,128)(2,1)S(1)}, bf16[8,32,128]{2,1,0:T(8,128)(2,1)S(1)}, u32[]{:S(2)}, u32[]{:S(2)}) %collective-permute-start.63) | collective-permute-done | bytes 65568 | tf_op jit(solution)/shard_map/ppermute | solution.py:1032
  254.9 2.1 last_join.3
  257.5 4.6 %factor_grads.1 = (f32[2048,2,128]{2,1,0:T(2,128)}, f32[2048,2,128]{2,1,0:T(2,128)}, f32[32,128]{1,0:T(8,128)S(1)}) custom-call(f32[8,128]{1,0:T(8,128)S(1)} %scale.1, bf16[2048,256]{1,0:T(8,128)(2,1)S(1)} %factors.1.left, bf16[16,32,128]{2,1,0:T(8,128)(2,1)S(1)} %stack.42.small0, bf16[16,32,128]{2,1,0:T(8,128)(2,1)S(1)} %collective-permute-done.64.small1), custom_call_target="tpu_custom_call" | custom-call | tf_op jit(solution)/shard_map/factor_grads/pallas_call | solution.py:1446
  264.3 2.1 last_join.5
  (211 shorter events, 80.3 us)
Async XLA Ops:
  1.4 21.8 %collective-permute-start = (bf16[4608,128]{1,0:T(8,128)(2,1)}, bf16[4608,128]{1,0:T(8,128)(2,1)S(1)}, u32[]{:S(2)}, u32[]{:S(2)}) collective-permute-start(bf16[4608,128]{1,0:T(8,128)(2,1)} %bitcast.80), channel_id=1, source_target_pairs={{0,1},{1,0},{2,3},{3,2},{4,5},{5,4},{6,7},{7,6},{8,9},{9,8},{10,11... | collective-permute-start | bytes 3538952 | tf_op jit(solution)/shard_map/ppermute | solution.py:1032
  5.9 17.3 %collective-permute-start.2 = (bf16[2304,128]{1,0:T(8,128)(2,1)}, bf16[2304,128]{1,0:T(8,128)(2,1)S(1)}, u32[]{:S(2)}, u32[]{:S(2)}) collective-permute-start(bf16[2304,128]{1,0:T(8,128)(2,1)} %constant_dynamic-slice_fusion.3), channel_id=1, source_target_pairs={{0,2},{1,3},{2,0},{3,1},{4,6},{5,7},{6,4},{7,5},{8,10},{9,11},{10,... | collective-permute-start | bytes 1769480 | tf_op jit(solution)/shard_map/ppermute | solution.py:1032
  9.7 24.4 %collective-permute-start.3 = (bf16[2,1024,128]{2,1,0:T(8,128)(2,1)}, bf16[2,1024,128]{2,1,0:T(8,128)(2,1)}, u32[]{:S(2)}, u32[]{:S(2)}) collective-permute-start(bf16[2,1024,128]{2,1,0:T(8,128)(2,1)} %pad_maximum_fusion.1), channel_id=1, source_target_pairs={{0,2},{1,3},{2,0},{3,1},{4,6},{5,7},{6,4},{7,5},{8,10},{9,11},{10,... | collective-permute-start | bytes 1572872 | tf_op jit(solution)/shard_map/ppermute | solution.py:1032
  36.5 21.4 %collective-permute-start.14 = (bf16[6656,128]{1,0:T(8,128)(2,1)S(1)}, bf16[6656,128]{1,0:T(8,128)(2,1)S(1)}, u32[]{:S(2)}, u32[]{:S(2)}) collective-permute-start(bf16[6656,128]{1,0:T(8,128)(2,1)S(1)} %pad_maximum_fusion.w0), channel_id=1, source_target_pairs={{0,1},{1,0},{2,3},{3,2},{4,5},{5,4},{6,7},{7,6},{8,9},{9,8},{10,11... | collective-permute-start | bytes 5111816 | tf_op jit(solution)/shard_map/ppermute | solution.py:1032
  36.6 21.4 %collective-permute-start.13 = (bf16[3328,128]{1,0:T(8,128)(2,1)S(1)}, bf16[3328,128]{1,0:T(8,128)(2,1)S(1)}, u32[]{:S(2)}, u32[]{:S(2)}) collective-permute-start(bf16[3328,128]{1,0:T(8,128)(2,1)S(1)} %constant_dynamic-slice_fusion), channel_id=1, source_target_pairs={{0,2},{1,3},{2,0},{3,1},{4,6},{5,7},{6,4},{7,5},{8,10},{9,11},{10,... | collective-permute-start | bytes 2555912 | tf_op jit(solution)/shard_map/ppermute | solution.py:1032
  38.3 16.8 %collective-permute-start.15 = (bf16[1,4,8,2048]{3,2,1,0:T(8,128)(2,1)S(1)}, bf16[1,4,8,2048]{3,2,1,0:T(8,128)(2,1)S(1)}, u32[]{:S(2)}, u32[]{:S(2)}) collective-permute-start(bf16[1,4,8,2048]{3,2,1,0:T(8,128)(2,1)S(1)} %fusion.9.refs_0_), channel_id=1, source_target_pairs={{0,4},{4,0},{8,12},{12,8},{16,20},{20,16},{24,28},{28,24},{1,5},{5... | collective-permute-start | bytes 393224 | tf_op jit(solution)/shard_map/ppermute | solution.py:1032
  58.0 11.4 %collective-permute-start.16 = (bf16[1664,128]{1,0:T(8,128)(2,1)S(1)}, bf16[1664,128]{1,0:T(8,128)(2,1)S(1)}, u32[]{:S(2)}, u32[]{:S(2)}) collective-permute-start(bf16[1664,128]{1,0:T(8,128)(2,1)S(1)} %get-tuple-element.298), channel_id=1, source_target_pairs={{0,4},{4,0},{8,12},{12,8},{16,20},{20,16},{24,28},{28,24},{1,5},{5... | collective-permute-start | bytes 1277960 | tf_op jit(solution)/shard_map/ppermute | solution.py:1032
  60.4 13.3 %collective-permute-start.18 = (bf16[3328,128]{1,0:T(8,128)(2,1)S(1)}, bf16[3328,128]{1,0:T(8,128)(2,1)S(1)}, u32[]{:S(2)}, u32[]{:S(2)}) collective-permute-start(bf16[3328,128]{1,0:T(8,128)(2,1)S(1)} %collective-permute-done.13.source.w2), channel_id=1, source_target_pairs={{0,1},{1,0},{2,3},{3,2},{4,5},{5,4},{6,7},{7,6},{8,9},{9,8},{10,11... | collective-permute-start | bytes 2555912 | tf_op jit(solution)/shard_map/ppermute | solution.py:1032
  70.7 16.4 %collective-permute-start.22 = (bf16[1024,128]{1,0:T(8,128)(2,1)S(1)}, bf16[1024,128]{1,0:T(8,128)(2,1)S(1)}, u32[]{:S(2)}, u32[]{:S(2)}) collective-permute-start(bf16[1024,128]{1,0:T(8,128)(2,1)S(1)} %get-tuple-element.317), channel_id=1, source_target_pairs={{0,1},{1,0},{2,3},{3,2},{4,5},{5,4},{6,7},{7,6},{8,9},{9,8},{10,11... | collective-permute-start | bytes 786440 | tf_op jit(solution)/shard_map/ppermute | solution.py:1032
  71.2 15.9 %collective-permute-start.23 = (bf16[1024,128]{1,0:T(8,128)(2,1)S(1)}, bf16[1024,128]{1,0:T(8,128)(2,1)S(1)}, u32[]{:S(2)}, u32[]{:S(2)}) collective-permute-start(bf16[1024,128]{1,0:T(8,128)(2,1)S(1)} %get-tuple-element.318), channel_id=1, source_target_pairs={{0,2},{1,3},{2,0},{3,1},{4,6},{5,7},{6,4},{7,5},{8,10},{9,11},{10,... | collective-permute-start | bytes 786440 | tf_op jit(solution)/shard_map/ppermute | solution.py:1032
  72.7 14.3 %collective-permute-start.24 = (bf16[1024,128]{1,0:T(8,128)(2,1)S(1)}, bf16[1024,128]{1,0:T(8,128)(2,1)S(1)}, u32[]{:S(2)}, u32[]{:S(2)}) collective-permute-start(bf16[1024,128]{1,0:T(8,128)(2,1)S(1)} %get-tuple-element.319), channel_id=1, source_target_pairs={{0,3},{1,2},{2,1},{3,0},{4,7},{5,6},{6,5},{7,4},{8,11},{9,10},{10,... | collective-permute-start | bytes 786440 | tf_op jit(solution)/shard_map/ppermute | solution.py:1032
  72.8 14.2 %collective-permute-start.21 = (bf16[2,4,8,2048]{3,2,1,0:T(8,128)(2,1)S(1)}, bf16[2,4,8,2048]{3,2,1,0:T(8,128)(2,1)S(1)}, u32[]{:S(2)}, u32[]{:S(2)}) collective-permute-start(bf16[2,4,8,2048]{3,2,1,0:T(8,128)(2,1)S(1)} %stack.38.refs_0_), channel_id=1, source_target_pairs={{0,8},{4,12},{8,0},{12,4},{16,24},{20,28},{24,16},{28,20},{1,9},{5... | collective-permute-start | bytes 786440 | tf_op jit(solution)/shard_map/ppermute | solution.py:1032
  87.1 42.4 %collective-permute-start.25 = (bf16[4,128,1024]{2,1,0:T(8,128)(2,1)S(1)}, bf16[4,128,1024]{2,1,0:T(8,128)(2,1)S(1)}, u32[]{:S(2)}, u32[]{:S(2)}) collective-permute-start(bf16[4,128,1024]{2,1,0:T(8,128)(2,1)S(1)} %get-tuple-element.332.u0), channel_id=1, source_target_pairs={{0,2},{1,3},{2,0},{3,1},{4,6},{5,7},{6,4},{7,5},{8,10},{9,11},{10,... | collective-permute-start | bytes 3145736 | tf_op jit(solution)/shard_map/ppermute | solution.py:1032
  88.4 41.1 %collective-permute-start.26 = (bf16[4,128,1024]{2,1,0:T(8,128)(2,1)S(1)}, bf16[4,128,1024]{2,1,0:T(8,128)(2,1)S(1)}, u32[]{:S(2)}, u32[]{:S(2)}) collective-permute-start(bf16[4,128,1024]{2,1,0:T(8,128)(2,1)S(1)} %get-tuple-element.332.u0), channel_id=1, source_target_pairs={{0,1},{1,0},{2,3},{3,2},{4,5},{5,4},{6,7},{7,6},{8,9},{9,8},{10,11... | collective-permute-start | bytes 3145736 | tf_op jit(solution)/shard_map/ppermute | solution.py:1032
  88.7 40.8 %collective-permute-start.27 = (bf16[4,4,8,2048]{3,2,1,0:T(8,128)(2,1)S(1)}, bf16[4,4,8,2048]{3,2,1,0:T(8,128)(2,1)S(1)}, u32[]{:S(2)}, u32[]{:S(2)}) collective-permute-start(bf16[4,4,8,2048]{3,2,1,0:T(8,128)(2,1)S(1)} %stack.39.factors0), channel_id=1, source_target_pairs={{0,16},{4,20},{8,24},{12,28},{16,0},{20,4},{24,8},{28,12},{1,17},{... | collective-permute-start | bytes 1572872 | tf_op jit(solution)/shard_map/ppermute | solution.py:1032
  91.3 43.6 %collective-permute-start.29 = (bf16[4,128,1024]{2,1,0:T(8,128)(2,1)S(1)}, bf16[4,128,1024]{2,1,0:T(8,128)(2,1)S(1)}, u32[]{:S(2)}, u32[]{:S(2)}) collective-permute-start(bf16[4,128,1024]{2,1,0:T(8,128)(2,1)S(1)} %get-tuple-element.344.u0), channel_id=1, source_target_pairs={{0,2},{1,3},{2,0},{3,1},{4,6},{5,7},{6,4},{7,5},{8,10},{9,11},{10,... | collective-permute-start | bytes 3145736 | tf_op jit(solution)/shard_map/ppermute | solution.py:1032
  91.8 43.1 %collective-permute-start.30 = (bf16[4,128,1024]{2,1,0:T(8,128)(2,1)S(1)}, bf16[4,128,1024]{2,1,0:T(8,128)(2,1)S(1)}, u32[]{:S(2)}, u32[]{:S(2)}) collective-permute-start(bf16[4,128,1024]{2,1,0:T(8,128)(2,1)S(1)} %get-tuple-element.344.u0), channel_id=1, source_target_pairs={{0,1},{1,0},{2,3},{3,2},{4,5},{5,4},{6,7},{7,6},{8,9},{9,8},{10,11... | collective-permute-start | bytes 3145736 | tf_op jit(solution)/shard_map/ppermute | solution.py:1032
  134.9 16.3 %collective-permute-start.36 = (bf16[4,128,1024]{2,1,0:T(8,128)(2,1)S(1)}, bf16[4,128,1024]{2,1,0:T(8,128)(2,1)S(1)}, u32[]{:S(2)}, u32[]{:S(2)}) collective-permute-start(bf16[4,128,1024]{2,1,0:T(8,128)(2,1)S(1)} %collective-permute-done.29.u2), channel_id=1, source_target_pairs={{0,1},{1,0},{2,3},{3,2},{4,5},{5,4},{6,7},{7,6},{8,9},{9,8},{10,11... | collective-permute-start | bytes 3145736 | tf_op jit(solution)/shard_map/ppermute | solution.py:1032
  136.1 15.1 %collective-permute-start.35 = (bf16[8,256,128]{2,1,0:T(8,128)(2,1)S(1)}, bf16[8,256,128]{2,1,0:T(8,128)(2,1)S(1)}, u32[]{:S(2)}, u32[]{:S(2)}) collective-permute-start(bf16[8,256,128]{2,1,0:T(8,128)(2,1)S(1)} %get-tuple-element.369), channel_id=1, source_target_pairs={{0,4},{4,0},{8,12},{12,8},{16,20},{20,16},{24,28},{28,24},{1,5},{5... | collective-permute-start | bytes 1572872 | tf_op jit(solution)/shard_map/ppermute | solution.py:1032
  138.2 13.0 %collective-permute-start.34 = (bf16[1024,128]{1,0:T(8,128)(2,1)S(1)}, bf16[1024,128]{1,0:T(8,128)(2,1)S(1)}, u32[]{:S(2)}, u32[]{:S(2)}) collective-permute-start(bf16[1024,128]{1,0:T(8,128)(2,1)S(1)} %get-tuple-element.367), channel_id=1, source_target_pairs={{0,3},{1,2},{2,1},{3,0},{4,7},{5,6},{6,5},{7,4},{8,11},{9,10},{10,... | collective-permute-start | bytes 786440 | tf_op jit(solution)/shard_map/ppermute | solution.py:1032
  158.0 24.2 %collective-permute-start.43 = (bf16[9,256,128]{2,1,0:T(8,128)(2,1)S(1)}, bf16[9,256,128]{2,1,0:T(8,128)(2,1)S(1)}, u32[]{:S(2)}, u32[]{:S(2)}) collective-permute-start(bf16[9,256,128]{2,1,0:T(8,128)(2,1)S(1)} %get-tuple-element.420), channel_id=1, source_target_pairs={{0,4},{4,0},{8,12},{12,8},{16,20},{20,16},{24,28},{28,24},{1,5},{5... | collective-permute-start | bytes 1769480 | tf_op jit(solution)/shard_map/ppermute | solution.py:1032
  159.0 17.7 %collective-permute-start.39 = (bf16[1024,128]{1,0:T(8,128)(2,1)S(1)}, bf16[1024,128]{1,0:T(8,128)(2,1)S(1)}, u32[]{:S(2)}, u32[]{:S(2)}) collective-permute-start(bf16[1024,128]{1,0:T(8,128)(2,1)S(1)} %get-tuple-element.403), channel_id=1, source_target_pairs={{0,1},{1,0},{2,3},{3,2},{4,5},{5,4},{6,7},{7,6},{8,9},{9,8},{10,11... | collective-permute-start | bytes 786440 | tf_op jit(solution)/shard_map/ppermute | solution.py:1032
  159.0 17.7 %collective-permute-start.40 = (bf16[1024,128]{1,0:T(8,128)(2,1)S(1)}, bf16[1024,128]{1,0:T(8,128)(2,1)S(1)}, u32[]{:S(2)}, u32[]{:S(2)}) collective-permute-start(bf16[1024,128]{1,0:T(8,128)(2,1)S(1)} %get-tuple-element.404), channel_id=1, source_target_pairs={{0,2},{1,3},{2,0},{3,1},{4,6},{5,7},{6,4},{7,5},{8,10},{9,11},{10,... | collective-permute-start | bytes 786440 | tf_op jit(solution)/shard_map/ppermute | solution.py:1032
  160.5 16.3 %collective-permute-start.41 = (bf16[1024,128]{1,0:T(8,128)(2,1)S(1)}, bf16[1024,128]{1,0:T(8,128)(2,1)S(1)}, u32[]{:S(2)}, u32[]{:S(2)}) collective-permute-start(bf16[1024,128]{1,0:T(8,128)(2,1)S(1)} %get-tuple-element.405), channel_id=1, source_target_pairs={{0,3},{1,2},{2,1},{3,0},{4,7},{5,6},{6,5},{7,4},{8,11},{9,10},{10,... | collective-permute-start | bytes 786440 | tf_op jit(solution)/shard_map/ppermute | solution.py:1032
  181.6 16.2 %collective-permute-start.46 = (bf16[9,256,128]{2,1,0:T(8,128)(2,1)S(1)}, bf16[9,256,128]{2,1,0:T(8,128)(2,1)S(1)}, u32[]{:S(2)}, u32[]{:S(2)}) collective-permute-start(bf16[9,256,128]{2,1,0:T(8,128)(2,1)S(1)} %get-tuple-element.440), channel_id=1, source_target_pairs={{0,4},{4,0},{8,12},{12,8},{16,20},{20,16},{24,28},{28,24},{1,5},{5... | collective-permute-start | bytes 1769480 | tf_op jit(solution)/shard_map/ppermute | solution.py:1032
  183.0 19.7 %collective-permute-start.50 = (bf16[2,1024,128]{2,1,0:T(8,128)(2,1)S(1)}, bf16[2,1024,128]{2,1,0:T(8,128)(2,1)S(1)}, u32[]{:S(2)}, u32[]{:S(2)}) collective-permute-start(bf16[2,1024,128]{2,1,0:T(8,128)(2,1)S(1)} %copy-done.14), channel_id=1, source_target_pairs={{0,2},{1,3},{2,0},{3,1},{4,6},{5,7},{6,4},{7,5},{8,10},{9,11},{10,... | collective-permute-start | bytes 1572872 | tf_op jit(solution)/shard_map/ppermute | solution.py:1032
  198.4 11.6 %collective-permute-start.49 = (bf16[9,128,128]{2,1,0:T(8,128)(2,1)S(1)}, bf16[9,128,128]{2,1,0:T(8,128)(2,1)S(1)}, u32[]{:S(2)}, u32[]{:S(2)}) collective-permute-start(bf16[9,128,128]{2,1,0:T(8,128)(2,1)S(1)} %get-tuple-element.455), channel_id=1, source_target_pairs={{0,8},{4,12},{8,0},{12,4},{16,24},{20,28},{24,16},{28,20},{1,9},{5... | collective-permute-start | bytes 884744 | tf_op jit(solution)/shard_map/ppermute | solution.py:1032
  210.0 20.0 %collective-permute-start.54 = (bf16[2,1056,128]{2,1,0:T(8,128)(2,1)S(1)}, bf16[2,1056,128]{2,1,0:T(8,128)(2,1)S(1)}, u32[]{:S(2)}, u32[]{:S(2)}) collective-permute-start(bf16[2,1056,128]{2,1,0:T(8,128)(2,1)S(1)} %get-tuple-element.468), channel_id=1, source_target_pairs={{0,2},{1,3},{2,0},{3,1},{4,6},{5,7},{6,4},{7,5},{8,10},{9,11},{10,... | collective-permute-start | bytes 1622024 | tf_op jit(solution)/shard_map/ppermute | solution.py:1032
  224.2 19.9 %collective-permute-start.60 = (bf16[9,256,128]{2,1,0:T(8,128)(2,1)S(1)}, bf16[9,256,128]{2,1,0:T(8,128)(2,1)S(1)}, u32[]{:S(2)}, u32[]{:S(2)}) collective-permute-start(bf16[9,256,128]{2,1,0:T(8,128)(2,1)S(1)} %join.10.mine), channel_id=1, source_target_pairs={{0,4},{4,0},{8,12},{12,8},{16,20},{20,16},{24,28},{28,24},{1,5},{5... | collective-permute-start | bytes 1769480 | tf_op jit(solution)/shard_map/ppermute | solution.py:1032
  231.9 12.2 %collective-permute-start.61 = (bf16[4,256,128]{2,1,0:T(8,128)(2,1)S(1)}, bf16[4,256,128]{2,1,0:T(8,128)(2,1)S(1)}, u32[]{:S(2)}, u32[]{:S(2)}) collective-permute-start(bf16[4,256,128]{2,1,0:T(8,128)(2,1)S(1)} %join.11.mine), channel_id=1, source_target_pairs={{0,4},{4,0},{8,12},{12,8},{16,20},{20,16},{24,28},{28,24},{1,5},{5... | collective-permute-start | bytes 786440 | tf_op jit(solution)/shard_map/ppermute | solution.py:1032
  233.1 11.4 %collective-permute-start.59 = (bf16[4,32,128]{2,1,0:T(8,128)(2,1)S(1)}, bf16[4,32,128]{2,1,0:T(8,128)(2,1)S(1)}, u32[]{:S(2)}, u32[]{:S(2)}) collective-permute-start(bf16[4,32,128]{2,1,0:T(8,128)(2,1)S(1)} %stack.40.refs_0_), channel_id=1, source_target_pairs={{0,4},{4,0},{8,12},{12,8},{16,20},{20,16},{24,28},{28,24},{1,5},{5... | collective-permute-start | bytes 98312 | tf_op jit(solution)/shard_map/ppermute | solution.py:1032
  250.4 13.9 %collective-permute-start.62 = (bf16[9,256,128]{2,1,0:T(8,128)(2,1)S(1)}, bf16[9,256,128]{2,1,0:T(8,128)(2,1)S(1)}, u32[]{:S(2)}, u32[]{:S(2)}) collective-permute-start(bf16[9,256,128]{2,1,0:T(8,128)(2,1)S(1)} %join.9.mine), channel_id=1, source_target_pairs={{0,4},{4,0},{8,12},{12,8},{16,20},{20,16},{24,28},{28,24},{1,5},{5... | collective-permute-start | bytes 1769480 | tf_op jit(solution)/shard_map/ppermute | solution.py:1032
  (57 other events, 362.1 us)
